TPU v7x, 128 devices: a whole 4x4x4 slice. The times are simulated.
128 devices in a mesh: ens: 4 (over z_hi, core), elem: 32 (over y, z_lo, x).
Axes of the slice: x: 4, y: 4, z: 4 (z_hi: 2, z_lo: 2; z = z_hi * 2 + z_lo), core: 2. Of those that a mesh axis runs over, the one named last changes fastest.
Arguments:
- scalars: float32 [8, 512, 4096], P('ens', None, 'elem'), parts along dimension 0, may hold values from -6 to 6
- transport: float32 [3, 512, 4096], P(None, None, 'elem'), may hold values from -6 to 6
- mass: float32 [512, 4096], P(None, 'elem'), may hold values from 0.5 to 2
- element_order: int32 [32, 128], P('elem'), may hold values from 0 to 127, each once within a row
Outputs:
- advected: float32 [8, 512, 4096], P('ens', None, 'elem'), parts along dimension 0
There are 4 independent parts, one for each index of `ens`. A program takes and returns all parts, laid end to end along the dimension named above; an argument that names none is the same for every part. Nothing has to cross between parts.
Inputs may be any that keep to these rules, and one draw needn't show every extreme that they name: `element_order`: each row is a permutation of the device's slots.
All inputs are finite; a program needn't handle non-finite values.
Results may differ from a plain program's by a relative error of at most 0.0001.
Values sent between devices are 32-bit elements; how exact they have to be, the bound alone decides.
No kernel may reach another device: no remote copies, remote signals or barrier semaphores. Data moves between devices by JAX's collectives and lax.ppermute only.
A program may use at most 64 MiB of HBM per device.

v0:
```python
import jax
import jax.numpy as jnp
import numpy as np
from jax import lax
from jax.experimental import pallas as pl
from jax.experimental.pallas import tpu as pltpu
from jax.sharding import PartitionSpec as P

ORDER = 7
EXT = ORDER + 1
SUBSTEPS = 2
STAGES = 4
EY = 8
EZ = 16
LANES = EY * EZ
SUB = 8

time_step = 0.015


def legendre_table(points, degree):
    table = np.zeros((points.shape[0], degree + 1))
    table[:, 0] = 1.0
    table[:, 1] = points
    for level in range(2, degree + 1):
        table[:, level] = (
            (2 * level - 1) * points * table[:, level - 1] - (level - 1) * table[:, level - 2]
        ) / level
    return table


def gll_derivative(degree):
    extent = degree + 1
    points = np.cos(np.pi * np.arange(extent) / degree)
    for sweep in range(60):
        table = legendre_table(points, degree)
        points = points - (points * table[:, degree] - table[:, degree - 1]) / (
            extent * table[:, degree]
        )
    points = points[::-1].copy()
    values = legendre_table(points, degree)[:, degree]
    matrix = np.zeros((extent, extent))
    for target in range(extent):
        for source in range(extent):
            if target != source:
                matrix[target, source] = values[target] / (
                    values[source] * (points[target] - points[source])
                )
    matrix[0, 0] = -degree * (degree + 1) / 4.0
    matrix[extent - 1, extent - 1] = degree * (degree + 1) / 4.0
    return matrix


DM = gll_derivative(ORDER)
SUM_PART = [[(DM[j, a] + DM[j, 7 - a]) / 2 for a in range(4)] for j in range(4)]
DIF_PART = [[(DM[j, a] - DM[j, 7 - a]) / 2 for a in range(4)] for j in range(4)]
ROT = np.array([[DM[k, (k - r) % 8] for k in range(8)] for r in range(8)], np.float32)


def combine(coefs, items):
    total = None
    for c, x in zip(coefs, items):
        term = x * np.float32(c)
        total = term if total is None else total + term
    return total


def along_second(plane):
    even = [plane[a] + plane[7 - a] for a in range(4)]
    odd = [plane[a] - plane[7 - a] for a in range(4)]
    out = [None] * 8
    for j in range(4):
        e = combine(SUM_PART[j], even)
        o = combine(DIF_PART[j], odd)
        out[j] = o + e
        out[7 - j] = o - e
    return out


def along_third(x, rot):
    total = x * rot[0]
    for r in range(1, 8):
        total = total + pltpu.roll(x, r, 0) * rot[r]
    return total


def gather_lanes(x, idx):
    return jnp.take_along_axis(x, idx, axis=1, mode="promise_in_bounds")


def third_tables():
    lane = lax.broadcasted_iota(jnp.int32, (SUB, LANES), 1)
    k = lax.broadcasted_iota(jnp.int32, (SUB, LANES), 0)
    z = lane % EZ
    back = jnp.where(z == 0, lane + (EZ - 1), lane - 1)
    ahead = jnp.where(z == EZ - 1, lane - (EZ - 1), lane + 1)
    return jnp.where(k == 0, back, ahead), k == 0, k == ORDER


def plane_sum(plane, tables):
    idx, first, last = tables
    up = plane[7] + pltpu.roll(plane[0], LANES - EZ, 1)
    plane = [pltpu.roll(up, EZ, 1)] + list(plane[1:7]) + [up]
    out = []
    for v in plane:
        x = jnp.where(first, pltpu.roll(v, 1, 0), jnp.where(last, pltpu.roll(v, 7, 0), 0.0))
        out.append(v + gather_lanes(x, idx))
    return out


def brick_index(order_ref):
    order = jnp.broadcast_to(order_ref[...], (LANES, LANES))
    pos = lax.broadcasted_iota(jnp.int32, (LANES, LANES), 0)
    hot = jnp.where(order == pos, 1.0, 0.0).astype(jnp.bfloat16)
    slot = lax.broadcasted_iota(jnp.int32, (SUB, LANES), 1).astype(jnp.float32).astype(jnp.bfloat16)
    found = lax.dot_general(
        slot, hot, (((1,), (1,)), ((), ())), preferred_element_type=jnp.float32
    )
    return found.astype(jnp.int32)


def source_plane(parity, i):
    return jnp.where(parity == 1, ORDER - i, i)


def project_faces(order_ref, scal_ref, mass_ref, od_ref, ev_ref):
    parity = lax.axis_index("elem") % 2
    idx = brick_index(order_ref)
    tables = third_tables()
    for face, out in ((0, od_ref), (ORDER, ev_ref)):
        src = source_plane(parity, face)
        weight = [gather_lanes(mass_ref[src, j], idx) for j in range(8)]
        for j, v in enumerate(plane_sum(weight, tables)):
            out[2, j] = v
        for m in range(2):
            plane = [gather_lanes(scal_ref[m, src, j], idx) * weight[j] for j in range(8)]
            for j, v in enumerate(plane_sum(plane, tables)):
                out[m, j] = v


def prepare(order_ref, scal_ref, mass_ref, tr_ref, gi_ref, q_ref, ri_ref, ti_ref, tf_ref):
    parity = lax.axis_index("elem") % 2
    idx = brick_index(order_ref)
    tables = third_tables()
    sign = jnp.where(parity == 1, time_step, -time_step).astype(jnp.float32)

    for face in range(2):
        src = source_plane(parity, face * ORDER)
        for j in range(8):
            tf_ref[face, 0, j] = gather_lanes(tr_ref[0, src, j], idx) * sign
            tf_ref[face, 1, j] = gather_lanes(tr_ref[1, src, j], idx) * np.float32(-time_step)
            tf_ref[face, 2, j] = gather_lanes(tr_ref[2, src, j], idx) * np.float32(-time_step)

    def body(i, carry):
        src = source_plane(parity, i + 1)
        for j in range(8):
            ti_ref[i, 0, j] = gather_lanes(tr_ref[0, src, j], idx) * sign
            ti_ref[i, 1, j] = gather_lanes(tr_ref[1, src, j], idx) * np.float32(-time_step)
            ti_ref[i, 2, j] = gather_lanes(tr_ref[2, src, j], idx) * np.float32(-time_step)
        weight = [gather_lanes(mass_ref[src, j], idx) for j in range(8)]
        inverse = [1.0 / v for v in plane_sum(weight, tables)]
        for j in range(8):
            ri_ref[i, j] = inverse[j]
        for m in range(2):
            plane = [gather_lanes(scal_ref[m, src, j], idx) * weight[j] for j in range(8)]
            plane = plane_sum(plane, tables)
            for j in range(8):
                gi_ref[m, i, j] = plane[j] * inverse[j]
        return carry

    lax.fori_loop(0, 6, body, 0)
    face_partials(gi_ref, q_ref)


def face_partials(gi_ref, q_ref):
    for face in range(2):
        coefs = DM[face * ORDER, 1:7]
        for m in range(2):
            for j in range(8):
                q_ref[face, m, j] = combine(coefs, [gi_ref[m, i, j] for i in range(6)])


def face_terms(p, q_ref, tf_ref, rot, tables, outs):
    for face in range(2):
        out = outs[face]
        for m in range(2):
            mine = p[face][m]
            second = along_second(mine)
            plane = []
            for j in range(8):
                first = (
                    q_ref[face, m, j]
                    + p[0][m][j] * np.float32(DM[face * ORDER, 0])
                    + p[1][m][j] * np.float32(DM[face * ORDER, ORDER])
                )
                third = along_third(mine[j], rot)
                plane.append(
                    tf_ref[face, 0, j] * first
                    + tf_ref[face, 1, j] * second[j]
                    + tf_ref[face, 2, j] * third
                )
            for j, v in enumerate(plane_sum(plane, tables)):
                out[m, j] = v


def start_faces(od_ref, ev_ref, rod_ref, rev_ref, q_ref, tf_ref, rot_ref,
                p_ref, rf_ref, sod_ref, sev_ref):
    rot = [rot_ref[r] for r in range(8)]
    tables = third_tables()
    p = []
    for face, (own, got) in enumerate(((od_ref, rod_ref), (ev_ref, rev_ref))):
        inverse = [1.0 / (own[2, j] + got[2, j]) for j in range(8)]
        for j in range(8):
            rf_ref[face, j] = inverse[j]
        p.append([[(own[m, j] + got[m, j]) * inverse[j] for j in range(8)] for m in range(2)])
        for m in range(2):
            for j in range(8):
                p_ref[face, m, j] = p[face][m][j]
    face_terms(p, q_ref, tf_ref, rot, tables, (sod_ref, sev_ref))


def make_stage_faces(scale, total):
    def stage_faces(od_ref, ev_ref, rod_ref, rev_ref, rf_ref, accf_ref, q_ref, tf_ref, rot_ref,
                    p_ref, sod_ref, sev_ref):
        rot = [rot_ref[r] for r in range(8)]
        tables = third_tables()
        p = []
        for face, (own, got) in enumerate(((od_ref, rod_ref), (ev_ref, rev_ref))):
            rows = []
            for m in range(2):
                row = [
                    (own[m, j] + got[m, j]) * (rf_ref[face, j] * np.float32(scale))
                    for j in range(8)
                ]
                if total:
                    row = [row[j] + accf_ref[face, m, j] for j in range(8)]
                rows.append(row)
                for j in range(8):
                    p_ref[face, m, j] = row[j]
            p.append(rows)
        face_terms(p, q_ref, tf_ref, rot, tables, (sod_ref, sev_ref))

    return stage_faces


def make_stage_inner(scale, opening, closing):
    def stage_inner(p_ref, gi_ref, acci_ref, accf_ref, ri_ref, ti_ref, rot_ref, d_ref,
                    gn_ref, q_ref, an_ref, afn_ref):
        rot = [rot_ref[r] for r in range(8)]
        tables = third_tables()

        def body(i, carry):
            row = [d_ref[i + 1, a] for a in range(8)]
            for m in range(2):
                mine = [gi_ref[m, i, j] for j in range(8)]
                second = along_second(mine)
                plane = []
                for j in range(8):
                    first = p_ref[0, m, j] * row[0] + p_ref[1, m, j] * row[7]
                    for a in range(6):
                        first = first + gi_ref[m, a, j] * row[a + 1]
                    third = along_third(mine[j], rot)
                    plane.append(
                        ti_ref[i, 0, j] * first
                        + ti_ref[i, 1, j] * second[j]
                        + ti_ref[i, 2, j] * third
                    )
                plane = plane_sum(plane, tables)
                for j in range(8):
                    value = plane[j] * (ri_ref[i, j] * np.float32(scale))
                    total = (mine[j] if opening else acci_ref[m, i, j]) + value
                    gn_ref[m, i, j] = total if closing else value
                    if not closing:
                        an_ref[m, i, j] = total
            return carry

        lax.fori_loop(0, 6, body, 0)
        face_partials(gn_ref, q_ref)
        for face in range(2):
            for m in range(2):
                for j in range(8):
                    value = p_ref[face, m, j]
                    afn_ref[face, m, j] = value if opening else value + accf_ref[face, m, j]

    return stage_inner


def make_finish(scale):
    def finish(order_ref, od_ref, ev_ref, rod_ref, rev_ref, rf_ref, accf_ref, gi_ref, out_ref):
        parity = lax.axis_index("elem") % 2
        idx = jnp.broadcast_to(order_ref[...], (SUB, LANES))
        for face, (own, got) in enumerate(((od_ref, rod_ref), (ev_ref, rev_ref))):
            dst = source_plane(parity, face * ORDER)
            for m in range(2):
                for j in range(8):
                    value = (own[m, j] + got[m, j]) * (rf_ref[face, j] * np.float32(scale))
                    out_ref[m, dst, j] = gather_lanes(value + accf_ref[face, m, j], idx)
        for i in range(6):
            dst = source_plane(parity, i + 1)
            for m in range(2):
                for j in range(8):
                    out_ref[m, dst, j] = gather_lanes(gi_ref[m, i, j], idx)

    return finish


VM = pl.BlockSpec(memory_space=pltpu.VMEM)
SM = pl.BlockSpec(memory_space=pltpu.SMEM)


def call(kernel, outs, args, name, cost, smem_last=False):
    specs = [VM] * len(args)
    if smem_last:
        specs[-1] = SM
    shapes = [jax.ShapeDtypeStruct(s, jnp.float32) for s in outs]
    return pl.pallas_call(
        kernel,
        out_shape=shapes if len(shapes) > 1 else shapes[0],
        in_specs=specs,
        out_specs=[VM] * len(shapes) if len(shapes) > 1 else VM,
        name=name,
        compiler_params=pltpu.CompilerParams(vmem_limit_bytes=8 << 20),
        cost_estimate=pl.CostEstimate(flops=cost * 1000000, bytes_accessed=1 << 20, transcendentals=0),
    )(*args)


def per_device(scalars, transport, mass, element_order):
    count = lax.axis_size("elem")
    even_pairs = [(i, i ^ 1) for i in range(count)]
    odd_pairs = [(i, (i + 1) % count if i % 2 else (i - 1) % count) for i in range(count)]
    swap_od = lambda x: lax.ppermute(x, "elem", odd_pairs)
    swap_ev = lambda x: lax.ppermute(x, "elem", even_pairs)
    rot = jnp.asarray(np.broadcast_to(ROT[:, :, None], (8, SUB, LANES)))
    dmat = jnp.asarray(DM, jnp.float32)
    members = scalars.shape[0]
    grid = (EXT, EXT, SUB, LANES)
    scal = scalars.reshape((members,) + grid)
    tr = transport.reshape((3,) + grid)
    mas = mass.reshape(grid)
    tile = (EXT, SUB, LANES)

    od, ev = call(project_faces, [(3,) + tile] * 2, (element_order, scal, mas), "project", 1)
    rod, rev = swap_od(od), swap_ev(ev)
    gi, q, ri, ti, tf = call(
        prepare,
        [(2, 6) + tile, (2, 2) + tile, (6,) + tile, (6, 3) + tile, (2, 3) + tile],
        (element_order, scal, mas, tr), "prepare", 4000)
    p, rf, od, ev = call(
        start_faces, [(2, 2) + tile, (2,) + tile, (2,) + tile, (2,) + tile],
        (od, ev, rod, rev, q, tf, rot), "faces", 1)
    acci, accf = gi, p
    last = SUBSTEPS * STAGES
    for n in range(1, last + 1):
        s = (n - 1) % STAGES + 1
        rod, rev = swap_od(od), swap_ev(ev)
        gi, q, acci, accf = call(
            make_stage_inner(1.0 / s, s == 1, s == STAGES),
            [(2, 6) + tile, (2, 2) + tile, (2, 6) + tile, (2, 2) + tile],
            (p, gi, acci, accf, ri, ti, rot, dmat), "inner", 4000, smem_last=True)
        if n < last:
            p, od, ev = call(
                make_stage_faces(1.0 / s, s == STAGES),
                [(2, 2) + tile, (2,) + tile, (2,) + tile],
                (od, ev, rod, rev, rf, accf, q, tf, rot), "faces", 1)
    out = call(
        make_finish(1.0 / STAGES), [(members,) + grid],
        (element_order, od, ev, rod, rev, rf, accf, gi), "finish", 1)
    return out.reshape(scalars.shape)


def solution(mesh):
    in_specs = (P("ens", None, "elem"), P(None, None, "elem"), P(None, "elem"), P("elem", None))
    out_specs = P("ens", None, "elem")
    return jax.shard_map(
        per_device, mesh=mesh, in_specs=in_specs, out_specs=out_specs, check_vma=False
    )
```

profile of v0, /device:TPU:0, one launch (start us, length us, event | category | flops | bytes accessed | tf_op | source)
XLA Modules:
  0.0 86.7 jit_solution(6075887483995638066)
XLA Ops:
  0.0 0.7 copy-done.2
  0.7 1.0 %copy-done = f32[2,512,128]{2,1,0:T(8,128)S(1)} copy-done((f32[2,512,128]{2,1,0:T(8,128)S(1)}, f32[2,512,128]{2,1,0:T(8,128)}, u32[]{:S(2)}) %copy-start) | copy-done | bytes 524312
  1.7 0.9 %copy-done.1 = f32[512,128]{1,0:T(8,128)S(1)} copy-done((f32[512,128]{1,0:T(8,128)S(1)}, f32[512,128]{1,0:T(8,128)}, u32[]{:S(2)}) %copy-start.1) | copy-done | bytes 262168
  3.1 6.7 %collective-permute-start = (f32[3,8,8,128]{3,2,1,0:T(8,128)S(1)}, f32[3,8,8,128]{3,2,1,0:T(8,128)S(1)}, u32[]{:S(2)}, u32[]{:S(2)}) collective-permute-start(f32[3,8,8,128]{3,2,1,0:T(8,128)S(1)} %get-tuple-element.67.od_ref), channel_id=1, source_target_pairs={{0,31},{1,2},{2,1},{3,4},{4,3},{5,6},{6,5},{7,8},{8,7},{9,10},{10,... | collective-permute-start | bytes 294920 | tf_op jit(solution)/shard_map/ppermute | solution.py:331
  9.8 2.2 %prepare.1 = (f32[2,6,8,8,128]{4,3,2,1,0:T(8,128)S(1)}, f32[2,2,8,8,128]{4,3,2,1,0:T(8,128)S(1)}, f32[6,8,8,128]{3,2,1,0:T(8,128)S(1)}, f32[6,3,8,8,128]{4,3,2,1,0:T(8,128)S(1)}, f32[2,3,8,8,128]{4,3,2,1,0:T(8,128)S(1)}) custom-call(s32[1,128]{1,0:T(1,128)S(1)} %copy-done.2, f32[2,8,8,8,128]{4,3,2,1,0:T(8,128)S(1)} %bitcast.5, f32[8,8,8,128]{3,2,1,0:T(8,128)S(1)} %bitcast.7, ...), custom_call_target="tpu_custom_call" | custom-call | flops 4000000000 | bytes 1048576 | tf_op jit(solution)/shard_map/prepare/pallas_call | solution.py:316
  12.6 1.8 %collective-permute-done.1.rev_ref = f32[3,8,8,128]{3,2,1,0:T(8,128)S(1)} collective-permute-done((f32[3,8,8,128]{3,2,1,0:T(8,128)S(1)}, f32[3,8,8,128]{3,2,1,0:T(8,128)S(1)}, u32[]{:S(2)}, u32[]{:S(2)}) %collective-permute-start.1) | collective-permute-done | bytes 98336 | tf_op jit(solution)/shard_map/ppermute | solution.py:332
  14.8 4.3 %collective-permute-start.2 = (f32[2,8,8,128]{3,2,1,0:T(8,128)S(1)}, f32[2,8,8,128]{3,2,1,0:T(8,128)S(1)}, u32[]{:S(2)}, u32[]{:S(2)}) collective-permute-start(f32[2,8,8,128]{3,2,1,0:T(8,128)S(1)} %get-tuple-element.71.od_ref), channel_id=1, source_target_pairs={{0,31},{1,2},{2,1},{3,4},{4,3},{5,6},{6,5},{7,8},{8,7},{9,10},{10,... | collective-permute-start | bytes 196616 | tf_op jit(solution)/shard_map/ppermute | solution.py:331
  19.1 0.7 copy-done.4
  19.8 2.1 %inner.8 = (f32[2,6,8,8,128]{4,3,2,1,0:T(8,128)S(1)}, f32[2,2,8,8,128]{4,3,2,1,0:T(8,128)S(1)}, f32[2,6,8,8,128]{4,3,2,1,0:T(8,128)S(1)}, f32[2,2,8,8,128]{4,3,2,1,0:T(8,128)S(1)}) custom-call(f32[2,2,8,8,128]{4,3,2,1,0:T(8,128)S(1)} %get-tuple-element.74.p_ref.accf_ref, f32[2,6,8,8,128]{4,3,2,1,0:T(8,128)S(1)} %get-tuple-element.75.gi_ref.acci_ref, ...), custom_call_target="tpu_custom_call" | custom-call | flops 4000000000 | bytes 1048576 | tf_op jit(solution)/shard_map/inner/pallas_call | solution.py:316
  21.9 1.4 %collective-permute-done.2.rod_ref = f32[2,8,8,128]{3,2,1,0:T(8,128)S(1)} collective-permute-done((f32[2,8,8,128]{3,2,1,0:T(8,128)S(1)}, f32[2,8,8,128]{3,2,1,0:T(8,128)S(1)}, u32[]{:S(2)}, u32[]{:S(2)}) %collective-permute-start.2) | collective-permute-done | bytes 65568 | tf_op jit(solution)/shard_map/ppermute | solution.py:331
  23.7 4.3 %collective-permute-start.4 = (f32[2,8,8,128]{3,2,1,0:T(8,128)S(1)}, f32[2,8,8,128]{3,2,1,0:T(8,128)S(1)}, u32[]{:S(2)}, u32[]{:S(2)}) collective-permute-start(f32[2,8,8,128]{3,2,1,0:T(8,128)S(1)} %get-tuple-element.80.od_ref), channel_id=1, source_target_pairs={{0,31},{1,2},{2,1},{3,4},{4,3},{5,6},{6,5},{7,8},{8,7},{9,10},{10,... | collective-permute-start | bytes 196616 | tf_op jit(solution)/shard_map/ppermute | solution.py:331
  28.0 2.1 %inner.9 = (f32[2,6,8,8,128]{4,3,2,1,0:T(8,128)S(1)}, f32[2,2,8,8,128]{4,3,2,1,0:T(8,128)S(1)}, f32[2,6,8,8,128]{4,3,2,1,0:T(8,128)S(1)}, f32[2,2,8,8,128]{4,3,2,1,0:T(8,128)S(1)}) custom-call(f32[2,2,8,8,128]{4,3,2,1,0:T(8,128)S(1)} %get-tuple-element.82.p_ref, f32[2,6,8,8,128]{4,3,2,1,0:T(8,128)S(1)} %get-tuple-element.83.gi_ref, ...), custom_call_target="tpu_custom_call" | custom-call | flops 4000000000 | bytes 1048576 | tf_op jit(solution)/shard_map/inner/pallas_call | solution.py:316
  30.1 2.1 %collective-permute-done.4.rod_ref = f32[2,8,8,128]{3,2,1,0:T(8,128)S(1)} collective-permute-done((f32[2,8,8,128]{3,2,1,0:T(8,128)S(1)}, f32[2,8,8,128]{3,2,1,0:T(8,128)S(1)}, u32[]{:S(2)}, u32[]{:S(2)}) %collective-permute-start.4) | collective-permute-done | bytes 65568 | tf_op jit(solution)/shard_map/ppermute | solution.py:331
  32.5 4.3 %collective-permute-start.6 = (f32[2,8,8,128]{3,2,1,0:T(8,128)S(1)}, f32[2,8,8,128]{3,2,1,0:T(8,128)S(1)}, u32[]{:S(2)}, u32[]{:S(2)}) collective-permute-start(f32[2,8,8,128]{3,2,1,0:T(8,128)S(1)} %get-tuple-element.87.od_ref), channel_id=1, source_target_pairs={{0,31},{1,2},{2,1},{3,4},{4,3},{5,6},{6,5},{7,8},{8,7},{9,10},{10,... | collective-permute-start | bytes 196616 | tf_op jit(solution)/shard_map/ppermute | solution.py:331
  36.8 2.1 %inner.10 = (f32[2,6,8,8,128]{4,3,2,1,0:T(8,128)S(1)}, f32[2,2,8,8,128]{4,3,2,1,0:T(8,128)S(1)}, f32[2,6,8,8,128]{4,3,2,1,0:T(8,128)S(1)}, f32[2,2,8,8,128]{4,3,2,1,0:T(8,128)S(1)}) custom-call(f32[2,2,8,8,128]{4,3,2,1,0:T(8,128)S(1)} %get-tuple-element.89.p_ref, f32[2,6,8,8,128]{4,3,2,1,0:T(8,128)S(1)} %get-tuple-element.90.gi_ref, ...), custom_call_target="tpu_custom_call" | custom-call | flops 4000000000 | bytes 1048576 | tf_op jit(solution)/shard_map/inner/pallas_call | solution.py:316
  38.9 2.1 %collective-permute-done.6.rod_ref = f32[2,8,8,128]{3,2,1,0:T(8,128)S(1)} collective-permute-done((f32[2,8,8,128]{3,2,1,0:T(8,128)S(1)}, f32[2,8,8,128]{3,2,1,0:T(8,128)S(1)}, u32[]{:S(2)}, u32[]{:S(2)}) %collective-permute-start.6) | collective-permute-done | bytes 65568 | tf_op jit(solution)/shard_map/ppermute | solution.py:331
  41.4 4.3 %collective-permute-start.8 = (f32[2,8,8,128]{3,2,1,0:T(8,128)S(1)}, f32[2,8,8,128]{3,2,1,0:T(8,128)S(1)}, u32[]{:S(2)}, u32[]{:S(2)}) collective-permute-start(f32[2,8,8,128]{3,2,1,0:T(8,128)S(1)} %get-tuple-element.94.od_ref), channel_id=1, source_target_pairs={{0,31},{1,2},{2,1},{3,4},{4,3},{5,6},{6,5},{7,8},{8,7},{9,10},{10,... | collective-permute-start | bytes 196616 | tf_op jit(solution)/shard_map/ppermute | solution.py:331
  45.7 2.1 %inner.11 = (f32[2,6,8,8,128]{4,3,2,1,0:T(8,128)S(1)}, f32[2,2,8,8,128]{4,3,2,1,0:T(8,128)S(1)}, f32[2,6,8,8,128]{4,3,2,1,0:T(8,128)S(1)}, f32[2,2,8,8,128]{4,3,2,1,0:T(8,128)S(1)}) custom-call(f32[2,2,8,8,128]{4,3,2,1,0:T(8,128)S(1)} %get-tuple-element.96.p_ref, f32[2,6,8,8,128]{4,3,2,1,0:T(8,128)S(1)} %get-tuple-element.97.gi_ref, ...), custom_call_target="tpu_custom_call" | custom-call | flops 4000000000 | bytes 1048576 | tf_op jit(solution)/shard_map/inner/pallas_call | solution.py:316
  47.8 2.1 %collective-permute-done.8.rod_ref = f32[2,8,8,128]{3,2,1,0:T(8,128)S(1)} collective-permute-done((f32[2,8,8,128]{3,2,1,0:T(8,128)S(1)}, f32[2,8,8,128]{3,2,1,0:T(8,128)S(1)}, u32[]{:S(2)}, u32[]{:S(2)}) %collective-permute-start.8) | collective-permute-done | bytes 65568 | tf_op jit(solution)/shard_map/ppermute | solution.py:331
  50.2 4.3 %collective-permute-start.10 = (f32[2,8,8,128]{3,2,1,0:T(8,128)S(1)}, f32[2,8,8,128]{3,2,1,0:T(8,128)S(1)}, u32[]{:S(2)}, u32[]{:S(2)}) collective-permute-start(f32[2,8,8,128]{3,2,1,0:T(8,128)S(1)} %get-tuple-element.101.od_ref), channel_id=1, source_target_pairs={{0,31},{1,2},{2,1},{3,4},{4,3},{5,6},{6,5},{7,8},{8,7},{9,10},{10,... | collective-permute-start | bytes 196616 | tf_op jit(solution)/shard_map/ppermute | solution.py:331
  54.5 2.1 %inner.12 = (f32[2,6,8,8,128]{4,3,2,1,0:T(8,128)S(1)}, f32[2,2,8,8,128]{4,3,2,1,0:T(8,128)S(1)}, f32[2,6,8,8,128]{4,3,2,1,0:T(8,128)S(1)}, f32[2,2,8,8,128]{4,3,2,1,0:T(8,128)S(1)}) custom-call(f32[2,2,8,8,128]{4,3,2,1,0:T(8,128)S(1)} %get-tuple-element.103.p_ref, f32[2,6,8,8,128]{4,3,2,1,0:T(8,128)S(1)} %get-tuple-element.104.gi_ref, ...), custom_call_target="tpu_custom_call" | custom-call | flops 4000000000 | bytes 1048576 | tf_op jit(solution)/shard_map/inner/pallas_call | solution.py:316
  56.6 2.4 %collective-permute-done.10.rod_ref = f32[2,8,8,128]{3,2,1,0:T(8,128)S(1)} collective-permute-done((f32[2,8,8,128]{3,2,1,0:T(8,128)S(1)}, f32[2,8,8,128]{3,2,1,0:T(8,128)S(1)}, u32[]{:S(2)}, u32[]{:S(2)}) %collective-permute-start.10) | collective-permute-done | bytes 65568 | tf_op jit(solution)/shard_map/ppermute | solution.py:331
  59.3 4.1 %collective-permute-start.12 = (f32[2,8,8,128]{3,2,1,0:T(8,128)S(1)}, f32[2,8,8,128]{3,2,1,0:T(8,128)S(1)}, u32[]{:S(2)}, u32[]{:S(2)}) collective-permute-start(f32[2,8,8,128]{3,2,1,0:T(8,128)S(1)} %get-tuple-element.108.od_ref), channel_id=1, source_target_pairs={{0,31},{1,2},{2,1},{3,4},{4,3},{5,6},{6,5},{7,8},{8,7},{9,10},{10,... | collective-permute-start | bytes 196616 | tf_op jit(solution)/shard_map/ppermute | solution.py:331
  63.4 2.1 %inner.13 = (f32[2,6,8,8,128]{4,3,2,1,0:T(8,128)S(1)}, f32[2,2,8,8,128]{4,3,2,1,0:T(8,128)S(1)}, f32[2,6,8,8,128]{4,3,2,1,0:T(8,128)S(1)}, f32[2,2,8,8,128]{4,3,2,1,0:T(8,128)S(1)}) custom-call(f32[2,2,8,8,128]{4,3,2,1,0:T(8,128)S(1)} %get-tuple-element.110.p_ref, f32[2,6,8,8,128]{4,3,2,1,0:T(8,128)S(1)} %get-tuple-element.111.gi_ref, ...), custom_call_target="tpu_custom_call" | custom-call | flops 4000000000 | bytes 1048576 | tf_op jit(solution)/shard_map/inner/pallas_call | solution.py:316
  65.5 2.4 %collective-permute-done.12.rod_ref = f32[2,8,8,128]{3,2,1,0:T(8,128)S(1)} collective-permute-done((f32[2,8,8,128]{3,2,1,0:T(8,128)S(1)}, f32[2,8,8,128]{3,2,1,0:T(8,128)S(1)}, u32[]{:S(2)}, u32[]{:S(2)}) %collective-permute-start.12) | collective-permute-done | bytes 65568 | tf_op jit(solution)/shard_map/ppermute | solution.py:331
  68.2 4.4 %collective-permute-start.14 = (f32[2,8,8,128]{3,2,1,0:T(8,128)S(1)}, f32[2,8,8,128]{3,2,1,0:T(8,128)S(1)}, u32[]{:S(2)}, u32[]{:S(2)}) collective-permute-start(f32[2,8,8,128]{3,2,1,0:T(8,128)S(1)} %get-tuple-element.115.od_ref), channel_id=1, source_target_pairs={{0,31},{1,2},{2,1},{3,4},{4,3},{5,6},{6,5},{7,8},{8,7},{9,10},{10,... | collective-permute-start | bytes 196616 | tf_op jit(solution)/shard_map/ppermute | solution.py:331
  72.6 2.1 %inner.14 = (f32[2,6,8,8,128]{4,3,2,1,0:T(8,128)S(1)}, f32[2,2,8,8,128]{4,3,2,1,0:T(8,128)S(1)}, f32[2,6,8,8,128]{4,3,2,1,0:T(8,128)S(1)}, f32[2,2,8,8,128]{4,3,2,1,0:T(8,128)S(1)}) custom-call(f32[2,2,8,8,128]{4,3,2,1,0:T(8,128)S(1)} %get-tuple-element.117.p_ref, f32[2,6,8,8,128]{4,3,2,1,0:T(8,128)S(1)} %get-tuple-element.118.gi_ref, ...), custom_call_target="tpu_custom_call" | custom-call | flops 4000000000 | bytes 1048576 | tf_op jit(solution)/shard_map/inner/pallas_call | solution.py:316
  74.7 2.0 %collective-permute-done.14.rod_ref = f32[2,8,8,128]{3,2,1,0:T(8,128)S(1)} collective-permute-done((f32[2,8,8,128]{3,2,1,0:T(8,128)S(1)}, f32[2,8,8,128]{3,2,1,0:T(8,128)S(1)}, u32[]{:S(2)}, u32[]{:S(2)}) %collective-permute-start.14) | collective-permute-done | bytes 65568 | tf_op jit(solution)/shard_map/ppermute | solution.py:331
  77.1 4.3 %collective-permute-start.16 = (f32[2,8,8,128]{3,2,1,0:T(8,128)S(1)}, f32[2,8,8,128]{3,2,1,0:T(8,128)S(1)}, u32[]{:S(2)}, u32[]{:S(2)}) collective-permute-start(f32[2,8,8,128]{3,2,1,0:T(8,128)S(1)} %get-tuple-element.122.od_ref), channel_id=1, source_target_pairs={{0,31},{1,2},{2,1},{3,4},{4,3},{5,6},{6,5},{7,8},{8,7},{9,10},{10,... | collective-permute-start | bytes 196616 | tf_op jit(solution)/shard_map/ppermute | solution.py:331
  81.4 2.9 %inner.15 = (f32[2,6,8,8,128]{4,3,2,1,0:T(8,128)S(1)}, f32[2,2,8,8,128]{4,3,2,1,0:T(8,128)}, f32[2,6,8,8,128]{4,3,2,1,0:T(8,128)}, f32[2,2,8,8,128]{4,3,2,1,0:T(8,128)S(1)}) custom-call(f32[2,2,8,8,128]{4,3,2,1,0:T(8,128)S(1)} %get-tuple-element.124.p_ref, f32[2,6,8,8,128]{4,3,2,1,0:T(8,128)S(1)} %get-tuple-element.125.gi_ref, ...), custom_call_target="tpu_custom_call" | custom-call | flops 4000000000 | bytes 1048576 | tf_op jit(solution)/shard_map/inner/pallas_call | solution.py:316
  84.3 1.4 %collective-permute-done.16.rod_ref = f32[2,8,8,128]{3,2,1,0:T(8,128)S(1)} collective-permute-done((f32[2,8,8,128]{3,2,1,0:T(8,128)S(1)}, f32[2,8,8,128]{3,2,1,0:T(8,128)S(1)}, u32[]{:S(2)}, u32[]{:S(2)}) %collective-permute-start.16) | collective-permute-done | bytes 65568 | tf_op jit(solution)/shard_map/ppermute | solution.py:331
  85.7 1.0 %finish.1 = f32[2,8,8,8,128]{4,3,2,1,0:T(8,128)} custom-call(s32[1,128]{1,0:T(1,128)S(1)} %copy-done.2, f32[2,8,8,128]{3,2,1,0:T(8,128)S(1)} %get-tuple-element.122.od_ref, f32[2,8,8,128]{3,2,1,0:T(8,128)S(1)} %get-tuple-element.123.ev_ref, f32[2,8,8,128]{3,2,1,0:T(8,128)S(1)} %collective-permute-done.16.rod_ref, ...), custom_call_target="tpu_custom_call" | custom-call | flops 1000000 | bytes 1048576 | tf_op jit(solution)/shard_map/finish/pallas_call | solution.py:316
  (36 shorter events, 3.5 us)
Async XLA Ops:
  0.0 0.7 copy-start.2
  0.7 1.0 %copy-start = (f32[2,512,128]{2,1,0:T(8,128)S(1)}, f32[2,512,128]{2,1,0:T(8,128)}, u32[]{:S(2)}) copy-start(f32[2,512,128]{2,1,0:T(8,128)} %param.6) | copy-start | bytes 1572868
  1.7 0.9 %copy-start.1 = (f32[512,128]{1,0:T(8,128)S(1)}, f32[512,128]{1,0:T(8,128)}, u32[]{:S(2)}) copy-start(f32[512,128]{1,0:T(8,128)} %param.8) | copy-start | bytes 786436
  2.6 7.2 %copy-start.3 = (f32[3,512,128]{2,1,0:T(8,128)S(1)}, f32[3,512,128]{2,1,0:T(8,128)}, u32[]{:S(2)}) copy-start(f32[3,512,128]{2,1,0:T(8,128)} %param.7) | copy-start | bytes 2359300
  3.1 9.5 %collective-permute-start = (f32[3,8,8,128]{3,2,1,0:T(8,128)S(1)}, f32[3,8,8,128]{3,2,1,0:T(8,128)S(1)}, u32[]{:S(2)}, u32[]{:S(2)}) collective-permute-start(f32[3,8,8,128]{3,2,1,0:T(8,128)S(1)} %get-tuple-element.67.od_ref), channel_id=1, source_target_pairs={{0,31},{1,2},{2,1},{3,4},{4,3},{5,6},{6,5},{7,8},{8,7},{9,10},{10,... | collective-permute-start | bytes 294920 | tf_op jit(solution)/shard_map/ppermute | solution.py:331
  9.8 4.6 %collective-permute-start.1 = (f32[3,8,8,128]{3,2,1,0:T(8,128)S(1)}, f32[3,8,8,128]{3,2,1,0:T(8,128)S(1)}, u32[]{:S(2)}, u32[]{:S(2)}) collective-permute-start(f32[3,8,8,128]{3,2,1,0:T(8,128)S(1)} %get-tuple-element.68.ev_ref), channel_id=1, source_target_pairs={{0,1},{1,0},{2,3},{3,2},{4,5},{5,4},{6,7},{7,6},{8,9},{9,8},{10,11... | collective-permute-start | bytes 294920 | tf_op jit(solution)/shard_map/ppermute | solution.py:332
  9.8 4.6 %copy-start.5 = (f32[8,8]{1,0:T(8,128)S(1)}, f32[8,8]{1,0:T(8,128)}, u32[]{:S(2)}) copy-start(f32[8,8]{1,0:T(8,128)} %constant.4.clone) | copy-start | bytes 772
  14.8 8.6 %collective-permute-start.2 = (f32[2,8,8,128]{3,2,1,0:T(8,128)S(1)}, f32[2,8,8,128]{3,2,1,0:T(8,128)S(1)}, u32[]{:S(2)}, u32[]{:S(2)}) collective-permute-start(f32[2,8,8,128]{3,2,1,0:T(8,128)S(1)} %get-tuple-element.71.od_ref), channel_id=1, source_target_pairs={{0,31},{1,2},{2,1},{3,4},{4,3},{5,6},{6,5},{7,8},{8,7},{9,10},{10,... | collective-permute-start | bytes 196616 | tf_op jit(solution)/shard_map/ppermute | solution.py:331
  19.1 0.7 copy-start.4
  19.1 4.3 %collective-permute-start.3 = (f32[2,8,8,128]{3,2,1,0:T(8,128)S(1)}, f32[2,8,8,128]{3,2,1,0:T(8,128)S(1)}, u32[]{:S(2)}, u32[]{:S(2)}) collective-permute-start(f32[2,8,8,128]{3,2,1,0:T(8,128)S(1)} %get-tuple-element.72.ev_ref), channel_id=1, source_target_pairs={{0,1},{1,0},{2,3},{3,2},{4,5},{5,4},{6,7},{7,6},{8,9},{9,8},{10,11... | collective-permute-start | bytes 196616 | tf_op jit(solution)/shard_map/ppermute | solution.py:332
  23.7 8.6 %collective-permute-start.4 = (f32[2,8,8,128]{3,2,1,0:T(8,128)S(1)}, f32[2,8,8,128]{3,2,1,0:T(8,128)S(1)}, u32[]{:S(2)}, u32[]{:S(2)}) collective-permute-start(f32[2,8,8,128]{3,2,1,0:T(8,128)S(1)} %get-tuple-element.80.od_ref), channel_id=1, source_target_pairs={{0,31},{1,2},{2,1},{3,4},{4,3},{5,6},{6,5},{7,8},{8,7},{9,10},{10,... | collective-permute-start | bytes 196616 | tf_op jit(solution)/shard_map/ppermute | solution.py:331
  28.0 4.3 %collective-permute-start.5 = (f32[2,8,8,128]{3,2,1,0:T(8,128)S(1)}, f32[2,8,8,128]{3,2,1,0:T(8,128)S(1)}, u32[]{:S(2)}, u32[]{:S(2)}) collective-permute-start(f32[2,8,8,128]{3,2,1,0:T(8,128)S(1)} %get-tuple-element.81.ev_ref), channel_id=1, source_target_pairs={{0,1},{1,0},{2,3},{3,2},{4,5},{5,4},{6,7},{7,6},{8,9},{9,8},{10,11... | collective-permute-start | bytes 196616 | tf_op jit(solution)/shard_map/ppermute | solution.py:332
  32.5 8.6 %collective-permute-start.6 = (f32[2,8,8,128]{3,2,1,0:T(8,128)S(1)}, f32[2,8,8,128]{3,2,1,0:T(8,128)S(1)}, u32[]{:S(2)}, u32[]{:S(2)}) collective-permute-start(f32[2,8,8,128]{3,2,1,0:T(8,128)S(1)} %get-tuple-element.87.od_ref), channel_id=1, source_target_pairs={{0,31},{1,2},{2,1},{3,4},{4,3},{5,6},{6,5},{7,8},{8,7},{9,10},{10,... | collective-permute-start | bytes 196616 | tf_op jit(solution)/shard_map/ppermute | solution.py:331
  36.8 4.3 %collective-permute-start.7 = (f32[2,8,8,128]{3,2,1,0:T(8,128)S(1)}, f32[2,8,8,128]{3,2,1,0:T(8,128)S(1)}, u32[]{:S(2)}, u32[]{:S(2)}) collective-permute-start(f32[2,8,8,128]{3,2,1,0:T(8,128)S(1)} %get-tuple-element.88.ev_ref), channel_id=1, source_target_pairs={{0,1},{1,0},{2,3},{3,2},{4,5},{5,4},{6,7},{7,6},{8,9},{9,8},{10,11... | collective-permute-start | bytes 196616 | tf_op jit(solution)/shard_map/ppermute | solution.py:332
  41.4 8.6 %collective-permute-start.8 = (f32[2,8,8,128]{3,2,1,0:T(8,128)S(1)}, f32[2,8,8,128]{3,2,1,0:T(8,128)S(1)}, u32[]{:S(2)}, u32[]{:S(2)}) collective-permute-start(f32[2,8,8,128]{3,2,1,0:T(8,128)S(1)} %get-tuple-element.94.od_ref), channel_id=1, source_target_pairs={{0,31},{1,2},{2,1},{3,4},{4,3},{5,6},{6,5},{7,8},{8,7},{9,10},{10,... | collective-permute-start | bytes 196616 | tf_op jit(solution)/shard_map/ppermute | solution.py:331
  45.7 4.3 %collective-permute-start.9 = (f32[2,8,8,128]{3,2,1,0:T(8,128)S(1)}, f32[2,8,8,128]{3,2,1,0:T(8,128)S(1)}, u32[]{:S(2)}, u32[]{:S(2)}) collective-permute-start(f32[2,8,8,128]{3,2,1,0:T(8,128)S(1)} %get-tuple-element.95.ev_ref), channel_id=1, source_target_pairs={{0,1},{1,0},{2,3},{3,2},{4,5},{5,4},{6,7},{7,6},{8,9},{9,8},{10,11... | collective-permute-start | bytes 196616 | tf_op jit(solution)/shard_map/ppermute | solution.py:332
  50.2 8.8 %collective-permute-start.10 = (f32[2,8,8,128]{3,2,1,0:T(8,128)S(1)}, f32[2,8,8,128]{3,2,1,0:T(8,128)S(1)}, u32[]{:S(2)}, u32[]{:S(2)}) collective-permute-start(f32[2,8,8,128]{3,2,1,0:T(8,128)S(1)} %get-tuple-element.101.od_ref), channel_id=1, source_target_pairs={{0,31},{1,2},{2,1},{3,4},{4,3},{5,6},{6,5},{7,8},{8,7},{9,10},{10,... | collective-permute-start | bytes 196616 | tf_op jit(solution)/shard_map/ppermute | solution.py:331
  54.5 4.5 %collective-permute-start.11 = (f32[2,8,8,128]{3,2,1,0:T(8,128)S(1)}, f32[2,8,8,128]{3,2,1,0:T(8,128)S(1)}, u32[]{:S(2)}, u32[]{:S(2)}) collective-permute-start(f32[2,8,8,128]{3,2,1,0:T(8,128)S(1)} %get-tuple-element.102.ev_ref), channel_id=1, source_target_pairs={{0,1},{1,0},{2,3},{3,2},{4,5},{5,4},{6,7},{7,6},{8,9},{9,8},{10,11... | collective-permute-start | bytes 196616 | tf_op jit(solution)/shard_map/ppermute | solution.py:332
  59.3 8.6 %collective-permute-start.12 = (f32[2,8,8,128]{3,2,1,0:T(8,128)S(1)}, f32[2,8,8,128]{3,2,1,0:T(8,128)S(1)}, u32[]{:S(2)}, u32[]{:S(2)}) collective-permute-start(f32[2,8,8,128]{3,2,1,0:T(8,128)S(1)} %get-tuple-element.108.od_ref), channel_id=1, source_target_pairs={{0,31},{1,2},{2,1},{3,4},{4,3},{5,6},{6,5},{7,8},{8,7},{9,10},{10,... | collective-permute-start | bytes 196616 | tf_op jit(solution)/shard_map/ppermute | solution.py:331
  63.4 4.5 %collective-permute-start.13 = (f32[2,8,8,128]{3,2,1,0:T(8,128)S(1)}, f32[2,8,8,128]{3,2,1,0:T(8,128)S(1)}, u32[]{:S(2)}, u32[]{:S(2)}) collective-permute-start(f32[2,8,8,128]{3,2,1,0:T(8,128)S(1)} %get-tuple-element.109.ev_ref), channel_id=1, source_target_pairs={{0,1},{1,0},{2,3},{3,2},{4,5},{5,4},{6,7},{7,6},{8,9},{9,8},{10,11... | collective-permute-start | bytes 196616 | tf_op jit(solution)/shard_map/ppermute | solution.py:332
  68.2 8.6 %collective-permute-start.14 = (f32[2,8,8,128]{3,2,1,0:T(8,128)S(1)}, f32[2,8,8,128]{3,2,1,0:T(8,128)S(1)}, u32[]{:S(2)}, u32[]{:S(2)}) collective-permute-start(f32[2,8,8,128]{3,2,1,0:T(8,128)S(1)} %get-tuple-element.115.od_ref), channel_id=1, source_target_pairs={{0,31},{1,2},{2,1},{3,4},{4,3},{5,6},{6,5},{7,8},{8,7},{9,10},{10,... | collective-permute-start | bytes 196616 | tf_op jit(solution)/shard_map/ppermute | solution.py:331
  72.6 4.3 %collective-permute-start.15 = (f32[2,8,8,128]{3,2,1,0:T(8,128)S(1)}, f32[2,8,8,128]{3,2,1,0:T(8,128)S(1)}, u32[]{:S(2)}, u32[]{:S(2)}) collective-permute-start(f32[2,8,8,128]{3,2,1,0:T(8,128)S(1)} %get-tuple-element.116.ev_ref), channel_id=1, source_target_pairs={{0,1},{1,0},{2,3},{3,2},{4,5},{5,4},{6,7},{7,6},{8,9},{9,8},{10,11... | collective-permute-start | bytes 196616 | tf_op jit(solution)/shard_map/ppermute | solution.py:332
  77.1 8.6 %collective-permute-start.16 = (f32[2,8,8,128]{3,2,1,0:T(8,128)S(1)}, f32[2,8,8,128]{3,2,1,0:T(8,128)S(1)}, u32[]{:S(2)}, u32[]{:S(2)}) collective-permute-start(f32[2,8,8,128]{3,2,1,0:T(8,128)S(1)} %get-tuple-element.122.od_ref), channel_id=1, source_target_pairs={{0,31},{1,2},{2,1},{3,4},{4,3},{5,6},{6,5},{7,8},{8,7},{9,10},{10,... | collective-permute-start | bytes 196616 | tf_op jit(solution)/shard_map/ppermute | solution.py:331
  81.4 4.3 %collective-permute-start.17 = (f32[2,8,8,128]{3,2,1,0:T(8,128)S(1)}, f32[2,8,8,128]{3,2,1,0:T(8,128)S(1)}, u32[]{:S(2)}, u32[]{:S(2)}) collective-permute-start(f32[2,8,8,128]{3,2,1,0:T(8,128)S(1)} %get-tuple-element.123.ev_ref), channel_id=1, source_target_pairs={{0,1},{1,0},{2,3},{3,2},{4,5},{5,4},{6,7},{7,6},{8,9},{9,8},{10,11... | collective-permute-start | bytes 196616 | tf_op jit(solution)/shard_map/ppermute | solution.py:332
where the time goes:
time: 86.9 us; the launch traced here: 86.7 us
  starting transfers between devices  41 us (47%)
  Pallas kernels  23.7 us (27%)
  waiting for transfers between devices  18.5 us (21%)
  local copies, waits for them, and re-layouts  3.41 us (4%)
    ppermute x9, starting transfers between devices, per_device(): swap_od = lambda x: lax.ppermute(x, 'elem', odd_pairs)  41 us
    pallas_call x19, Pallas kernels, call(): pl.pallas_call(kernel, out_shape=shapes if len(shapes) > 1 else shapes[0]...  23.7 us
    ppermute x9, waiting for transfers between devices, per_device(): swap_od = lambda x: lax.ppermute(x, 'elem', odd_pairs)  16.6 us
    unnamed x12, local copies, waits for them, and re-layouts  3.34 us
    ppermute x9, waiting for transfers between devices, per_device(): swap_ev = lambda x: lax.ppermute(x, 'elem', even_pairs)  1.95 us
  transfers between devices with their start and end apart: 18, of which 11 were waited for; matrix products, arithmetic and copies ran while one was open for 0% of the time, Pallas kernels for 23%

commit v1 on v0

v1 whole, which is shorter than its diff:
```python
import jax
import jax.numpy as jnp
import numpy as np
from jax import lax
from jax.experimental import pallas as pl
from jax.experimental.pallas import tpu as pltpu
from jax.sharding import PartitionSpec as P

ORDER = 7
EXT = ORDER + 1
SUBSTEPS = 2
STAGES = 4
EY = 8
EZ = 16
LANES = EY * EZ
SUB = 8

time_step = 0.015


def legendre_table(points, degree):
    table = np.zeros((points.shape[0], degree + 1))
    table[:, 0] = 1.0
    table[:, 1] = points
    for level in range(2, degree + 1):
        table[:, level] = (
            (2 * level - 1) * points * table[:, level - 1] - (level - 1) * table[:, level - 2]
        ) / level
    return table


def gll_derivative(degree):
    extent = degree + 1
    points = np.cos(np.pi * np.arange(extent) / degree)
    for sweep in range(60):
        table = legendre_table(points, degree)
        points = points - (points * table[:, degree] - table[:, degree - 1]) / (
            extent * table[:, degree]
        )
    points = points[::-1].copy()
    values = legendre_table(points, degree)[:, degree]
    matrix = np.zeros((extent, extent))
    for target in range(extent):
        for source in range(extent):
            if target != source:
                matrix[target, source] = values[target] / (
                    values[source] * (points[target] - points[source])
                )
    matrix[0, 0] = -degree * (degree + 1) / 4.0
    matrix[extent - 1, extent - 1] = degree * (degree + 1) / 4.0
    return matrix


DM = gll_derivative(ORDER)
SUM_PART = [[(DM[j, a] + DM[j, 7 - a]) / 2 for a in range(4)] for j in range(4)]
DIF_PART = [[(DM[j, a] - DM[j, 7 - a]) / 2 for a in range(4)] for j in range(4)]
ROT = np.array([[DM[k, (k - r) % 8] for k in range(8)] for r in range(8)], np.float32)


def combine(coefs, items):
    total = None
    for c, x in zip(coefs, items):
        term = x * np.float32(c)
        total = term if total is None else total + term
    return total


def along_second(plane):
    even = [plane[a] + plane[7 - a] for a in range(4)]
    odd = [plane[a] - plane[7 - a] for a in range(4)]
    out = [None] * 8
    for j in range(4):
        e = combine(SUM_PART[j], even)
        o = combine(DIF_PART[j], odd)
        out[j] = o + e
        out[7 - j] = o - e
    return out


def along_third(x, rot):
    total = x * rot[0]
    for r in range(1, 8):
        total = total + pltpu.roll(x, r, 0) * rot[r]
    return total


def gather_lanes(x, idx):
    return jnp.take_along_axis(x, idx, axis=1, mode="promise_in_bounds")


def third_tables():
    lane = lax.broadcasted_iota(jnp.int32, (SUB, LANES), 1)
    k = lax.broadcasted_iota(jnp.int32, (SUB, LANES), 0)
    z = lane % EZ
    back = jnp.where(z == 0, lane + (EZ - 1), lane - 1)
    ahead = jnp.where(z == EZ - 1, lane - (EZ - 1), lane + 1)
    return jnp.where(k == 0, back, ahead), k == 0, k == ORDER


def plane_sum(plane, tables):
    idx, first, last = tables
    up = plane[7] + pltpu.roll(plane[0], LANES - EZ, 1)
    plane = [pltpu.roll(up, EZ, 1)] + list(plane[1:7]) + [up]
    out = []
    for v in plane:
        x = jnp.where(first, pltpu.roll(v, 1, 0), jnp.where(last, pltpu.roll(v, 7, 0), 0.0))
        out.append(v + gather_lanes(x, idx))
    return out


def write(ref, lead, plane):
    for j, v in enumerate(plane):
        ref[lead + (j,)] = v


def read(ref, *lead):
    return [ref[lead + (j,)] for j in range(8)]


def brick_index(order_ref):
    order = jnp.broadcast_to(order_ref[...], (LANES, LANES))
    pos = lax.broadcasted_iota(jnp.int32, (LANES, LANES), 0)
    hot = jnp.where(order == pos, 1.0, 0.0).astype(jnp.bfloat16)
    slot = lax.broadcasted_iota(jnp.int32, (SUB, LANES), 1).astype(jnp.float32).astype(jnp.bfloat16)
    found = lax.dot_general(
        slot, hot, (((1,), (1,)), ((), ())), preferred_element_type=jnp.float32
    )
    return found.astype(jnp.int32)


def source_plane(parity, i):
    return jnp.where(parity == 1, ORDER - i, i)


def source_plane(parity, i):
    return jnp.where(parity == 1, ORDER - i, i)


def project_faces(order_ref, scal_ref, mass_ref, od_ref, ev_ref, order_buf, scal_buf, mass_buf, sems):
    parity = lax.axis_index("elem") % 2
    copies = [pltpu.make_async_copy(order_ref, order_buf, sems.at[6])]
    for face in range(2):
        src = source_plane(parity, face * ORDER)
        copies.append(pltpu.make_async_copy(mass_ref.at[src], mass_buf.at[face], sems.at[face]))
        for m in range(2):
            copies.append(
                pltpu.make_async_copy(
                    scal_ref.at[m, src], scal_buf.at[face, m], sems.at[2 + 2 * face + m]
                )
            )
    for copy in copies:
        copy.start()
    tables = third_tables()
    copies[0].wait()
    idx = brick_index(order_buf)
    for copy in copies[1:]:
        copy.wait()
    for face, out in ((0, od_ref), (1, ev_ref)):
        weight = [gather_lanes(mass_buf[face, j], idx) for j in range(8)]
        write(out, (2,), plane_sum(weight, tables))
        for m in range(2):
            plane = [gather_lanes(scal_buf[face, m, j], idx) * weight[j] for j in range(8)]
            write(out, (m,), plane_sum(plane, tables))


def prepare(order_ref, scal_ref, mass_ref, tr_ref, gi_ref, q_ref, ri_ref, ti_ref, tf_ref):
    parity = lax.axis_index("elem") % 2
    idx = brick_index(order_ref)
    tables = third_tables()
    sign = jnp.where(parity == 1, time_step, -time_step).astype(jnp.float32)
    signs = (sign, np.float32(-time_step), np.float32(-time_step))

    for face in range(2):
        src = source_plane(parity, face * ORDER)
        for r in range(3):
            for j in range(8):
                tf_ref[face, r, j] = gather_lanes(tr_ref[r, src, j], idx) * signs[r]

    def body(i, carry):
        src = source_plane(parity, i + 1)
        for r in range(3):
            for j in range(8):
                ti_ref[i, r, j] = gather_lanes(tr_ref[r, src, j], idx) * signs[r]
        weight = [gather_lanes(mass_ref[src, j], idx) for j in range(8)]
        inverse = [1.0 / v for v in plane_sum(weight, tables)]
        write(ri_ref, (i,), inverse)
        for m in range(2):
            plane = [gather_lanes(scal_ref[m, src, j], idx) * weight[j] for j in range(8)]
            plane = plane_sum(plane, tables)
            write(gi_ref, (m, i), [plane[j] * inverse[j] for j in range(8)])
        return carry

    lax.fori_loop(0, 6, body, 0)
    face_partials(gi_ref, q_ref)


def face_partials(gi_ref, q_ref):
    for m in range(2):
        for j in range(8):
            rows = [gi_ref[m, i, j] for i in range(6)]
            for face in range(2):
                q_ref[face, m, j] = combine(DM[face * ORDER, 1:7], rows)


def in_plane(plane, t_ref, lead, rot):
    second = along_second(plane)
    return [
        t_ref[lead + (1, j)] * second[j] + t_ref[lead + (2, j)] * along_third(plane[j], rot)
        for j in range(8)
    ]


def inner_open(gi_ref, ti_ref, rot, d_ref, wp_ref):
    def body(i, carry):
        row = [d_ref[i + 1, a + 1] for a in range(6)]
        for m in range(2):
            rest = in_plane(read(gi_ref, m, i), ti_ref, (i,), rot)
            for j in range(8):
                first = gi_ref[m, 0, j] * row[0]
                for a in range(1, 6):
                    first = first + gi_ref[m, a, j] * row[a]
                wp_ref[m, i, j] = rest[j] + ti_ref[i, 0, j] * first
        return carry

    lax.fori_loop(0, 6, body, 0)


def inner_close(p0_ref, p7_ref, wp_ref, ri_ref, ti_ref, d_ref, scale, put):
    tables = third_tables()

    def body(i, carry):
        near, far = d_ref[i + 1, 0], d_ref[i + 1, ORDER]
        inverse = [ri_ref[i, j] * np.float32(scale) for j in range(8)]
        for m in range(2):
            plane = [
                wp_ref[m, i, j] + ti_ref[i, 0, j] * (p0_ref[m, j] * near + p7_ref[m, j] * far)
                for j in range(8)
            ]
            plane = plane_sum(plane, tables)
            put(m, i, [plane[j] * inverse[j] for j in range(8)])
        return carry

    lax.fori_loop(0, 6, body, 0)


def rotations(rot_ref):
    return [rot_ref[r] for r in range(8)]


def both_faces(p0, p7, q_ref, tf_ref, rot, tables, sod_ref, sev_ref):
    for face, own, out in ((1, p7, sev_ref), (0, p0, sod_ref)):
        for m in range(2):
            rest = in_plane(own[m], tf_ref, (face,), rot)
            plane = [
                rest[j]
                + tf_ref[face, 0, j]
                * (
                    q_ref[face, m, j]
                    + p0[m][j] * np.float32(DM[face * ORDER, 0])
                    + p7[m][j] * np.float32(DM[face * ORDER, ORDER])
                )
                for j in range(8)
            ]
            write(out, (m,), plane_sum(plane, tables))


def start_faces(od_ref, ev_ref, rod_ref, rev_ref, q_ref, tf_ref, rot_ref,
                p0_ref, p7_ref, rf_ref, sod_ref, sev_ref):
    p = []
    for face, (own, got, out) in enumerate(((od_ref, rod_ref, p0_ref), (ev_ref, rev_ref, p7_ref))):
        inverse = [1.0 / (own[2, j] + got[2, j]) for j in range(8)]
        write(rf_ref, (face,), inverse)
        p.append([[(own[m, j] + got[m, j]) * inverse[j] for j in range(8)] for m in range(2)])
        for m in range(2):
            write(out, (m,), p[face][m])
    both_faces(p[0], p[1], q_ref, tf_ref, rotations(rot_ref), third_tables(), sod_ref, sev_ref)


def shared_terms(p0, t_ref, rot, tables):
    rest = in_plane(p0, t_ref, (), rot)
    plane = [rest[j] + t_ref[0, j] * (p0[j] * np.float32(DM[0, 0])) for j in range(8)]
    return plane_sum(plane, tables)


def make_odd_face(scale, total, early):
    def odd_face(*refs):
        od_ref, rod_ref, e_ref, rf_ref, accf_ref, q_ref, tf_ref, rot_ref = refs[:8]
        p0_ref, w0_ref, w7_ref = refs[8:11]
        rot = rotations(rot_ref)
        tables = third_tables()
        if early:
            ts_ref = refs[11]
            for r in range(3):
                write(ts_ref, (r,), [tf_ref[0, r, j] + rod_ref[2 + r, j] for j in range(8)])
        for m in range(2):
            shared = read(e_ref, m)
            if early:
                shared = shared_terms(shared, ts_ref, rot, tables)
            p0 = [
                (od_ref[m, j] + rod_ref[m, j] + shared[j]) * (rf_ref[0, j] * np.float32(scale))
                for j in range(8)
            ]
            if total:
                p0 = [p0[j] + accf_ref[0, m, j] for j in range(8)]
            write(p0_ref, (m,), p0)
            rest = in_plane(p0, tf_ref, (0,), rot)
            write(w0_ref, (m,), [
                rest[j] + tf_ref[0, 0, j] * (q_ref[0, m, j] + p0[j] * np.float32(DM[0, 0]))
                for j in range(8)
            ])
            write(w7_ref, (m,), [
                tf_ref[1, 0, j] * (q_ref[1, m, j] + p0[j] * np.float32(DM[ORDER, 0]))
                for j in range(8)
            ])

    return odd_face


def make_even_face(scale, total):
    def even_face(ev_ref, rev_ref, w0_ref, w7_ref, rf_ref, accf_ref, tf_ref, rot_ref,
                  p7_ref, sod_ref, sev_ref):
        rot = rotations(rot_ref)
        tables = third_tables()
        for m in range(2):
            p7 = [
                (ev_ref[m, j] + rev_ref[m, j]) * (rf_ref[1, j] * np.float32(scale))
                for j in range(8)
            ]
            if total:
                p7 = [p7[j] + accf_ref[1, m, j] for j in range(8)]
            write(p7_ref, (m,), p7)
            rest = in_plane(p7, tf_ref, (1,), rot)
            plane = [
                rest[j] + w7_ref[m, j] + tf_ref[1, 0, j] * (p7[j] * np.float32(DM[ORDER, ORDER]))
                for j in range(8)
            ]
            write(sev_ref, (m,), plane_sum(plane, tables))
            plane = [
                w0_ref[m, j] + tf_ref[0, 0, j] * (p7[j] * np.float32(DM[0, ORDER]))
                for j in range(8)
            ]
            write(sod_ref, (m,), plane_sum(plane, tables))

    return even_face


def make_first_inner(scale, opening):
    def first_inner(p0_ref, p7_ref, gi_ref, acci_ref, wp_ref, ri_ref, ti_ref, d_ref,
                    gn_ref, an_ref, q_ref):
        def put(m, i, value):
            write(gn_ref, (m, i), value)
            base = gi_ref if opening else acci_ref
            write(an_ref, (m, i), [base[m, i, j] + value[j] for j in range(8)])

        inner_close(p0_ref, p7_ref, wp_ref, ri_ref, ti_ref, d_ref, scale, put)
        face_partials(gn_ref, q_ref)

    return first_inner


def make_ahead(scale, carry_transport):
    def ahead(ev_ref, rev_ref, rf_ref, q_ref, tf_ref, p7_ref, sod_ref):
        tables = third_tables()
        for m in range(2):
            p7 = [
                (ev_ref[m, j] + rev_ref[m, j]) * (rf_ref[1, j] * np.float32(scale))
                for j in range(8)
            ]
            write(p7_ref, (m,), p7)
            plane = [
                tf_ref[0, 0, j] * (q_ref[0, m, j] + p7[j] * np.float32(DM[0, ORDER]))
                for j in range(8)
            ]
            write(sod_ref, (m,), plane_sum(plane, tables))
        if carry_transport:
            for r in range(3):
                write(sod_ref, (2 + r,), read(tf_ref, 0, r))

    return ahead


def between(p7_ref, gi_ref, q_ref, tf_ref, ti_ref, rot_ref, d_ref, wp_ref, w7_ref):
    rot = rotations(rot_ref)
    for m in range(2):
        p7 = read(p7_ref, m)
        rest = in_plane(p7, tf_ref, (1,), rot)
        write(w7_ref, (m,), [
            rest[j] + tf_ref[1, 0, j] * (q_ref[1, m, j] + p7[j] * np.float32(DM[ORDER, ORDER]))
            for j in range(8)
        ])
    inner_open(gi_ref, ti_ref, rot, d_ref, wp_ref)


def make_behind(scale):
    def behind(od_ref, rod_ref, rf_ref, w7_ref, tf_ref, p0_ref, sev_ref):
        tables = third_tables()
        for m in range(2):
            p0 = [
                (od_ref[m, j] + rod_ref[m, j]) * (rf_ref[0, j] * np.float32(scale))
                for j in range(8)
            ]
            write(p0_ref, (m,), p0)
            plane = [
                w7_ref[m, j] + tf_ref[1, 0, j] * (p0[j] * np.float32(DM[ORDER, 0]))
                for j in range(8)
            ]
            write(sev_ref, (m,), plane_sum(plane, tables))

    return behind


def make_second_inner(scale, opening, closing, early):
    def second_inner(*refs):
        (p0_ref, p7_ref, b0_ref, b7_ref, accf_ref, acci_ref, wp_ref, ri_ref, ti_ref, ts_ref,
         rot_ref, d_ref) = refs[:12]
        gn_ref, q_ref, an_ref, afn_ref, wn_ref = refs[12:17]
        rot = rotations(rot_ref)
        if not early:
            e_ref = refs[17]
            tables = third_tables()
            for m in range(2):
                write(e_ref, (m,), shared_terms(read(p0_ref, m), ts_ref, rot, tables))
        for face, (now, before) in enumerate(((p0_ref, b0_ref), (p7_ref, b7_ref))):
            for m in range(2):
                for j in range(8):
                    value = now[m, j] + before[m, j]
                    afn_ref[face, m, j] = value if opening else value + accf_ref[face, m, j]

        def put(m, i, value):
            total = [acci_ref[m, i, j] + value[j] for j in range(8)]
            write(gn_ref, (m, i), total if closing else value)
            if not closing:
                write(an_ref, (m, i), total)

        inner_close(p0_ref, p7_ref, wp_ref, ri_ref, ti_ref, d_ref, scale, put)
        face_partials(gn_ref, q_ref)
        inner_open(gn_ref, ti_ref, rot, d_ref, wn_ref)

    return second_inner


def make_last_inner(scale):
    def last_inner(order_ref, p0_ref, p7_ref, b0_ref, b7_ref, accf_ref, acci_ref, wp_ref, ri_ref,
                   ti_ref, ts_ref, rot_ref, d_ref, out_ref, afn_ref, e_ref, buf, sems):
        parity = lax.axis_index("elem") % 2
        idx = jnp.broadcast_to(order_ref[...], (SUB, LANES))

        def put(m, i, value):
            total = [acci_ref[m, i, j] + value[j] for j in range(8)]
            dst = source_plane(parity, i + 1) - 1
            write(buf, (m, dst), [gather_lanes(v, idx) for v in total])

        inner_close(p0_ref, p7_ref, wp_ref, ri_ref, ti_ref, d_ref, scale, put)
        copies = [
            pltpu.make_async_copy(buf.at[m], out_ref.at[m, pl.ds(1, 6)], sems.at[m])
            for m in range(2)
        ]
        for copy in copies:
            copy.start()
        rot = rotations(rot_ref)
        tables = third_tables()
        for m in range(2):
            write(e_ref, (m,), shared_terms(read(p0_ref, m), ts_ref, rot, tables))
        for face, (now, before) in enumerate(((p0_ref, b0_ref), (p7_ref, b7_ref))):
            for m in range(2):
                for j in range(8):
                    afn_ref[face, m, j] = now[m, j] + before[m, j] + accf_ref[face, m, j]
        for copy in copies:
            copy.wait()

    return last_inner


def make_finish(face, scale):
    def finish(order_ref, own_ref, got_ref, e_ref, rf_ref, accf_ref, part_ref, out_ref, buf, sems):
        parity = lax.axis_index("elem") % 2
        idx = jnp.broadcast_to(order_ref[...], (SUB, LANES))
        dst = source_plane(parity, face * ORDER)
        copies = []
        for m in range(2):
            for j in range(8):
                value = own_ref[m, j] + got_ref[m, j]
                if face == 0:
                    value = value + e_ref[m, j]
                value = value * (rf_ref[face, j] * np.float32(scale)) + accf_ref[face, m, j]
                buf[m, j] = gather_lanes(value, idx)
            copy = pltpu.make_async_copy(buf.at[m], out_ref.at[m, dst], sems.at[m])
            copy.start()
            copies.append(copy)
        for copy in copies:
            copy.wait()

    return finish


VM = pl.BlockSpec(memory_space=pltpu.VMEM)
SM = pl.BlockSpec(memory_space=pltpu.SMEM)
HB = pl.BlockSpec(memory_space=pltpu.HBM)


def call(kernel, outs, args, name, cost, smem=(), hbm=(), hbm_out=(), scratch=(), alias={}):
    specs = [SM if n in smem else HB if n in hbm else VM for n in range(len(args))]
    out_specs = [HB if n in hbm_out else VM for n in range(len(outs))]
    shapes = [jax.ShapeDtypeStruct(s, jnp.float32) for s in outs]
    single = len(outs) == 1
    return pl.pallas_call(
        kernel,
        out_shape=shapes[0] if single else shapes,
        in_specs=specs,
        out_specs=out_specs[0] if single else out_specs,
        scratch_shapes=list(scratch),
        input_output_aliases=alias,
        name=name,
        compiler_params=pltpu.CompilerParams(vmem_limit_bytes=8 << 20),
        cost_estimate=pl.CostEstimate(
            flops=cost * 1000000, bytes_accessed=1 << 10, transcendentals=0
        ),
    )(*args)


def per_device(scalars, transport, mass, element_order):
    count = lax.axis_size("elem")
    even_pairs = [(i, i ^ 1) for i in range(count)]
    odd_pairs = [(i, (i + 1) % count if i % 2 else (i - 1) % count) for i in range(count)]
    swap_od = lambda x: lax.ppermute(x, "elem", odd_pairs)
    swap_ev = lambda x: lax.ppermute(x, "elem", even_pairs)
    rot = jnp.asarray(np.broadcast_to(ROT[:, :, None], (8, SUB, LANES)))
    dmat = jnp.asarray(DM, jnp.float32)
    members = scalars.shape[0]
    grid = (EXT, EXT, SUB, LANES)
    scal = scalars.reshape((members,) + grid)
    tr = transport.reshape((3,) + grid)
    mas = mass.reshape(grid)
    tile = (EXT, SUB, LANES)
    face, inner = (2,) + tile, (2, 6) + tile

    od, ev = call(
        project_faces, [(3,) + tile] * 2, (element_order, scal, mas), "project", 1, hbm=(0, 1, 2),
        scratch=[pltpu.VMEM((1, LANES), jnp.int32), pltpu.VMEM((2, 2) + tile, jnp.float32),
                 pltpu.VMEM((2,) + tile, jnp.float32), pltpu.SemaphoreType.DMA((7,))])
    rod, rev = swap_od(od), swap_ev(ev)
    gi, q, ri, ti, tf = call(
        prepare, [inner, (2,) + face, (6,) + tile, (6, 3) + tile, (2, 3) + tile],
        (element_order, scal, mas, tr), "prepare", 4000)

    def opening_terms(gi_ref, ti_ref, rot_ref, d_ref, wp_ref):
        inner_open(gi_ref, ti_ref, rotations(rot_ref), d_ref, wp_ref)

    wp = call(opening_terms, [inner], (gi, ti, rot, dmat), "terms", 2000, smem=(3,))
    p0, p7, rf, od, ev = call(
        start_faces, [face, face, (2,) + tile, face, face],
        (od, ev, rod, rev, q, tf, rot), "faces", 1)
    acci, accf, ts, shared = gi, q, tf, None
    pairs = SUBSTEPS * STAGES // 2
    for n in range(pairs):
        s = 2 * n % STAGES + 1
        opening, closing, early = s == 1, s + 1 == STAGES, n == 0
        rev, rod = swap_ev(ev), swap_od(od)
        gm, acci, q = call(
            make_first_inner(1.0 / s, opening), [inner, inner, (2,) + face],
            (p0, p7, gi, acci, wp, ri, ti, dmat), "first", 1000, smem=(7,))
        m7, od2 = call(
            make_ahead(1.0 / s, early), [face, ((5 if early else 2),) + tile],
            (ev, rev, rf, q, tf), "ahead", 1)
        rod2 = swap_od(od2)
        wp, w7 = call(
            between, [inner, face], (m7, gm, q, tf, ti, rot, dmat), "between", 2000, smem=(6,))
        m0, ev2 = call(
            make_behind(1.0 / s), [face, face], (od, rod, rf, w7, tf), "behind", 1)
        rev2 = swap_ev(ev2)
        if n < pairs - 1:
            outs = [inner, (2,) + face, inner, (2,) + face, inner] + ([] if early else [face])
            res = call(
                make_second_inner(1.0 / (s + 1), opening, closing, early), outs,
                (m0, m7, p0, p7, accf, acci, wp, ri, ti, ts, rot, dmat), "second", 3000, smem=(11,))
            gi, q, acci, accf, wp = res[:5]
            extra = m0 if early else res[5]
            res = call(
                make_odd_face(1.0 / (s + 1), closing, early),
                [face] * 3 + ([(3,) + tile] if early else []),
                (od2, rod2, extra, rf, accf, q, tf, rot), "odd", 3000)
            p0, w0, w7 = res[:3]
            if early:
                ts = res[3]
            p7, od, ev = call(
                make_even_face(1.0 / (s + 1), closing), [face] * 3,
                (ev2, rev2, w0, w7, rf, accf, tf, rot), "even", 1)
        else:
            out, accf, shared = call(
                make_last_inner(1.0 / (s + 1)), [(members,) + grid, (2,) + face, face],
                (element_order, m0, m7, p0, p7, accf, acci, wp, ri, ti, ts, rot, dmat), "last", 3000,
                smem=(12,), hbm_out=(0,),
                scratch=[pltpu.VMEM(inner, jnp.float32), pltpu.SemaphoreType.DMA((2,))])
            for side, own, got in ((0, od2, rod2), (1, ev2, rev2)):
                out = call(
                    make_finish(side, 1.0 / (s + 1)), [(members,) + grid],
                    (element_order, own, got, shared, rf, accf, out), "finish", 3000 - 2999 * side,
                    hbm=(6,), hbm_out=(0,), alias={6: 0},
                    scratch=[pltpu.VMEM(face, jnp.float32), pltpu.SemaphoreType.DMA((2,))])
    return out.reshape(scalars.shape)


def solution(mesh):
    in_specs = (P("ens", None, "elem"), P(None, None, "elem"), P(None, "elem"), P("elem", None))
    out_specs = P("ens", None, "elem")
    return jax.shard_map(
        per_device, mesh=mesh, in_specs=in_specs, out_specs=out_specs, check_vma=False
    )
```

time: 86.9 us -> 78.9 us (0.908)
  waiting for transfers between devices: 18.5 us -> 6.02 us
  Pallas kernels: 23.7 us -> 33.9 us
  starting transfers between devices: 41 us -> 35.1 us
    ppermute x9, waiting for transfers between devices: 16.6 us -> 4.7 us  [per_device(): swap_od = lambda x: lax.ppermute(x, 'elem', odd_pairs)]
    pallas_call x19 -> x32, Pallas kernels: 23.7 us -> 33.9 us  [call(): pl.pallas_call(kernel, out_shape=shapes[0] if single else shapes, in_spec...]
    ppermute x9, starting transfers between devices: 41 us -> 31.8 us  [per_device(): swap_od = lambda x: lax.ppermute(x, 'elem', odd_pairs)]
    ppermute x9, starting transfers between devices: 0.02 us -> 3.33 us  [per_device(): swap_ev = lambda x: lax.ppermute(x, 'elem', even_pairs)]
  transfers between devices with their start and end apart: 18 -> 18, of which waited for: 11 -> 7; matrix products, arithmetic and copies ran while one was open for 0% -> 0% of each run, Pallas kernels for 23% -> 40%
where the time goes in v1:
time: 78.9 us; the launch traced here: 78.6 us
  starting transfers between devices  35.1 us (44%)
  Pallas kernels  33.9 us (43%)
  waiting for transfers between devices  6.02 us (8%)
  local copies, waits for them, and re-layouts  3.33 us (4%)
    pallas_call x32, Pallas kernels, call(): pl.pallas_call(kernel, out_shape=shapes[0] if single else shapes, in_spec...  33.9 us
    ppermute x9, starting transfers between devices, per_device(): swap_od = lambda x: lax.ppermute(x, 'elem', odd_pairs)  31.8 us
    ppermute x9, waiting for transfers between devices, per_device(): swap_od = lambda x: lax.ppermute(x, 'elem', odd_pairs)  4.7 us
    ppermute x9, starting transfers between devices, per_device(): swap_ev = lambda x: lax.ppermute(x, 'elem', even_pairs)  3.33 us
    unnamed x12, local copies, waits for them, and re-layouts  3.26 us
  transfers between devices with their start and end apart: 18, of which 7 were waited for; matrix products, arithmetic and copies ran while one was open for 0% of the time, Pallas kernels for 40%

profile of v1, /device:TPU:0, one launch (start us, length us, event | category | flops | bytes accessed | tf_op | source)
XLA Modules:
  0.0 78.6 jit_solution(11047840446881126046)
XLA Ops:
  0.7 1.0 %copy-done = f32[2,512,128]{2,1,0:T(8,128)S(1)} copy-done((f32[2,512,128]{2,1,0:T(8,128)S(1)}, f32[2,512,128]{2,1,0:T(8,128)}, u32[]{:S(2)}) %copy-start) | copy-done | bytes 524312
  1.7 0.9 %copy-done.1 = f32[512,128]{1,0:T(8,128)S(1)} copy-done((f32[512,128]{1,0:T(8,128)S(1)}, f32[512,128]{1,0:T(8,128)}, u32[]{:S(2)}) %copy-start.1) | copy-done | bytes 262168
  2.7 0.8 project.1
  3.4 6.7 %collective-permute-start = (f32[3,8,8,128]{3,2,1,0:T(8,128)S(1)}, f32[3,8,8,128]{3,2,1,0:T(8,128)S(1)}, u32[]{:S(2)}, u32[]{:S(2)}) collective-permute-start(f32[3,8,8,128]{3,2,1,0:T(8,128)S(1)} %get-tuple-element.92.od_ref), channel_id=1, source_target_pairs={{0,31},{1,2},{2,1},{3,4},{4,3},{5,6},{6,5},{7,8},{8,7},{9,10},{10,... | collective-permute-start | bytes 294920 | tf_op jit(solution)/shard_map/ppermute | solution.py:525
  10.2 2.2 %prepare.1 = (f32[2,6,8,8,128]{4,3,2,1,0:T(8,128)S(1)}, f32[2,2,8,8,128]{4,3,2,1,0:T(8,128)S(1)}, f32[6,8,8,128]{3,2,1,0:T(8,128)S(1)}, f32[6,3,8,8,128]{4,3,2,1,0:T(8,128)S(1)}, f32[2,3,8,8,128]{4,3,2,1,0:T(8,128)S(1)}) custom-call(s32[1,128]{1,0:T(1,128)S(1)} %copy-done.2, f32[2,8,8,8,128]{4,3,2,1,0:T(8,128)S(1)} %bitcast.5, f32[8,8,8,128]{3,2,1,0:T(8,128)S(1)} %bitcast.7, ...), custom_call_target="tpu_custom_call" | custom-call | flops 4000000000 | bytes 1024 | tf_op jit(solution)/shard_map/prepare/pallas_call | solution.py:506
  13.1 1.3 %terms.1.wp_ref = f32[2,6,8,8,128]{4,3,2,1,0:T(8,128)S(1)} custom-call(f32[2,6,8,8,128]{4,3,2,1,0:T(8,128)S(1)} %get-tuple-element.101.gi_ref.acci_ref, f32[6,3,8,8,128]{4,3,2,1,0:T(8,128)S(1)} %get-tuple-element.102.ti_ref.refs_8_, f32[8,8,128]{2,1,0:T(8,128)S(1)} %jit_solution_.3.rot_ref.refs_10_.refs_7_, f32[8,8]{1,0:T(8,128)S(1)} %copy-done.4), custom_call_target="tpu_custom_call" | custom-call | flops 2000000000 | bytes 1024 | tf_op jit(solution)/shard_map/terms/pallas_call | solution.py:506
  15.1 1.7 %collective-permute-start.3 = (f32[2,8,8,128]{3,2,1,0:T(8,128)S(1)}, f32[2,8,8,128]{3,2,1,0:T(8,128)S(1)}, u32[]{:S(2)}, u32[]{:S(2)}) collective-permute-start(f32[2,8,8,128]{3,2,1,0:T(8,128)S(1)} %get-tuple-element.98.ev_ref), channel_id=1, source_target_pairs={{0,1},{1,0},{2,3},{3,2},{4,5},{5,4},{6,7},{7,6},{8,9},{9,8},{10,11... | collective-permute-start | bytes 196616 | tf_op jit(solution)/shard_map/ppermute | solution.py:526
  16.7 2.7 %collective-permute-start.2 = (f32[2,8,8,128]{3,2,1,0:T(8,128)S(1)}, f32[2,8,8,128]{3,2,1,0:T(8,128)S(1)}, u32[]{:S(2)}, u32[]{:S(2)}) collective-permute-start(f32[2,8,8,128]{3,2,1,0:T(8,128)S(1)} %get-tuple-element.96.od_ref), channel_id=1, source_target_pairs={{0,31},{1,2},{2,1},{3,4},{4,3},{5,6},{6,5},{7,8},{8,7},{9,10},{10,... | collective-permute-start | bytes 196616 | tf_op jit(solution)/shard_map/ppermute | solution.py:525
  19.4 2.0 %first.4 = (f32[2,6,8,8,128]{4,3,2,1,0:T(8,128)S(1)}, f32[2,6,8,8,128]{4,3,2,1,0:T(8,128)S(1)}, f32[2,2,8,8,128]{4,3,2,1,0:T(8,128)S(1)}) custom-call(f32[2,8,8,128]{3,2,1,0:T(8,128)S(1)} %get-tuple-element.99.p0_ref.refs_2_, f32[2,8,8,128]{3,2,1,0:T(8,128)S(1)} %get-tuple-element.100.p7_ref.refs_3_, ...), custom_call_target="tpu_custom_call" | custom-call | flops 1000000000 | bytes 1024 | tf_op jit(solution)/shard_map/first/pallas_call | solution.py:506
  21.7 3.5 %collective-permute-start.5 = (f32[5,8,8,128]{3,2,1,0:T(8,128)S(1)}, f32[5,8,8,128]{3,2,1,0:T(8,128)S(1)}, u32[]{:S(2)}, u32[]{:S(2)}) collective-permute-start(f32[5,8,8,128]{3,2,1,0:T(8,128)S(1)} %get-tuple-element.109.refs_0_), channel_id=1, source_target_pairs={{0,31},{1,2},{2,1},{3,4},{4,3},{5,6},{6,5},{7,8},{8,7},{9,10},{10,... | collective-permute-start | bytes 491528 | tf_op jit(solution)/shard_map/ppermute | solution.py:525
  25.2 1.3 %between.4 = (f32[2,6,8,8,128]{4,3,2,1,0:T(8,128)S(1)}, f32[2,8,8,128]{3,2,1,0:T(8,128)S(1)}) custom-call(f32[2,8,8,128]{3,2,1,0:T(8,128)S(1)} %get-tuple-element.105.p7_ref.refs_1_, f32[2,6,8,8,128]{4,3,2,1,0:T(8,128)S(1)} %get-tuple-element.106.gi_ref, f32[2,2,8,8,128]{4,3,2,1,0:T(8,128)S(1)} %get-tuple-element.104.q_ref, ...), custom_call_target="tpu_custom_call" | custom-call | flops 2000000000 | bytes 1024 | tf_op jit(solution)/shard_map/between/pallas_call | solution.py:506
  26.9 2.7 %second.3 = (f32[2,6,8,8,128]{4,3,2,1,0:T(8,128)S(1)}, f32[2,2,8,8,128]{4,3,2,1,0:T(8,128)S(1)}, f32[2,6,8,8,128]{4,3,2,1,0:T(8,128)S(1)}, f32[2,2,8,8,128]{4,3,2,1,0:T(8,128)S(1)}, f32[2,6,8,8,128]{4,3,2,1,0:T(8,128)S(1)}) custom-call(f32[2,8,8,128]{3,2,1,0:T(8,128)S(1)} %get-tuple-element.110.refs_0_.refs_2_, ...), custom_call_target="tpu_custom_call" | custom-call | flops 3000000000 | bytes 1024 | tf_op jit(solution)/shard_map/second/pallas_call | solution.py:506
  29.5 1.7 %collective-permute-done.5.refs_1_ = f32[5,8,8,128]{3,2,1,0:T(8,128)S(1)} collective-permute-done((f32[5,8,8,128]{3,2,1,0:T(8,128)S(1)}, f32[5,8,8,128]{3,2,1,0:T(8,128)S(1)}, u32[]{:S(2)}, u32[]{:S(2)}) %collective-permute-start.5) | collective-permute-done | bytes 163872 | tf_op jit(solution)/shard_map/ppermute | solution.py:525
  32.1 3.3 %collective-permute-start.6 = (f32[2,8,8,128]{3,2,1,0:T(8,128)S(1)}, f32[2,8,8,128]{3,2,1,0:T(8,128)S(1)}, u32[]{:S(2)}, u32[]{:S(2)}) collective-permute-start(f32[2,8,8,128]{3,2,1,0:T(8,128)S(1)} %get-tuple-element.117.od_ref), channel_id=1, source_target_pairs={{0,31},{1,2},{2,1},{3,4},{4,3},{5,6},{6,5},{7,8},{8,7},{9,10},{10,... | collective-permute-start | bytes 196616 | tf_op jit(solution)/shard_map/ppermute | solution.py:525
  35.5 2.0 %first.5 = (f32[2,6,8,8,128]{4,3,2,1,0:T(8,128)S(1)}, f32[2,6,8,8,128]{4,3,2,1,0:T(8,128)S(1)}, f32[2,2,8,8,128]{4,3,2,1,0:T(8,128)S(1)}) custom-call(f32[2,8,8,128]{3,2,1,0:T(8,128)S(1)} %get-tuple-element.119.p0_ref.refs_2_, f32[2,8,8,128]{3,2,1,0:T(8,128)S(1)} %get-tuple-element.120.p7_ref.refs_3_, f32[2,6,8,8,128]{4,3,2,1,0:T(8,128)S(1)} %get-tuple-element.121.gi_ref, ...), custom_call_target="tpu_custom_call" | custom-call | flops 1000000000 | bytes 1024 | tf_op jit(solution)/shard_map/first/pallas_call | solution.py:506
  37.7 3.0 %collective-permute-start.9 = (f32[2,8,8,128]{3,2,1,0:T(8,128)S(1)}, f32[2,8,8,128]{3,2,1,0:T(8,128)S(1)}, u32[]{:S(2)}, u32[]{:S(2)}) collective-permute-start(f32[2,8,8,128]{3,2,1,0:T(8,128)S(1)} %get-tuple-element.129.refs_0_), channel_id=1, source_target_pairs={{0,31},{1,2},{2,1},{3,4},{4,3},{5,6},{6,5},{7,8},{8,7},{9,10},{10,... | collective-permute-start | bytes 196616 | tf_op jit(solution)/shard_map/ppermute | solution.py:525
  40.7 1.3 %between.5 = (f32[2,6,8,8,128]{4,3,2,1,0:T(8,128)S(1)}, f32[2,8,8,128]{3,2,1,0:T(8,128)S(1)}) custom-call(f32[2,8,8,128]{3,2,1,0:T(8,128)S(1)} %get-tuple-element.125.p7_ref.refs_1_, f32[2,6,8,8,128]{4,3,2,1,0:T(8,128)S(1)} %get-tuple-element.126.gi_ref, f32[2,2,8,8,128]{4,3,2,1,0:T(8,128)S(1)} %get-tuple-element.124.q_ref, ...), custom_call_target="tpu_custom_call" | custom-call | flops 2000000000 | bytes 1024 | tf_op jit(solution)/shard_map/between/pallas_call | solution.py:506
  42.3 2.9 %second.4 = (f32[2,6,8,8,128]{4,3,2,1,0:T(8,128)S(1)}, f32[2,2,8,8,128]{4,3,2,1,0:T(8,128)S(1)}, f32[2,6,8,8,128]{4,3,2,1,0:T(8,128)S(1)}, f32[2,2,8,8,128]{4,3,...) custom-call(f32[2,8,8,128]{3,2,1,0:T(8,128)S(1)} %get-tuple-element.130.refs_0_, ...), custom_call_target="tpu_custom_call" | custom-call | flops 3000000000 | bytes 1024 | tf_op jit(solution)/shard_map/second/pallas_call | solution.py:506
  45.2 1.1 %collective-permute-done.9.refs_1_ = f32[2,8,8,128]{3,2,1,0:T(8,128)S(1)} collective-permute-done((f32[2,8,8,128]{3,2,1,0:T(8,128)S(1)}, f32[2,8,8,128]{3,2,1,0:T(8,128)S(1)}, u32[]{:S(2)}, u32[]{:S(2)}) %collective-permute-start.9) | collective-permute-done | bytes 65568 | tf_op jit(solution)/shard_map/ppermute | solution.py:525
  47.6 3.3 %collective-permute-start.10 = (f32[2,8,8,128]{3,2,1,0:T(8,128)S(1)}, f32[2,8,8,128]{3,2,1,0:T(8,128)S(1)}, u32[]{:S(2)}, u32[]{:S(2)}) collective-permute-start(f32[2,8,8,128]{3,2,1,0:T(8,128)S(1)} %get-tuple-element.139.od_ref), channel_id=1, source_target_pairs={{0,31},{1,2},{2,1},{3,4},{4,3},{5,6},{6,5},{7,8},{8,7},{9,10},{10,... | collective-permute-start | bytes 196616 | tf_op jit(solution)/shard_map/ppermute | solution.py:525
  51.0 2.0 %first.6 = (f32[2,6,8,8,128]{4,3,2,1,0:T(8,128)S(1)}, f32[2,6,8,8,128]{4,3,2,1,0:T(8,128)S(1)}, f32[2,2,8,8,128]{4,3,2,1,0:T(8,128)S(1)}) custom-call(f32[2,8,8,128]{3,2,1,0:T(8,128)S(1)} %get-tuple-element.141.p0_ref.refs_2_, f32[2,8,8,128]{3,2,1,0:T(8,128)S(1)} %get-tuple-element.142.p7_ref.refs_3_, f32[2,6,8,8,128]{4,3,2,1,0:T(8,128)S(1)} %get-tuple-element.143.gi_ref, ...), custom_call_target="tpu_custom_call" | custom-call | flops 1000000000 | bytes 1024 | tf_op jit(solution)/shard_map/first/pallas_call | solution.py:506
  53.2 3.0 %collective-permute-start.13 = (f32[2,8,8,128]{3,2,1,0:T(8,128)S(1)}, f32[2,8,8,128]{3,2,1,0:T(8,128)S(1)}, u32[]{:S(2)}, u32[]{:S(2)}) collective-permute-start(f32[2,8,8,128]{3,2,1,0:T(8,128)S(1)} %get-tuple-element.151.refs_0_), channel_id=1, source_target_pairs={{0,31},{1,2},{2,1},{3,4},{4,3},{5,6},{6,5},{7,8},{8,7},{9,10},{10,... | collective-permute-start | bytes 196616 | tf_op jit(solution)/shard_map/ppermute | solution.py:525
  56.1 1.3 %between.6 = (f32[2,6,8,8,128]{4,3,2,1,0:T(8,128)S(1)}, f32[2,8,8,128]{3,2,1,0:T(8,128)S(1)}) custom-call(f32[2,8,8,128]{3,2,1,0:T(8,128)S(1)} %get-tuple-element.147.p7_ref.refs_1_, f32[2,6,8,8,128]{4,3,2,1,0:T(8,128)S(1)} %get-tuple-element.148.gi_ref, f32[2,2,8,8,128]{4,3,2,1,0:T(8,128)S(1)} %get-tuple-element.146.q_ref, ...), custom_call_target="tpu_custom_call" | custom-call | flops 2000000000 | bytes 1024 | tf_op jit(solution)/shard_map/between/pallas_call | solution.py:506
  57.8 2.9 %second.5 = (f32[2,6,8,8,128]{4,3,2,1,0:T(8,128)S(1)}, f32[2,2,8,8,128]{4,3,2,1,0:T(8,128)S(1)}, f32[2,6,8,8,128]{4,3,2,1,0:T(8,128)S(1)}, f32[2,2,8,8,128]{4,3,...) custom-call(f32[2,8,8,128]{3,2,1,0:T(8,128)S(1)} %get-tuple-element.152.refs_0_, ...), custom_call_target="tpu_custom_call" | custom-call | flops 3000000000 | bytes 1024 | tf_op jit(solution)/shard_map/second/pallas_call | solution.py:506
  60.6 1.1 %collective-permute-done.13.refs_1_ = f32[2,8,8,128]{3,2,1,0:T(8,128)S(1)} collective-permute-done((f32[2,8,8,128]{3,2,1,0:T(8,128)S(1)}, f32[2,8,8,128]{3,2,1,0:T(8,128)S(1)}, u32[]{:S(2)}, u32[]{:S(2)}) %collective-permute-start.13) | collective-permute-done | bytes 65568 | tf_op jit(solution)/shard_map/ppermute | solution.py:525
  62.3 0.8 %collective-permute-start.15 = (f32[2,8,8,128]{3,2,1,0:T(8,128)S(1)}, f32[2,8,8,128]{3,2,1,0:T(8,128)S(1)}, u32[]{:S(2)}, u32[]{:S(2)}) collective-permute-start(f32[2,8,8,128]{3,2,1,0:T(8,128)S(1)} %get-tuple-element.161.ev_ref), channel_id=1, source_target_pairs={{0,1},{1,0},{2,3},{3,2},{4,5},{5,4},{6,7},{7,6},{8,9},{9,8},{10,11... | collective-permute-start | bytes 196616 | tf_op jit(solution)/shard_map/ppermute | solution.py:526
  63.1 3.3 %collective-permute-start.14 = (f32[2,8,8,128]{3,2,1,0:T(8,128)S(1)}, f32[2,8,8,128]{3,2,1,0:T(8,128)S(1)}, u32[]{:S(2)}, u32[]{:S(2)}) collective-permute-start(f32[2,8,8,128]{3,2,1,0:T(8,128)S(1)} %get-tuple-element.160.od_ref), channel_id=1, source_target_pairs={{0,31},{1,2},{2,1},{3,4},{4,3},{5,6},{6,5},{7,8},{8,7},{9,10},{10,... | collective-permute-start | bytes 196616 | tf_op jit(solution)/shard_map/ppermute | solution.py:525
  66.4 2.0 %first.7 = (f32[2,6,8,8,128]{4,3,2,1,0:T(8,128)S(1)}, f32[2,6,8,8,128]{4,3,2,1,0:T(8,128)S(1)}, f32[2,2,8,8,128]{4,3,2,1,0:T(8,128)S(1)}) custom-call(f32[2,8,8,128]{3,2,1,0:T(8,128)S(1)} %get-tuple-element.162.p0_ref.b0_ref, f32[2,8,8,128]{3,2,1,0:T(8,128)S(1)} %get-tuple-element.163.p7_ref.b7_ref, f32[2,6,8,8,128]{4,3,2,1,0:T(8,128)S(1)} %get-tuple-element.164.gi_ref, ...), custom_call_target="tpu_custom_call" | custom-call | flops 1000000000 | bytes 1024 | tf_op jit(solution)/shard_map/first/pallas_call | solution.py:506
  68.7 2.9 %collective-permute-start.17 = (f32[2,8,8,128]{3,2,1,0:T(8,128)S(1)}, f32[2,8,8,128]{3,2,1,0:T(8,128)S(1)}, u32[]{:S(2)}, u32[]{:S(2)}) collective-permute-start(f32[2,8,8,128]{3,2,1,0:T(8,128)S(1)} %get-tuple-element.177.own_ref), channel_id=1, source_target_pairs={{0,31},{1,2},{2,1},{3,4},{4,3},{5,6},{6,5},{7,8},{8,7},{9,10},{10,... | collective-permute-start | bytes 196616 | tf_op jit(solution)/shard_map/ppermute | solution.py:525
  71.6 1.3 %between.7 = (f32[2,6,8,8,128]{4,3,2,1,0:T(8,128)S(1)}, f32[2,8,8,128]{3,2,1,0:T(8,128)S(1)}) custom-call(f32[2,8,8,128]{3,2,1,0:T(8,128)S(1)} %get-tuple-element.168.p7_ref, f32[2,6,8,8,128]{4,3,2,1,0:T(8,128)S(1)} %get-tuple-element.169.gi_ref, f32[2,2,8,8,128]{4,3,2,1,0:T(8,128)S(1)} %get-tuple-element.167.q_ref, ...), custom_call_target="tpu_custom_call" | custom-call | flops 2000000000 | bytes 1024 | tf_op jit(solution)/shard_map/between/pallas_call | solution.py:506
  73.2 3.1 %last.1 = (f32[2,8,8,8,128]{4,3,2,1,0:T(8,128)}, f32[2,2,8,8,128]{4,3,2,1,0:T(8,128)S(1)}, f32[2,8,8,128]{3,2,1,0:T(8,128)S(1)}) custom-call(s32[1,128]{1,0:T(1,128)S(1)} %copy-done.2, f32[2,8,8,128]{3,2,1,0:T(8,128)S(1)} %get-tuple-element.172.p0_ref, f32[2,8,8,128]{3,2,1,0:T(8,128)S(1)} %get-tuple-element.168.p7_ref, ...), custom_call_target="tpu_custom_call" | custom-call | flops 3000000000 | bytes 1024 | tf_op jit(solution)/shard_map/last/pallas_call | solution.py:506
  76.3 0.8 %collective-permute-done.17.got_ref = f32[2,8,8,128]{3,2,1,0:T(8,128)S(1)} collective-permute-done((f32[2,8,8,128]{3,2,1,0:T(8,128)S(1)}, f32[2,8,8,128]{3,2,1,0:T(8,128)S(1)}, u32[]{:S(2)}, u32[]{:S(2)}) %collective-permute-start.17) | collective-permute-done | bytes 65568 | tf_op jit(solution)/shard_map/ppermute | solution.py:525
  (49 shorter events, 8.3 us)
Async XLA Ops:
  0.0 0.7 copy-start.2
  0.7 1.0 %copy-start = (f32[2,512,128]{2,1,0:T(8,128)S(1)}, f32[2,512,128]{2,1,0:T(8,128)}, u32[]{:S(2)}) copy-start(f32[2,512,128]{2,1,0:T(8,128)} %param.6) | copy-start | bytes 1572868
  1.7 0.9 %copy-start.1 = (f32[512,128]{1,0:T(8,128)S(1)}, f32[512,128]{1,0:T(8,128)}, u32[]{:S(2)}) copy-start(f32[512,128]{1,0:T(8,128)} %param.8) | copy-start | bytes 786436
  2.6 7.5 %copy-start.3 = (f32[3,512,128]{2,1,0:T(8,128)S(1)}, f32[3,512,128]{2,1,0:T(8,128)}, u32[]{:S(2)}) copy-start(f32[3,512,128]{2,1,0:T(8,128)} %param.7) | copy-start | bytes 2359300
  3.4 10.9 %collective-permute-start = (f32[3,8,8,128]{3,2,1,0:T(8,128)S(1)}, f32[3,8,8,128]{3,2,1,0:T(8,128)S(1)}, u32[]{:S(2)}, u32[]{:S(2)}) collective-permute-start(f32[3,8,8,128]{3,2,1,0:T(8,128)S(1)} %get-tuple-element.92.od_ref), channel_id=1, source_target_pairs={{0,31},{1,2},{2,1},{3,4},{4,3},{5,6},{6,5},{7,8},{8,7},{9,10},{10,... | collective-permute-start | bytes 294920 | tf_op jit(solution)/shard_map/ppermute | solution.py:525
  10.2 4.6 %collective-permute-start.1 = (f32[3,8,8,128]{3,2,1,0:T(8,128)S(1)}, f32[3,8,8,128]{3,2,1,0:T(8,128)S(1)}, u32[]{:S(2)}, u32[]{:S(2)}) collective-permute-start(f32[3,8,8,128]{3,2,1,0:T(8,128)S(1)} %get-tuple-element.93.ev_ref), channel_id=1, source_target_pairs={{0,1},{1,0},{2,3},{3,2},{4,5},{5,4},{6,7},{7,6},{8,9},{9,8},{10,11... | collective-permute-start | bytes 294920 | tf_op jit(solution)/shard_map/ppermute | solution.py:526
  10.2 2.2 %copy-start.5 = (f32[8,8]{1,0:T(8,128)S(1)}, f32[8,8]{1,0:T(8,128)}, u32[]{:S(2)}) copy-start(f32[8,8]{1,0:T(8,128)} %constant.4.clone) | copy-start | bytes 772
  12.4 0.7 copy-start.4
  15.1 6.4 %collective-permute-start.3 = (f32[2,8,8,128]{3,2,1,0:T(8,128)S(1)}, f32[2,8,8,128]{3,2,1,0:T(8,128)S(1)}, u32[]{:S(2)}, u32[]{:S(2)}) collective-permute-start(f32[2,8,8,128]{3,2,1,0:T(8,128)S(1)} %get-tuple-element.98.ev_ref), channel_id=1, source_target_pairs={{0,1},{1,0},{2,3},{3,2},{4,5},{5,4},{6,7},{7,6},{8,9},{9,8},{10,11... | collective-permute-start | bytes 196616 | tf_op jit(solution)/shard_map/ppermute | solution.py:526
  16.7 9.9 %collective-permute-start.2 = (f32[2,8,8,128]{3,2,1,0:T(8,128)S(1)}, f32[2,8,8,128]{3,2,1,0:T(8,128)S(1)}, u32[]{:S(2)}, u32[]{:S(2)}) collective-permute-start(f32[2,8,8,128]{3,2,1,0:T(8,128)S(1)} %get-tuple-element.96.od_ref), channel_id=1, source_target_pairs={{0,31},{1,2},{2,1},{3,4},{4,3},{5,6},{6,5},{7,8},{8,7},{9,10},{10,... | collective-permute-start | bytes 196616 | tf_op jit(solution)/shard_map/ppermute | solution.py:525
  21.7 9.6 %collective-permute-start.5 = (f32[5,8,8,128]{3,2,1,0:T(8,128)S(1)}, f32[5,8,8,128]{3,2,1,0:T(8,128)S(1)}, u32[]{:S(2)}, u32[]{:S(2)}) collective-permute-start(f32[5,8,8,128]{3,2,1,0:T(8,128)S(1)} %get-tuple-element.109.refs_0_), channel_id=1, source_target_pairs={{0,31},{1,2},{2,1},{3,4},{4,3},{5,6},{6,5},{7,8},{8,7},{9,10},{10,... | collective-permute-start | bytes 491528 | tf_op jit(solution)/shard_map/ppermute | solution.py:525
  26.8 4.7 %collective-permute-start.4 = (f32[2,8,8,128]{3,2,1,0:T(8,128)S(1)}, f32[2,8,8,128]{3,2,1,0:T(8,128)S(1)}, u32[]{:S(2)}, u32[]{:S(2)}) collective-permute-start(f32[2,8,8,128]{3,2,1,0:T(8,128)S(1)} %get-tuple-element.108.ev_ref), channel_id=1, source_target_pairs={{0,1},{1,0},{2,3},{3,2},{4,5},{5,4},{6,7},{7,6},{8,9},{9,8},{10,11... | collective-permute-start | bytes 196616 | tf_op jit(solution)/shard_map/ppermute | solution.py:526
  31.8 5.7 %collective-permute-start.7 = (f32[2,8,8,128]{3,2,1,0:T(8,128)S(1)}, f32[2,8,8,128]{3,2,1,0:T(8,128)S(1)}, u32[]{:S(2)}, u32[]{:S(2)}) collective-permute-start(f32[2,8,8,128]{3,2,1,0:T(8,128)S(1)} %get-tuple-element.118.ev_ref), channel_id=1, source_target_pairs={{0,1},{1,0},{2,3},{3,2},{4,5},{5,4},{6,7},{7,6},{8,9},{9,8},{10,11... | collective-permute-start | bytes 196616 | tf_op jit(solution)/shard_map/ppermute | solution.py:526
  32.1 9.9 %collective-permute-start.6 = (f32[2,8,8,128]{3,2,1,0:T(8,128)S(1)}, f32[2,8,8,128]{3,2,1,0:T(8,128)S(1)}, u32[]{:S(2)}, u32[]{:S(2)}) collective-permute-start(f32[2,8,8,128]{3,2,1,0:T(8,128)S(1)} %get-tuple-element.117.od_ref), channel_id=1, source_target_pairs={{0,31},{1,2},{2,1},{3,4},{4,3},{5,6},{6,5},{7,8},{8,7},{9,10},{10,... | collective-permute-start | bytes 196616 | tf_op jit(solution)/shard_map/ppermute | solution.py:525
  37.7 8.5 %collective-permute-start.9 = (f32[2,8,8,128]{3,2,1,0:T(8,128)S(1)}, f32[2,8,8,128]{3,2,1,0:T(8,128)S(1)}, u32[]{:S(2)}, u32[]{:S(2)}) collective-permute-start(f32[2,8,8,128]{3,2,1,0:T(8,128)S(1)} %get-tuple-element.129.refs_0_), channel_id=1, source_target_pairs={{0,31},{1,2},{2,1},{3,4},{4,3},{5,6},{6,5},{7,8},{8,7},{9,10},{10,... | collective-permute-start | bytes 196616 | tf_op jit(solution)/shard_map/ppermute | solution.py:525
  42.3 4.8 %collective-permute-start.8 = (f32[2,8,8,128]{3,2,1,0:T(8,128)S(1)}, f32[2,8,8,128]{3,2,1,0:T(8,128)S(1)}, u32[]{:S(2)}, u32[]{:S(2)}) collective-permute-start(f32[2,8,8,128]{3,2,1,0:T(8,128)S(1)} %get-tuple-element.128.ev_ref), channel_id=1, source_target_pairs={{0,1},{1,0},{2,3},{3,2},{4,5},{5,4},{6,7},{7,6},{8,9},{9,8},{10,11... | collective-permute-start | bytes 196616 | tf_op jit(solution)/shard_map/ppermute | solution.py:526
  47.3 5.7 %collective-permute-start.11 = (f32[2,8,8,128]{3,2,1,0:T(8,128)S(1)}, f32[2,8,8,128]{3,2,1,0:T(8,128)S(1)}, u32[]{:S(2)}, u32[]{:S(2)}) collective-permute-start(f32[2,8,8,128]{3,2,1,0:T(8,128)S(1)} %get-tuple-element.140.ev_ref), channel_id=1, source_target_pairs={{0,1},{1,0},{2,3},{3,2},{4,5},{5,4},{6,7},{7,6},{8,9},{9,8},{10,11... | collective-permute-start | bytes 196616 | tf_op jit(solution)/shard_map/ppermute | solution.py:526
  47.6 9.9 %collective-permute-start.10 = (f32[2,8,8,128]{3,2,1,0:T(8,128)S(1)}, f32[2,8,8,128]{3,2,1,0:T(8,128)S(1)}, u32[]{:S(2)}, u32[]{:S(2)}) collective-permute-start(f32[2,8,8,128]{3,2,1,0:T(8,128)S(1)} %get-tuple-element.139.od_ref), channel_id=1, source_target_pairs={{0,31},{1,2},{2,1},{3,4},{4,3},{5,6},{6,5},{7,8},{8,7},{9,10},{10,... | collective-permute-start | bytes 196616 | tf_op jit(solution)/shard_map/ppermute | solution.py:525
  53.2 8.5 %collective-permute-start.13 = (f32[2,8,8,128]{3,2,1,0:T(8,128)S(1)}, f32[2,8,8,128]{3,2,1,0:T(8,128)S(1)}, u32[]{:S(2)}, u32[]{:S(2)}) collective-permute-start(f32[2,8,8,128]{3,2,1,0:T(8,128)S(1)} %get-tuple-element.151.refs_0_), channel_id=1, source_target_pairs={{0,31},{1,2},{2,1},{3,4},{4,3},{5,6},{6,5},{7,8},{8,7},{9,10},{10,... | collective-permute-start | bytes 196616 | tf_op jit(solution)/shard_map/ppermute | solution.py:525
  57.7 4.3 %collective-permute-start.12 = (f32[2,8,8,128]{3,2,1,0:T(8,128)S(1)}, f32[2,8,8,128]{3,2,1,0:T(8,128)S(1)}, u32[]{:S(2)}, u32[]{:S(2)}) collective-permute-start(f32[2,8,8,128]{3,2,1,0:T(8,128)S(1)} %get-tuple-element.150.ev_ref), channel_id=1, source_target_pairs={{0,1},{1,0},{2,3},{3,2},{4,5},{5,4},{6,7},{7,6},{8,9},{9,8},{10,11... | collective-permute-start | bytes 196616 | tf_op jit(solution)/shard_map/ppermute | solution.py:526
  62.3 6.2 %collective-permute-start.15 = (f32[2,8,8,128]{3,2,1,0:T(8,128)S(1)}, f32[2,8,8,128]{3,2,1,0:T(8,128)S(1)}, u32[]{:S(2)}, u32[]{:S(2)}) collective-permute-start(f32[2,8,8,128]{3,2,1,0:T(8,128)S(1)} %get-tuple-element.161.ev_ref), channel_id=1, source_target_pairs={{0,1},{1,0},{2,3},{3,2},{4,5},{5,4},{6,7},{7,6},{8,9},{9,8},{10,11... | collective-permute-start | bytes 196616 | tf_op jit(solution)/shard_map/ppermute | solution.py:526
  63.1 9.9 %collective-permute-start.14 = (f32[2,8,8,128]{3,2,1,0:T(8,128)S(1)}, f32[2,8,8,128]{3,2,1,0:T(8,128)S(1)}, u32[]{:S(2)}, u32[]{:S(2)}) collective-permute-start(f32[2,8,8,128]{3,2,1,0:T(8,128)S(1)} %get-tuple-element.160.od_ref), channel_id=1, source_target_pairs={{0,31},{1,2},{2,1},{3,4},{4,3},{5,6},{6,5},{7,8},{8,7},{9,10},{10,... | collective-permute-start | bytes 196616 | tf_op jit(solution)/shard_map/ppermute | solution.py:525
  68.7 8.5 %collective-permute-start.17 = (f32[2,8,8,128]{3,2,1,0:T(8,128)S(1)}, f32[2,8,8,128]{3,2,1,0:T(8,128)S(1)}, u32[]{:S(2)}, u32[]{:S(2)}) collective-permute-start(f32[2,8,8,128]{3,2,1,0:T(8,128)S(1)} %get-tuple-element.177.own_ref), channel_id=1, source_target_pairs={{0,31},{1,2},{2,1},{3,4},{4,3},{5,6},{6,5},{7,8},{8,7},{9,10},{10,... | collective-permute-start | bytes 196616 | tf_op jit(solution)/shard_map/ppermute | solution.py:525
  73.2 4.7 %collective-permute-start.16 = (f32[2,8,8,128]{3,2,1,0:T(8,128)S(1)}, f32[2,8,8,128]{3,2,1,0:T(8,128)S(1)}, u32[]{:S(2)}, u32[]{:S(2)}) collective-permute-start(f32[2,8,8,128]{3,2,1,0:T(8,128)S(1)} %get-tuple-element.171.own_ref), channel_id=1, source_target_pairs={{0,1},{1,0},{2,3},{3,2},{4,5},{5,4},{6,7},{7,6},{8,9},{9,8},{10,11... | collective-permute-start | bytes 196616 | tf_op jit(solution)/shard_map/ppermute | solution.py:526

commit v2 on v1

--- a/solution.py
+++ b/solution.py
@@ -136,18 +136,13 @@
     return jnp.where(parity == 1, ORDER - i, i)
 
 
-def project_faces(order_ref, scal_ref, mass_ref, od_ref, ev_ref, order_buf, scal_buf, mass_buf, sems):
+def project_odd(order_ref, scal_ref, mass_ref, od_ref, order_buf, scal_buf, mass_buf, sems):
     parity = lax.axis_index("elem") % 2
-    copies = [pltpu.make_async_copy(order_ref, order_buf, sems.at[6])]
-    for face in range(2):
-        src = source_plane(parity, face * ORDER)
-        copies.append(pltpu.make_async_copy(mass_ref.at[src], mass_buf.at[face], sems.at[face]))
-        for m in range(2):
-            copies.append(
-                pltpu.make_async_copy(
-                    scal_ref.at[m, src], scal_buf.at[face, m], sems.at[2 + 2 * face + m]
-                )
-            )
+    src = source_plane(parity, 0)
+    copies = [pltpu.make_async_copy(order_ref, order_buf, sems.at[0])]
+    copies.append(pltpu.make_async_copy(mass_ref.at[src], mass_buf, sems.at[1]))
+    for m in range(2):
+        copies.append(pltpu.make_async_copy(scal_ref.at[m, src], scal_buf.at[m], sems.at[2 + m]))
     for copy in copies:
         copy.start()
     tables = third_tables()
@@ -155,12 +150,21 @@
     idx = brick_index(order_buf)
     for copy in copies[1:]:
         copy.wait()
-    for face, out in ((0, od_ref), (1, ev_ref)):
-        weight = [gather_lanes(mass_buf[face, j], idx) for j in range(8)]
-        write(out, (2,), plane_sum(weight, tables))
-        for m in range(2):
-            plane = [gather_lanes(scal_buf[face, m, j], idx) * weight[j] for j in range(8)]
-            write(out, (m,), plane_sum(plane, tables))
+    project(read(mass_buf), [read(scal_buf, m) for m in range(2)], idx, tables, od_ref)
+
+
+def project_even(order_ref, scal_ref, mass_ref, ev_ref):
+    src = source_plane(lax.axis_index("elem") % 2, ORDER)
+    idx = brick_index(order_ref)
+    project(read(mass_ref, src), [read(scal_ref, m, src) for m in range(2)], idx, third_tables(), ev_ref)
+
+
+def project(weight, scal, idx, tables, out_ref):
+    weight = [gather_lanes(v, idx) for v in weight]
+    planes = [[gather_lanes(plane[j], idx) * weight[j] for j in range(8)] for plane in scal]
+    planes = [plane_sum(plane, tables) for plane in planes + [weight]]
+    for r in range(3):
+        write(out_ref, (r,), planes[r])
 
 
 def prepare(order_ref, scal_ref, mass_ref, tr_ref, gi_ref, q_ref, ri_ref, ti_ref, tf_ref):
@@ -225,22 +229,24 @@
     lax.fori_loop(0, 6, body, 0)
 
 
-def inner_close(p0_ref, p7_ref, wp_ref, ri_ref, ti_ref, d_ref, scale, put):
+def inner_close(p0_ref, p7_ref, wp_ref, ri_ref, ti_ref, scale, put, q_ref=None):
     tables = third_tables()
-
-    def body(i, carry):
-        near, far = d_ref[i + 1, 0], d_ref[i + 1, ORDER]
-        inverse = [ri_ref[i, j] * np.float32(scale) for j in range(8)]
-        for m in range(2):
+    for m in range(2):
+        sums = [[], []]
+        for i in range(6):
+            near, far = np.float32(DM[i + 1, 0]), np.float32(DM[i + 1, ORDER])
             plane = [
                 wp_ref[m, i, j] + ti_ref[i, 0, j] * (p0_ref[m, j] * near + p7_ref[m, j] * far)
                 for j in range(8)
             ]
             plane = plane_sum(plane, tables)
-            put(m, i, [plane[j] * inverse[j] for j in range(8)])
-        return carry
-
-    lax.fori_loop(0, 6, body, 0)
+            kept = put(m, i, [plane[j] * (ri_ref[i, j] * np.float32(scale)) for j in range(8)])
+            for face in range(2):
+                terms = [v * np.float32(DM[face * ORDER, i + 1]) for v in kept]
+                sums[face] = [x + y for x, y in zip(sums[face], terms)] if i else terms
+        if q_ref is not None:
+            for face in range(2):
+                write(q_ref, (face, m), sums[face])
 
 
 def rotations(rot_ref):
@@ -321,39 +327,42 @@
                   p7_ref, sod_ref, sev_ref):
         rot = rotations(rot_ref)
         tables = third_tables()
-        for m in range(2):
-            p7 = [
-                (ev_ref[m, j] + rev_ref[m, j]) * (rf_ref[1, j] * np.float32(scale))
-                for j in range(8)
-            ]
-            if total:
-                p7 = [p7[j] + accf_ref[1, m, j] for j in range(8)]
-            write(p7_ref, (m,), p7)
-            rest = in_plane(p7, tf_ref, (1,), rot)
-            plane = [
-                rest[j] + w7_ref[m, j] + tf_ref[1, 0, j] * (p7[j] * np.float32(DM[ORDER, ORDER]))
-                for j in range(8)
-            ]
-            write(sev_ref, (m,), plane_sum(plane, tables))
-            plane = [
-                w0_ref[m, j] + tf_ref[0, 0, j] * (p7[j] * np.float32(DM[0, ORDER]))
-                for j in range(8)
-            ]
-            write(sod_ref, (m,), plane_sum(plane, tables))
+        weight = [rf_ref[1, j] * np.float32(scale) for j in range(8)]
+        p7 = [[(ev_ref[m, j] + rev_ref[m, j]) * weight[j] for j in range(8)] for m in range(2)]
+        if total:
+            p7 = [[p7[m][j] + accf_ref[1, m, j] for j in range(8)] for m in range(2)]
+        evens, odds = [], []
+        for m in range(2):
+            rest = in_plane(p7[m], tf_ref, (1,), rot)
+            evens.append([
+                rest[j] + w7_ref[m, j] + tf_ref[1, 0, j] * (p7[m][j] * np.float32(DM[ORDER, ORDER]))
+                for j in range(8)
+            ])
+            odds.append([
+                w0_ref[m, j] + tf_ref[0, 0, j] * (p7[m][j] * np.float32(DM[0, ORDER]))
+                for j in range(8)
+            ])
+        evens = [plane_sum(plane, tables) for plane in evens]
+        odds = [plane_sum(plane, tables) for plane in odds]
+        for m in range(2):
+            write(sev_ref, (m,), evens[m])
+            write(sod_ref, (m,), odds[m])
+            write(p7_ref, (m,), p7[m])
 
     return even_face
 
 
 def make_first_inner(scale, opening):
-    def first_inner(p0_ref, p7_ref, gi_ref, acci_ref, wp_ref, ri_ref, ti_ref, d_ref,
+    def first_inner(p0_ref, p7_ref, gi_ref, acci_ref, wp_ref, ri_ref, ti_ref,
                     gn_ref, an_ref, q_ref):
         def put(m, i, value):
+            base = gi_ref if opening else acci_ref
+            total = [base[m, i, j] + value[j] for j in range(8)]
             write(gn_ref, (m, i), value)
-            base = gi_ref if opening else acci_ref
-            write(an_ref, (m, i), [base[m, i, j] + value[j] for j in range(8)])
-
-        inner_close(p0_ref, p7_ref, wp_ref, ri_ref, ti_ref, d_ref, scale, put)
-        face_partials(gn_ref, q_ref)
+            write(an_ref, (m, i), total)
+            return value
+
+        inner_close(p0_ref, p7_ref, wp_ref, ri_ref, ti_ref, scale, put, q_ref)
 
     return first_inner
 
@@ -361,17 +370,19 @@
 def make_ahead(scale, carry_transport):
     def ahead(ev_ref, rev_ref, rf_ref, q_ref, tf_ref, p7_ref, sod_ref):
         tables = third_tables()
-        for m in range(2):
-            p7 = [
-                (ev_ref[m, j] + rev_ref[m, j]) * (rf_ref[1, j] * np.float32(scale))
+        weight = [rf_ref[1, j] * np.float32(scale) for j in range(8)]
+        p7 = [[(ev_ref[m, j] + rev_ref[m, j]) * weight[j] for j in range(8)] for m in range(2)]
+        planes = [
+            [
+                tf_ref[0, 0, j] * (q_ref[0, m, j] + p7[m][j] * np.float32(DM[0, ORDER]))
                 for j in range(8)
             ]
-            write(p7_ref, (m,), p7)
-            plane = [
-                tf_ref[0, 0, j] * (q_ref[0, m, j] + p7[j] * np.float32(DM[0, ORDER]))
-                for j in range(8)
-            ]
-            write(sod_ref, (m,), plane_sum(plane, tables))
+            for m in range(2)
+        ]
+        planes = [plane_sum(plane, tables) for plane in planes]
+        for m in range(2):
+            write(sod_ref, (m,), planes[m])
+            write(p7_ref, (m,), p7[m])
         if carry_transport:
             for r in range(3):
                 write(sod_ref, (2 + r,), read(tf_ref, 0, r))
@@ -394,17 +405,19 @@
 def make_behind(scale):
     def behind(od_ref, rod_ref, rf_ref, w7_ref, tf_ref, p0_ref, sev_ref):
         tables = third_tables()
-        for m in range(2):
-            p0 = [
-                (od_ref[m, j] + rod_ref[m, j]) * (rf_ref[0, j] * np.float32(scale))
+        weight = [rf_ref[0, j] * np.float32(scale) for j in range(8)]
+        p0 = [[(od_ref[m, j] + rod_ref[m, j]) * weight[j] for j in range(8)] for m in range(2)]
+        planes = [
+            [
+                w7_ref[m, j] + tf_ref[1, 0, j] * (p0[m][j] * np.float32(DM[ORDER, 0]))
                 for j in range(8)
             ]
-            write(p0_ref, (m,), p0)
-            plane = [
-                w7_ref[m, j] + tf_ref[1, 0, j] * (p0[j] * np.float32(DM[ORDER, 0]))
-                for j in range(8)
-            ]
-            write(sev_ref, (m,), plane_sum(plane, tables))
+            for m in range(2)
+        ]
+        planes = [plane_sum(plane, tables) for plane in planes]
+        for m in range(2):
+            write(sev_ref, (m,), planes[m])
+            write(p0_ref, (m,), p0[m])
 
     return behind
 
@@ -428,12 +441,13 @@
 
         def put(m, i, value):
             total = [acci_ref[m, i, j] + value[j] for j in range(8)]
-            write(gn_ref, (m, i), total if closing else value)
+            kept = total if closing else value
+            write(gn_ref, (m, i), kept)
             if not closing:
                 write(an_ref, (m, i), total)
-
-        inner_close(p0_ref, p7_ref, wp_ref, ri_ref, ti_ref, d_ref, scale, put)
-        face_partials(gn_ref, q_ref)
+            return kept
+
+        inner_close(p0_ref, p7_ref, wp_ref, ri_ref, ti_ref, scale, put, q_ref)
         inner_open(gn_ref, ti_ref, rot, d_ref, wn_ref)
 
     return second_inner
@@ -441,7 +455,7 @@
 
 def make_last_inner(scale):
     def last_inner(order_ref, p0_ref, p7_ref, b0_ref, b7_ref, accf_ref, acci_ref, wp_ref, ri_ref,
-                   ti_ref, ts_ref, rot_ref, d_ref, out_ref, afn_ref, e_ref, buf, sems):
+                   ti_ref, ts_ref, rot_ref, out_ref, afn_ref, e_ref, buf, sems):
         parity = lax.axis_index("elem") % 2
         idx = jnp.broadcast_to(order_ref[...], (SUB, LANES))
 
@@ -449,8 +463,9 @@
             total = [acci_ref[m, i, j] + value[j] for j in range(8)]
             dst = source_plane(parity, i + 1) - 1
             write(buf, (m, dst), [gather_lanes(v, idx) for v in total])
-
-        inner_close(p0_ref, p7_ref, wp_ref, ri_ref, ti_ref, d_ref, scale, put)
+            return total
+
+        inner_close(p0_ref, p7_ref, wp_ref, ri_ref, ti_ref, scale, put)
         copies = [
             pltpu.make_async_copy(buf.at[m], out_ref.at[m, pl.ds(1, 6)], sems.at[m])
             for m in range(2)
@@ -471,26 +486,50 @@
     return last_inner
 
 
-def make_finish(face, scale):
-    def finish(order_ref, own_ref, got_ref, e_ref, rf_ref, accf_ref, part_ref, out_ref, buf, sems):
+def make_finish_odd(scale):
+    def finish_odd(order_ref, own_ref, got_ref, e_ref, rf_ref, accf_ref, face_ref):
+        idx = jnp.broadcast_to(order_ref[...], (SUB, LANES))
+        for m in range(2):
+            write(face_ref, (m,), [
+                gather_lanes(
+                    (own_ref[m, j] + got_ref[m, j] + e_ref[m, j])
+                    * (rf_ref[0, j] * np.float32(scale))
+                    + accf_ref[0, m, j],
+                    idx,
+                )
+                for j in range(8)
+            ])
+
+    return finish_odd
+
+
+def make_finish_even(scale):
+    def finish_even(order_ref, own_ref, got_ref, rf_ref, accf_ref, face_ref, part_ref,
+                    out_ref, buf, sems):
         parity = lax.axis_index("elem") % 2
         idx = jnp.broadcast_to(order_ref[...], (SUB, LANES))
-        dst = source_plane(parity, face * ORDER)
+        dst = source_plane(parity, ORDER)
         copies = []
         for m in range(2):
-            for j in range(8):
-                value = own_ref[m, j] + got_ref[m, j]
-                if face == 0:
-                    value = value + e_ref[m, j]
-                value = value * (rf_ref[face, j] * np.float32(scale)) + accf_ref[face, m, j]
-                buf[m, j] = gather_lanes(value, idx)
-            copy = pltpu.make_async_copy(buf.at[m], out_ref.at[m, dst], sems.at[m])
-            copy.start()
-            copies.append(copy)
+            write(buf, (m,), [
+                gather_lanes(
+                    (own_ref[m, j] + got_ref[m, j]) * (rf_ref[1, j] * np.float32(scale))
+                    + accf_ref[1, m, j],
+                    idx,
+                )
+                for j in range(8)
+            ])
+            copies.append(pltpu.make_async_copy(buf.at[m], out_ref.at[m, dst], sems.at[0, m]))
+            copies[-1].start()
+        for m in range(2):
+            copies.append(
+                pltpu.make_async_copy(face_ref.at[m], out_ref.at[m, ORDER - dst], sems.at[1, m])
+            )
+            copies[-1].start()
         for copy in copies:
             copy.wait()
 
-    return finish
+    return finish_even
 
 
 VM = pl.BlockSpec(memory_space=pltpu.VMEM)
@@ -534,10 +573,13 @@
     tile = (EXT, SUB, LANES)
     face, inner = (2,) + tile, (2, 6) + tile
 
-    od, ev = call(
-        project_faces, [(3,) + tile] * 2, (element_order, scal, mas), "project", 1, hbm=(0, 1, 2),
-        scratch=[pltpu.VMEM((1, LANES), jnp.int32), pltpu.VMEM((2, 2) + tile, jnp.float32),
-                 pltpu.VMEM((2,) + tile, jnp.float32), pltpu.SemaphoreType.DMA((7,))])
+    stay = lambda x: pltpu.with_memory_space_constraint(x, pltpu.HBM)
+    od = call(
+        project_odd, [(3,) + tile], (stay(element_order), stay(scal), stay(mas)), "project", 1,
+        hbm=(0, 1, 2),
+        scratch=[pltpu.VMEM((1, LANES), jnp.int32), pltpu.VMEM(face, jnp.float32),
+                 pltpu.VMEM(tile, jnp.float32), pltpu.SemaphoreType.DMA((4,))])
+    ev = call(project_even, [(3,) + tile], (element_order, scal, mas), "project", 1)
     rod, rev = swap_od(od), swap_ev(ev)
     gi, q, ri, ti, tf = call(
         prepare, [inner, (2,) + face, (6,) + tile, (6, 3) + tile, (2, 3) + tile],
@@ -558,7 +600,7 @@
         rev, rod = swap_ev(ev), swap_od(od)
         gm, acci, q = call(
             make_first_inner(1.0 / s, opening), [inner, inner, (2,) + face],
-            (p0, p7, gi, acci, wp, ri, ti, dmat), "first", 1000, smem=(7,))
+            (p0, p7, gi, acci, wp, ri, ti), "first", 1000)
         m7, od2 = call(
             make_ahead(1.0 / s, early), [face, ((5 if early else 2),) + tile],
             (ev, rev, rf, q, tf), "ahead", 1)
@@ -588,15 +630,17 @@
         else:
             out, accf, shared = call(
                 make_last_inner(1.0 / (s + 1)), [(members,) + grid, (2,) + face, face],
-                (element_order, m0, m7, p0, p7, accf, acci, wp, ri, ti, ts, rot, dmat), "last", 3000,
-                smem=(12,), hbm_out=(0,),
+                (element_order, m0, m7, p0, p7, accf, acci, wp, ri, ti, ts, rot), "last", 3000,
+                hbm_out=(0,),
                 scratch=[pltpu.VMEM(inner, jnp.float32), pltpu.SemaphoreType.DMA((2,))])
-            for side, own, got in ((0, od2, rod2), (1, ev2, rev2)):
-                out = call(
-                    make_finish(side, 1.0 / (s + 1)), [(members,) + grid],
-                    (element_order, own, got, shared, rf, accf, out), "finish", 3000 - 2999 * side,
-                    hbm=(6,), hbm_out=(0,), alias={6: 0},
-                    scratch=[pltpu.VMEM(face, jnp.float32), pltpu.SemaphoreType.DMA((2,))])
+            odd = call(
+                make_finish_odd(1.0 / (s + 1)), [face],
+                (element_order, od2, rod2, shared, rf, accf), "finish", 3000)
+            out = call(
+                make_finish_even(1.0 / (s + 1)), [(members,) + grid],
+                (element_order, ev2, rev2, rf, accf, odd, out), "finish", 1,
+                hbm=(6,), hbm_out=(0,), alias={6: 0},
+                scratch=[pltpu.VMEM(face, jnp.float32), pltpu.SemaphoreType.DMA((2, 2))])
     return out.reshape(scalars.shape)
 
 

time: 78.9 us -> 71.5 us (0.906)
  Pallas kernels: 33.9 us -> 22.6 us
  waiting for transfers between devices: 6.02 us -> 14.2 us
  local copies, waits for them, and re-layouts: 3.33 us -> 0.7 us
  starting transfers between devices: 35.1 us -> 33.5 us
    pallas_call x32 -> x33, Pallas kernels: 33.9 us -> 22.6 us  [call(): pl.pallas_call(kernel, out_shape=shapes[0] if single else shapes, in_spec...]
    ppermute x9, waiting for transfers between devices: 1.32 us -> 5.56 us  [per_device(): swap_ev = lambda x: lax.ppermute(x, 'elem', even_pairs)]
    ppermute x9, waiting for transfers between devices: 4.7 us -> 8.68 us  [per_device(): swap_od = lambda x: lax.ppermute(x, 'elem', odd_pairs)]
    unnamed x12, local copies, waits for them, and re-layouts: 3.26 us -> 0.63 us
    ppermute x9, starting transfers between devices: 3.33 us -> 2.11 us  [per_device(): swap_ev = lambda x: lax.ppermute(x, 'elem', even_pairs)]
  transfers between devices with their start and end apart: 18 -> 18, of which waited for: 7 -> 15; matrix products, arithmetic and copies ran while one was open for 0% -> 0% of each run, Pallas kernels for 40% -> 28%
where the time goes in v2:
time: 71.5 us; the launch traced here: 71.3 us
  starting transfers between devices  33.5 us (47%)
  Pallas kernels  22.6 us (32%)
  waiting for transfers between devices  14.2 us (20%)
    ppermute x9, starting transfers between devices, per_device(): swap_od = lambda x: lax.ppermute(x, 'elem', odd_pairs)  31.4 us
    pallas_call x33, Pallas kernels, call(): pl.pallas_call(kernel, out_shape=shapes[0] if single else shapes, in_spec...  22.6 us
    ppermute x9, waiting for transfers between devices, per_device(): swap_od = lambda x: lax.ppermute(x, 'elem', odd_pairs)  8.68 us
    ppermute x9, waiting for transfers between devices, per_device(): swap_ev = lambda x: lax.ppermute(x, 'elem', even_pairs)  5.56 us
    ppermute x9, starting transfers between devices, per_device(): swap_ev = lambda x: lax.ppermute(x, 'elem', even_pairs)  2.11 us
  transfers between devices with their start and end apart: 18, of which 15 were waited for; matrix products, arithmetic and copies ran while one was open for 0% of the time, Pallas kernels for 28%

profile of v2, /device:TPU:0, one launch (start us, length us, event | category | flops | bytes accessed | tf_op | source)
XLA Modules:
  0.0 71.3 jit_solution(7411853852576632529)
XLA Ops:
  0.0 1.2 %project.2.od_ref = f32[3,8,8,128]{3,2,1,0:T(8,128)S(1)} custom-call(s32[1,128]{1,0:T(1,128)} %order_ref.11, f32[2,8,8,8,128]{4,3,2,1,0:T(8,128)} %bitcast.4, f32[8,8,8,128]{3,2,1,0:T(8,128)} %bitcast.7), custom_call_target="tpu_custom_call" | custom-call | flops 1000000 | bytes 1024 | tf_op jit(solution)/shard_map/project/pallas_call | solution.py:545
  1.3 6.7 %collective-permute-start = (f32[3,8,8,128]{3,2,1,0:T(8,128)S(1)}, f32[3,8,8,128]{3,2,1,0:T(8,128)S(1)}, u32[]{:S(2)}, u32[]{:S(2)}) collective-permute-start(f32[3,8,8,128]{3,2,1,0:T(8,128)S(1)} %project.2.od_ref), channel_id=1, source_target_pairs={{0,31},{1,2},{2,1},{3,4},{4,3},{5,6},{6,5},{7,8},{8,7},{9,10},{10,... | collective-permute-start | bytes 294920 | tf_op jit(solution)/shard_map/ppermute | solution.py:564
  8.5 2.2 %prepare.1 = (f32[2,6,8,8,128]{4,3,2,1,0:T(8,128)S(1)}, f32[2,2,8,8,128]{4,3,2,1,0:T(8,128)S(1)}, f32[6,8,8,128]{3,2,1,0:T(8,128)S(1)}, f32[6,3,8,8,128]{4,3,2,1,0:T(8,128)S(1)}, f32[2,3,8,8,128]{4,3,2,1,0:T(8,128)S(1)}) custom-call(s32[1,128]{1,0:T(1,128)S(1)} %copy-done.2, f32[2,8,8,8,128]{4,3,2,1,0:T(8,128)S(1)} %bitcast.6, f32[8,8,8,128]{3,2,1,0:T(8,128)S(1)} %bitcast.9, ...), custom_call_target="tpu_custom_call" | custom-call | flops 4000000000 | bytes 1024 | tf_op jit(solution)/shard_map/prepare/pallas_call | solution.py:545
  10.8 0.6 copy-done.4
  11.4 1.3 %terms.1.wp_ref = f32[2,6,8,8,128]{4,3,2,1,0:T(8,128)S(1)} custom-call(f32[2,6,8,8,128]{4,3,2,1,0:T(8,128)S(1)} %get-tuple-element.97.gi_ref.acci_ref, f32[6,3,8,8,128]{4,3,2,1,0:T(8,128)S(1)} %get-tuple-element.98.ti_ref.refs_8_, f32[8,8,128]{2,1,0:T(8,128)S(1)} %jit_solution_.3.rot_ref.refs_10_.refs_7_, f32[8,8]{1,0:T(8,128)S(1)} %copy-done.4), custom_call_target="tpu_custom_call" | custom-call | flops 2000000000 | bytes 1024 | tf_op jit(solution)/shard_map/terms/pallas_call | solution.py:545
  13.4 1.7 %collective-permute-start.3 = (f32[2,8,8,128]{3,2,1,0:T(8,128)S(1)}, f32[2,8,8,128]{3,2,1,0:T(8,128)S(1)}, u32[]{:S(2)}, u32[]{:S(2)}) collective-permute-start(f32[2,8,8,128]{3,2,1,0:T(8,128)S(1)} %get-tuple-element.94.ev_ref), channel_id=1, source_target_pairs={{0,1},{1,0},{2,3},{3,2},{4,5},{5,4},{6,7},{7,6},{8,9},{9,8},{10,11... | collective-permute-start | bytes 196616 | tf_op jit(solution)/shard_map/ppermute | solution.py:565
  15.1 2.2 %collective-permute-start.2 = (f32[2,8,8,128]{3,2,1,0:T(8,128)S(1)}, f32[2,8,8,128]{3,2,1,0:T(8,128)S(1)}, u32[]{:S(2)}, u32[]{:S(2)}) collective-permute-start(f32[2,8,8,128]{3,2,1,0:T(8,128)S(1)} %get-tuple-element.92.od_ref), channel_id=1, source_target_pairs={{0,31},{1,2},{2,1},{3,4},{4,3},{5,6},{6,5},{7,8},{8,7},{9,10},{10,... | collective-permute-start | bytes 196616 | tf_op jit(solution)/shard_map/ppermute | solution.py:564
  18.0 3.9 %collective-permute-start.5 = (f32[5,8,8,128]{3,2,1,0:T(8,128)S(1)}, f32[5,8,8,128]{3,2,1,0:T(8,128)S(1)}, u32[]{:S(2)}, u32[]{:S(2)}) collective-permute-start(f32[5,8,8,128]{3,2,1,0:T(8,128)S(1)} %get-tuple-element.105.refs_0_), channel_id=1, source_target_pairs={{0,31},{1,2},{2,1},{3,4},{4,3},{5,6},{6,5},{7,8},{8,7},{9,10},{10,... | collective-permute-start | bytes 491528 | tf_op jit(solution)/shard_map/ppermute | solution.py:564
  21.9 1.3 %between.4 = (f32[2,6,8,8,128]{4,3,2,1,0:T(8,128)S(1)}, f32[2,8,8,128]{3,2,1,0:T(8,128)S(1)}) custom-call(f32[2,8,8,128]{3,2,1,0:T(8,128)S(1)} %get-tuple-element.101.p7_ref.refs_1_, f32[2,6,8,8,128]{4,3,2,1,0:T(8,128)S(1)} %get-tuple-element.102.gi_ref, f32[2,2,8,8,128]{4,3,2,1,0:T(8,128)S(1)} %get-tuple-element.100.q_ref, ...), custom_call_target="tpu_custom_call" | custom-call | flops 2000000000 | bytes 1024 | tf_op jit(solution)/shard_map/between/pallas_call | solution.py:545
  23.2 0.8 %collective-permute-done.2.rod_ref = f32[2,8,8,128]{3,2,1,0:T(8,128)S(1)} collective-permute-done((f32[2,8,8,128]{3,2,1,0:T(8,128)S(1)}, f32[2,8,8,128]{3,2,1,0:T(8,128)S(1)}, u32[]{:S(2)}, u32[]{:S(2)}) %collective-permute-start.2) | collective-permute-done | bytes 65568 | tf_op jit(solution)/shard_map/ppermute | solution.py:564
  24.3 1.6 %second.3 = (f32[2,6,8,8,128]{4,3,2,1,0:T(8,128)S(1)}, f32[2,2,8,8,128]{4,3,2,1,0:T(8,128)S(1)}, f32[2,6,8,8,128]{4,3,2,1,0:T(8,128)S(1)}, f32[2,2,8,8,128]{4,3,2,1,0:T(8,128)S(1)}, f32[2,6,8,8,128]{4,3,2,1,0:T(8,128)S(1)}) custom-call(f32[2,8,8,128]{3,2,1,0:T(8,128)S(1)} %get-tuple-element.106.refs_0_.refs_2_, ...), custom_call_target="tpu_custom_call" | custom-call | flops 3000000000 | bytes 1024 | tf_op jit(solution)/shard_map/second/pallas_call | solution.py:545
  25.9 1.7 %collective-permute-done.5.refs_1_ = f32[5,8,8,128]{3,2,1,0:T(8,128)S(1)} collective-permute-done((f32[5,8,8,128]{3,2,1,0:T(8,128)S(1)}, f32[5,8,8,128]{3,2,1,0:T(8,128)S(1)}, u32[]{:S(2)}, u32[]{:S(2)}) %collective-permute-start.5) | collective-permute-done | bytes 163872 | tf_op jit(solution)/shard_map/ppermute | solution.py:564
  27.8 1.0 %collective-permute-done.4.rev_ref = f32[2,8,8,128]{3,2,1,0:T(8,128)S(1)} collective-permute-done((f32[2,8,8,128]{3,2,1,0:T(8,128)S(1)}, f32[2,8,8,128]{3,2,1,0:T(8,128)S(1)}, u32[]{:S(2)}, u32[]{:S(2)}) %collective-permute-start.4) | collective-permute-done | bytes 65568 | tf_op jit(solution)/shard_map/ppermute | solution.py:565
  29.1 3.0 %collective-permute-start.6 = (f32[2,8,8,128]{3,2,1,0:T(8,128)S(1)}, f32[2,8,8,128]{3,2,1,0:T(8,128)S(1)}, u32[]{:S(2)}, u32[]{:S(2)}) collective-permute-start(f32[2,8,8,128]{3,2,1,0:T(8,128)S(1)} %get-tuple-element.113.od_ref), channel_id=1, source_target_pairs={{0,31},{1,2},{2,1},{3,4},{4,3},{5,6},{6,5},{7,8},{8,7},{9,10},{10,... | collective-permute-start | bytes 196616 | tf_op jit(solution)/shard_map/ppermute | solution.py:564
  32.4 1.0 %collective-permute-done.7.rev_ref = f32[2,8,8,128]{3,2,1,0:T(8,128)S(1)} collective-permute-done((f32[2,8,8,128]{3,2,1,0:T(8,128)S(1)}, f32[2,8,8,128]{3,2,1,0:T(8,128)S(1)}, u32[]{:S(2)}, u32[]{:S(2)}) %collective-permute-start.7) | collective-permute-done | bytes 65568 | tf_op jit(solution)/shard_map/ppermute | solution.py:565
  33.6 2.9 %collective-permute-start.9 = (f32[2,8,8,128]{3,2,1,0:T(8,128)S(1)}, f32[2,8,8,128]{3,2,1,0:T(8,128)S(1)}, u32[]{:S(2)}, u32[]{:S(2)}) collective-permute-start(f32[2,8,8,128]{3,2,1,0:T(8,128)S(1)} %get-tuple-element.125.refs_0_), channel_id=1, source_target_pairs={{0,31},{1,2},{2,1},{3,4},{4,3},{5,6},{6,5},{7,8},{8,7},{9,10},{10,... | collective-permute-start | bytes 196616 | tf_op jit(solution)/shard_map/ppermute | solution.py:564
  36.5 1.3 %between.5 = (f32[2,6,8,8,128]{4,3,2,1,0:T(8,128)S(1)}, f32[2,8,8,128]{3,2,1,0:T(8,128)S(1)}) custom-call(f32[2,8,8,128]{3,2,1,0:T(8,128)S(1)} %get-tuple-element.121.p7_ref.refs_1_, f32[2,6,8,8,128]{4,3,2,1,0:T(8,128)S(1)} %get-tuple-element.122.gi_ref, f32[2,2,8,8,128]{4,3,2,1,0:T(8,128)S(1)} %get-tuple-element.120.q_ref, ...), custom_call_target="tpu_custom_call" | custom-call | flops 2000000000 | bytes 1024 | tf_op jit(solution)/shard_map/between/pallas_call | solution.py:545
  38.4 1.7 %second.4 = (f32[2,6,8,8,128]{4,3,2,1,0:T(8,128)S(1)}, f32[2,2,8,8,128]{4,3,2,1,0:T(8,128)S(1)}, f32[2,6,8,8,128]{4,3,2,1,0:T(8,128)S(1)}, f32[2,2,8,8,128]{4,3,...) custom-call(f32[2,8,8,128]{3,2,1,0:T(8,128)S(1)} %get-tuple-element.126.refs_0_, ...), custom_call_target="tpu_custom_call" | custom-call | flops 3000000000 | bytes 1024 | tf_op jit(solution)/shard_map/second/pallas_call | solution.py:545
  40.2 1.9 %collective-permute-done.9.refs_1_ = f32[2,8,8,128]{3,2,1,0:T(8,128)S(1)} collective-permute-done((f32[2,8,8,128]{3,2,1,0:T(8,128)S(1)}, f32[2,8,8,128]{3,2,1,0:T(8,128)S(1)}, u32[]{:S(2)}, u32[]{:S(2)}) %collective-permute-start.9) | collective-permute-done | bytes 65568 | tf_op jit(solution)/shard_map/ppermute | solution.py:564
  43.1 3.1 %collective-permute-start.10 = (f32[2,8,8,128]{3,2,1,0:T(8,128)S(1)}, f32[2,8,8,128]{3,2,1,0:T(8,128)S(1)}, u32[]{:S(2)}, u32[]{:S(2)}) collective-permute-start(f32[2,8,8,128]{3,2,1,0:T(8,128)S(1)} %get-tuple-element.135.od_ref), channel_id=1, source_target_pairs={{0,31},{1,2},{2,1},{3,4},{4,3},{5,6},{6,5},{7,8},{8,7},{9,10},{10,... | collective-permute-start | bytes 196616 | tf_op jit(solution)/shard_map/ppermute | solution.py:564
  46.4 0.8 %collective-permute-done.11.rev_ref = f32[2,8,8,128]{3,2,1,0:T(8,128)S(1)} collective-permute-done((f32[2,8,8,128]{3,2,1,0:T(8,128)S(1)}, f32[2,8,8,128]{3,2,1,0:T(8,128)S(1)}, u32[]{:S(2)}, u32[]{:S(2)}) %collective-permute-start.11) | collective-permute-done | bytes 65568 | tf_op jit(solution)/shard_map/ppermute | solution.py:565
  47.5 3.1 %collective-permute-start.13 = (f32[2,8,8,128]{3,2,1,0:T(8,128)S(1)}, f32[2,8,8,128]{3,2,1,0:T(8,128)S(1)}, u32[]{:S(2)}, u32[]{:S(2)}) collective-permute-start(f32[2,8,8,128]{3,2,1,0:T(8,128)S(1)} %get-tuple-element.147.refs_0_), channel_id=1, source_target_pairs={{0,31},{1,2},{2,1},{3,4},{4,3},{5,6},{6,5},{7,8},{8,7},{9,10},{10,... | collective-permute-start | bytes 196616 | tf_op jit(solution)/shard_map/ppermute | solution.py:564
  50.6 1.3 %between.6 = (f32[2,6,8,8,128]{4,3,2,1,0:T(8,128)S(1)}, f32[2,8,8,128]{3,2,1,0:T(8,128)S(1)}) custom-call(f32[2,8,8,128]{3,2,1,0:T(8,128)S(1)} %get-tuple-element.143.p7_ref.refs_1_, f32[2,6,8,8,128]{4,3,2,1,0:T(8,128)S(1)} %get-tuple-element.144.gi_ref, f32[2,2,8,8,128]{4,3,2,1,0:T(8,128)S(1)} %get-tuple-element.142.q_ref, ...), custom_call_target="tpu_custom_call" | custom-call | flops 2000000000 | bytes 1024 | tf_op jit(solution)/shard_map/between/pallas_call | solution.py:545
  52.2 1.7 %second.5 = (f32[2,6,8,8,128]{4,3,2,1,0:T(8,128)S(1)}, f32[2,2,8,8,128]{4,3,2,1,0:T(8,128)S(1)}, f32[2,6,8,8,128]{4,3,2,1,0:T(8,128)S(1)}, f32[2,2,8,8,128]{4,3,...) custom-call(f32[2,8,8,128]{3,2,1,0:T(8,128)S(1)} %get-tuple-element.148.refs_0_, ...), custom_call_target="tpu_custom_call" | custom-call | flops 3000000000 | bytes 1024 | tf_op jit(solution)/shard_map/second/pallas_call | solution.py:545
  53.9 2.1 %collective-permute-done.13.refs_1_ = f32[2,8,8,128]{3,2,1,0:T(8,128)S(1)} collective-permute-done((f32[2,8,8,128]{3,2,1,0:T(8,128)S(1)}, f32[2,8,8,128]{3,2,1,0:T(8,128)S(1)}, u32[]{:S(2)}, u32[]{:S(2)}) %collective-permute-start.13) | collective-permute-done | bytes 65568 | tf_op jit(solution)/shard_map/ppermute | solution.py:564
  56.7 3.3 %collective-permute-start.14 = (f32[2,8,8,128]{3,2,1,0:T(8,128)S(1)}, f32[2,8,8,128]{3,2,1,0:T(8,128)S(1)}, u32[]{:S(2)}, u32[]{:S(2)}) collective-permute-start(f32[2,8,8,128]{3,2,1,0:T(8,128)S(1)} %get-tuple-element.156.od_ref), channel_id=1, source_target_pairs={{0,31},{1,2},{2,1},{3,4},{4,3},{5,6},{6,5},{7,8},{8,7},{9,10},{10,... | collective-permute-start | bytes 196616 | tf_op jit(solution)/shard_map/ppermute | solution.py:564
  60.3 0.9 %collective-permute-done.15.rev_ref = f32[2,8,8,128]{3,2,1,0:T(8,128)S(1)} collective-permute-done((f32[2,8,8,128]{3,2,1,0:T(8,128)S(1)}, f32[2,8,8,128]{3,2,1,0:T(8,128)S(1)}, u32[]{:S(2)}, u32[]{:S(2)}) %collective-permute-start.15) | collective-permute-done | bytes 65568 | tf_op jit(solution)/shard_map/ppermute | solution.py:565
  61.5 3.2 %collective-permute-start.17 = (f32[2,8,8,128]{3,2,1,0:T(8,128)S(1)}, f32[2,8,8,128]{3,2,1,0:T(8,128)S(1)}, u32[]{:S(2)}, u32[]{:S(2)}) collective-permute-start(f32[2,8,8,128]{3,2,1,0:T(8,128)S(1)} %get-tuple-element.172.own_ref), channel_id=1, source_target_pairs={{0,31},{1,2},{2,1},{3,4},{4,3},{5,6},{6,5},{7,8},{8,7},{9,10},{10,... | collective-permute-start | bytes 196616 | tf_op jit(solution)/shard_map/ppermute | solution.py:564
  64.7 1.3 %between.7 = (f32[2,6,8,8,128]{4,3,2,1,0:T(8,128)S(1)}, f32[2,8,8,128]{3,2,1,0:T(8,128)S(1)}) custom-call(f32[2,8,8,128]{3,2,1,0:T(8,128)S(1)} %get-tuple-element.164.p7_ref, f32[2,6,8,8,128]{4,3,2,1,0:T(8,128)S(1)} %get-tuple-element.165.gi_ref, f32[2,2,8,8,128]{4,3,2,1,0:T(8,128)S(1)} %get-tuple-element.163.q_ref, ...), custom_call_target="tpu_custom_call" | custom-call | flops 2000000000 | bytes 1024 | tf_op jit(solution)/shard_map/between/pallas_call | solution.py:545
  66.3 1.8 %last.1 = (f32[2,8,8,8,128]{4,3,2,1,0:T(8,128)}, f32[2,2,8,8,128]{4,3,2,1,0:T(8,128)S(1)}, f32[2,8,8,128]{3,2,1,0:T(8,128)S(1)}) custom-call(s32[1,128]{1,0:T(1,128)S(1)} %copy-done.2, f32[2,8,8,128]{3,2,1,0:T(8,128)S(1)} %get-tuple-element.168.p0_ref, f32[2,8,8,128]{3,2,1,0:T(8,128)S(1)} %get-tuple-element.164.p7_ref, ...), custom_call_target="tpu_custom_call" | custom-call | flops 3000000000 | bytes 1024 | tf_op jit(solution)/shard_map/last/pallas_call | solution.py:545
  68.1 1.8 %collective-permute-done.17.got_ref = f32[2,8,8,128]{3,2,1,0:T(8,128)S(1)} collective-permute-done((f32[2,8,8,128]{3,2,1,0:T(8,128)S(1)}, f32[2,8,8,128]{3,2,1,0:T(8,128)S(1)}, u32[]{:S(2)}, u32[]{:S(2)}) %collective-permute-start.17) | collective-permute-done | bytes 65568 | tf_op jit(solution)/shard_map/ppermute | solution.py:564
  70.6 0.8 %finish.3 = f32[2,8,8,8,128]{4,3,2,1,0:T(8,128)} custom-call(s32[1,128]{1,0:T(1,128)S(1)} %copy-done.2, f32[2,8,8,128]{3,2,1,0:T(8,128)S(1)} %get-tuple-element.167.own_ref, f32[2,8,8,128]{3,2,1,0:T(8,128)S(1)} %collective-permute-done.16.got_ref, f32[2,8,8,128]{3,2,1,0:T(8,128)S(1)} %get-tuple-element.93.rf_ref.refs_3_, ...), custom_call_target="tpu_custom_call", output_to_operand_aliasing={{}: (6, {})} | custom-call | flops 1000000 | bytes 1024 | tf_op jit(solution)/shard_map/finish/pallas_call | solution.py:545
  (50 shorter events, 7.7 us)
Async XLA Ops:
  0.0 8.0 %copy-start = (f32[2,512,128]{2,1,0:T(8,128)S(1)}, f32[2,512,128]{2,1,0:T(8,128)}, u32[]{:S(2)}) copy-start(f32[2,512,128]{2,1,0:T(8,128)} %param.6) | copy-start | bytes 1572868
  0.0 8.0 %copy-start.1 = (f32[512,128]{1,0:T(8,128)S(1)}, f32[512,128]{1,0:T(8,128)}, u32[]{:S(2)}) copy-start(f32[512,128]{1,0:T(8,128)} %param.8) | copy-start | bytes 786436
  0.0 8.0 %copy-start.2 = (s32[1,128]{1,0:T(1,128)S(1)}, s32[1,128]{1,0:T(1,128)}, u32[]{:S(2)}) copy-start(s32[1,128]{1,0:T(1,128)} %order_ref.11) | copy-start | bytes 1540
  0.0 8.5 %copy-start.3 = (f32[3,512,128]{2,1,0:T(8,128)S(1)}, f32[3,512,128]{2,1,0:T(8,128)}, u32[]{:S(2)}) copy-start(f32[3,512,128]{2,1,0:T(8,128)} %param.7) | copy-start | bytes 2359300
  1.3 11.4 %collective-permute-start = (f32[3,8,8,128]{3,2,1,0:T(8,128)S(1)}, f32[3,8,8,128]{3,2,1,0:T(8,128)S(1)}, u32[]{:S(2)}, u32[]{:S(2)}) collective-permute-start(f32[3,8,8,128]{3,2,1,0:T(8,128)S(1)} %project.2.od_ref), channel_id=1, source_target_pairs={{0,31},{1,2},{2,1},{3,4},{4,3},{5,6},{6,5},{7,8},{8,7},{9,10},{10,... | collective-permute-start | bytes 294920 | tf_op jit(solution)/shard_map/ppermute | solution.py:564
  8.4 4.7 %collective-permute-start.1 = (f32[3,8,8,128]{3,2,1,0:T(8,128)S(1)}, f32[3,8,8,128]{3,2,1,0:T(8,128)S(1)}, u32[]{:S(2)}, u32[]{:S(2)}) collective-permute-start(f32[3,8,8,128]{3,2,1,0:T(8,128)S(1)} %project.3.ev_ref), channel_id=1, source_target_pairs={{0,1},{1,0},{2,3},{3,2},{4,5},{5,4},{6,7},{7,6},{8,9},{9,8},{10,11... | collective-permute-start | bytes 294920 | tf_op jit(solution)/shard_map/ppermute | solution.py:565
  8.5 2.2 %copy-start.5 = (f32[8,8]{1,0:T(8,128)S(1)}, f32[8,8]{1,0:T(8,128)}, u32[]{:S(2)}) copy-start(f32[8,8]{1,0:T(8,128)} %constant.4.clone) | copy-start | bytes 772
  10.7 0.7 copy-start.4
  13.4 4.3 %collective-permute-start.3 = (f32[2,8,8,128]{3,2,1,0:T(8,128)S(1)}, f32[2,8,8,128]{3,2,1,0:T(8,128)S(1)}, u32[]{:S(2)}, u32[]{:S(2)}) collective-permute-start(f32[2,8,8,128]{3,2,1,0:T(8,128)S(1)} %get-tuple-element.94.ev_ref), channel_id=1, source_target_pairs={{0,1},{1,0},{2,3},{3,2},{4,5},{5,4},{6,7},{7,6},{8,9},{9,8},{10,11... | collective-permute-start | bytes 196616 | tf_op jit(solution)/shard_map/ppermute | solution.py:565
  15.1 8.9 %collective-permute-start.2 = (f32[2,8,8,128]{3,2,1,0:T(8,128)S(1)}, f32[2,8,8,128]{3,2,1,0:T(8,128)S(1)}, u32[]{:S(2)}, u32[]{:S(2)}) collective-permute-start(f32[2,8,8,128]{3,2,1,0:T(8,128)S(1)} %get-tuple-element.92.od_ref), channel_id=1, source_target_pairs={{0,31},{1,2},{2,1},{3,4},{4,3},{5,6},{6,5},{7,8},{8,7},{9,10},{10,... | collective-permute-start | bytes 196616 | tf_op jit(solution)/shard_map/ppermute | solution.py:564
  18.0 9.6 %collective-permute-start.5 = (f32[5,8,8,128]{3,2,1,0:T(8,128)S(1)}, f32[5,8,8,128]{3,2,1,0:T(8,128)S(1)}, u32[]{:S(2)}, u32[]{:S(2)}) collective-permute-start(f32[5,8,8,128]{3,2,1,0:T(8,128)S(1)} %get-tuple-element.105.refs_0_), channel_id=1, source_target_pairs={{0,31},{1,2},{2,1},{3,4},{4,3},{5,6},{6,5},{7,8},{8,7},{9,10},{10,... | collective-permute-start | bytes 491528 | tf_op jit(solution)/shard_map/ppermute | solution.py:564
  24.2 4.6 %collective-permute-start.4 = (f32[2,8,8,128]{3,2,1,0:T(8,128)S(1)}, f32[2,8,8,128]{3,2,1,0:T(8,128)S(1)}, u32[]{:S(2)}, u32[]{:S(2)}) collective-permute-start(f32[2,8,8,128]{3,2,1,0:T(8,128)S(1)} %get-tuple-element.104.ev_ref), channel_id=1, source_target_pairs={{0,1},{1,0},{2,3},{3,2},{4,5},{5,4},{6,7},{7,6},{8,9},{9,8},{10,11... | collective-permute-start | bytes 196616 | tf_op jit(solution)/shard_map/ppermute | solution.py:565
  29.1 4.3 %collective-permute-start.7 = (f32[2,8,8,128]{3,2,1,0:T(8,128)S(1)}, f32[2,8,8,128]{3,2,1,0:T(8,128)S(1)}, u32[]{:S(2)}, u32[]{:S(2)}) collective-permute-start(f32[2,8,8,128]{3,2,1,0:T(8,128)S(1)} %get-tuple-element.114.ev_ref), channel_id=1, source_target_pairs={{0,1},{1,0},{2,3},{3,2},{4,5},{5,4},{6,7},{7,6},{8,9},{9,8},{10,11... | collective-permute-start | bytes 196616 | tf_op jit(solution)/shard_map/ppermute | solution.py:565
  29.1 9.1 %collective-permute-start.6 = (f32[2,8,8,128]{3,2,1,0:T(8,128)S(1)}, f32[2,8,8,128]{3,2,1,0:T(8,128)S(1)}, u32[]{:S(2)}, u32[]{:S(2)}) collective-permute-start(f32[2,8,8,128]{3,2,1,0:T(8,128)S(1)} %get-tuple-element.113.od_ref), channel_id=1, source_target_pairs={{0,31},{1,2},{2,1},{3,4},{4,3},{5,6},{6,5},{7,8},{8,7},{9,10},{10,... | collective-permute-start | bytes 196616 | tf_op jit(solution)/shard_map/ppermute | solution.py:564
  33.6 8.5 %collective-permute-start.9 = (f32[2,8,8,128]{3,2,1,0:T(8,128)S(1)}, f32[2,8,8,128]{3,2,1,0:T(8,128)S(1)}, u32[]{:S(2)}, u32[]{:S(2)}) collective-permute-start(f32[2,8,8,128]{3,2,1,0:T(8,128)S(1)} %get-tuple-element.125.refs_0_), channel_id=1, source_target_pairs={{0,31},{1,2},{2,1},{3,4},{4,3},{5,6},{6,5},{7,8},{8,7},{9,10},{10,... | collective-permute-start | bytes 196616 | tf_op jit(solution)/shard_map/ppermute | solution.py:564
  38.4 4.3 %collective-permute-start.8 = (f32[2,8,8,128]{3,2,1,0:T(8,128)S(1)}, f32[2,8,8,128]{3,2,1,0:T(8,128)S(1)}, u32[]{:S(2)}, u32[]{:S(2)}) collective-permute-start(f32[2,8,8,128]{3,2,1,0:T(8,128)S(1)} %get-tuple-element.124.ev_ref), channel_id=1, source_target_pairs={{0,1},{1,0},{2,3},{3,2},{4,5},{5,4},{6,7},{7,6},{8,9},{9,8},{10,11... | collective-permute-start | bytes 196616 | tf_op jit(solution)/shard_map/ppermute | solution.py:565
  42.9 4.3 %collective-permute-start.11 = (f32[2,8,8,128]{3,2,1,0:T(8,128)S(1)}, f32[2,8,8,128]{3,2,1,0:T(8,128)S(1)}, u32[]{:S(2)}, u32[]{:S(2)}) collective-permute-start(f32[2,8,8,128]{3,2,1,0:T(8,128)S(1)} %get-tuple-element.136.ev_ref), channel_id=1, source_target_pairs={{0,1},{1,0},{2,3},{3,2},{4,5},{5,4},{6,7},{7,6},{8,9},{9,8},{10,11... | collective-permute-start | bytes 196616 | tf_op jit(solution)/shard_map/ppermute | solution.py:565
  43.1 8.8 %collective-permute-start.10 = (f32[2,8,8,128]{3,2,1,0:T(8,128)S(1)}, f32[2,8,8,128]{3,2,1,0:T(8,128)S(1)}, u32[]{:S(2)}, u32[]{:S(2)}) collective-permute-start(f32[2,8,8,128]{3,2,1,0:T(8,128)S(1)} %get-tuple-element.135.od_ref), channel_id=1, source_target_pairs={{0,31},{1,2},{2,1},{3,4},{4,3},{5,6},{6,5},{7,8},{8,7},{9,10},{10,... | collective-permute-start | bytes 196616 | tf_op jit(solution)/shard_map/ppermute | solution.py:564
  47.5 8.5 %collective-permute-start.13 = (f32[2,8,8,128]{3,2,1,0:T(8,128)S(1)}, f32[2,8,8,128]{3,2,1,0:T(8,128)S(1)}, u32[]{:S(2)}, u32[]{:S(2)}) collective-permute-start(f32[2,8,8,128]{3,2,1,0:T(8,128)S(1)} %get-tuple-element.147.refs_0_), channel_id=1, source_target_pairs={{0,31},{1,2},{2,1},{3,4},{4,3},{5,6},{6,5},{7,8},{8,7},{9,10},{10,... | collective-permute-start | bytes 196616 | tf_op jit(solution)/shard_map/ppermute | solution.py:564
  52.1 4.3 %collective-permute-start.12 = (f32[2,8,8,128]{3,2,1,0:T(8,128)S(1)}, f32[2,8,8,128]{3,2,1,0:T(8,128)S(1)}, u32[]{:S(2)}, u32[]{:S(2)}) collective-permute-start(f32[2,8,8,128]{3,2,1,0:T(8,128)S(1)} %get-tuple-element.146.ev_ref), channel_id=1, source_target_pairs={{0,1},{1,0},{2,3},{3,2},{4,5},{5,4},{6,7},{7,6},{8,9},{9,8},{10,11... | collective-permute-start | bytes 196616 | tf_op jit(solution)/shard_map/ppermute | solution.py:565
  56.7 4.6 %collective-permute-start.15 = (f32[2,8,8,128]{3,2,1,0:T(8,128)S(1)}, f32[2,8,8,128]{3,2,1,0:T(8,128)S(1)}, u32[]{:S(2)}, u32[]{:S(2)}) collective-permute-start(f32[2,8,8,128]{3,2,1,0:T(8,128)S(1)} %get-tuple-element.157.ev_ref), channel_id=1, source_target_pairs={{0,1},{1,0},{2,3},{3,2},{4,5},{5,4},{6,7},{7,6},{8,9},{9,8},{10,11... | collective-permute-start | bytes 196616 | tf_op jit(solution)/shard_map/ppermute | solution.py:565
  56.7 9.3 %collective-permute-start.14 = (f32[2,8,8,128]{3,2,1,0:T(8,128)S(1)}, f32[2,8,8,128]{3,2,1,0:T(8,128)S(1)}, u32[]{:S(2)}, u32[]{:S(2)}) collective-permute-start(f32[2,8,8,128]{3,2,1,0:T(8,128)S(1)} %get-tuple-element.156.od_ref), channel_id=1, source_target_pairs={{0,31},{1,2},{2,1},{3,4},{4,3},{5,6},{6,5},{7,8},{8,7},{9,10},{10,... | collective-permute-start | bytes 196616 | tf_op jit(solution)/shard_map/ppermute | solution.py:564
  61.5 8.5 %collective-permute-start.17 = (f32[2,8,8,128]{3,2,1,0:T(8,128)S(1)}, f32[2,8,8,128]{3,2,1,0:T(8,128)S(1)}, u32[]{:S(2)}, u32[]{:S(2)}) collective-permute-start(f32[2,8,8,128]{3,2,1,0:T(8,128)S(1)} %get-tuple-element.172.own_ref), channel_id=1, source_target_pairs={{0,31},{1,2},{2,1},{3,4},{4,3},{5,6},{6,5},{7,8},{8,7},{9,10},{10,... | collective-permute-start | bytes 196616 | tf_op jit(solution)/shard_map/ppermute | solution.py:564
  66.3 4.3 %collective-permute-start.16 = (f32[2,8,8,128]{3,2,1,0:T(8,128)S(1)}, f32[2,8,8,128]{3,2,1,0:T(8,128)S(1)}, u32[]{:S(2)}, u32[]{:S(2)}) collective-permute-start(f32[2,8,8,128]{3,2,1,0:T(8,128)S(1)} %get-tuple-element.167.own_ref), channel_id=1, source_target_pairs={{0,1},{1,0},{2,3},{3,2},{4,5},{5,4},{6,7},{7,6},{8,9},{9,8},{10,11... | collective-permute-start | bytes 196616 | tf_op jit(solution)/shard_map/ppermute | solution.py:565

commit v3 on v0

v3 whole, which is shorter than its diff:
```python
import jax
import jax.numpy as jnp
import numpy as np
from jax import lax
from jax.experimental import pallas as pl
from jax.experimental.pallas import tpu as pltpu
from jax.sharding import PartitionSpec as P

ORDER = 7
EXT = ORDER + 1
SUBSTEPS = 2
STAGES = 4
EY = 8
EZ = 16
LANES = EY * EZ
SUB = 8
ROWS = 7

time_step = 0.015


def legendre_table(points, degree):
    table = np.zeros((points.shape[0], degree + 1))
    table[:, 0] = 1.0
    table[:, 1] = points
    for level in range(2, degree + 1):
        table[:, level] = (
            (2 * level - 1) * points * table[:, level - 1] - (level - 1) * table[:, level - 2]
        ) / level
    return table


def gll_derivative(degree):
    extent = degree + 1
    points = np.cos(np.pi * np.arange(extent) / degree)
    for sweep in range(60):
        table = legendre_table(points, degree)
        points = points - (points * table[:, degree] - table[:, degree - 1]) / (
            extent * table[:, degree]
        )
    points = points[::-1].copy()
    values = legendre_table(points, degree)[:, degree]
    matrix = np.zeros((extent, extent))
    for target in range(extent):
        for source in range(extent):
            if target != source:
                matrix[target, source] = values[target] / (
                    values[source] * (points[target] - points[source])
                )
    matrix[0, 0] = -degree * (degree + 1) / 4.0
    matrix[extent - 1, extent - 1] = degree * (degree + 1) / 4.0
    return matrix


DM = gll_derivative(ORDER)
SUM_PART = [[(DM[j, a] + DM[j, 7 - a]) / 2 for a in range(4)] for j in range(4)]
DIF_PART = [[(DM[j, a] - DM[j, 7 - a]) / 2 for a in range(4)] for j in range(4)]
ROT = np.array([[DM[k, (k - r) % 8] for k in range(8)] for r in range(8)], np.float32)


def combine(coefs, items):
    total = None
    for c, x in zip(coefs, items):
        term = x * np.float32(c)
        total = term if total is None else total + term
    return total


def along_second(plane):
    even = [plane[a] + plane[7 - a] for a in range(4)]
    odd = [plane[a] - plane[7 - a] for a in range(4)]
    out = [None] * 8
    for j in range(4):
        e = combine(SUM_PART[j], even)
        o = combine(DIF_PART[j], odd)
        out[j] = o + e
        out[7 - j] = o - e
    return out


def along_third(x, rot):
    total = x * rot[0]
    for r in range(1, 8):
        total = total + pltpu.roll(x, r, 0) * rot[r]
    return total


def gather_lanes(x, idx):
    return jnp.take_along_axis(x, idx, axis=1, mode="promise_in_bounds")


def third_tables():
    lane = lax.broadcasted_iota(jnp.int32, (SUB, LANES), 1)
    k = lax.broadcasted_iota(jnp.int32, (SUB, LANES), 0)
    z = lane % EZ
    back = jnp.where(z == 0, lane + (EZ - 1), lane - 1)
    ahead = jnp.where(z == EZ - 1, lane - (EZ - 1), lane + 1)
    return jnp.where(k == 0, back, ahead), k == 0, k == ORDER


def plane_sum(plane, tables, rows=EXT):
    idx, first, last = tables
    up = plane[7] + pltpu.roll(plane[0], LANES - EZ, 1)
    plane = [pltpu.roll(up, EZ, 1)] + list(plane[1:7]) + [up]
    out = []
    for v in plane[:rows]:
        x = jnp.where(first, pltpu.roll(v, 1, 0), jnp.where(last, pltpu.roll(v, 7, 0), 0.0))
        out.append(v + gather_lanes(x, idx))
    return out


def full(rows):
    return list(rows) + [pltpu.roll(rows[0], LANES - EZ, 1)]


def write(ref, lead, plane):
    for j, v in enumerate(plane):
        ref[lead + (j,)] = v


def read(ref, *lead, rows=EXT):
    return [ref[lead + (j,)] for j in range(rows)]


def brick_index(order_ref):
    order = jnp.broadcast_to(order_ref[...], (LANES, LANES))
    pos = lax.broadcasted_iota(jnp.int32, (LANES, LANES), 0)
    hot = jnp.where(order == pos, 1.0, 0.0).astype(jnp.bfloat16)
    slot = lax.broadcasted_iota(jnp.int32, (SUB, LANES), 1).astype(jnp.float32).astype(jnp.bfloat16)
    found = lax.dot_general(
        slot, hot, (((1,), (1,)), ((), ())), preferred_element_type=jnp.float32
    )
    return found.astype(jnp.int32)


def source_plane(parity, i):
    return jnp.where(parity == 1, ORDER - i, i)


def source_plane(parity, i):
    return jnp.where(parity == 1, ORDER - i, i)


def project(weight, scal, idx, tables):
    weight = [gather_lanes(v, idx) for v in weight]
    planes = [[gather_lanes(plane[j], idx) * weight[j] for j in range(8)] for plane in scal]
    return [plane_sum(plane, tables, ROWS) for plane in planes + [weight]]


def project_odd(order_ref, scal_ref, mass_ref, od_ref, idx_ref, order_buf, scal_buf, mass_buf, sems):
    src = source_plane(lax.axis_index("elem") % 2, 0)
    copies = [pltpu.make_async_copy(order_ref, order_buf, sems.at[0])]
    copies.append(pltpu.make_async_copy(mass_ref.at[src], mass_buf, sems.at[1]))
    for m in range(2):
        copies.append(pltpu.make_async_copy(scal_ref.at[m, src], scal_buf.at[m], sems.at[2 + m]))
    for copy in copies:
        copy.start()
    tables = third_tables()
    copies[0].wait()
    idx = brick_index(order_buf)
    idx_ref[...] = idx
    for copy in copies[1:]:
        copy.wait()
    planes = project(read(mass_buf), [read(scal_buf, m) for m in range(2)], idx, tables)
    for r in range(3):
        write(od_ref, (r,), planes[r])


def signs_of(parity):
    first = jnp.where(parity == 1, time_step, -time_step).astype(jnp.float32)
    return first, np.float32(-time_step), np.float32(-time_step)


def project_even(idx_ref, scal_ref, mass_ref, tr_ref, ev_ref):
    parity = lax.axis_index("elem") % 2
    src = source_plane(parity, ORDER)
    idx = idx_ref[...]
    signs = signs_of(parity)
    planes = project(
        read(mass_ref, src), [read(scal_ref, m, src) for m in range(2)], idx, third_tables())
    planes.extend([gather_lanes(v, idx) * signs[r] for v in read(tr_ref, r, src)] for r in range(3))
    write(ev_ref, (), sum(planes, []))


def prepare(idx_ref, scal_ref, mass_ref, tr_ref,
            gi_ref, q_ref, ri_ref, rt_ref, ti_ref, tf_ref, st_ref):
    parity = lax.axis_index("elem") % 2
    idx = idx_ref[...]
    tables = third_tables()
    signs = signs_of(parity)
    for face in range(2):
        src = source_plane(parity, face * ORDER)
        first = [gather_lanes(v, idx) * signs[0] for v in read(tr_ref, 0, src)]
        write(st_ref, (face,), plane_sum(first, tables, ROWS))
        if face == 0:
            write(tf_ref, (0,), first)
            for r in (1, 2):
                write(tf_ref, (r,), [gather_lanes(v, idx) * signs[r] for v in read(tr_ref, r, src)])
    sums = [[None, None], [None, None]]
    for i in range(6):
        src = source_plane(parity, i + 1)
        for r in (1, 2):
            write(ti_ref, (i, r - 1), [gather_lanes(v, idx) * signs[r] for v in read(tr_ref, r, src)])
        first = plane_sum([gather_lanes(v, idx) * signs[0] for v in read(tr_ref, 0, src)], tables)
        weight = [gather_lanes(v, idx) for v in read(mass_ref, src)]
        inverse = [1.0 / v for v in plane_sum(weight, tables)]
        write(ri_ref, (i,), inverse)
        write(rt_ref, (i,), [first[j] * inverse[j] for j in range(8)])
        for m in range(2):
            scal = read(scal_ref, m, src)
            plane = plane_sum([gather_lanes(scal[j], idx) * weight[j] for j in range(8)], tables)
            plane = [plane[j] * inverse[j] for j in range(8)]
            write(gi_ref, (m, i), plane)
            for face in range(2):
                terms = [v * np.float32(DM[face * ORDER, i + 1]) for v in plane[:ROWS]]
                old = sums[face][m]
                sums[face][m] = [x + y for x, y in zip(old, terms)] if old else terms
    for face in range(2):
        for m in range(2):
            write(q_ref, (face, m), sums[face][m])


def rotations(rot_ref):
    return [rot_ref[r] for r in range(8)]


def in_plane(plane, second_t, third_t, rot):
    second = along_second(plane)
    return [second_t[j] * second[j] + third_t[j] * along_third(plane[j], rot) for j in range(8)]


def inner_open(gi_ref, ri_ref, rt_ref, ti_ref, rot, wp_ref):
    tables = third_tables()
    for m in range(2):
        for j in range(8):
            rows = [gi_ref[m, a, j] for a in range(6)]
            even = [rows[a] + rows[5 - a] for a in range(3)]
            odd = [rows[a] - rows[5 - a] for a in range(3)]
            for i in range(3):
                e = combine([(DM[i + 1, a + 1] + DM[i + 1, 6 - a]) / 2 for a in range(3)], even)
                o = combine([(DM[i + 1, a + 1] - DM[i + 1, 6 - a]) / 2 for a in range(3)], odd)
                wp_ref[m, i, j] = (o + e) * rt_ref[i, j]
                wp_ref[m, 5 - i, j] = (o - e) * rt_ref[5 - i, j]
    for i in range(6):
        for m in range(2):
            plane = in_plane(read(gi_ref, m, i), read(ti_ref, i, 0), read(ti_ref, i, 1), rot)
            plane = plane_sum(plane, tables)
            write(wp_ref, (m, i), [wp_ref[m, i, j] + ri_ref[i, j] * plane[j] for j in range(8)])


def inner_close(p0_ref, p7_ref, wp_ref, rt_ref, scale, put, q_ref=None):
    for m in range(2):
        p0, p7 = full(read(p0_ref, m, rows=ROWS)), full(read(p7_ref, m, rows=ROWS))
        sums = [[], []]
        for i in range(6):
            near, far = np.float32(scale * DM[i + 1, 0]), np.float32(scale * DM[i + 1, ORDER])
            kept = put(m, i, [
                wp_ref[m, i, j] * np.float32(scale) + rt_ref[i, j] * (p0[j] * near + p7[j] * far)
                for j in range(8)
            ])
            for face in range(2):
                terms = [v * np.float32(DM[face * ORDER, i + 1]) for v in kept[:ROWS]]
                sums[face] = [x + y for x, y in zip(sums[face], terms)] if i else terms
        if q_ref is not None:
            for face in range(2):
                write(q_ref, (face, m), sums[face])


def own_terms(p_ref, a_ref, rf_ref, face, rot, tables, e_ref):
    second_t, third_t = read(a_ref, 0), read(a_ref, 1)
    for m in range(2):
        p = full(read(p_ref, m, rows=ROWS))
        plane = plane_sum(in_plane(p, second_t, third_t, rot), tables, ROWS)
        write(e_ref, (m,), [
            rf_ref[j] * (plane[j] + a_ref[2, j] * (p[j] * np.float32(DM[face * ORDER, face * ORDER])))
            for j in range(ROWS)
        ])


def both_sides(own, got, tables, a_ref):
    total = [[own[r][j] + got[r][j] for j in range(8)] for r in range(3)]
    write(a_ref, (0,), total[1])
    write(a_ref, (1,), total[2])
    write(a_ref, (2,), plane_sum(total[0], tables, ROWS))


def transports(ref, start):
    return [[ref[start + 8 * r + j] for j in range(8)] for r in range(3)]


def make_field_face(face, carry):
    far = np.float32(DM[ORDER - face * ORDER, face * ORDER])

    def field_face(own_ref, got_ref, q_ref, st_ref, *refs):
        tf_ref = refs[0] if carry else None
        p_ref, rf_ref, send_ref = refs[-3:]
        inverse = [1.0 / (own_ref[14 + j] + got_ref[14 + j]) for j in range(ROWS)]
        p = [
            [(own_ref[ROWS * m + j] + got_ref[ROWS * m + j]) * inverse[j] for j in range(ROWS)]
            for m in range(2)
        ]
        sent = [
            [st_ref[1 - face, j] * (q_ref[1 - face, m, j] + p[m][j] * far) for j in range(ROWS)]
            for m in range(2)
        ]
        write(send_ref, (), sent[0] + sent[1])
        for m in range(2):
            write(p_ref, (m,), p[m])
        write(rf_ref, (), inverse)
        if carry:
            for r in range(3):
                for j in range(8):
                    send_ref[2 * ROWS + 8 * r + j] = tf_ref[r, j]

    return field_face


def make_stage_face(face, scale, total, raw, early):
    far = np.float32(DM[ORDER - face * ORDER, face * ORDER])
    scale = np.float32(scale)

    def stage_face(*refs):
        own_ref, got_ref, e_ref, acc_ref, q_ref, rt_ref, rf_ref = refs[:7]
        if early:
            tf_ref, rot_ref, p_ref, send_ref, a_ref, e_buf = refs[7:]
            tables = third_tables()
            both_sides([read(tf_ref, r) for r in range(3)], transports(got_ref, 2 * ROWS), tables, a_ref)
            own_terms(e_ref, a_ref, rf_ref, face, rotations(rot_ref), tables, e_buf)
            e_ref = e_buf
        else:
            p_ref, send_ref = refs[7:]
        p = []
        for m in range(2):
            value = [own_ref[ROWS * m + j] + got_ref[ROWS * m + j] for j in range(ROWS)]
            if raw:
                value = [value[j] * rf_ref[j] for j in range(ROWS)]
            value = [(value[j] + e_ref[m, j]) * scale for j in range(ROWS)]
            if total:
                value = [value[j] + acc_ref[face, m, j] for j in range(ROWS)]
            p.append(value)
        sent = [
            [rt_ref[1 - face, j] * (q_ref[1 - face, m, j] + p[m][j] * far) for j in range(ROWS)]
            for m in range(2)
        ]
        write(send_ref, (), sent[0] + sent[1])
        for m in range(2):
            write(p_ref, (m,), p[m])

    return stage_face


def make_first_inner(scale, opening, start):
    def first_inner(*refs):
        p0_ref, p7_ref, gi_ref, acci_ref, wp_ref, rt_ref, r7_ref, rot_ref = refs[:8]
        tables = third_tables()
        if start:
            ev_ref, rev_ref, st_ref, r0_ref = refs[8:12]
            gn_ref, an_ref, q_ref, e7_ref, a7_ref, rs_ref = refs[12:]
            both_sides(transports(ev_ref, 3 * ROWS), transports(rev_ref, 3 * ROWS), tables, a7_ref)
            write(rs_ref, (0,), [st_ref[0, j] * r0_ref[j] for j in range(ROWS)])
            write(rs_ref, (1,), [st_ref[1, j] * r7_ref[j] for j in range(ROWS)])
        else:
            a7_ref = refs[8]
            gn_ref, an_ref, q_ref, e7_ref = refs[9:]
        own_terms(p7_ref, a7_ref, r7_ref, 1, rotations(rot_ref), tables, e7_ref)

        def put(m, i, value):
            base = gi_ref if opening else acci_ref
            write(gn_ref, (m, i), value)
            write(an_ref, (m, i), [base[m, i, j] + value[j] for j in range(8)])
            return value

        inner_close(p0_ref, p7_ref, wp_ref, rt_ref, scale, put, q_ref)

    return first_inner


def make_between(early):
    def between(*refs):
        m7_ref, gi_ref, a7_ref, r7_ref, ri_ref, rt_ref, ti_ref, rot_ref = refs[:8]
        rot = rotations(rot_ref)
        tables = third_tables()
        if early:
            wp_ref, e7_ref = refs[8:]
        else:
            p0_ref, a0_ref, r0_ref, wp_ref, e7_ref, e0_ref = refs[8:]
            own_terms(p0_ref, a0_ref, r0_ref, 0, rot, tables, e0_ref)
        own_terms(m7_ref, a7_ref, r7_ref, 1, rot, tables, e7_ref)
        inner_open(gi_ref, ri_ref, rt_ref, ti_ref, rot, wp_ref)

    return between


def face_totals(now, before, accf_ref, afn_ref, opening):
    for face in range(2):
        for m in range(2):
            for j in range(ROWS):
                value = now[face][m, j] + before[face][m, j]
                afn_ref[face, m, j] = value if opening else value + accf_ref[face, m, j]


def make_second_inner(scale, opening, closing):
    def second_inner(m0_ref, m7_ref, p0_ref, p7_ref, accf_ref, acci_ref, wp_ref, ri_ref, rt_ref,
                     ti_ref, a0_ref, r0_ref, rot_ref, gn_ref, q_ref, an_ref, afn_ref, wn_ref, e0_ref):
        rot = rotations(rot_ref)

        def put(m, i, value):
            total = [acci_ref[m, i, j] + value[j] for j in range(8)]
            kept = total if closing else value
            write(gn_ref, (m, i), kept)
            if not closing:
                write(an_ref, (m, i), total)
            return kept

        inner_close(m0_ref, m7_ref, wp_ref, rt_ref, scale, put, q_ref)
        own_terms(m0_ref, a0_ref, r0_ref, 0, rot, third_tables(), e0_ref)
        face_totals((m0_ref, m7_ref), (p0_ref, p7_ref), accf_ref, afn_ref, opening)
        inner_open(gn_ref, ri_ref, rt_ref, ti_ref, rot, wn_ref)

    return second_inner


def make_last_inner(scale):
    def last_inner(order_ref, m0_ref, m7_ref, p0_ref, p7_ref, accf_ref, acci_ref, wp_ref, rt_ref,
                   a0_ref, r0_ref, rot_ref, out_ref, afn_ref, e0_ref, buf, sems):
        parity = lax.axis_index("elem") % 2
        idx = jnp.broadcast_to(order_ref[...], (SUB, LANES))

        def put(m, i, value):
            total = [acci_ref[m, i, j] + value[j] for j in range(8)]
            dst = source_plane(parity, i + 1) - 1
            write(buf, (m, dst), [gather_lanes(v, idx) for v in total])
            return total

        inner_close(m0_ref, m7_ref, wp_ref, rt_ref, scale, put)
        copies = [
            pltpu.make_async_copy(buf.at[m], out_ref.at[m, pl.ds(1, 6)], sems.at[m])
            for m in range(2)
        ]
        for copy in copies:
            copy.start()
        own_terms(m0_ref, a0_ref, r0_ref, 0, rotations(rot_ref), third_tables(), e0_ref)
        face_totals((m0_ref, m7_ref), (p0_ref, p7_ref), accf_ref, afn_ref, False)
        for copy in copies:
            copy.wait()

    return last_inner


def final_face(face, scale, order_ref, own_ref, got_ref, e_ref, accf_ref, m):
    idx = jnp.broadcast_to(order_ref[...], (SUB, LANES))
    rows = [
        (own_ref[ROWS * m + j] + got_ref[ROWS * m + j] + e_ref[m, j]) * np.float32(scale)
        + accf_ref[face, m, j]
        for j in range(ROWS)
    ]
    return [gather_lanes(v, idx) for v in full(rows)]


def make_finish_near(face, scale):
    def finish_near(order_ref, own_ref, got_ref, e_ref, accf_ref, face_ref):
        for m in range(2):
            write(face_ref, (m,), final_face(face, scale, order_ref, own_ref, got_ref, e_ref, accf_ref, m))

    return finish_near


def make_finish_far(face, scale):
    def finish_far(order_ref, own_ref, got_ref, e_ref, accf_ref, near_ref, part_ref,
                   out_ref, buf, sems):
        dst = source_plane(lax.axis_index("elem") % 2, face * ORDER)
        copies = []
        for m in range(2):
            copies.append(
                pltpu.make_async_copy(near_ref.at[m], out_ref.at[m, ORDER - dst], sems.at[1, m])
            )
            copies[-1].start()
        for m in range(2):
            write(buf, (m,), final_face(face, scale, order_ref, own_ref, got_ref, e_ref, accf_ref, m))
            copies.append(pltpu.make_async_copy(buf.at[m], out_ref.at[m, dst], sems.at[0, m]))
            copies[-1].start()
        for copy in copies:
            copy.wait()

    return finish_far


VM = pl.BlockSpec(memory_space=pltpu.VMEM)
HB = pl.BlockSpec(memory_space=pltpu.HBM)


def call(kernel, outs, args, name, cost, hbm=(), hbm_out=(), scratch=(), alias={}):
    specs = [HB if n in hbm else VM for n in range(len(args))]
    out_specs = [HB if n in hbm_out else VM for n in range(len(outs))]
    shapes = [jax.ShapeDtypeStruct(s, jnp.int32 if s == (SUB, LANES) else jnp.float32) for s in outs]
    single = len(outs) == 1
    return pl.pallas_call(
        kernel,
        out_shape=shapes[0] if single else shapes,
        in_specs=specs,
        out_specs=out_specs[0] if single else out_specs,
        scratch_shapes=list(scratch),
        input_output_aliases=alias,
        name=name,
        compiler_params=pltpu.CompilerParams(vmem_limit_bytes=8 << 20),
        cost_estimate=pl.CostEstimate(
            flops=cost * 1000000, bytes_accessed=1 << 10, transcendentals=0
        ),
    )(*args)


def per_device(scalars, transport, mass, element_order):
    count = lax.axis_size("elem")
    even_pairs = [(i, i ^ 1) for i in range(count)]
    odd_pairs = [(i, (i + 1) % count if i % 2 else (i - 1) % count) for i in range(count)]
    swap_od = lambda x: lax.ppermute(x, "elem", odd_pairs)
    swap_ev = lambda x: lax.ppermute(x, "elem", even_pairs)
    rot = jnp.asarray(np.broadcast_to(ROT[:, :, None], (8, SUB, LANES)))
    members = scalars.shape[0]
    grid = (EXT, EXT, SUB, LANES)
    scal = scalars.reshape((members,) + grid)
    tr = transport.reshape((3,) + grid)
    mas = mass.reshape(grid)
    tile, part = (EXT, SUB, LANES), (ROWS, SUB, LANES)
    inner, face, faces = (2, 6) + tile, (2,) + part, (2, 2) + part
    sent, geometry = (2 * ROWS, SUB, LANES), (3,) + tile
    f32 = jnp.float32

    stay = lambda x: pltpu.with_memory_space_constraint(x, pltpu.HBM)
    od, idx = call(
        project_odd, [(3,) + part, (SUB, LANES)], (stay(element_order), stay(scal), stay(mas)), "project", 1,
        hbm=(0, 1, 2),
        scratch=[pltpu.VMEM((1, LANES), jnp.int32), pltpu.VMEM((2,) + tile, f32),
                 pltpu.VMEM(tile, f32), pltpu.SemaphoreType.DMA((4,))])
    od = od.reshape(3 * ROWS, SUB, LANES)
    rod = swap_od(od)
    ev = call(
        project_even, [(3 * ROWS + 24, SUB, LANES)], (idx, scal, mas, tr), "project", 1)
    rev = swap_ev(ev)
    gi, q, ri, rt, ti, tf, st = call(
        prepare,
        [inner, faces, (6,) + tile, (6,) + tile, (6, 2) + tile, geometry, (2,) + part],
        (idx, scal, mas, tr), "prepare", 1)

    def opening_terms(gi_ref, ri_ref, rt_ref, ti_ref, rot_ref, wp_ref):
        inner_open(gi_ref, ri_ref, rt_ref, ti_ref, rotations(rot_ref), wp_ref)

    wp = call(opening_terms, [inner], (gi, ri, rt, ti, rot), "terms", 1)
    p0, r0, cev = call(
        make_field_face(0, False), [face, part, sent], (od, rod, q, st), "odd", 3000)
    p7, r7, cod = call(
        make_field_face(1, True), [face, part, (2 * ROWS + 24, SUB, LANES)],
        (ev, rev, q, st, tf), "even", 1)
    acci, accf = gi, q
    pairs = SUBSTEPS * STAGES // 2
    for n in range(pairs):
        s = 2 * n % STAGES + 1
        opening, closing, early = s == 1, s + 1 == STAGES, n == 0
        got_ev, got_od = swap_ev(cev), swap_od(cod)
        extra = (ev, rev, st, r0) if early else (a7,)
        res = call(
            make_first_inner(1.0 / s, opening, early),
            [inner, inner, faces, face] + ([geometry, (2,) + part] if early else []),
            (p0, p7, gi, acci, wp, rt, r7, rot) + extra, "first", 1000)
        gm, acci, q, e7 = res[:4]
        if early:
            a7, rs = res[4:]
        m7, cod2 = call(
            make_stage_face(1, 1.0 / s, False, early, False), [face, sent],
            (cev, got_ev, e7, accf, q, rs, r7), "ahead", 1)
        got_od2 = swap_od(cod2)
        res = call(
            make_between(early), [inner, face] + ([] if early else [face]),
            (m7, gm, a7, r7, ri, rt, ti, rot) + (() if early else (p0, a0, r0)), "between", 2000)
        wp, e7 = res[:2]
        if early:
            m0, cev2, a0 = call(
                make_stage_face(0, 1.0 / s, False, True, True), [face, sent, geometry],
                (cod, got_od, p0, accf, q, rs, r0, tf, rot), "behind", 1,
                scratch=[pltpu.VMEM(face, f32)])
        else:
            m0, cev2 = call(
                make_stage_face(0, 1.0 / s, False, False, False), [face, sent],
                (cod, got_od, res[2], accf, q, rs, r0), "behind", 1)
        got_ev2 = swap_ev(cev2)
        scale = 1.0 / (s + 1)
        if n < pairs - 1:
            gi, q, acci, accf, wp, e0 = call(
                make_second_inner(scale, opening, closing),
                [inner, faces, inner, faces, inner, face],
                (m0, m7, p0, p7, accf, acci, wp, ri, rt, ti, a0, r0, rot), "second", 3000)
            p0, cev = call(
                make_stage_face(0, scale, closing, False, False), [face, sent],
                (cod2, got_od2, e0, accf, q, rs, r0), "odd", 3000)
            p7, cod = call(
                make_stage_face(1, scale, closing, False, False), [face, sent],
                (cev2, got_ev2, e7, accf, q, rs, r7), "even", 1)
        else:
            out, accf, e0 = call(
                make_last_inner(scale), [(members,) + grid, faces, face],
                (element_order, m0, m7, p0, p7, accf, acci, wp, rt, a0, r0, rot), "last", 3000,
                hbm_out=(0,), scratch=[pltpu.VMEM(inner, f32), pltpu.SemaphoreType.DMA((2,))])
            near = call(
                make_finish_near(0, scale), [(2,) + tile],
                (element_order, cod2, got_od2, e0, accf), "finish", 3000)
            out = call(
                make_finish_far(1, scale), [(members,) + grid],
                (element_order, cev2, got_ev2, e7, accf, near, out), "finish", 1,
                hbm=(6,), hbm_out=(0,), alias={6: 0},
                scratch=[pltpu.VMEM((2,) + tile, f32), pltpu.SemaphoreType.DMA((2, 2))])
    return out.reshape(scalars.shape)


def solution(mesh):
    in_specs = (P("ens", None, "elem"), P(None, None, "elem"), P(None, "elem"), P("elem", None))
    out_specs = P("ens", None, "elem")
    return jax.shard_map(
        per_device, mesh=mesh, in_specs=in_specs, out_specs=out_specs, check_vma=False
    )
```

time: 86.9 us -> 70.4 us (0.81)
  Pallas kernels: 23.7 us -> 16.1 us
  waiting for transfers between devices: 18.5 us -> 13.2 us
  starting transfers between devices: 41 us -> 38.1 us
    ppermute x9, starting transfers between devices: 41 us -> 31.2 us  [per_device(): swap_od = lambda x: lax.ppermute(x, 'elem', odd_pairs)]
    ppermute x9, waiting for transfers between devices: 16.6 us -> 7.73 us  [per_device(): swap_od = lambda x: lax.ppermute(x, 'elem', odd_pairs)]
    pallas_call x19 -> x34, Pallas kernels: 23.7 us -> 16.1 us  [call(): pl.pallas_call(kernel, out_shape=shapes[0] if single else shapes, in_spec...]
    ppermute x9, starting transfers between devices: 0.02 us -> 6.89 us  [per_device(): swap_ev = lambda x: lax.ppermute(x, 'elem', even_pairs)]
    ppermute x9, waiting for transfers between devices: 1.95 us -> 5.45 us  [per_device(): swap_ev = lambda x: lax.ppermute(x, 'elem', even_pairs)]
    unnamed x12 -> x10, local copies, waits for them, and re-layouts: 3.34 us -> 2.47 us
  transfers between devices with their start and end apart: 18 -> 18, of which waited for: 11 -> 13; matrix products, arithmetic and copies ran while one was open for 0% -> 0% of each run, Pallas kernels for 23% -> 20%
where the time goes in v3:
time: 70.4 us; the launch traced here: 70.2 us
  starting transfers between devices  38.1 us (54%)
  Pallas kernels  16.1 us (23%)
  waiting for transfers between devices  13.2 us (19%)
  local copies, waits for them, and re-layouts  2.55 us (4%)
    ppermute x9, starting transfers between devices, per_device(): swap_od = lambda x: lax.ppermute(x, 'elem', odd_pairs)  31.2 us
    pallas_call x34, Pallas kernels, call(): pl.pallas_call(kernel, out_shape=shapes[0] if single else shapes, in_spec...  16.1 us
    ppermute x9, waiting for transfers between devices, per_device(): swap_od = lambda x: lax.ppermute(x, 'elem', odd_pairs)  7.73 us
    ppermute x9, starting transfers between devices, per_device(): swap_ev = lambda x: lax.ppermute(x, 'elem', even_pairs)  6.89 us
    ppermute x9, waiting for transfers between devices, per_device(): swap_ev = lambda x: lax.ppermute(x, 'elem', even_pairs)  5.45 us
    unnamed x10, local copies, waits for them, and re-layouts  2.47 us
  transfers between devices with their start and end apart: 18, of which 13 were waited for; matrix products, arithmetic and copies ran while one was open for 0% of the time, Pallas kernels for 20%

profile of v3, /device:TPU:0, one launch (start us, length us, event | category | flops | bytes accessed | tf_op | source)
XLA Modules:
  0.0 70.2 jit_solution(2002805906801232845)
XLA Ops:
  0.0 1.2 %project.2 = (f32[3,7,8,128]{3,2,1,0:T(8,128)S(1)}, s32[8,128]{1,0:T(8,128)S(1)}) custom-call(s32[1,128]{1,0:T(1,128)} %order_ref.7, f32[2,8,8,8,128]{4,3,2,1,0:T(8,128)} %bitcast.5, f32[8,8,8,128]{3,2,1,0:T(8,128)} %bitcast.10), custom_call_target="tpu_custom_call" | custom-call | flops 1000000 | bytes 1024 | tf_op jit(solution)/shard_map/project/pallas_call | solution.py:497
  1.2 6.7 %collective-permute-start.2 = (f32[21,8,128]{2,1,0:T(8,128)S(1)}, f32[21,8,128]{2,1,0:T(8,128)S(1)}, u32[]{:S(2)}, u32[]{:S(2)}) collective-permute-start(f32[21,8,128]{2,1,0:T(8,128)S(1)} %bitcast.13), channel_id=1, source_target_pairs={{0,31},{1,2},{2,1},{3,4},{4,3},{5,6},{6,5},{7,8},{8,7},{9,10},{10,... | collective-permute-start | bytes 258056 | tf_op jit(solution)/shard_map/ppermute | solution.py:516
  7.9 1.1 %copy-done.1 = f32[3,512,128]{2,1,0:T(8,128)S(1)} copy-done((f32[3,512,128]{2,1,0:T(8,128)S(1)}, f32[3,512,128]{2,1,0:T(8,128)}, u32[]{:S(2)}) %copy-start.1) | copy-done | bytes 786456
  9.5 3.2 %prepare.1 = (f32[2,6,8,8,128]{4,3,2,1,0:T(8,128)S(1)}, f32[2,2,7,8,128]{4,3,2,1,0:T(8,128)S(1)}, f32[6,8,8,128]{3,2,1,0:T(8,128)S(1)}, f32[6,8,8,128]{3,2,1,0:T...) custom-call(s32[8,128]{1,0:T(8,128)S(1)} %get-tuple-element.99.idx_ref, ...), custom_call_target="tpu_custom_call" | custom-call | flops 1000000 | bytes 1024 | tf_op jit(solution)/shard_map/prepare/pallas_call | solution.py:497
  14.1 2.1 %collective-permute-start.4 = (f32[14,8,128]{2,1,0:T(8,128)S(1)}, f32[14,8,128]{2,1,0:T(8,128)S(1)}, u32[]{:S(2)}, u32[]{:S(2)}) collective-permute-start(f32[14,8,128]{2,1,0:T(8,128)S(1)} %get-tuple-element.116.refs_0_), channel_id=1, source_target_pairs={{0,1},{1,0},{2,3},{3,2},{4,5},{5,4},{6,7},{7,6},{8,9},{9,8},{10,11... | collective-permute-start | bytes 172040 | tf_op jit(solution)/shard_map/ppermute | solution.py:517
  17.2 1.2 %collective-permute-done.4.refs_1_ = f32[14,8,128]{2,1,0:T(8,128)S(1)} collective-permute-done((f32[14,8,128]{2,1,0:T(8,128)S(1)}, f32[14,8,128]{2,1,0:T(8,128)S(1)}, u32[]{:S(2)}, u32[]{:S(2)}) %collective-permute-start.4) | collective-permute-done | bytes 57376 | tf_op jit(solution)/shard_map/ppermute | solution.py:517
  18.4 4.6 %collective-permute-start.6 = (f32[14,8,128]{2,1,0:T(8,128)S(1)}, f32[14,8,128]{2,1,0:T(8,128)S(1)}, u32[]{:S(2)}, u32[]{:S(2)}) collective-permute-start(f32[14,8,128]{2,1,0:T(8,128)S(1)} %get-tuple-element.129.refs_0_), channel_id=1, source_target_pairs={{0,31},{1,2},{2,1},{3,4},{4,3},{5,6},{6,5},{7,8},{8,7},{9,10},{10,... | collective-permute-start | bytes 172040 | tf_op jit(solution)/shard_map/ppermute | solution.py:516
  23.1 0.8 %between.4 = (f32[2,6,8,8,128]{4,3,2,1,0:T(8,128)S(1)}, f32[2,7,8,128]{3,2,1,0:T(8,128)S(1)}) custom-call(f32[2,7,8,128]{3,2,1,0:T(8,128)S(1)} %get-tuple-element.118.refs_0_.m7_ref, f32[2,6,8,8,128]{4,3,2,1,0:T(8,128)S(1)} %get-tuple-element.119.refs_1_, f32[3,8,8,128]{3,2,1,0:T(8,128)S(1)} %get-tuple-element.120.refs_2_.refs_8_, ...), custom_call_target="tpu_custom_call" | custom-call | flops 2000000000 | bytes 1024 | tf_op jit(solution)/shard_map/between/pallas_call | solution.py:497
  23.9 2.2 %collective-permute-done.1.refs_1_ = f32[38,8,128]{2,1,0:T(8,128)S(1)} collective-permute-done((f32[38,8,128]{2,1,0:T(8,128)S(1)}, f32[38,8,128]{2,1,0:T(8,128)S(1)}, u32[]{:S(2)}, u32[]{:S(2)}) %collective-permute-start.1) | collective-permute-done | bytes 155680 | tf_op jit(solution)/shard_map/ppermute | solution.py:516
  26.5 1.0 %second.3 = (f32[2,6,8,8,128]{4,3,2,1,0:T(8,128)S(1)}, f32[2,2,7,8,128]{4,3,2,1,0:T(8,128)S(1)}, f32[2,6,8,8,128]{4,3,2,1,0:T(8,128)S(1)}, f32[2,2,7,8,128]{4,3,...) custom-call(f32[2,7,8,128]{3,2,1,0:T(8,128)S(1)} %get-tuple-element.122.m0_ref, ...), custom_call_target="tpu_custom_call" | custom-call | flops 3000000000 | bytes 1024 | tf_op jit(solution)/shard_map/second/pallas_call | solution.py:497
  27.5 2.1 %collective-permute-start.7 = (f32[14,8,128]{2,1,0:T(8,128)S(1)}, f32[14,8,128]{2,1,0:T(8,128)S(1)}, u32[]{:S(2)}, u32[]{:S(2)}) collective-permute-start(f32[14,8,128]{2,1,0:T(8,128)S(1)} %get-tuple-element.131.refs_0_), channel_id=1, source_target_pairs={{0,1},{1,0},{2,3},{3,2},{4,5},{5,4},{6,7},{7,6},{8,9},{9,8},{10,11... | collective-permute-start | bytes 172040 | tf_op jit(solution)/shard_map/ppermute | solution.py:517
  29.6 1.1 %collective-permute-done.3.refs_1_ = f32[14,8,128]{2,1,0:T(8,128)S(1)} collective-permute-done((f32[14,8,128]{2,1,0:T(8,128)S(1)}, f32[14,8,128]{2,1,0:T(8,128)S(1)}, u32[]{:S(2)}, u32[]{:S(2)}) %collective-permute-start.3) | collective-permute-done | bytes 57376 | tf_op jit(solution)/shard_map/ppermute | solution.py:517
  30.7 1.0 %collective-permute-start.5 = (f32[14,8,128]{2,1,0:T(8,128)S(1)}, f32[14,8,128]{2,1,0:T(8,128)S(1)}, u32[]{:S(2)}, u32[]{:S(2)}) collective-permute-start(f32[14,8,128]{2,1,0:T(8,128)S(1)} %get-tuple-element.128.refs_0_), channel_id=1, source_target_pairs={{0,31},{1,2},{2,1},{3,4},{4,3},{5,6},{6,5},{7,8},{8,7},{9,10},{10,... | collective-permute-start | bytes 172040 | tf_op jit(solution)/shard_map/ppermute | solution.py:516
  32.1 5.4 %collective-permute-start.10 = (f32[14,8,128]{2,1,0:T(8,128)S(1)}, f32[14,8,128]{2,1,0:T(8,128)S(1)}, u32[]{:S(2)}, u32[]{:S(2)}) collective-permute-start(f32[14,8,128]{2,1,0:T(8,128)S(1)} %get-tuple-element.150.refs_0_), channel_id=1, source_target_pairs={{0,31},{1,2},{2,1},{3,4},{4,3},{5,6},{6,5},{7,8},{8,7},{9,10},{10,... | collective-permute-start | bytes 172040 | tf_op jit(solution)/shard_map/ppermute | solution.py:516
  37.5 0.9 %between.5 = (f32[2,6,8,8,128]{4,3,2,1,0:T(8,128)S(1)}, f32[2,7,8,128]{3,2,1,0:T(8,128)S(1)}, f32[2,7,8,128]{3,2,1,0:T(8,128)S(1)}) custom-call(f32[2,7,8,128]{3,2,1,0:T(8,128)S(1)} %get-tuple-element.139.refs_0_.m7_ref, f32[2,6,8,8,128]{4,3,2,1,0:T(8,128)S(1)} %get-tuple-element.140.refs_1_, f32[3,8,8,128]{3,2,1,0:T(8,128)S(1)} %get-tuple-element.120.refs_2_.refs_8_, ...), custom_call_target="tpu_custom_call" | custom-call | flops 2000000000 | bytes 1024 | tf_op jit(solution)/shard_map/between/pallas_call | solution.py:497
  39.3 1.0 %second.4 = (f32[2,6,8,8,128]{4,3,2,1,0:T(8,128)S(1)}, f32[2,2,7,8,128]{4,3,2,1,0:T(8,128)S(1)}, f32[2,6,8,8,128]{4,3,2,1,0:T(8,128)S(1)}, f32[2,2,7,8,128]{4,3,...) custom-call(f32[2,7,8,128]{3,2,1,0:T(8,128)S(1)} %get-tuple-element.144.m0_ref, ...), custom_call_target="tpu_custom_call" | custom-call | flops 3000000000 | bytes 1024 | tf_op jit(solution)/shard_map/second/pallas_call | solution.py:497
  40.6 1.8 %collective-permute-start.11 = (f32[14,8,128]{2,1,0:T(8,128)S(1)}, f32[14,8,128]{2,1,0:T(8,128)S(1)}, u32[]{:S(2)}, u32[]{:S(2)}) collective-permute-start(f32[14,8,128]{2,1,0:T(8,128)S(1)} %get-tuple-element.152.refs_0_), channel_id=1, source_target_pairs={{0,1},{1,0},{2,3},{3,2},{4,5},{5,4},{6,7},{7,6},{8,9},{9,8},{10,11... | collective-permute-start | bytes 172040 | tf_op jit(solution)/shard_map/ppermute | solution.py:517
  42.4 1.1 %collective-permute-done.8.refs_1_ = f32[14,8,128]{2,1,0:T(8,128)S(1)} collective-permute-done((f32[14,8,128]{2,1,0:T(8,128)S(1)}, f32[14,8,128]{2,1,0:T(8,128)S(1)}, u32[]{:S(2)}, u32[]{:S(2)}) %collective-permute-start.8) | collective-permute-done | bytes 57376 | tf_op jit(solution)/shard_map/ppermute | solution.py:517
  43.5 2.7 %collective-permute-start.9 = (f32[14,8,128]{2,1,0:T(8,128)S(1)}, f32[14,8,128]{2,1,0:T(8,128)S(1)}, u32[]{:S(2)}, u32[]{:S(2)}) collective-permute-start(f32[14,8,128]{2,1,0:T(8,128)S(1)} %get-tuple-element.149.refs_0_), channel_id=1, source_target_pairs={{0,31},{1,2},{2,1},{3,4},{4,3},{5,6},{6,5},{7,8},{8,7},{9,10},{10,... | collective-permute-start | bytes 172040 | tf_op jit(solution)/shard_map/ppermute | solution.py:516
  46.5 3.8 %collective-permute-start.14 = (f32[14,8,128]{2,1,0:T(8,128)S(1)}, f32[14,8,128]{2,1,0:T(8,128)S(1)}, u32[]{:S(2)}, u32[]{:S(2)}) collective-permute-start(f32[14,8,128]{2,1,0:T(8,128)S(1)} %get-tuple-element.171.refs_0_), channel_id=1, source_target_pairs={{0,31},{1,2},{2,1},{3,4},{4,3},{5,6},{6,5},{7,8},{8,7},{9,10},{10,... | collective-permute-start | bytes 172040 | tf_op jit(solution)/shard_map/ppermute | solution.py:516
  50.3 0.9 %between.6 = (f32[2,6,8,8,128]{4,3,2,1,0:T(8,128)S(1)}, f32[2,7,8,128]{3,2,1,0:T(8,128)S(1)}, f32[2,7,8,128]{3,2,1,0:T(8,128)S(1)}) custom-call(f32[2,7,8,128]{3,2,1,0:T(8,128)S(1)} %get-tuple-element.160.refs_0_.m7_ref, f32[2,6,8,8,128]{4,3,2,1,0:T(8,128)S(1)} %get-tuple-element.161.refs_1_, f32[3,8,8,128]{3,2,1,0:T(8,128)S(1)} %get-tuple-element.120.refs_2_.refs_8_, ...), custom_call_target="tpu_custom_call" | custom-call | flops 2000000000 | bytes 1024 | tf_op jit(solution)/shard_map/between/pallas_call | solution.py:497
  51.2 0.8 %collective-permute-done.9.refs_1_ = f32[14,8,128]{2,1,0:T(8,128)S(1)} collective-permute-done((f32[14,8,128]{2,1,0:T(8,128)S(1)}, f32[14,8,128]{2,1,0:T(8,128)S(1)}, u32[]{:S(2)}, u32[]{:S(2)}) %collective-permute-start.9) | collective-permute-done | bytes 57376 | tf_op jit(solution)/shard_map/ppermute | solution.py:516
  52.2 1.0 %second.5 = (f32[2,6,8,8,128]{4,3,2,1,0:T(8,128)S(1)}, f32[2,2,7,8,128]{4,3,2,1,0:T(8,128)S(1)}, f32[2,6,8,8,128]{4,3,2,1,0:T(8,128)S(1)}, f32[2,2,7,8,128]{4,3,...) custom-call(f32[2,7,8,128]{3,2,1,0:T(8,128)S(1)} %get-tuple-element.165.m0_ref, ...), custom_call_target="tpu_custom_call" | custom-call | flops 3000000000 | bytes 1024 | tf_op jit(solution)/shard_map/second/pallas_call | solution.py:497
  53.2 1.8 %collective-permute-done.14.refs_1_ = f32[14,8,128]{2,1,0:T(8,128)S(1)} collective-permute-done((f32[14,8,128]{2,1,0:T(8,128)S(1)}, f32[14,8,128]{2,1,0:T(8,128)S(1)}, u32[]{:S(2)}, u32[]{:S(2)}) %collective-permute-start.14) | collective-permute-done | bytes 57376 | tf_op jit(solution)/shard_map/ppermute | solution.py:516
  55.4 1.1 %collective-permute-done.12.refs_1_ = f32[14,8,128]{2,1,0:T(8,128)S(1)} collective-permute-done((f32[14,8,128]{2,1,0:T(8,128)S(1)}, f32[14,8,128]{2,1,0:T(8,128)S(1)}, u32[]{:S(2)}, u32[]{:S(2)}) %collective-permute-start.12) | collective-permute-done | bytes 57376 | tf_op jit(solution)/shard_map/ppermute | solution.py:517
  56.4 2.7 %collective-permute-start.13 = (f32[14,8,128]{2,1,0:T(8,128)S(1)}, f32[14,8,128]{2,1,0:T(8,128)S(1)}, u32[]{:S(2)}, u32[]{:S(2)}) collective-permute-start(f32[14,8,128]{2,1,0:T(8,128)S(1)} %get-tuple-element.170.refs_0_), channel_id=1, source_target_pairs={{0,31},{1,2},{2,1},{3,4},{4,3},{5,6},{6,5},{7,8},{8,7},{9,10},{10,... | collective-permute-start | bytes 172040 | tf_op jit(solution)/shard_map/ppermute | solution.py:516
  59.8 3.8 %collective-permute-start.17 = (f32[14,8,128]{2,1,0:T(8,128)S(1)}, f32[14,8,128]{2,1,0:T(8,128)S(1)}, u32[]{:S(2)}, u32[]{:S(2)}) collective-permute-start(f32[14,8,128]{2,1,0:T(8,128)S(1)} %get-tuple-element.190.own_ref), channel_id=1, source_target_pairs={{0,31},{1,2},{2,1},{3,4},{4,3},{5,6},{6,5},{7,8},{8,7},{9,10},{10,... | collective-permute-start | bytes 172040 | tf_op jit(solution)/shard_map/ppermute | solution.py:516
  63.5 0.9 %between.7 = (f32[2,6,8,8,128]{4,3,2,1,0:T(8,128)S(1)}, f32[2,7,8,128]{3,2,1,0:T(8,128)S(1)}, f32[2,7,8,128]{3,2,1,0:T(8,128)S(1)}) custom-call(f32[2,7,8,128]{3,2,1,0:T(8,128)S(1)} %get-tuple-element.181.refs_0_.m7_ref, f32[2,6,8,8,128]{4,3,2,1,0:T(8,128)S(1)} %get-tuple-element.182.refs_1_, f32[3,8,8,128]{3,2,1,0:T(8,128)S(1)} %get-tuple-element.120.refs_2_.refs_8_, ...), custom_call_target="tpu_custom_call" | custom-call | flops 2000000000 | bytes 1024 | tf_op jit(solution)/shard_map/between/pallas_call | solution.py:497
  65.7 1.1 %last.1 = (f32[2,8,8,8,128]{4,3,2,1,0:T(8,128)}, f32[2,2,7,8,128]{4,3,2,1,0:T(8,128)S(1)}, f32[2,7,8,128]{3,2,1,0:T(8,128)S(1)}) custom-call(s32[1,128]{1,0:T(1,128)S(1)} %copy-done.3, f32[2,7,8,128]{3,2,1,0:T(8,128)S(1)} %get-tuple-element.186.m0_ref, f32[2,7,8,128]{3,2,1,0:T(8,128)S(1)} %get-tuple-element.181.refs_0_.m7_ref, ...), custom_call_target="tpu_custom_call" | custom-call | flops 3000000000 | bytes 1024 | tf_op jit(solution)/shard_map/last/pallas_call | solution.py:497
  66.8 1.4 %collective-permute-done.17.got_ref = f32[14,8,128]{2,1,0:T(8,128)S(1)} collective-permute-done((f32[14,8,128]{2,1,0:T(8,128)S(1)}, f32[14,8,128]{2,1,0:T(8,128)S(1)}, u32[]{:S(2)}, u32[]{:S(2)}) %collective-permute-start.17) | collective-permute-done | bytes 57376 | tf_op jit(solution)/shard_map/ppermute | solution.py:516
  68.4 0.8 %collective-permute-done.16.got_ref = f32[14,8,128]{2,1,0:T(8,128)S(1)} collective-permute-done((f32[14,8,128]{2,1,0:T(8,128)S(1)}, f32[14,8,128]{2,1,0:T(8,128)S(1)}, u32[]{:S(2)}, u32[]{:S(2)}) %collective-permute-start.16) | collective-permute-done | bytes 57376 | tf_op jit(solution)/shard_map/ppermute | solution.py:517
  69.2 0.8 %finish.3 = f32[2,8,8,8,128]{4,3,2,1,0:T(8,128)} custom-call(s32[1,128]{1,0:T(1,128)S(1)} %copy-done.3, f32[14,8,128]{2,1,0:T(8,128)S(1)} %get-tuple-element.184.own_ref, f32[14,8,128]{2,1,0:T(8,128)S(1)} %collective-permute-done.16.got_ref, f32[2,7,8,128]{3,2,1,0:T(8,128)S(1)} %get-tuple-element.185.e_ref, ...), custom_call_target="tpu_custom_call", output_to_operand_aliasing={{}: (6, {})} | custom-call | flops 1000000 | bytes 1024 | tf_op jit(solution)/shard_map/finish/pallas_call | solution.py:497
  (49 shorter events, 8.1 us)
Async XLA Ops:
  0.0 7.9 %copy-start = (f32[2,512,128]{2,1,0:T(8,128)S(1)}, f32[2,512,128]{2,1,0:T(8,128)}, u32[]{:S(2)}) copy-start(f32[2,512,128]{2,1,0:T(8,128)} %param.5) | copy-start | bytes 1572868
  0.0 7.9 %copy-start.2 = (f32[512,128]{1,0:T(8,128)S(1)}, f32[512,128]{1,0:T(8,128)}, u32[]{:S(2)}) copy-start(f32[512,128]{1,0:T(8,128)} %param.7) | copy-start | bytes 786436
  1.2 12.9 %collective-permute-start.2 = (f32[21,8,128]{2,1,0:T(8,128)S(1)}, f32[21,8,128]{2,1,0:T(8,128)S(1)}, u32[]{:S(2)}, u32[]{:S(2)}) collective-permute-start(f32[21,8,128]{2,1,0:T(8,128)S(1)} %bitcast.13), channel_id=1, source_target_pairs={{0,31},{1,2},{2,1},{3,4},{4,3},{5,6},{6,5},{7,8},{8,7},{9,10},{10,... | collective-permute-start | bytes 258056 | tf_op jit(solution)/shard_map/ppermute | solution.py:516
  7.9 1.1 %copy-start.1 = (f32[3,512,128]{2,1,0:T(8,128)S(1)}, f32[3,512,128]{2,1,0:T(8,128)}, u32[]{:S(2)}) copy-start(f32[3,512,128]{2,1,0:T(8,128)} %param.6) | copy-start | bytes 2359300
  9.4 6.9 %collective-permute-start = (f32[45,8,128]{2,1,0:T(8,128)S(1)}, f32[45,8,128]{2,1,0:T(8,128)S(1)}, u32[]{:S(2)}, u32[]{:S(2)}) collective-permute-start(f32[45,8,128]{2,1,0:T(8,128)S(1)} %project.3.own_ref.refs_8_), channel_id=1, source_target_pairs={{0,1},{1,0},{2,3},{3,2},{4,5},{5,4},{6,7},{7,6},{8,9},{9,8},{10,11... | collective-permute-start | bytes 552968 | tf_op jit(solution)/shard_map/ppermute | solution.py:517
  12.7 0.7 copy-start.4
  14.1 4.3 %collective-permute-start.4 = (f32[14,8,128]{2,1,0:T(8,128)S(1)}, f32[14,8,128]{2,1,0:T(8,128)S(1)}, u32[]{:S(2)}, u32[]{:S(2)}) collective-permute-start(f32[14,8,128]{2,1,0:T(8,128)S(1)} %get-tuple-element.116.refs_0_), channel_id=1, source_target_pairs={{0,1},{1,0},{2,3},{3,2},{4,5},{5,4},{6,7},{7,6},{8,9},{9,8},{10,11... | collective-permute-start | bytes 172040 | tf_op jit(solution)/shard_map/ppermute | solution.py:517
  16.3 9.8 %collective-permute-start.1 = (f32[38,8,128]{2,1,0:T(8,128)S(1)}, f32[38,8,128]{2,1,0:T(8,128)S(1)}, u32[]{:S(2)}, u32[]{:S(2)}) collective-permute-start(f32[38,8,128]{2,1,0:T(8,128)S(1)} %get-tuple-element.103.refs_0_), channel_id=1, source_target_pairs={{0,31},{1,2},{2,1},{3,4},{4,3},{5,6},{6,5},{7,8},{8,7},{9,10},{10,... | collective-permute-start | bytes 466952 | tf_op jit(solution)/shard_map/ppermute | solution.py:516
  18.4 9.0 %collective-permute-start.6 = (f32[14,8,128]{2,1,0:T(8,128)S(1)}, f32[14,8,128]{2,1,0:T(8,128)S(1)}, u32[]{:S(2)}, u32[]{:S(2)}) collective-permute-start(f32[14,8,128]{2,1,0:T(8,128)S(1)} %get-tuple-element.129.refs_0_), channel_id=1, source_target_pairs={{0,31},{1,2},{2,1},{3,4},{4,3},{5,6},{6,5},{7,8},{8,7},{9,10},{10,... | collective-permute-start | bytes 172040 | tf_op jit(solution)/shard_map/ppermute | solution.py:516
  26.4 4.3 %collective-permute-start.3 = (f32[14,8,128]{2,1,0:T(8,128)S(1)}, f32[14,8,128]{2,1,0:T(8,128)S(1)}, u32[]{:S(2)}, u32[]{:S(2)}) collective-permute-start(f32[14,8,128]{2,1,0:T(8,128)S(1)} %get-tuple-element.115.refs_0_), channel_id=1, source_target_pairs={{0,1},{1,0},{2,3},{3,2},{4,5},{5,4},{6,7},{7,6},{8,9},{9,8},{10,11... | collective-permute-start | bytes 172040 | tf_op jit(solution)/shard_map/ppermute | solution.py:517
  27.5 4.6 %collective-permute-start.7 = (f32[14,8,128]{2,1,0:T(8,128)S(1)}, f32[14,8,128]{2,1,0:T(8,128)S(1)}, u32[]{:S(2)}, u32[]{:S(2)}) collective-permute-start(f32[14,8,128]{2,1,0:T(8,128)S(1)} %get-tuple-element.131.refs_0_), channel_id=1, source_target_pairs={{0,1},{1,0},{2,3},{3,2},{4,5},{5,4},{6,7},{7,6},{8,9},{9,8},{10,11... | collective-permute-start | bytes 172040 | tf_op jit(solution)/shard_map/ppermute | solution.py:517
  30.7 8.5 %collective-permute-start.5 = (f32[14,8,128]{2,1,0:T(8,128)S(1)}, f32[14,8,128]{2,1,0:T(8,128)S(1)}, u32[]{:S(2)}, u32[]{:S(2)}) collective-permute-start(f32[14,8,128]{2,1,0:T(8,128)S(1)} %get-tuple-element.128.refs_0_), channel_id=1, source_target_pairs={{0,31},{1,2},{2,1},{3,4},{4,3},{5,6},{6,5},{7,8},{8,7},{9,10},{10,... | collective-permute-start | bytes 172040 | tf_op jit(solution)/shard_map/ppermute | solution.py:516
  32.1 8.5 %collective-permute-start.10 = (f32[14,8,128]{2,1,0:T(8,128)S(1)}, f32[14,8,128]{2,1,0:T(8,128)S(1)}, u32[]{:S(2)}, u32[]{:S(2)}) collective-permute-start(f32[14,8,128]{2,1,0:T(8,128)S(1)} %get-tuple-element.150.refs_0_), channel_id=1, source_target_pairs={{0,31},{1,2},{2,1},{3,4},{4,3},{5,6},{6,5},{7,8},{8,7},{9,10},{10,... | collective-permute-start | bytes 172040 | tf_op jit(solution)/shard_map/ppermute | solution.py:516
  39.2 4.3 %collective-permute-start.8 = (f32[14,8,128]{2,1,0:T(8,128)S(1)}, f32[14,8,128]{2,1,0:T(8,128)S(1)}, u32[]{:S(2)}, u32[]{:S(2)}) collective-permute-start(f32[14,8,128]{2,1,0:T(8,128)S(1)} %get-tuple-element.142.refs_0_), channel_id=1, source_target_pairs={{0,1},{1,0},{2,3},{3,2},{4,5},{5,4},{6,7},{7,6},{8,9},{9,8},{10,11... | collective-permute-start | bytes 172040 | tf_op jit(solution)/shard_map/ppermute | solution.py:517
  40.6 5.9 %collective-permute-start.11 = (f32[14,8,128]{2,1,0:T(8,128)S(1)}, f32[14,8,128]{2,1,0:T(8,128)S(1)}, u32[]{:S(2)}, u32[]{:S(2)}) collective-permute-start(f32[14,8,128]{2,1,0:T(8,128)S(1)} %get-tuple-element.152.refs_0_), channel_id=1, source_target_pairs={{0,1},{1,0},{2,3},{3,2},{4,5},{5,4},{6,7},{7,6},{8,9},{9,8},{10,11... | collective-permute-start | bytes 172040 | tf_op jit(solution)/shard_map/ppermute | solution.py:517
  43.5 8.5 %collective-permute-start.9 = (f32[14,8,128]{2,1,0:T(8,128)S(1)}, f32[14,8,128]{2,1,0:T(8,128)S(1)}, u32[]{:S(2)}, u32[]{:S(2)}) collective-permute-start(f32[14,8,128]{2,1,0:T(8,128)S(1)} %get-tuple-element.149.refs_0_), channel_id=1, source_target_pairs={{0,31},{1,2},{2,1},{3,4},{4,3},{5,6},{6,5},{7,8},{8,7},{9,10},{10,... | collective-permute-start | bytes 172040 | tf_op jit(solution)/shard_map/ppermute | solution.py:516
  46.5 8.5 %collective-permute-start.14 = (f32[14,8,128]{2,1,0:T(8,128)S(1)}, f32[14,8,128]{2,1,0:T(8,128)S(1)}, u32[]{:S(2)}, u32[]{:S(2)}) collective-permute-start(f32[14,8,128]{2,1,0:T(8,128)S(1)} %get-tuple-element.171.refs_0_), channel_id=1, source_target_pairs={{0,31},{1,2},{2,1},{3,4},{4,3},{5,6},{6,5},{7,8},{8,7},{9,10},{10,... | collective-permute-start | bytes 172040 | tf_op jit(solution)/shard_map/ppermute | solution.py:516
  52.0 4.4 %collective-permute-start.12 = (f32[14,8,128]{2,1,0:T(8,128)S(1)}, f32[14,8,128]{2,1,0:T(8,128)S(1)}, u32[]{:S(2)}, u32[]{:S(2)}) collective-permute-start(f32[14,8,128]{2,1,0:T(8,128)S(1)} %get-tuple-element.163.refs_0_), channel_id=1, source_target_pairs={{0,1},{1,0},{2,3},{3,2},{4,5},{5,4},{6,7},{7,6},{8,9},{9,8},{10,11... | collective-permute-start | bytes 172040 | tf_op jit(solution)/shard_map/ppermute | solution.py:517
  55.0 4.7 %collective-permute-start.15 = (f32[14,8,128]{2,1,0:T(8,128)S(1)}, f32[14,8,128]{2,1,0:T(8,128)S(1)}, u32[]{:S(2)}, u32[]{:S(2)}) collective-permute-start(f32[14,8,128]{2,1,0:T(8,128)S(1)} %get-tuple-element.173.refs_0_), channel_id=1, source_target_pairs={{0,1},{1,0},{2,3},{3,2},{4,5},{5,4},{6,7},{7,6},{8,9},{9,8},{10,11... | collective-permute-start | bytes 172040 | tf_op jit(solution)/shard_map/ppermute | solution.py:517
  56.4 8.5 %collective-permute-start.13 = (f32[14,8,128]{2,1,0:T(8,128)S(1)}, f32[14,8,128]{2,1,0:T(8,128)S(1)}, u32[]{:S(2)}, u32[]{:S(2)}) collective-permute-start(f32[14,8,128]{2,1,0:T(8,128)S(1)} %get-tuple-element.170.refs_0_), channel_id=1, source_target_pairs={{0,31},{1,2},{2,1},{3,4},{4,3},{5,6},{6,5},{7,8},{8,7},{9,10},{10,... | collective-permute-start | bytes 172040 | tf_op jit(solution)/shard_map/ppermute | solution.py:516
  59.8 8.5 %collective-permute-start.17 = (f32[14,8,128]{2,1,0:T(8,128)S(1)}, f32[14,8,128]{2,1,0:T(8,128)S(1)}, u32[]{:S(2)}, u32[]{:S(2)}) collective-permute-start(f32[14,8,128]{2,1,0:T(8,128)S(1)} %get-tuple-element.190.own_ref), channel_id=1, source_target_pairs={{0,31},{1,2},{2,1},{3,4},{4,3},{5,6},{6,5},{7,8},{8,7},{9,10},{10,... | collective-permute-start | bytes 172040 | tf_op jit(solution)/shard_map/ppermute | solution.py:516
  64.9 4.3 %collective-permute-start.16 = (f32[14,8,128]{2,1,0:T(8,128)S(1)}, f32[14,8,128]{2,1,0:T(8,128)S(1)}, u32[]{:S(2)}, u32[]{:S(2)}) collective-permute-start(f32[14,8,128]{2,1,0:T(8,128)S(1)} %get-tuple-element.184.own_ref), channel_id=1, source_target_pairs={{0,1},{1,0},{2,3},{3,2},{4,5},{5,4},{6,7},{7,6},{8,9},{9,8},{10,11... | collective-permute-start | bytes 172040 | tf_op jit(solution)/shard_map/ppermute | solution.py:517
  65.0 0.7 copy-start.3

commit v4 on v3

--- a/solution.py
+++ b/solution.py
@@ -55,7 +55,6 @@
 DM = gll_derivative(ORDER)
 SUM_PART = [[(DM[j, a] + DM[j, 7 - a]) / 2 for a in range(4)] for j in range(4)]
 DIF_PART = [[(DM[j, a] - DM[j, 7 - a]) / 2 for a in range(4)] for j in range(4)]
-ROT = np.array([[DM[k, (k - r) % 8] for k in range(8)] for r in range(8)], np.float32)
 
 
 def combine(coefs, items):
@@ -147,23 +146,32 @@
     return [plane_sum(plane, tables, ROWS) for plane in planes + [weight]]
 
 
-def project_odd(order_ref, scal_ref, mass_ref, od_ref, idx_ref, order_buf, scal_buf, mass_buf, sems):
-    src = source_plane(lax.axis_index("elem") % 2, 0)
+def project_odd(order_ref, scal_ref, mass_ref, tr_ref, od_ref, idx_ref, slot_ref, far_ref,
+                order_buf, near_buf, sems):
+    parity = lax.axis_index("elem") % 2
+    near, far = source_plane(parity, 0), source_plane(parity, ORDER)
     copies = [pltpu.make_async_copy(order_ref, order_buf, sems.at[0])]
-    copies.append(pltpu.make_async_copy(mass_ref.at[src], mass_buf, sems.at[1]))
-    for m in range(2):
-        copies.append(pltpu.make_async_copy(scal_ref.at[m, src], scal_buf.at[m], sems.at[2 + m]))
-    for copy in copies:
+    for r, source in enumerate((scal_ref.at[0, near], scal_ref.at[1, near], mass_ref.at[near])):
+        copies.append(pltpu.make_async_copy(source, near_buf.at[r], sems.at[1 + r]))
+    late = []
+    sources = [scal_ref.at[0, far], scal_ref.at[1, far], mass_ref.at[far]]
+    sources += [tr_ref.at[r, far] for r in range(3)]
+    for r, source in enumerate(sources):
+        late.append(pltpu.make_async_copy(source, far_ref.at[r], sems.at[4 + r]))
+    for copy in copies + late:
         copy.start()
     tables = third_tables()
     copies[0].wait()
     idx = brick_index(order_buf)
     idx_ref[...] = idx
+    slot_ref[...] = jnp.broadcast_to(order_buf[...], (SUB, LANES))
     for copy in copies[1:]:
         copy.wait()
-    planes = project(read(mass_buf), [read(scal_buf, m) for m in range(2)], idx, tables)
+    planes = project(read(near_buf, 2), [read(near_buf, m) for m in range(2)], idx, tables)
     for r in range(3):
         write(od_ref, (r,), planes[r])
+    for copy in late:
+        copy.wait()
 
 
 def signs_of(parity):
@@ -171,14 +179,12 @@
     return first, np.float32(-time_step), np.float32(-time_step)
 
 
-def project_even(idx_ref, scal_ref, mass_ref, tr_ref, ev_ref):
-    parity = lax.axis_index("elem") % 2
-    src = source_plane(parity, ORDER)
+def project_even(idx_ref, far_ref, ev_ref):
     idx = idx_ref[...]
-    signs = signs_of(parity)
-    planes = project(
-        read(mass_ref, src), [read(scal_ref, m, src) for m in range(2)], idx, third_tables())
-    planes.extend([gather_lanes(v, idx) * signs[r] for v in read(tr_ref, r, src)] for r in range(3))
+    signs = signs_of(lax.axis_index("elem") % 2)
+    planes = project(read(far_ref, 2), [read(far_ref, m) for m in range(2)], idx, third_tables())
+    planes.extend(
+        [gather_lanes(v, idx) * signs[r] for v in read(far_ref, 3 + r)] for r in range(3))
     write(ev_ref, (), sum(planes, []))
 
 
@@ -188,31 +194,44 @@
     idx = idx_ref[...]
     tables = third_tables()
     signs = signs_of(parity)
+
+    def load(i):
+        src = source_plane(parity, i)
+        planes = [read(scal_ref, m, src) for m in range(2)] + [read(mass_ref, src)]
+        return planes + [read(tr_ref, r, src) for r in range(3)]
+
+    near, far = source_plane(parity, 0), source_plane(parity, ORDER)
+    faces = [read(tr_ref, r, near) for r in range(3)] + [read(tr_ref, 0, far)]
+    faces = [
+        [gather_lanes(v, idx) * signs[r] for v in plane] for r, plane in zip((0, 1, 2, 0), faces)
+    ]
+    assembled = [plane_sum(faces[0], tables, ROWS), plane_sum(faces[3], tables, ROWS)]
+    ahead = load(1)
+    for r in range(3):
+        write(tf_ref, (r,), faces[r])
     for face in range(2):
-        src = source_plane(parity, face * ORDER)
-        first = [gather_lanes(v, idx) * signs[0] for v in read(tr_ref, 0, src)]
-        write(st_ref, (face,), plane_sum(first, tables, ROWS))
-        if face == 0:
-            write(tf_ref, (0,), first)
-            for r in (1, 2):
-                write(tf_ref, (r,), [gather_lanes(v, idx) * signs[r] for v in read(tr_ref, r, src)])
+        write(st_ref, (face,), assembled[face])
     sums = [[None, None], [None, None]]
     for i in range(6):
-        src = source_plane(parity, i + 1)
-        for r in (1, 2):
-            write(ti_ref, (i, r - 1), [gather_lanes(v, idx) * signs[r] for v in read(tr_ref, r, src)])
-        first = plane_sum([gather_lanes(v, idx) * signs[0] for v in read(tr_ref, 0, src)], tables)
-        weight = [gather_lanes(v, idx) for v in read(mass_ref, src)]
+        raw = [[gather_lanes(v, idx) for v in plane] for plane in ahead]
+        weight = raw[2]
+        first = plane_sum([v * signs[0] for v in raw[3]], tables)
         inverse = [1.0 / v for v in plane_sum(weight, tables)]
+        rest = [[v * signs[r] for v in raw[3 + r]] for r in (1, 2)]
+        planes = []
+        for m in range(2):
+            plane = plane_sum([raw[m][j] * weight[j] for j in range(8)], tables)
+            planes.append([plane[j] * inverse[j] for j in range(8)])
+        if i < 5:
+            ahead = load(i + 2)
+        for r in range(2):
+            write(ti_ref, (i, r), rest[r])
         write(ri_ref, (i,), inverse)
         write(rt_ref, (i,), [first[j] * inverse[j] for j in range(8)])
         for m in range(2):
-            scal = read(scal_ref, m, src)
-            plane = plane_sum([gather_lanes(scal[j], idx) * weight[j] for j in range(8)], tables)
-            plane = [plane[j] * inverse[j] for j in range(8)]
-            write(gi_ref, (m, i), plane)
+            write(gi_ref, (m, i), planes[m])
             for face in range(2):
-                terms = [v * np.float32(DM[face * ORDER, i + 1]) for v in plane[:ROWS]]
+                terms = [v * np.float32(DM[face * ORDER, i + 1]) for v in planes[m][:ROWS]]
                 old = sums[face][m]
                 sums[face][m] = [x + y for x, y in zip(old, terms)] if old else terms
     for face in range(2):
@@ -220,8 +239,15 @@
             write(q_ref, (face, m), sums[face][m])
 
 
-def rotations(rot_ref):
-    return [rot_ref[r] for r in range(8)]
+def rotations():
+    k = lax.broadcasted_iota(jnp.int32, (SUB, LANES), 0)
+    out = []
+    for r in range(8):
+        value = jnp.full((SUB, LANES), np.float32(DM[7, (7 - r) % 8]))
+        for row in range(7):
+            value = jnp.where(k == row, np.float32(DM[row, (row - r) % 8]), value)
+        out.append(value)
+    return out
 
 
 def in_plane(plane, second_t, third_t, rot):
@@ -322,10 +348,10 @@
     def stage_face(*refs):
         own_ref, got_ref, e_ref, acc_ref, q_ref, rt_ref, rf_ref = refs[:7]
         if early:
-            tf_ref, rot_ref, p_ref, send_ref, a_ref, e_buf = refs[7:]
+            tf_ref, p_ref, send_ref, a_ref, e_buf = refs[7:]
             tables = third_tables()
             both_sides([read(tf_ref, r) for r in range(3)], transports(got_ref, 2 * ROWS), tables, a_ref)
-            own_terms(e_ref, a_ref, rf_ref, face, rotations(rot_ref), tables, e_buf)
+            own_terms(e_ref, a_ref, rf_ref, face, rotations(), tables, e_buf)
             e_ref = e_buf
         else:
             p_ref, send_ref = refs[7:]
@@ -351,18 +377,18 @@
 
 def make_first_inner(scale, opening, start):
     def first_inner(*refs):
-        p0_ref, p7_ref, gi_ref, acci_ref, wp_ref, rt_ref, r7_ref, rot_ref = refs[:8]
+        p0_ref, p7_ref, gi_ref, acci_ref, wp_ref, rt_ref, r7_ref = refs[:7]
         tables = third_tables()
         if start:
-            ev_ref, rev_ref, st_ref, r0_ref = refs[8:12]
-            gn_ref, an_ref, q_ref, e7_ref, a7_ref, rs_ref = refs[12:]
+            ev_ref, rev_ref, st_ref, r0_ref = refs[7:11]
+            gn_ref, an_ref, q_ref, e7_ref, a7_ref, rs_ref = refs[11:]
             both_sides(transports(ev_ref, 3 * ROWS), transports(rev_ref, 3 * ROWS), tables, a7_ref)
             write(rs_ref, (0,), [st_ref[0, j] * r0_ref[j] for j in range(ROWS)])
             write(rs_ref, (1,), [st_ref[1, j] * r7_ref[j] for j in range(ROWS)])
         else:
-            a7_ref = refs[8]
-            gn_ref, an_ref, q_ref, e7_ref = refs[9:]
-        own_terms(p7_ref, a7_ref, r7_ref, 1, rotations(rot_ref), tables, e7_ref)
+            a7_ref = refs[7]
+            gn_ref, an_ref, q_ref, e7_ref = refs[8:]
+        own_terms(p7_ref, a7_ref, r7_ref, 1, rotations(), tables, e7_ref)
 
         def put(m, i, value):
             base = gi_ref if opening else acci_ref
@@ -377,13 +403,13 @@
 
 def make_between(early):
     def between(*refs):
-        m7_ref, gi_ref, a7_ref, r7_ref, ri_ref, rt_ref, ti_ref, rot_ref = refs[:8]
-        rot = rotations(rot_ref)
+        m7_ref, gi_ref, a7_ref, r7_ref, ri_ref, rt_ref, ti_ref = refs[:7]
+        rot = rotations()
         tables = third_tables()
         if early:
-            wp_ref, e7_ref = refs[8:]
+            wp_ref, e7_ref = refs[7:]
         else:
-            p0_ref, a0_ref, r0_ref, wp_ref, e7_ref, e0_ref = refs[8:]
+            p0_ref, a0_ref, r0_ref, wp_ref, e7_ref, e0_ref = refs[7:]
             own_terms(p0_ref, a0_ref, r0_ref, 0, rot, tables, e0_ref)
         own_terms(m7_ref, a7_ref, r7_ref, 1, rot, tables, e7_ref)
         inner_open(gi_ref, ri_ref, rt_ref, ti_ref, rot, wp_ref)
@@ -401,8 +427,8 @@
 
 def make_second_inner(scale, opening, closing):
     def second_inner(m0_ref, m7_ref, p0_ref, p7_ref, accf_ref, acci_ref, wp_ref, ri_ref, rt_ref,
-                     ti_ref, a0_ref, r0_ref, rot_ref, gn_ref, q_ref, an_ref, afn_ref, wn_ref, e0_ref):
-        rot = rotations(rot_ref)
+                     ti_ref, a0_ref, r0_ref, gn_ref, q_ref, an_ref, afn_ref, wn_ref, e0_ref):
+        rot = rotations()
 
         def put(m, i, value):
             total = [acci_ref[m, i, j] + value[j] for j in range(8)]
@@ -421,10 +447,10 @@
 
 
 def make_last_inner(scale):
-    def last_inner(order_ref, m0_ref, m7_ref, p0_ref, p7_ref, accf_ref, acci_ref, wp_ref, rt_ref,
-                   a0_ref, r0_ref, rot_ref, out_ref, afn_ref, e0_ref, buf, sems):
+    def last_inner(slot_ref, m0_ref, m7_ref, p0_ref, p7_ref, accf_ref, acci_ref, wp_ref, rt_ref,
+                   a0_ref, r0_ref, out_ref, afn_ref, e0_ref, buf, sems):
         parity = lax.axis_index("elem") % 2
-        idx = jnp.broadcast_to(order_ref[...], (SUB, LANES))
+        idx = slot_ref[...]
 
         def put(m, i, value):
             total = [acci_ref[m, i, j] + value[j] for j in range(8)]
@@ -439,7 +465,7 @@
         ]
         for copy in copies:
             copy.start()
-        own_terms(m0_ref, a0_ref, r0_ref, 0, rotations(rot_ref), third_tables(), e0_ref)
+        own_terms(m0_ref, a0_ref, r0_ref, 0, rotations(), third_tables(), e0_ref)
         face_totals((m0_ref, m7_ref), (p0_ref, p7_ref), accf_ref, afn_ref, False)
         for copy in copies:
             copy.wait()
@@ -447,8 +473,8 @@
     return last_inner
 
 
-def final_face(face, scale, order_ref, own_ref, got_ref, e_ref, accf_ref, m):
-    idx = jnp.broadcast_to(order_ref[...], (SUB, LANES))
+def final_face(face, scale, slot_ref, own_ref, got_ref, e_ref, accf_ref, m):
+    idx = slot_ref[...]
     rows = [
         (own_ref[ROWS * m + j] + got_ref[ROWS * m + j] + e_ref[m, j]) * np.float32(scale)
         + accf_ref[face, m, j]
@@ -458,15 +484,15 @@
 
 
 def make_finish_near(face, scale):
-    def finish_near(order_ref, own_ref, got_ref, e_ref, accf_ref, face_ref):
-        for m in range(2):
-            write(face_ref, (m,), final_face(face, scale, order_ref, own_ref, got_ref, e_ref, accf_ref, m))
+    def finish_near(slot_ref, own_ref, got_ref, e_ref, accf_ref, face_ref):
+        for m in range(2):
+            write(face_ref, (m,), final_face(face, scale, slot_ref, own_ref, got_ref, e_ref, accf_ref, m))
 
     return finish_near
 
 
 def make_finish_far(face, scale):
-    def finish_far(order_ref, own_ref, got_ref, e_ref, accf_ref, near_ref, part_ref,
+    def finish_far(slot_ref, own_ref, got_ref, e_ref, accf_ref, near_ref, part_ref,
                    out_ref, buf, sems):
         dst = source_plane(lax.axis_index("elem") % 2, face * ORDER)
         copies = []
@@ -476,7 +502,7 @@
             )
             copies[-1].start()
         for m in range(2):
-            write(buf, (m,), final_face(face, scale, order_ref, own_ref, got_ref, e_ref, accf_ref, m))
+            write(buf, (m,), final_face(face, scale, slot_ref, own_ref, got_ref, e_ref, accf_ref, m))
             copies.append(pltpu.make_async_copy(buf.at[m], out_ref.at[m, dst], sems.at[0, m]))
             copies[-1].start()
         for copy in copies:
@@ -515,7 +541,6 @@
     odd_pairs = [(i, (i + 1) % count if i % 2 else (i - 1) % count) for i in range(count)]
     swap_od = lambda x: lax.ppermute(x, "elem", odd_pairs)
     swap_ev = lambda x: lax.ppermute(x, "elem", even_pairs)
-    rot = jnp.asarray(np.broadcast_to(ROT[:, :, None], (8, SUB, LANES)))
     members = scalars.shape[0]
     grid = (EXT, EXT, SUB, LANES)
     scal = scalars.reshape((members,) + grid)
@@ -527,25 +552,24 @@
     f32 = jnp.float32
 
     stay = lambda x: pltpu.with_memory_space_constraint(x, pltpu.HBM)
-    od, idx = call(
-        project_odd, [(3,) + part, (SUB, LANES)], (stay(element_order), stay(scal), stay(mas)), "project", 1,
-        hbm=(0, 1, 2),
-        scratch=[pltpu.VMEM((1, LANES), jnp.int32), pltpu.VMEM((2,) + tile, f32),
-                 pltpu.VMEM(tile, f32), pltpu.SemaphoreType.DMA((4,))])
+    od, idx, slots, far = call(
+        project_odd, [(3,) + part, (SUB, LANES), (SUB, LANES), (6,) + tile],
+        (stay(element_order), stay(scal), stay(mas), stay(tr)), "project", 1, hbm=(0, 1, 2, 3),
+        scratch=[pltpu.VMEM((1, LANES), jnp.int32), pltpu.VMEM((3,) + tile, f32),
+                 pltpu.SemaphoreType.DMA((10,))])
     od = od.reshape(3 * ROWS, SUB, LANES)
     rod = swap_od(od)
-    ev = call(
-        project_even, [(3 * ROWS + 24, SUB, LANES)], (idx, scal, mas, tr), "project", 1)
+    ev = call(project_even, [(3 * ROWS + 24, SUB, LANES)], (idx, far), "project", 1)
     rev = swap_ev(ev)
     gi, q, ri, rt, ti, tf, st = call(
         prepare,
         [inner, faces, (6,) + tile, (6,) + tile, (6, 2) + tile, geometry, (2,) + part],
         (idx, scal, mas, tr), "prepare", 1)
 
-    def opening_terms(gi_ref, ri_ref, rt_ref, ti_ref, rot_ref, wp_ref):
-        inner_open(gi_ref, ri_ref, rt_ref, ti_ref, rotations(rot_ref), wp_ref)
-
-    wp = call(opening_terms, [inner], (gi, ri, rt, ti, rot), "terms", 1)
+    def opening_terms(gi_ref, ri_ref, rt_ref, ti_ref, wp_ref):
+        inner_open(gi_ref, ri_ref, rt_ref, ti_ref, rotations(), wp_ref)
+
+    wp = call(opening_terms, [inner], (gi, ri, rt, ti), "terms", 1)
     p0, r0, cev = call(
         make_field_face(0, False), [face, part, sent], (od, rod, q, st), "odd", 3000)
     p7, r7, cod = call(
@@ -561,7 +585,7 @@
         res = call(
             make_first_inner(1.0 / s, opening, early),
             [inner, inner, faces, face] + ([geometry, (2,) + part] if early else []),
-            (p0, p7, gi, acci, wp, rt, r7, rot) + extra, "first", 1000)
+            (p0, p7, gi, acci, wp, rt, r7) + extra, "first", 1000)
         gm, acci, q, e7 = res[:4]
         if early:
             a7, rs = res[4:]
@@ -571,12 +595,12 @@
         got_od2 = swap_od(cod2)
         res = call(
             make_between(early), [inner, face] + ([] if early else [face]),
-            (m7, gm, a7, r7, ri, rt, ti, rot) + (() if early else (p0, a0, r0)), "between", 2000)
+            (m7, gm, a7, r7, ri, rt, ti) + (() if early else (p0, a0, r0)), "between", 2000)
         wp, e7 = res[:2]
         if early:
             m0, cev2, a0 = call(
                 make_stage_face(0, 1.0 / s, False, True, True), [face, sent, geometry],
-                (cod, got_od, p0, accf, q, rs, r0, tf, rot), "behind", 1,
+                (cod, got_od, p0, accf, q, rs, r0, tf), "behind", 1,
                 scratch=[pltpu.VMEM(face, f32)])
         else:
             m0, cev2 = call(
@@ -588,7 +612,7 @@
             gi, q, acci, accf, wp, e0 = call(
                 make_second_inner(scale, opening, closing),
                 [inner, faces, inner, faces, inner, face],
-                (m0, m7, p0, p7, accf, acci, wp, ri, rt, ti, a0, r0, rot), "second", 3000)
+                (m0, m7, p0, p7, accf, acci, wp, ri, rt, ti, a0, r0), "second", 3000)
             p0, cev = call(
                 make_stage_face(0, scale, closing, False, False), [face, sent],
                 (cod2, got_od2, e0, accf, q, rs, r0), "odd", 3000)
@@ -598,14 +622,14 @@
         else:
             out, accf, e0 = call(
                 make_last_inner(scale), [(members,) + grid, faces, face],
-                (element_order, m0, m7, p0, p7, accf, acci, wp, rt, a0, r0, rot), "last", 3000,
+                (slots, m0, m7, p0, p7, accf, acci, wp, rt, a0, r0), "last", 3000,
                 hbm_out=(0,), scratch=[pltpu.VMEM(inner, f32), pltpu.SemaphoreType.DMA((2,))])
             near = call(
                 make_finish_near(0, scale), [(2,) + tile],
-                (element_order, cod2, got_od2, e0, accf), "finish", 3000)
+                (slots, cod2, got_od2, e0, accf), "finish", 3000)
             out = call(
                 make_finish_far(1, scale), [(members,) + grid],
-                (element_order, cev2, got_ev2, e7, accf, near, out), "finish", 1,
+                (slots, cev2, got_ev2, e7, accf, near, out), "finish", 1,
                 hbm=(6,), hbm_out=(0,), alias={6: 0},
                 scratch=[pltpu.VMEM((2,) + tile, f32), pltpu.SemaphoreType.DMA((2, 2))])
     return out.reshape(scalars.shape)

time: 70.4 us -> 69.1 us (0.982)
  local copies, waits for them, and re-layouts: 2.55 us -> 0.01 us
  waiting for transfers between devices: 13.2 us -> 14.5 us
    unnamed x10 -> x6, local copies, waits for them, and re-layouts: 2.47 us -> 0.01 us
    ppermute x9, waiting for transfers between devices: 7.73 us -> 9.62 us  [per_device(): swap_od = lambda x: lax.ppermute(x, 'elem', odd_pairs)]
    ppermute x9, starting transfers between devices: 31.2 us -> 32 us  [per_device(): swap_od = lambda x: lax.ppermute(x, 'elem', odd_pairs)]
where the time goes in v4:
time: 69.1 us; the launch traced here: 68.9 us
  starting transfers between devices  38.3 us (55%)
  Pallas kernels  15.8 us (23%)
  waiting for transfers between devices  14.5 us (21%)
    ppermute x9, starting transfers between devices, per_device(): swap_od = lambda x: lax.ppermute(x, 'elem', odd_pairs)  32 us
    pallas_call x34, Pallas kernels, call(): pl.pallas_call(kernel, out_shape=shapes[0] if single else shapes, in_spec...  15.8 us
    ppermute x9, waiting for transfers between devices, per_device(): swap_od = lambda x: lax.ppermute(x, 'elem', odd_pairs)  9.62 us
    ppermute x9, starting transfers between devices, per_device(): swap_ev = lambda x: lax.ppermute(x, 'elem', even_pairs)  6.24 us
    ppermute x9, waiting for transfers between devices, per_device(): swap_ev = lambda x: lax.ppermute(x, 'elem', even_pairs)  4.92 us
  transfers between devices with their start and end apart: 18, of which 13 were waited for; matrix products, arithmetic and copies ran while one was open for 0% of the time, Pallas kernels for 20%

profile of v4, /device:TPU:0, one launch (start us, length us, event | category | flops | bytes accessed | tf_op | source)
XLA Modules:
  0.0 68.9 jit_solution(1244125335744324372)
XLA Ops:
  0.0 1.3 %project.2 = (f32[3,7,8,128]{3,2,1,0:T(8,128)S(1)}, s32[8,128]{1,0:T(8,128)S(1)}, s32[8,128]{1,0:T(8,128)S(1)}, f32[6,8,8,128]{3,2,1,0:T(8,128)S(1)}) custom-call(s32[1,128]{1,0:T(1,128)} %order_ref.1, f32[2,8,8,8,128]{4,3,2,1,0:T(8,128)} %bitcast.7, f32[8,8,8,128]{3,2,1,0:T(8,128)} %bitcast.9, f32[3,8,8,8,128]{4,3,2,1,0:T(8,128)} %bitcast.5), custom_call_target="tpu_custom_call" | custom-call | flops 1000000 | bytes 1024 | tf_op jit(solution)/shard_map/project/pallas_call | solution.py:523
  1.3 6.7 %collective-permute-start.2 = (f32[21,8,128]{2,1,0:T(8,128)S(1)}, f32[21,8,128]{2,1,0:T(8,128)S(1)}, u32[]{:S(2)}, u32[]{:S(2)}) collective-permute-start(f32[21,8,128]{2,1,0:T(8,128)S(1)} %bitcast.11), channel_id=1, source_target_pairs={{0,31},{1,2},{2,1},{3,4},{4,3},{5,6},{6,5},{7,8},{8,7},{9,10},{10,... | collective-permute-start | bytes 258056 | tf_op jit(solution)/shard_map/ppermute | solution.py:542
  8.4 2.8 %prepare.1 = (f32[2,6,8,8,128]{4,3,2,1,0:T(8,128)S(1)}, f32[2,2,7,8,128]{4,3,2,1,0:T(8,128)S(1)}, f32[6,8,8,128]{3,2,1,0:T(8,128)S(1)}, f32[6,8,8,128]{3,2,1,0:T...) custom-call(s32[8,128]{1,0:T(8,128)S(1)} %get-tuple-element.102.idx_ref, ...), custom_call_target="tpu_custom_call" | custom-call | flops 1000000 | bytes 1024 | tf_op jit(solution)/shard_map/prepare/pallas_call | solution.py:523
  12.0 2.1 %collective-permute-start.4 = (f32[14,8,128]{2,1,0:T(8,128)S(1)}, f32[14,8,128]{2,1,0:T(8,128)S(1)}, u32[]{:S(2)}, u32[]{:S(2)}) collective-permute-start(f32[14,8,128]{2,1,0:T(8,128)S(1)} %get-tuple-element.120.refs_0_), channel_id=1, source_target_pairs={{0,1},{1,0},{2,3},{3,2},{4,5},{5,4},{6,7},{7,6},{8,9},{9,8},{10,11... | collective-permute-start | bytes 172040 | tf_op jit(solution)/shard_map/ppermute | solution.py:543
  14.7 2.3 %collective-permute-start.1 = (f32[38,8,128]{2,1,0:T(8,128)S(1)}, f32[38,8,128]{2,1,0:T(8,128)S(1)}, u32[]{:S(2)}, u32[]{:S(2)}) collective-permute-start(f32[38,8,128]{2,1,0:T(8,128)S(1)} %get-tuple-element.107.refs_0_), channel_id=1, source_target_pairs={{0,31},{1,2},{2,1},{3,4},{4,3},{5,6},{6,5},{7,8},{8,7},{9,10},{10,... | collective-permute-start | bytes 466952 | tf_op jit(solution)/shard_map/ppermute | solution.py:542
  17.4 4.1 %collective-permute-start.6 = (f32[14,8,128]{2,1,0:T(8,128)S(1)}, f32[14,8,128]{2,1,0:T(8,128)S(1)}, u32[]{:S(2)}, u32[]{:S(2)}) collective-permute-start(f32[14,8,128]{2,1,0:T(8,128)S(1)} %get-tuple-element.133.refs_0_), channel_id=1, source_target_pairs={{0,31},{1,2},{2,1},{3,4},{4,3},{5,6},{6,5},{7,8},{8,7},{9,10},{10,... | collective-permute-start | bytes 172040 | tf_op jit(solution)/shard_map/ppermute | solution.py:542
  21.5 0.8 %between.4 = (f32[2,6,8,8,128]{4,3,2,1,0:T(8,128)S(1)}, f32[2,7,8,128]{3,2,1,0:T(8,128)S(1)}) custom-call(f32[2,7,8,128]{3,2,1,0:T(8,128)S(1)} %get-tuple-element.122.refs_0_.m7_ref, f32[2,6,8,8,128]{4,3,2,1,0:T(8,128)S(1)} %get-tuple-element.123.refs_1_, f32[3,8,8,128]{3,2,1,0:T(8,128)S(1)} %get-tuple-element.124.refs_2_.refs_7_, ...), custom_call_target="tpu_custom_call" | custom-call | flops 2000000000 | bytes 1024 | tf_op jit(solution)/shard_map/between/pallas_call | solution.py:523
  22.4 2.5 %collective-permute-done.1.refs_1_ = f32[38,8,128]{2,1,0:T(8,128)S(1)} collective-permute-done((f32[38,8,128]{2,1,0:T(8,128)S(1)}, f32[38,8,128]{2,1,0:T(8,128)S(1)}, u32[]{:S(2)}, u32[]{:S(2)}) %collective-permute-start.1) | collective-permute-done | bytes 155680 | tf_op jit(solution)/shard_map/ppermute | solution.py:542
  25.3 1.0 %second.3 = (f32[2,6,8,8,128]{4,3,2,1,0:T(8,128)S(1)}, f32[2,2,7,8,128]{4,3,2,1,0:T(8,128)S(1)}, f32[2,6,8,8,128]{4,3,2,1,0:T(8,128)S(1)}, f32[2,2,7,8,128]{4,3,...) custom-call(f32[2,7,8,128]{3,2,1,0:T(8,128)S(1)} %get-tuple-element.126.m0_ref, ...), custom_call_target="tpu_custom_call" | custom-call | flops 3000000000 | bytes 1024 | tf_op jit(solution)/shard_map/second/pallas_call | solution.py:523
  26.3 2.1 %collective-permute-start.7 = (f32[14,8,128]{2,1,0:T(8,128)S(1)}, f32[14,8,128]{2,1,0:T(8,128)S(1)}, u32[]{:S(2)}, u32[]{:S(2)}) collective-permute-start(f32[14,8,128]{2,1,0:T(8,128)S(1)} %get-tuple-element.135.refs_0_), channel_id=1, source_target_pairs={{0,1},{1,0},{2,3},{3,2},{4,5},{5,4},{6,7},{7,6},{8,9},{9,8},{10,11... | collective-permute-start | bytes 172040 | tf_op jit(solution)/shard_map/ppermute | solution.py:543
  28.4 1.1 %collective-permute-done.3.refs_1_ = f32[14,8,128]{2,1,0:T(8,128)S(1)} collective-permute-done((f32[14,8,128]{2,1,0:T(8,128)S(1)}, f32[14,8,128]{2,1,0:T(8,128)S(1)}, u32[]{:S(2)}, u32[]{:S(2)}) %collective-permute-start.3) | collective-permute-done | bytes 57376 | tf_op jit(solution)/shard_map/ppermute | solution.py:543
  29.5 1.6 %collective-permute-start.5 = (f32[14,8,128]{2,1,0:T(8,128)S(1)}, f32[14,8,128]{2,1,0:T(8,128)S(1)}, u32[]{:S(2)}, u32[]{:S(2)}) collective-permute-start(f32[14,8,128]{2,1,0:T(8,128)S(1)} %get-tuple-element.132.refs_0_), channel_id=1, source_target_pairs={{0,31},{1,2},{2,1},{3,4},{4,3},{5,6},{6,5},{7,8},{8,7},{9,10},{10,... | collective-permute-start | bytes 172040 | tf_op jit(solution)/shard_map/ppermute | solution.py:542
  31.5 4.8 %collective-permute-start.10 = (f32[14,8,128]{2,1,0:T(8,128)S(1)}, f32[14,8,128]{2,1,0:T(8,128)S(1)}, u32[]{:S(2)}, u32[]{:S(2)}) collective-permute-start(f32[14,8,128]{2,1,0:T(8,128)S(1)} %get-tuple-element.154.refs_0_), channel_id=1, source_target_pairs={{0,31},{1,2},{2,1},{3,4},{4,3},{5,6},{6,5},{7,8},{8,7},{9,10},{10,... | collective-permute-start | bytes 172040 | tf_op jit(solution)/shard_map/ppermute | solution.py:542
  36.3 0.9 %between.5 = (f32[2,6,8,8,128]{4,3,2,1,0:T(8,128)S(1)}, f32[2,7,8,128]{3,2,1,0:T(8,128)S(1)}, f32[2,7,8,128]{3,2,1,0:T(8,128)S(1)}) custom-call(f32[2,7,8,128]{3,2,1,0:T(8,128)S(1)} %get-tuple-element.143.refs_0_.m7_ref, f32[2,6,8,8,128]{4,3,2,1,0:T(8,128)S(1)} %get-tuple-element.144.refs_1_, f32[3,8,8,128]{3,2,1,0:T(8,128)S(1)} %get-tuple-element.124.refs_2_.refs_7_, ...), custom_call_target="tpu_custom_call" | custom-call | flops 2000000000 | bytes 1024 | tf_op jit(solution)/shard_map/between/pallas_call | solution.py:523
  37.2 0.8 %collective-permute-done.5.refs_1_ = f32[14,8,128]{2,1,0:T(8,128)S(1)} collective-permute-done((f32[14,8,128]{2,1,0:T(8,128)S(1)}, f32[14,8,128]{2,1,0:T(8,128)S(1)}, u32[]{:S(2)}, u32[]{:S(2)}) %collective-permute-start.5) | collective-permute-done | bytes 57376 | tf_op jit(solution)/shard_map/ppermute | solution.py:542
  38.1 1.0 %second.4 = (f32[2,6,8,8,128]{4,3,2,1,0:T(8,128)S(1)}, f32[2,2,7,8,128]{4,3,2,1,0:T(8,128)S(1)}, f32[2,6,8,8,128]{4,3,2,1,0:T(8,128)S(1)}, f32[2,2,7,8,128]{4,3,...) custom-call(f32[2,7,8,128]{3,2,1,0:T(8,128)S(1)} %get-tuple-element.148.m0_ref, ...), custom_call_target="tpu_custom_call" | custom-call | flops 3000000000 | bytes 1024 | tf_op jit(solution)/shard_map/second/pallas_call | solution.py:523
  39.0 0.9 %collective-permute-done.10.refs_1_ = f32[14,8,128]{2,1,0:T(8,128)S(1)} collective-permute-done((f32[14,8,128]{2,1,0:T(8,128)S(1)}, f32[14,8,128]{2,1,0:T(8,128)S(1)}, u32[]{:S(2)}, u32[]{:S(2)}) %collective-permute-start.10) | collective-permute-done | bytes 57376 | tf_op jit(solution)/shard_map/ppermute | solution.py:542
  40.0 1.2 %collective-permute-start.11 = (f32[14,8,128]{2,1,0:T(8,128)S(1)}, f32[14,8,128]{2,1,0:T(8,128)S(1)}, u32[]{:S(2)}, u32[]{:S(2)}) collective-permute-start(f32[14,8,128]{2,1,0:T(8,128)S(1)} %get-tuple-element.156.refs_0_), channel_id=1, source_target_pairs={{0,1},{1,0},{2,3},{3,2},{4,5},{5,4},{6,7},{7,6},{8,9},{9,8},{10,11... | collective-permute-start | bytes 172040 | tf_op jit(solution)/shard_map/ppermute | solution.py:543
  41.2 1.1 %collective-permute-done.8.refs_1_ = f32[14,8,128]{2,1,0:T(8,128)S(1)} collective-permute-done((f32[14,8,128]{2,1,0:T(8,128)S(1)}, f32[14,8,128]{2,1,0:T(8,128)S(1)}, u32[]{:S(2)}, u32[]{:S(2)}) %collective-permute-start.8) | collective-permute-done | bytes 57376 | tf_op jit(solution)/shard_map/ppermute | solution.py:543
  42.3 2.6 %collective-permute-start.9 = (f32[14,8,128]{2,1,0:T(8,128)S(1)}, f32[14,8,128]{2,1,0:T(8,128)S(1)}, u32[]{:S(2)}, u32[]{:S(2)}) collective-permute-start(f32[14,8,128]{2,1,0:T(8,128)S(1)} %get-tuple-element.153.refs_0_), channel_id=1, source_target_pairs={{0,31},{1,2},{2,1},{3,4},{4,3},{5,6},{6,5},{7,8},{8,7},{9,10},{10,... | collective-permute-start | bytes 172040 | tf_op jit(solution)/shard_map/ppermute | solution.py:542
  45.3 3.8 %collective-permute-start.14 = (f32[14,8,128]{2,1,0:T(8,128)S(1)}, f32[14,8,128]{2,1,0:T(8,128)S(1)}, u32[]{:S(2)}, u32[]{:S(2)}) collective-permute-start(f32[14,8,128]{2,1,0:T(8,128)S(1)} %get-tuple-element.175.refs_0_), channel_id=1, source_target_pairs={{0,31},{1,2},{2,1},{3,4},{4,3},{5,6},{6,5},{7,8},{8,7},{9,10},{10,... | collective-permute-start | bytes 172040 | tf_op jit(solution)/shard_map/ppermute | solution.py:542
  49.1 0.9 %between.6 = (f32[2,6,8,8,128]{4,3,2,1,0:T(8,128)S(1)}, f32[2,7,8,128]{3,2,1,0:T(8,128)S(1)}, f32[2,7,8,128]{3,2,1,0:T(8,128)S(1)}) custom-call(f32[2,7,8,128]{3,2,1,0:T(8,128)S(1)} %get-tuple-element.164.refs_0_.m7_ref, f32[2,6,8,8,128]{4,3,2,1,0:T(8,128)S(1)} %get-tuple-element.165.refs_1_, f32[3,8,8,128]{3,2,1,0:T(8,128)S(1)} %get-tuple-element.124.refs_2_.refs_7_, ...), custom_call_target="tpu_custom_call" | custom-call | flops 2000000000 | bytes 1024 | tf_op jit(solution)/shard_map/between/pallas_call | solution.py:523
  51.0 1.0 %second.5 = (f32[2,6,8,8,128]{4,3,2,1,0:T(8,128)S(1)}, f32[2,2,7,8,128]{4,3,2,1,0:T(8,128)S(1)}, f32[2,6,8,8,128]{4,3,2,1,0:T(8,128)S(1)}, f32[2,2,7,8,128]{4,3,...) custom-call(f32[2,7,8,128]{3,2,1,0:T(8,128)S(1)} %get-tuple-element.169.m0_ref, ...), custom_call_target="tpu_custom_call" | custom-call | flops 3000000000 | bytes 1024 | tf_op jit(solution)/shard_map/second/pallas_call | solution.py:523
  52.0 1.8 %collective-permute-done.14.refs_1_ = f32[14,8,128]{2,1,0:T(8,128)S(1)} collective-permute-done((f32[14,8,128]{2,1,0:T(8,128)S(1)}, f32[14,8,128]{2,1,0:T(8,128)S(1)}, u32[]{:S(2)}, u32[]{:S(2)}) %collective-permute-start.14) | collective-permute-done | bytes 57376 | tf_op jit(solution)/shard_map/ppermute | solution.py:542
  54.1 1.1 %collective-permute-done.12.refs_1_ = f32[14,8,128]{2,1,0:T(8,128)S(1)} collective-permute-done((f32[14,8,128]{2,1,0:T(8,128)S(1)}, f32[14,8,128]{2,1,0:T(8,128)S(1)}, u32[]{:S(2)}, u32[]{:S(2)}) %collective-permute-start.12) | collective-permute-done | bytes 57376 | tf_op jit(solution)/shard_map/ppermute | solution.py:543
  55.2 2.6 %collective-permute-start.13 = (f32[14,8,128]{2,1,0:T(8,128)S(1)}, f32[14,8,128]{2,1,0:T(8,128)S(1)}, u32[]{:S(2)}, u32[]{:S(2)}) collective-permute-start(f32[14,8,128]{2,1,0:T(8,128)S(1)} %get-tuple-element.174.refs_0_), channel_id=1, source_target_pairs={{0,31},{1,2},{2,1},{3,4},{4,3},{5,6},{6,5},{7,8},{8,7},{9,10},{10,... | collective-permute-start | bytes 172040 | tf_op jit(solution)/shard_map/ppermute | solution.py:542
  58.6 3.5 %collective-permute-start.17 = (f32[14,8,128]{2,1,0:T(8,128)S(1)}, f32[14,8,128]{2,1,0:T(8,128)S(1)}, u32[]{:S(2)}, u32[]{:S(2)}) collective-permute-start(f32[14,8,128]{2,1,0:T(8,128)S(1)} %get-tuple-element.194.own_ref), channel_id=1, source_target_pairs={{0,31},{1,2},{2,1},{3,4},{4,3},{5,6},{6,5},{7,8},{8,7},{9,10},{10,... | collective-permute-start | bytes 172040 | tf_op jit(solution)/shard_map/ppermute | solution.py:542
  62.0 0.9 %between.7 = (f32[2,6,8,8,128]{4,3,2,1,0:T(8,128)S(1)}, f32[2,7,8,128]{3,2,1,0:T(8,128)S(1)}, f32[2,7,8,128]{3,2,1,0:T(8,128)S(1)}) custom-call(f32[2,7,8,128]{3,2,1,0:T(8,128)S(1)} %get-tuple-element.185.refs_0_.m7_ref, f32[2,6,8,8,128]{4,3,2,1,0:T(8,128)S(1)} %get-tuple-element.186.refs_1_, f32[3,8,8,128]{3,2,1,0:T(8,128)S(1)} %get-tuple-element.124.refs_2_.refs_7_, ...), custom_call_target="tpu_custom_call" | custom-call | flops 2000000000 | bytes 1024 | tf_op jit(solution)/shard_map/between/pallas_call | solution.py:523
  63.8 1.2 %last.1 = (f32[2,8,8,8,128]{4,3,2,1,0:T(8,128)}, f32[2,2,7,8,128]{4,3,2,1,0:T(8,128)S(1)}, f32[2,7,8,128]{3,2,1,0:T(8,128)S(1)}) custom-call(s32[8,128]{1,0:T(8,128)S(1)} %get-tuple-element.101.slot_ref, f32[2,7,8,128]{3,2,1,0:T(8,128)S(1)} %get-tuple-element.190.m0_ref, f32[2,7,8,128]{3,2,1,0:T(8,128)S(1)} %get-tuple-element.185.refs_0_.m7_ref, ...), custom_call_target="tpu_custom_call" | custom-call | flops 3000000000 | bytes 1024 | tf_op jit(solution)/shard_map/last/pallas_call | solution.py:523
  65.0 2.1 %collective-permute-done.17.got_ref = f32[14,8,128]{2,1,0:T(8,128)S(1)} collective-permute-done((f32[14,8,128]{2,1,0:T(8,128)S(1)}, f32[14,8,128]{2,1,0:T(8,128)S(1)}, u32[]{:S(2)}, u32[]{:S(2)}) %collective-permute-start.17) | collective-permute-done | bytes 57376 | tf_op jit(solution)/shard_map/ppermute | solution.py:542
  67.2 0.8 %collective-permute-done.16.got_ref = f32[14,8,128]{2,1,0:T(8,128)S(1)} collective-permute-done((f32[14,8,128]{2,1,0:T(8,128)S(1)}, f32[14,8,128]{2,1,0:T(8,128)S(1)}, u32[]{:S(2)}, u32[]{:S(2)}) %collective-permute-start.16) | collective-permute-done | bytes 57376 | tf_op jit(solution)/shard_map/ppermute | solution.py:543
  68.0 0.8 %finish.3 = f32[2,8,8,8,128]{4,3,2,1,0:T(8,128)} custom-call(s32[8,128]{1,0:T(8,128)S(1)} %get-tuple-element.101.slot_ref, f32[14,8,128]{2,1,0:T(8,128)S(1)} %get-tuple-element.188.own_ref, f32[14,8,128]{2,1,0:T(8,128)S(1)} %collective-permute-done.16.got_ref, f32[2,7,8,128]{3,2,1,0:T(8,128)S(1)} %get-tuple-element.189.e_ref, ...), custom_call_target="tpu_custom_call", output_to_operand_aliasing={{}: (6, {})} | custom-call | flops 1000000 | bytes 1024 | tf_op jit(solution)/shard_map/finish/pallas_call | solution.py:523
  (44 shorter events, 6.7 us)
Async XLA Ops:
  0.0 8.4 %copy-start = (f32[3,512,128]{2,1,0:T(8,128)S(1)}, f32[3,512,128]{2,1,0:T(8,128)}, u32[]{:S(2)}) copy-start(f32[3,512,128]{2,1,0:T(8,128)} %param.5) | copy-start | bytes 2359300
  0.0 8.4 %copy-start.1 = (f32[2,512,128]{2,1,0:T(8,128)S(1)}, f32[2,512,128]{2,1,0:T(8,128)}, u32[]{:S(2)}) copy-start(f32[2,512,128]{2,1,0:T(8,128)} %param.4) | copy-start | bytes 1572868
  1.3 7.1 %copy-start.2 = (f32[512,128]{1,0:T(8,128)S(1)}, f32[512,128]{1,0:T(8,128)}, u32[]{:S(2)}) copy-start(f32[512,128]{1,0:T(8,128)} %param.6) | copy-start | bytes 786436
  1.3 10.6 %collective-permute-start.2 = (f32[21,8,128]{2,1,0:T(8,128)S(1)}, f32[21,8,128]{2,1,0:T(8,128)S(1)}, u32[]{:S(2)}, u32[]{:S(2)}) collective-permute-start(f32[21,8,128]{2,1,0:T(8,128)S(1)} %bitcast.11), channel_id=1, source_target_pairs={{0,31},{1,2},{2,1},{3,4},{4,3},{5,6},{6,5},{7,8},{8,7},{9,10},{10,... | collective-permute-start | bytes 258056 | tf_op jit(solution)/shard_map/ppermute | solution.py:542
  8.3 6.4 %collective-permute-start = (f32[45,8,128]{2,1,0:T(8,128)S(1)}, f32[45,8,128]{2,1,0:T(8,128)S(1)}, u32[]{:S(2)}, u32[]{:S(2)}) collective-permute-start(f32[45,8,128]{2,1,0:T(8,128)S(1)} %project.3.own_ref.refs_7_), channel_id=1, source_target_pairs={{0,1},{1,0},{2,3},{3,2},{4,5},{5,4},{6,7},{7,6},{8,9},{9,8},{10,11... | collective-permute-start | bytes 552968 | tf_op jit(solution)/shard_map/ppermute | solution.py:543
  12.0 5.4 %collective-permute-start.4 = (f32[14,8,128]{2,1,0:T(8,128)S(1)}, f32[14,8,128]{2,1,0:T(8,128)S(1)}, u32[]{:S(2)}, u32[]{:S(2)}) collective-permute-start(f32[14,8,128]{2,1,0:T(8,128)S(1)} %get-tuple-element.120.refs_0_), channel_id=1, source_target_pairs={{0,1},{1,0},{2,3},{3,2},{4,5},{5,4},{6,7},{7,6},{8,9},{9,8},{10,11... | collective-permute-start | bytes 172040 | tf_op jit(solution)/shard_map/ppermute | solution.py:543
  14.7 10.1 %collective-permute-start.1 = (f32[38,8,128]{2,1,0:T(8,128)S(1)}, f32[38,8,128]{2,1,0:T(8,128)S(1)}, u32[]{:S(2)}, u32[]{:S(2)}) collective-permute-start(f32[38,8,128]{2,1,0:T(8,128)S(1)} %get-tuple-element.107.refs_0_), channel_id=1, source_target_pairs={{0,31},{1,2},{2,1},{3,4},{4,3},{5,6},{6,5},{7,8},{8,7},{9,10},{10,... | collective-permute-start | bytes 466952 | tf_op jit(solution)/shard_map/ppermute | solution.py:542
  17.4 8.9 %collective-permute-start.6 = (f32[14,8,128]{2,1,0:T(8,128)S(1)}, f32[14,8,128]{2,1,0:T(8,128)S(1)}, u32[]{:S(2)}, u32[]{:S(2)}) collective-permute-start(f32[14,8,128]{2,1,0:T(8,128)S(1)} %get-tuple-element.133.refs_0_), channel_id=1, source_target_pairs={{0,31},{1,2},{2,1},{3,4},{4,3},{5,6},{6,5},{7,8},{8,7},{9,10},{10,... | collective-permute-start | bytes 172040 | tf_op jit(solution)/shard_map/ppermute | solution.py:542
  25.2 4.3 %collective-permute-start.3 = (f32[14,8,128]{2,1,0:T(8,128)S(1)}, f32[14,8,128]{2,1,0:T(8,128)S(1)}, u32[]{:S(2)}, u32[]{:S(2)}) collective-permute-start(f32[14,8,128]{2,1,0:T(8,128)S(1)} %get-tuple-element.119.refs_0_), channel_id=1, source_target_pairs={{0,1},{1,0},{2,3},{3,2},{4,5},{5,4},{6,7},{7,6},{8,9},{9,8},{10,11... | collective-permute-start | bytes 172040 | tf_op jit(solution)/shard_map/ppermute | solution.py:543
  26.3 5.2 %collective-permute-start.7 = (f32[14,8,128]{2,1,0:T(8,128)S(1)}, f32[14,8,128]{2,1,0:T(8,128)S(1)}, u32[]{:S(2)}, u32[]{:S(2)}) collective-permute-start(f32[14,8,128]{2,1,0:T(8,128)S(1)} %get-tuple-element.135.refs_0_), channel_id=1, source_target_pairs={{0,1},{1,0},{2,3},{3,2},{4,5},{5,4},{6,7},{7,6},{8,9},{9,8},{10,11... | collective-permute-start | bytes 172040 | tf_op jit(solution)/shard_map/ppermute | solution.py:543
  29.5 8.5 %collective-permute-start.5 = (f32[14,8,128]{2,1,0:T(8,128)S(1)}, f32[14,8,128]{2,1,0:T(8,128)S(1)}, u32[]{:S(2)}, u32[]{:S(2)}) collective-permute-start(f32[14,8,128]{2,1,0:T(8,128)S(1)} %get-tuple-element.132.refs_0_), channel_id=1, source_target_pairs={{0,31},{1,2},{2,1},{3,4},{4,3},{5,6},{6,5},{7,8},{8,7},{9,10},{10,... | collective-permute-start | bytes 172040 | tf_op jit(solution)/shard_map/ppermute | solution.py:542
  31.5 8.5 %collective-permute-start.10 = (f32[14,8,128]{2,1,0:T(8,128)S(1)}, f32[14,8,128]{2,1,0:T(8,128)S(1)}, u32[]{:S(2)}, u32[]{:S(2)}) collective-permute-start(f32[14,8,128]{2,1,0:T(8,128)S(1)} %get-tuple-element.154.refs_0_), channel_id=1, source_target_pairs={{0,31},{1,2},{2,1},{3,4},{4,3},{5,6},{6,5},{7,8},{8,7},{9,10},{10,... | collective-permute-start | bytes 172040 | tf_op jit(solution)/shard_map/ppermute | solution.py:542
  38.0 4.3 %collective-permute-start.8 = (f32[14,8,128]{2,1,0:T(8,128)S(1)}, f32[14,8,128]{2,1,0:T(8,128)S(1)}, u32[]{:S(2)}, u32[]{:S(2)}) collective-permute-start(f32[14,8,128]{2,1,0:T(8,128)S(1)} %get-tuple-element.146.refs_0_), channel_id=1, source_target_pairs={{0,1},{1,0},{2,3},{3,2},{4,5},{5,4},{6,7},{7,6},{8,9},{9,8},{10,11... | collective-permute-start | bytes 172040 | tf_op jit(solution)/shard_map/ppermute | solution.py:543
  40.0 5.3 %collective-permute-start.11 = (f32[14,8,128]{2,1,0:T(8,128)S(1)}, f32[14,8,128]{2,1,0:T(8,128)S(1)}, u32[]{:S(2)}, u32[]{:S(2)}) collective-permute-start(f32[14,8,128]{2,1,0:T(8,128)S(1)} %get-tuple-element.156.refs_0_), channel_id=1, source_target_pairs={{0,1},{1,0},{2,3},{3,2},{4,5},{5,4},{6,7},{7,6},{8,9},{9,8},{10,11... | collective-permute-start | bytes 172040 | tf_op jit(solution)/shard_map/ppermute | solution.py:543
  42.3 8.5 %collective-permute-start.9 = (f32[14,8,128]{2,1,0:T(8,128)S(1)}, f32[14,8,128]{2,1,0:T(8,128)S(1)}, u32[]{:S(2)}, u32[]{:S(2)}) collective-permute-start(f32[14,8,128]{2,1,0:T(8,128)S(1)} %get-tuple-element.153.refs_0_), channel_id=1, source_target_pairs={{0,31},{1,2},{2,1},{3,4},{4,3},{5,6},{6,5},{7,8},{8,7},{9,10},{10,... | collective-permute-start | bytes 172040 | tf_op jit(solution)/shard_map/ppermute | solution.py:542
  45.3 8.5 %collective-permute-start.14 = (f32[14,8,128]{2,1,0:T(8,128)S(1)}, f32[14,8,128]{2,1,0:T(8,128)S(1)}, u32[]{:S(2)}, u32[]{:S(2)}) collective-permute-start(f32[14,8,128]{2,1,0:T(8,128)S(1)} %get-tuple-element.175.refs_0_), channel_id=1, source_target_pairs={{0,31},{1,2},{2,1},{3,4},{4,3},{5,6},{6,5},{7,8},{8,7},{9,10},{10,... | collective-permute-start | bytes 172040 | tf_op jit(solution)/shard_map/ppermute | solution.py:542
  50.8 4.4 %collective-permute-start.12 = (f32[14,8,128]{2,1,0:T(8,128)S(1)}, f32[14,8,128]{2,1,0:T(8,128)S(1)}, u32[]{:S(2)}, u32[]{:S(2)}) collective-permute-start(f32[14,8,128]{2,1,0:T(8,128)S(1)} %get-tuple-element.167.refs_0_), channel_id=1, source_target_pairs={{0,1},{1,0},{2,3},{3,2},{4,5},{5,4},{6,7},{7,6},{8,9},{9,8},{10,11... | collective-permute-start | bytes 172040 | tf_op jit(solution)/shard_map/ppermute | solution.py:543
  53.8 4.8 %collective-permute-start.15 = (f32[14,8,128]{2,1,0:T(8,128)S(1)}, f32[14,8,128]{2,1,0:T(8,128)S(1)}, u32[]{:S(2)}, u32[]{:S(2)}) collective-permute-start(f32[14,8,128]{2,1,0:T(8,128)S(1)} %get-tuple-element.177.refs_0_), channel_id=1, source_target_pairs={{0,1},{1,0},{2,3},{3,2},{4,5},{5,4},{6,7},{7,6},{8,9},{9,8},{10,11... | collective-permute-start | bytes 172040 | tf_op jit(solution)/shard_map/ppermute | solution.py:543
  55.2 8.5 %collective-permute-start.13 = (f32[14,8,128]{2,1,0:T(8,128)S(1)}, f32[14,8,128]{2,1,0:T(8,128)S(1)}, u32[]{:S(2)}, u32[]{:S(2)}) collective-permute-start(f32[14,8,128]{2,1,0:T(8,128)S(1)} %get-tuple-element.174.refs_0_), channel_id=1, source_target_pairs={{0,31},{1,2},{2,1},{3,4},{4,3},{5,6},{6,5},{7,8},{8,7},{9,10},{10,... | collective-permute-start | bytes 172040 | tf_op jit(solution)/shard_map/ppermute | solution.py:542
  58.6 8.5 %collective-permute-start.17 = (f32[14,8,128]{2,1,0:T(8,128)S(1)}, f32[14,8,128]{2,1,0:T(8,128)S(1)}, u32[]{:S(2)}, u32[]{:S(2)}) collective-permute-start(f32[14,8,128]{2,1,0:T(8,128)S(1)} %get-tuple-element.194.own_ref), channel_id=1, source_target_pairs={{0,31},{1,2},{2,1},{3,4},{4,3},{5,6},{6,5},{7,8},{8,7},{9,10},{10,... | collective-permute-start | bytes 172040 | tf_op jit(solution)/shard_map/ppermute | solution.py:542
  63.7 4.3 %collective-permute-start.16 = (f32[14,8,128]{2,1,0:T(8,128)S(1)}, f32[14,8,128]{2,1,0:T(8,128)S(1)}, u32[]{:S(2)}, u32[]{:S(2)}) collective-permute-start(f32[14,8,128]{2,1,0:T(8,128)S(1)} %get-tuple-element.188.own_ref), channel_id=1, source_target_pairs={{0,1},{1,0},{2,3},{3,2},{4,5},{5,4},{6,7},{7,6},{8,9},{9,8},{10,11... | collective-permute-start | bytes 172040 | tf_op jit(solution)/shard_map/ppermute | solution.py:543

commit v5 on v4

--- a/solution.py
+++ b/solution.py
@@ -151,13 +151,12 @@
     parity = lax.axis_index("elem") % 2
     near, far = source_plane(parity, 0), source_plane(parity, ORDER)
     copies = [pltpu.make_async_copy(order_ref, order_buf, sems.at[0])]
-    for r, source in enumerate((scal_ref.at[0, near], scal_ref.at[1, near], mass_ref.at[near])):
-        copies.append(pltpu.make_async_copy(source, near_buf.at[r], sems.at[1 + r]))
     late = []
-    sources = [scal_ref.at[0, far], scal_ref.at[1, far], mass_ref.at[far]]
-    sources += [tr_ref.at[r, far] for r in range(3)]
-    for r, source in enumerate(sources):
-        late.append(pltpu.make_async_copy(source, far_ref.at[r], sems.at[4 + r]))
+    for side, (plane, buf, group) in enumerate(((near, near_buf, copies), (far, far_ref, late))):
+        sources = [scal_ref.at[0, plane], scal_ref.at[1, plane], mass_ref.at[plane]]
+        sources += [tr_ref.at[r, plane] for r in range(3)]
+        for r, source in enumerate(sources):
+            group.append(pltpu.make_async_copy(source, buf.at[r], sems.at[1 + 6 * side + r]))
     for copy in copies + late:
         copy.start()
     tables = third_tables()
@@ -167,9 +166,7 @@
     slot_ref[...] = jnp.broadcast_to(order_buf[...], (SUB, LANES))
     for copy in copies[1:]:
         copy.wait()
-    planes = project(read(near_buf, 2), [read(near_buf, m) for m in range(2)], idx, tables)
-    for r in range(3):
-        write(od_ref, (r,), planes[r])
+    send_projection(near_buf, idx, tables, signs_of(parity), od_ref)
     for copy in late:
         copy.wait()
 
@@ -179,17 +176,20 @@
     return first, np.float32(-time_step), np.float32(-time_step)
 
 
+def send_projection(planes_ref, idx, tables, signs, out_ref):
+    planes = project(read(planes_ref, 2), [read(planes_ref, m) for m in range(2)], idx, tables)
+    planes.extend(
+        [gather_lanes(v, idx) * signs[r] for v in read(planes_ref, 3 + r)] for r in range(3))
+    write(out_ref, (), sum(planes, []))
+
+
 def project_even(idx_ref, far_ref, ev_ref):
-    idx = idx_ref[...]
     signs = signs_of(lax.axis_index("elem") % 2)
-    planes = project(read(far_ref, 2), [read(far_ref, m) for m in range(2)], idx, third_tables())
-    planes.extend(
-        [gather_lanes(v, idx) * signs[r] for v in read(far_ref, 3 + r)] for r in range(3))
-    write(ev_ref, (), sum(planes, []))
+    send_projection(far_ref, idx_ref[...], third_tables(), signs, ev_ref)
 
 
 def prepare(idx_ref, scal_ref, mass_ref, tr_ref,
-            gi_ref, q_ref, ri_ref, rt_ref, ti_ref, tf_ref, st_ref):
+            gi_ref, q_ref, ri_ref, rt_ref, ti_ref, st_ref):
     parity = lax.axis_index("elem") % 2
     idx = idx_ref[...]
     tables = third_tables()
@@ -200,17 +200,11 @@
         planes = [read(scal_ref, m, src) for m in range(2)] + [read(mass_ref, src)]
         return planes + [read(tr_ref, r, src) for r in range(3)]
 
-    near, far = source_plane(parity, 0), source_plane(parity, ORDER)
-    faces = [read(tr_ref, r, near) for r in range(3)] + [read(tr_ref, 0, far)]
-    faces = [
-        [gather_lanes(v, idx) * signs[r] for v in plane] for r, plane in zip((0, 1, 2, 0), faces)
-    ]
-    assembled = [plane_sum(faces[0], tables, ROWS), plane_sum(faces[3], tables, ROWS)]
+    faces = [read(tr_ref, 0, source_plane(parity, face * ORDER)) for face in range(2)]
     ahead = load(1)
-    for r in range(3):
-        write(tf_ref, (r,), faces[r])
     for face in range(2):
-        write(st_ref, (face,), assembled[face])
+        first = [gather_lanes(v, idx) * signs[0] for v in faces[face]]
+        write(st_ref, (face,), plane_sum(first, tables, ROWS))
     sums = [[None, None], [None, None]]
     for i in range(6):
         raw = [[gather_lanes(v, idx) for v in plane] for plane in ahead]
@@ -314,12 +308,10 @@
     return [[ref[start + 8 * r + j] for j in range(8)] for r in range(3)]
 
 
-def make_field_face(face, carry):
+def make_field_face(face):
     far = np.float32(DM[ORDER - face * ORDER, face * ORDER])
 
-    def field_face(own_ref, got_ref, q_ref, st_ref, *refs):
-        tf_ref = refs[0] if carry else None
-        p_ref, rf_ref, send_ref = refs[-3:]
+    def field_face(own_ref, got_ref, q_ref, st_ref, p_ref, rf_ref, send_ref):
         inverse = [1.0 / (own_ref[14 + j] + got_ref[14 + j]) for j in range(ROWS)]
         p = [
             [(own_ref[ROWS * m + j] + got_ref[ROWS * m + j]) * inverse[j] for j in range(ROWS)]
@@ -333,28 +325,15 @@
         for m in range(2):
             write(p_ref, (m,), p[m])
         write(rf_ref, (), inverse)
-        if carry:
-            for r in range(3):
-                for j in range(8):
-                    send_ref[2 * ROWS + 8 * r + j] = tf_ref[r, j]
 
     return field_face
 
 
-def make_stage_face(face, scale, total, raw, early):
+def make_stage_face(face, scale, total, raw):
     far = np.float32(DM[ORDER - face * ORDER, face * ORDER])
     scale = np.float32(scale)
 
-    def stage_face(*refs):
-        own_ref, got_ref, e_ref, acc_ref, q_ref, rt_ref, rf_ref = refs[:7]
-        if early:
-            tf_ref, p_ref, send_ref, a_ref, e_buf = refs[7:]
-            tables = third_tables()
-            both_sides([read(tf_ref, r) for r in range(3)], transports(got_ref, 2 * ROWS), tables, a_ref)
-            own_terms(e_ref, a_ref, rf_ref, face, rotations(), tables, e_buf)
-            e_ref = e_buf
-        else:
-            p_ref, send_ref = refs[7:]
+    def stage_face(own_ref, got_ref, e_ref, acc_ref, q_ref, rt_ref, rf_ref, p_ref, send_ref):
         p = []
         for m in range(2):
             value = [own_ref[ROWS * m + j] + got_ref[ROWS * m + j] for j in range(ROWS)]
@@ -377,18 +356,21 @@
 
 def make_first_inner(scale, opening, start):
     def first_inner(*refs):
-        p0_ref, p7_ref, gi_ref, acci_ref, wp_ref, rt_ref, r7_ref = refs[:7]
+        p0_ref, p7_ref, gi_ref, rt_ref, r7_ref = refs[:5]
         tables = third_tables()
+        rot = rotations()
         if start:
-            ev_ref, rev_ref, st_ref, r0_ref = refs[7:11]
-            gn_ref, an_ref, q_ref, e7_ref, a7_ref, rs_ref = refs[11:]
-            both_sides(transports(ev_ref, 3 * ROWS), transports(rev_ref, 3 * ROWS), tables, a7_ref)
+            od_ref, rod_ref, ev_ref, rev_ref, st_ref, r0_ref, ri_ref, ti_ref = refs[5:13]
+            gn_ref, an_ref, q_ref, e7_ref, a0_ref, a7_ref, rs_ref, wp_ref = refs[13:]
+            inner_open(gi_ref, ri_ref, rt_ref, ti_ref, rot, wp_ref)
+            for own, got, out in ((od_ref, rod_ref, a0_ref), (ev_ref, rev_ref, a7_ref)):
+                both_sides(transports(own, 3 * ROWS), transports(got, 3 * ROWS), tables, out)
             write(rs_ref, (0,), [st_ref[0, j] * r0_ref[j] for j in range(ROWS)])
             write(rs_ref, (1,), [st_ref[1, j] * r7_ref[j] for j in range(ROWS)])
         else:
-            a7_ref = refs[7]
+            acci_ref, wp_ref, a7_ref = refs[5:8]
             gn_ref, an_ref, q_ref, e7_ref = refs[8:]
-        own_terms(p7_ref, a7_ref, r7_ref, 1, rotations(), tables, e7_ref)
+        own_terms(p7_ref, a7_ref, r7_ref, 1, rot, tables, e7_ref)
 
         def put(m, i, value):
             base = gi_ref if opening else acci_ref
@@ -401,20 +383,13 @@
     return first_inner
 
 
-def make_between(early):
-    def between(*refs):
-        m7_ref, gi_ref, a7_ref, r7_ref, ri_ref, rt_ref, ti_ref = refs[:7]
-        rot = rotations()
-        tables = third_tables()
-        if early:
-            wp_ref, e7_ref = refs[7:]
-        else:
-            p0_ref, a0_ref, r0_ref, wp_ref, e7_ref, e0_ref = refs[7:]
-            own_terms(p0_ref, a0_ref, r0_ref, 0, rot, tables, e0_ref)
-        own_terms(m7_ref, a7_ref, r7_ref, 1, rot, tables, e7_ref)
-        inner_open(gi_ref, ri_ref, rt_ref, ti_ref, rot, wp_ref)
-
-    return between
+def between(m7_ref, gi_ref, a7_ref, r7_ref, ri_ref, rt_ref, ti_ref, p0_ref, a0_ref, r0_ref,
+            wp_ref, e7_ref, e0_ref):
+    rot = rotations()
+    tables = third_tables()
+    own_terms(p0_ref, a0_ref, r0_ref, 0, rot, tables, e0_ref)
+    own_terms(m7_ref, a7_ref, r7_ref, 1, rot, tables, e7_ref)
+    inner_open(gi_ref, ri_ref, rt_ref, ti_ref, rot, wp_ref)
 
 
 def face_totals(now, before, accf_ref, afn_ref, opening):
@@ -552,60 +527,44 @@
     f32 = jnp.float32
 
     stay = lambda x: pltpu.with_memory_space_constraint(x, pltpu.HBM)
+    bundle = (3 * ROWS + 24, SUB, LANES)
     od, idx, slots, far = call(
-        project_odd, [(3,) + part, (SUB, LANES), (SUB, LANES), (6,) + tile],
+        project_odd, [bundle, (SUB, LANES), (SUB, LANES), (6,) + tile],
         (stay(element_order), stay(scal), stay(mas), stay(tr)), "project", 1, hbm=(0, 1, 2, 3),
-        scratch=[pltpu.VMEM((1, LANES), jnp.int32), pltpu.VMEM((3,) + tile, f32),
-                 pltpu.SemaphoreType.DMA((10,))])
-    od = od.reshape(3 * ROWS, SUB, LANES)
+        scratch=[pltpu.VMEM((1, LANES), jnp.int32), pltpu.VMEM((6,) + tile, f32),
+                 pltpu.SemaphoreType.DMA((13,))])
     rod = swap_od(od)
-    ev = call(project_even, [(3 * ROWS + 24, SUB, LANES)], (idx, far), "project", 1)
+    ev = call(project_even, [bundle], (idx, far), "project", 1)
     rev = swap_ev(ev)
-    gi, q, ri, rt, ti, tf, st = call(
-        prepare,
-        [inner, faces, (6,) + tile, (6,) + tile, (6, 2) + tile, geometry, (2,) + part],
+    gi, q, ri, rt, ti, st = call(
+        prepare, [inner, faces, (6,) + tile, (6,) + tile, (6, 2) + tile, (2,) + part],
         (idx, scal, mas, tr), "prepare", 1)
-
-    def opening_terms(gi_ref, ri_ref, rt_ref, ti_ref, wp_ref):
-        inner_open(gi_ref, ri_ref, rt_ref, ti_ref, rotations(), wp_ref)
-
-    wp = call(opening_terms, [inner], (gi, ri, rt, ti), "terms", 1)
-    p0, r0, cev = call(
-        make_field_face(0, False), [face, part, sent], (od, rod, q, st), "odd", 3000)
-    p7, r7, cod = call(
-        make_field_face(1, True), [face, part, (2 * ROWS + 24, SUB, LANES)],
-        (ev, rev, q, st, tf), "even", 1)
-    acci, accf = gi, q
+    p0, r0, cev = call(make_field_face(0), [face, part, sent], (od, rod, q, st), "odd", 3000)
+    p7, r7, cod = call(make_field_face(1), [face, part, sent], (ev, rev, q, st), "even", 1)
+    acci, accf, wp = gi, q, gi
     pairs = SUBSTEPS * STAGES // 2
     for n in range(pairs):
         s = 2 * n % STAGES + 1
         opening, closing, early = s == 1, s + 1 == STAGES, n == 0
         got_ev, got_od = swap_ev(cev), swap_od(cod)
-        extra = (ev, rev, st, r0) if early else (a7,)
+        extra = (od, rod, ev, rev, st, r0, ri, ti) if early else (acci, wp, a7)
         res = call(
             make_first_inner(1.0 / s, opening, early),
-            [inner, inner, faces, face] + ([geometry, (2,) + part] if early else []),
-            (p0, p7, gi, acci, wp, rt, r7) + extra, "first", 1000)
+            [inner, inner, faces, face] + ([geometry, geometry, (2,) + part] if early else []),
+            (p0, p7, gi, rt, r7) + extra, "first", 1000,
+            scratch=[pltpu.VMEM(inner, f32)] if early else [])
         gm, acci, q, e7 = res[:4]
         if early:
-            a7, rs = res[4:]
+            a0, a7, rs = res[4:]
         m7, cod2 = call(
-            make_stage_face(1, 1.0 / s, False, early, False), [face, sent],
+            make_stage_face(1, 1.0 / s, False, early), [face, sent],
             (cev, got_ev, e7, accf, q, rs, r7), "ahead", 1)
         got_od2 = swap_od(cod2)
-        res = call(
-            make_between(early), [inner, face] + ([] if early else [face]),
-            (m7, gm, a7, r7, ri, rt, ti) + (() if early else (p0, a0, r0)), "between", 2000)
-        wp, e7 = res[:2]
-        if early:
-            m0, cev2, a0 = call(
-                make_stage_face(0, 1.0 / s, False, True, True), [face, sent, geometry],
-                (cod, got_od, p0, accf, q, rs, r0, tf), "behind", 1,
-                scratch=[pltpu.VMEM(face, f32)])
-        else:
-            m0, cev2 = call(
-                make_stage_face(0, 1.0 / s, False, False, False), [face, sent],
-                (cod, got_od, res[2], accf, q, rs, r0), "behind", 1)
+        wp, e7, e0 = call(
+            between, [inner, face, face], (m7, gm, a7, r7, ri, rt, ti, p0, a0, r0), "between", 2000)
+        m0, cev2 = call(
+            make_stage_face(0, 1.0 / s, False, early), [face, sent],
+            (cod, got_od, e0, accf, q, rs, r0), "behind", 1)
         got_ev2 = swap_ev(cev2)
         scale = 1.0 / (s + 1)
         if n < pairs - 1:
@@ -614,10 +573,10 @@
                 [inner, faces, inner, faces, inner, face],
                 (m0, m7, p0, p7, accf, acci, wp, ri, rt, ti, a0, r0), "second", 3000)
             p0, cev = call(
-                make_stage_face(0, scale, closing, False, False), [face, sent],
+                make_stage_face(0, scale, closing, False), [face, sent],
                 (cod2, got_od2, e0, accf, q, rs, r0), "odd", 3000)
             p7, cod = call(
-                make_stage_face(1, scale, closing, False, False), [face, sent],
+                make_stage_face(1, scale, closing, False), [face, sent],
                 (cev2, got_ev2, e7, accf, q, rs, r7), "even", 1)
         else:
             out, accf, e0 = call(

time: 69.1 us -> 68.3 us (0.988)
  starting transfers between devices: 38.3 us -> 35.8 us
  waiting for transfers between devices: 14.5 us -> 16.8 us
    ppermute x9, starting transfers between devices: 6.24 us -> 1.27 us  [per_device(): swap_ev = lambda x: lax.ppermute(x, 'elem', even_pairs)]
    ppermute x9, waiting for transfers between devices: 9.62 us -> 14.5 us  [per_device(): swap_od = lambda x: lax.ppermute(x, 'elem', odd_pairs)]
    ppermute x9, waiting for transfers between devices: 4.92 us -> 2.29 us  [per_device(): swap_ev = lambda x: lax.ppermute(x, 'elem', even_pairs)]
    ppermute x9, starting transfers between devices: 32 us -> 34.6 us  [per_device(): swap_od = lambda x: lax.ppermute(x, 'elem', odd_pairs)]
    pallas_call x34 -> x33, Pallas kernels: 15.8 us -> 15.2 us  [call(): pl.pallas_call(kernel, out_shape=shapes[0] if single else shapes, in_spec...]
  transfers between devices with their start and end apart: 18 -> 18, of which waited for: 13 -> 13; matrix products, arithmetic and copies ran while one was open for 0% -> 0% of each run, Pallas kernels for 20% -> 19%
where the time goes in v5:
time: 68.3 us; the launch traced here: 68.2 us
  starting transfers between devices  35.8 us (52%)
  waiting for transfers between devices  16.8 us (25%)
  Pallas kernels  15.2 us (22%)
    ppermute x9, starting transfers between devices, per_device(): swap_od = lambda x: lax.ppermute(x, 'elem', odd_pairs)  34.6 us
    pallas_call x33, Pallas kernels, call(): pl.pallas_call(kernel, out_shape=shapes[0] if single else shapes, in_spec...  15.2 us
    ppermute x9, waiting for transfers between devices, per_device(): swap_od = lambda x: lax.ppermute(x, 'elem', odd_pairs)  14.5 us
    ppermute x9, waiting for transfers between devices, per_device(): swap_ev = lambda x: lax.ppermute(x, 'elem', even_pairs)  2.29 us
  transfers between devices with their start and end apart: 18, of which 13 were waited for; matrix products, arithmetic and copies ran while one was open for 0% of the time, Pallas kernels for 19%

profile of v5, /device:TPU:0, one launch (start us, length us, event | category | flops | bytes accessed | tf_op | source)
XLA Modules:
  0.0 68.2 jit_solution(12200232637465217914)
XLA Ops:
  0.0 1.4 %project.2 = (f32[45,8,128]{2,1,0:T(8,128)S(1)}, s32[8,128]{1,0:T(8,128)S(1)}, s32[8,128]{1,0:T(8,128)S(1)}, f32[6,8,8,128]{3,2,1,0:T(8,128)S(1)}) custom-call(s32[1,128]{1,0:T(1,128)} %order_ref.1, f32[2,8,8,8,128]{4,3,2,1,0:T(8,128)} %bitcast.6, f32[8,8,8,128]{3,2,1,0:T(8,128)} %bitcast.8, f32[3,8,8,8,128]{4,3,2,1,0:T(8,128)} %bitcast.4), custom_call_target="tpu_custom_call" | custom-call | flops 1000000 | bytes 1024 | tf_op jit(solution)/shard_map/project/pallas_call | solution.py:498
  1.4 6.7 %collective-permute-start.2 = (f32[45,8,128]{2,1,0:T(8,128)S(1)}, f32[45,8,128]{2,1,0:T(8,128)S(1)}, u32[]{:S(2)}, u32[]{:S(2)}) collective-permute-start(f32[45,8,128]{2,1,0:T(8,128)S(1)} %get-tuple-element.107.own_ref.refs_5_), channel_id=1, source_target_pairs={{0,31},{1,2},{2,1},{3,4},{4,3},{5,6},{6,5},{7,8},{8,7},{9,10},{10,... | collective-permute-start | bytes 552968 | tf_op jit(solution)/shard_map/ppermute | solution.py:517
  8.5 2.6 %prepare.1 = (f32[2,6,8,8,128]{4,3,2,1,0:T(8,128)S(1)}, f32[2,2,7,8,128]{4,3,2,1,0:T(8,128)S(1)}, f32[6,8,8,128]{3,2,1,0:T(8,128)S(1)}, f32[6,8,8,128]{3,2,1,0:T...) custom-call(s32[8,128]{1,0:T(8,128)S(1)} %get-tuple-element.102.idx_ref, ...), custom_call_target="tpu_custom_call" | custom-call | flops 1000000 | bytes 1024 | tf_op jit(solution)/shard_map/prepare/pallas_call | solution.py:498
  11.1 1.6 %collective-permute-done.2.got_ref.refs_6_ = f32[45,8,128]{2,1,0:T(8,128)S(1)} collective-permute-done((f32[45,8,128]{2,1,0:T(8,128)S(1)}, f32[45,8,128]{2,1,0:T(8,128)S(1)}, u32[]{:S(2)}, u32[]{:S(2)}) %collective-permute-start.2) | collective-permute-done | bytes 184352 | tf_op jit(solution)/shard_map/ppermute | solution.py:517
  12.8 0.4 collective-permute-start.3
  13.2 1.4 %collective-permute-done.got_ref.refs_8_ = f32[45,8,128]{2,1,0:T(8,128)S(1)} collective-permute-done((f32[45,8,128]{2,1,0:T(8,128)S(1)}, f32[45,8,128]{2,1,0:T(8,128)S(1)}, u32[]{:S(2)}, u32[]{:S(2)}) %collective-permute-start) | collective-permute-done | bytes 184352 | tf_op jit(solution)/shard_map/ppermute | solution.py:518
  14.6 4.4 %collective-permute-start.1 = (f32[14,8,128]{2,1,0:T(8,128)S(1)}, f32[14,8,128]{2,1,0:T(8,128)S(1)}, u32[]{:S(2)}, u32[]{:S(2)}) collective-permute-start(f32[14,8,128]{2,1,0:T(8,128)S(1)} %get-tuple-element.106.own_ref), channel_id=1, source_target_pairs={{0,31},{1,2},{2,1},{3,4},{4,3},{5,6},{6,5},{7,8},{8,7},{9,10},{10,... | collective-permute-start | bytes 172040 | tf_op jit(solution)/shard_map/ppermute | solution.py:517
  19.0 0.9 %first.4 = (f32[2,6,8,8,128]{4,3,2,1,0:T(8,128)S(1)}, f32[2,6,8,8,128]{4,3,2,1,0:T(8,128)S(1)}, f32[2,2,7,8,128]{4,3,2,1,0:T(8,128)S(1)}, f32[2,7,8,128]{3,2,1,0...) custom-call(f32[2,7,8,128]{3,2,1,0:T(8,128)S(1)} %get-tuple-element.109.refs, ...), custom_call_target="tpu_custom_call" | custom-call | flops 1000000000 | bytes 1024 | tf_op jit(solution)/shard_map/first/pallas_call | solution.py:498
  19.9 3.2 %collective-permute-start.6 = (f32[14,8,128]{2,1,0:T(8,128)S(1)}, f32[14,8,128]{2,1,0:T(8,128)S(1)}, u32[]{:S(2)}, u32[]{:S(2)}) collective-permute-start(f32[14,8,128]{2,1,0:T(8,128)S(1)} %get-tuple-element.133.own_ref), channel_id=1, source_target_pairs={{0,31},{1,2},{2,1},{3,4},{4,3},{5,6},{6,5},{7,8},{8,7},{9,10},{10,... | collective-permute-start | bytes 172040 | tf_op jit(solution)/shard_map/ppermute | solution.py:517
  23.1 0.9 %between.4 = (f32[2,6,8,8,128]{4,3,2,1,0:T(8,128)S(1)}, f32[2,7,8,128]{3,2,1,0:T(8,128)S(1)}, f32[2,7,8,128]{3,2,1,0:T(8,128)S(1)}) custom-call(f32[2,7,8,128]{3,2,1,0:T(8,128)S(1)} %get-tuple-element.120.m7_ref, f32[2,6,8,8,128]{4,3,2,1,0:T(8,128)S(1)} %get-tuple-element.121.gi_ref, f32[3,8,8,128]{3,2,1,0:T(8,128)S(1)} %get-tuple-element.122.a7_ref.refs_7_, ...), custom_call_target="tpu_custom_call" | custom-call | flops 2000000000 | bytes 1024 | tf_op jit(solution)/shard_map/between/pallas_call | solution.py:498
  24.1 1.0 %second.3 = (f32[2,6,8,8,128]{4,3,2,1,0:T(8,128)S(1)}, f32[2,2,7,8,128]{4,3,2,1,0:T(8,128)S(1)}, f32[2,6,8,8,128]{4,3,2,1,0:T(8,128)S(1)}, f32[2,2,7,8,128]{4,3,...) custom-call(f32[2,7,8,128]{3,2,1,0:T(8,128)S(1)} %get-tuple-element.127.m0_ref, ...), custom_call_target="tpu_custom_call" | custom-call | flops 3000000000 | bytes 1024 | tf_op jit(solution)/shard_map/second/pallas_call | solution.py:498
  25.1 3.3 %collective-permute-done.6.got_ref = f32[14,8,128]{2,1,0:T(8,128)S(1)} collective-permute-done((f32[14,8,128]{2,1,0:T(8,128)S(1)}, f32[14,8,128]{2,1,0:T(8,128)S(1)}, u32[]{:S(2)}, u32[]{:S(2)}) %collective-permute-start.6) | collective-permute-done | bytes 57376 | tf_op jit(solution)/shard_map/ppermute | solution.py:517
  28.6 3.6 %collective-permute-start.5 = (f32[14,8,128]{2,1,0:T(8,128)S(1)}, f32[14,8,128]{2,1,0:T(8,128)S(1)}, u32[]{:S(2)}, u32[]{:S(2)}) collective-permute-start(f32[14,8,128]{2,1,0:T(8,128)S(1)} %get-tuple-element.132.own_ref), channel_id=1, source_target_pairs={{0,31},{1,2},{2,1},{3,4},{4,3},{5,6},{6,5},{7,8},{8,7},{9,10},{10,... | collective-permute-start | bytes 172040 | tf_op jit(solution)/shard_map/ppermute | solution.py:517
  32.7 3.2 %collective-permute-start.10 = (f32[14,8,128]{2,1,0:T(8,128)S(1)}, f32[14,8,128]{2,1,0:T(8,128)S(1)}, u32[]{:S(2)}, u32[]{:S(2)}) collective-permute-start(f32[14,8,128]{2,1,0:T(8,128)S(1)} %get-tuple-element.154.own_ref), channel_id=1, source_target_pairs={{0,31},{1,2},{2,1},{3,4},{4,3},{5,6},{6,5},{7,8},{8,7},{9,10},{10,... | collective-permute-start | bytes 172040 | tf_op jit(solution)/shard_map/ppermute | solution.py:517
  35.9 0.9 %between.5 = (f32[2,6,8,8,128]{4,3,2,1,0:T(8,128)S(1)}, f32[2,7,8,128]{3,2,1,0:T(8,128)S(1)}, f32[2,7,8,128]{3,2,1,0:T(8,128)S(1)}) custom-call(f32[2,7,8,128]{3,2,1,0:T(8,128)S(1)} %get-tuple-element.143.m7_ref, f32[2,6,8,8,128]{4,3,2,1,0:T(8,128)S(1)} %get-tuple-element.144.gi_ref, f32[3,8,8,128]{3,2,1,0:T(8,128)S(1)} %get-tuple-element.122.a7_ref.refs_7_, ...), custom_call_target="tpu_custom_call" | custom-call | flops 2000000000 | bytes 1024 | tf_op jit(solution)/shard_map/between/pallas_call | solution.py:498
  36.8 0.4 collective-permute-done.5.got_ref
  37.3 1.0 %second.4 = (f32[2,6,8,8,128]{4,3,2,1,0:T(8,128)S(1)}, f32[2,2,7,8,128]{4,3,2,1,0:T(8,128)S(1)}, f32[2,6,8,8,128]{4,3,2,1,0:T(8,128)S(1)}, f32[2,2,7,8,128]{4,3,...) custom-call(f32[2,7,8,128]{3,2,1,0:T(8,128)S(1)} %get-tuple-element.148.m0_ref, ...), custom_call_target="tpu_custom_call" | custom-call | flops 3000000000 | bytes 1024 | tf_op jit(solution)/shard_map/second/pallas_call | solution.py:498
  38.3 2.9 %collective-permute-done.10.got_ref = f32[14,8,128]{2,1,0:T(8,128)S(1)} collective-permute-done((f32[14,8,128]{2,1,0:T(8,128)S(1)}, f32[14,8,128]{2,1,0:T(8,128)S(1)}, u32[]{:S(2)}, u32[]{:S(2)}) %collective-permute-start.10) | collective-permute-done | bytes 57376 | tf_op jit(solution)/shard_map/ppermute | solution.py:517
  41.5 3.5 %collective-permute-start.9 = (f32[14,8,128]{2,1,0:T(8,128)S(1)}, f32[14,8,128]{2,1,0:T(8,128)S(1)}, u32[]{:S(2)}, u32[]{:S(2)}) collective-permute-start(f32[14,8,128]{2,1,0:T(8,128)S(1)} %get-tuple-element.153.own_ref), channel_id=1, source_target_pairs={{0,31},{1,2},{2,1},{3,4},{4,3},{5,6},{6,5},{7,8},{8,7},{9,10},{10,... | collective-permute-start | bytes 172040 | tf_op jit(solution)/shard_map/ppermute | solution.py:517
  45.5 3.2 %collective-permute-start.14 = (f32[14,8,128]{2,1,0:T(8,128)S(1)}, f32[14,8,128]{2,1,0:T(8,128)S(1)}, u32[]{:S(2)}, u32[]{:S(2)}) collective-permute-start(f32[14,8,128]{2,1,0:T(8,128)S(1)} %get-tuple-element.175.own_ref), channel_id=1, source_target_pairs={{0,31},{1,2},{2,1},{3,4},{4,3},{5,6},{6,5},{7,8},{8,7},{9,10},{10,... | collective-permute-start | bytes 172040 | tf_op jit(solution)/shard_map/ppermute | solution.py:517
  48.7 0.9 %between.6 = (f32[2,6,8,8,128]{4,3,2,1,0:T(8,128)S(1)}, f32[2,7,8,128]{3,2,1,0:T(8,128)S(1)}, f32[2,7,8,128]{3,2,1,0:T(8,128)S(1)}) custom-call(f32[2,7,8,128]{3,2,1,0:T(8,128)S(1)} %get-tuple-element.164.m7_ref, f32[2,6,8,8,128]{4,3,2,1,0:T(8,128)S(1)} %get-tuple-element.165.gi_ref, f32[3,8,8,128]{3,2,1,0:T(8,128)S(1)} %get-tuple-element.122.a7_ref.refs_7_, ...), custom_call_target="tpu_custom_call" | custom-call | flops 2000000000 | bytes 1024 | tf_op jit(solution)/shard_map/between/pallas_call | solution.py:498
  49.6 0.4 collective-permute-done.9.got_ref
  50.3 0.9 %second.5 = (f32[2,6,8,8,128]{4,3,2,1,0:T(8,128)S(1)}, f32[2,2,7,8,128]{4,3,2,1,0:T(8,128)S(1)}, f32[2,6,8,8,128]{4,3,2,1,0:T(8,128)S(1)}, f32[2,2,7,8,128]{4,3,...) custom-call(f32[2,7,8,128]{3,2,1,0:T(8,128)S(1)} %get-tuple-element.169.m0_ref, ...), custom_call_target="tpu_custom_call" | custom-call | flops 3000000000 | bytes 1024 | tf_op jit(solution)/shard_map/second/pallas_call | solution.py:498
  51.3 2.7 %collective-permute-done.14.got_ref = f32[14,8,128]{2,1,0:T(8,128)S(1)} collective-permute-done((f32[14,8,128]{2,1,0:T(8,128)S(1)}, f32[14,8,128]{2,1,0:T(8,128)S(1)}, u32[]{:S(2)}, u32[]{:S(2)}) %collective-permute-start.14) | collective-permute-done | bytes 57376 | tf_op jit(solution)/shard_map/ppermute | solution.py:517
  54.1 0.4 collective-permute-done.12.got_ref
  54.5 3.5 %collective-permute-start.13 = (f32[14,8,128]{2,1,0:T(8,128)S(1)}, f32[14,8,128]{2,1,0:T(8,128)S(1)}, u32[]{:S(2)}, u32[]{:S(2)}) collective-permute-start(f32[14,8,128]{2,1,0:T(8,128)S(1)} %get-tuple-element.174.own_ref), channel_id=1, source_target_pairs={{0,31},{1,2},{2,1},{3,4},{4,3},{5,6},{6,5},{7,8},{8,7},{9,10},{10,... | collective-permute-start | bytes 172040 | tf_op jit(solution)/shard_map/ppermute | solution.py:517
  58.4 3.2 %collective-permute-start.17 = (f32[14,8,128]{2,1,0:T(8,128)S(1)}, f32[14,8,128]{2,1,0:T(8,128)S(1)}, u32[]{:S(2)}, u32[]{:S(2)}) collective-permute-start(f32[14,8,128]{2,1,0:T(8,128)S(1)} %get-tuple-element.194.own_ref), channel_id=1, source_target_pairs={{0,31},{1,2},{2,1},{3,4},{4,3},{5,6},{6,5},{7,8},{8,7},{9,10},{10,... | collective-permute-start | bytes 172040 | tf_op jit(solution)/shard_map/ppermute | solution.py:517
  61.6 0.9 %between.7 = (f32[2,6,8,8,128]{4,3,2,1,0:T(8,128)S(1)}, f32[2,7,8,128]{3,2,1,0:T(8,128)S(1)}, f32[2,7,8,128]{3,2,1,0:T(8,128)S(1)}) custom-call(f32[2,7,8,128]{3,2,1,0:T(8,128)S(1)} %get-tuple-element.185.m7_ref, f32[2,6,8,8,128]{4,3,2,1,0:T(8,128)S(1)} %get-tuple-element.186.gi_ref, f32[3,8,8,128]{3,2,1,0:T(8,128)S(1)} %get-tuple-element.122.a7_ref.refs_7_, ...), custom_call_target="tpu_custom_call" | custom-call | flops 2000000000 | bytes 1024 | tf_op jit(solution)/shard_map/between/pallas_call | solution.py:498
  62.5 0.5 collective-permute-done.13.got_ref
  63.1 1.1 %last.1 = (f32[2,8,8,8,128]{4,3,2,1,0:T(8,128)}, f32[2,2,7,8,128]{4,3,2,1,0:T(8,128)S(1)}, f32[2,7,8,128]{3,2,1,0:T(8,128)S(1)}) custom-call(s32[8,128]{1,0:T(8,128)S(1)} %get-tuple-element.101.slot_ref, f32[2,7,8,128]{3,2,1,0:T(8,128)S(1)} %get-tuple-element.190.m0_ref, f32[2,7,8,128]{3,2,1,0:T(8,128)S(1)} %get-tuple-element.185.m7_ref, ...), custom_call_target="tpu_custom_call" | custom-call | flops 3000000000 | bytes 1024 | tf_op jit(solution)/shard_map/last/pallas_call | solution.py:498
  64.3 2.7 %collective-permute-done.17.got_ref = f32[14,8,128]{2,1,0:T(8,128)S(1)} collective-permute-done((f32[14,8,128]{2,1,0:T(8,128)S(1)}, f32[14,8,128]{2,1,0:T(8,128)S(1)}, u32[]{:S(2)}, u32[]{:S(2)}) %collective-permute-start.17) | collective-permute-done | bytes 57376 | tf_op jit(solution)/shard_map/ppermute | solution.py:517
  67.3 0.8 %finish.3 = f32[2,8,8,8,128]{4,3,2,1,0:T(8,128)} custom-call(s32[8,128]{1,0:T(8,128)S(1)} %get-tuple-element.101.slot_ref, f32[14,8,128]{2,1,0:T(8,128)S(1)} %get-tuple-element.188.own_ref, f32[14,8,128]{2,1,0:T(8,128)S(1)} %collective-permute-done.16.got_ref, f32[2,7,8,128]{3,2,1,0:T(8,128)S(1)} %get-tuple-element.189.e_ref, ...), custom_call_target="tpu_custom_call", output_to_operand_aliasing={{}: (6, {})} | custom-call | flops 1000000 | bytes 1024 | tf_op jit(solution)/shard_map/finish/pallas_call | solution.py:498
  (43 shorter events, 3.3 us)
Async XLA Ops:
  0.0 8.5 %copy-start = (f32[3,512,128]{2,1,0:T(8,128)S(1)}, f32[3,512,128]{2,1,0:T(8,128)}, u32[]{:S(2)}) copy-start(f32[3,512,128]{2,1,0:T(8,128)} %param.5) | copy-start | bytes 2359300
  0.0 8.5 %copy-start.1 = (f32[2,512,128]{2,1,0:T(8,128)S(1)}, f32[2,512,128]{2,1,0:T(8,128)}, u32[]{:S(2)}) copy-start(f32[2,512,128]{2,1,0:T(8,128)} %param.4) | copy-start | bytes 1572868
  1.4 7.1 %copy-start.2 = (f32[512,128]{1,0:T(8,128)S(1)}, f32[512,128]{1,0:T(8,128)}, u32[]{:S(2)}) copy-start(f32[512,128]{1,0:T(8,128)} %param.6) | copy-start | bytes 786436
  1.4 11.4 %collective-permute-start.2 = (f32[45,8,128]{2,1,0:T(8,128)S(1)}, f32[45,8,128]{2,1,0:T(8,128)S(1)}, u32[]{:S(2)}, u32[]{:S(2)}) collective-permute-start(f32[45,8,128]{2,1,0:T(8,128)S(1)} %get-tuple-element.107.own_ref.refs_5_), channel_id=1, source_target_pairs={{0,31},{1,2},{2,1},{3,4},{4,3},{5,6},{6,5},{7,8},{8,7},{9,10},{10,... | collective-permute-start | bytes 552968 | tf_op jit(solution)/shard_map/ppermute | solution.py:517
  8.4 6.2 %collective-permute-start = (f32[45,8,128]{2,1,0:T(8,128)S(1)}, f32[45,8,128]{2,1,0:T(8,128)S(1)}, u32[]{:S(2)}, u32[]{:S(2)}) collective-permute-start(f32[45,8,128]{2,1,0:T(8,128)S(1)} %project.3.own_ref.refs_7_), channel_id=1, source_target_pairs={{0,1},{1,0},{2,3},{3,2},{4,5},{5,4},{6,7},{7,6},{8,9},{9,8},{10,11... | collective-permute-start | bytes 552968 | tf_op jit(solution)/shard_map/ppermute | solution.py:518
  12.8 7.1 %collective-permute-start.3 = (f32[14,8,128]{2,1,0:T(8,128)S(1)}, f32[14,8,128]{2,1,0:T(8,128)S(1)}, u32[]{:S(2)}, u32[]{:S(2)}) collective-permute-start(f32[14,8,128]{2,1,0:T(8,128)S(1)} %get-tuple-element.108.own_ref), channel_id=1, source_target_pairs={{0,1},{1,0},{2,3},{3,2},{4,5},{5,4},{6,7},{7,6},{8,9},{9,8},{10,11... | collective-permute-start | bytes 172040 | tf_op jit(solution)/shard_map/ppermute | solution.py:518
  14.6 9.4 %collective-permute-start.1 = (f32[14,8,128]{2,1,0:T(8,128)S(1)}, f32[14,8,128]{2,1,0:T(8,128)S(1)}, u32[]{:S(2)}, u32[]{:S(2)}) collective-permute-start(f32[14,8,128]{2,1,0:T(8,128)S(1)} %get-tuple-element.106.own_ref), channel_id=1, source_target_pairs={{0,31},{1,2},{2,1},{3,4},{4,3},{5,6},{6,5},{7,8},{8,7},{9,10},{10,... | collective-permute-start | bytes 172040 | tf_op jit(solution)/shard_map/ppermute | solution.py:517
  19.9 8.5 %collective-permute-start.6 = (f32[14,8,128]{2,1,0:T(8,128)S(1)}, f32[14,8,128]{2,1,0:T(8,128)S(1)}, u32[]{:S(2)}, u32[]{:S(2)}) collective-permute-start(f32[14,8,128]{2,1,0:T(8,128)S(1)} %get-tuple-element.133.own_ref), channel_id=1, source_target_pairs={{0,31},{1,2},{2,1},{3,4},{4,3},{5,6},{6,5},{7,8},{8,7},{9,10},{10,... | collective-permute-start | bytes 172040 | tf_op jit(solution)/shard_map/ppermute | solution.py:517
  24.1 4.5 %collective-permute-start.4 = (f32[14,8,128]{2,1,0:T(8,128)S(1)}, f32[14,8,128]{2,1,0:T(8,128)S(1)}, u32[]{:S(2)}, u32[]{:S(2)}) collective-permute-start(f32[14,8,128]{2,1,0:T(8,128)S(1)} %get-tuple-element.125.own_ref), channel_id=1, source_target_pairs={{0,1},{1,0},{2,3},{3,2},{4,5},{5,4},{6,7},{7,6},{8,9},{9,8},{10,11... | collective-permute-start | bytes 172040 | tf_op jit(solution)/shard_map/ppermute | solution.py:518
  28.4 4.3 %collective-permute-start.7 = (f32[14,8,128]{2,1,0:T(8,128)S(1)}, f32[14,8,128]{2,1,0:T(8,128)S(1)}, u32[]{:S(2)}, u32[]{:S(2)}) collective-permute-start(f32[14,8,128]{2,1,0:T(8,128)S(1)} %get-tuple-element.135.own_ref), channel_id=1, source_target_pairs={{0,1},{1,0},{2,3},{3,2},{4,5},{5,4},{6,7},{7,6},{8,9},{9,8},{10,11... | collective-permute-start | bytes 172040 | tf_op jit(solution)/shard_map/ppermute | solution.py:518
  28.6 8.7 %collective-permute-start.5 = (f32[14,8,128]{2,1,0:T(8,128)S(1)}, f32[14,8,128]{2,1,0:T(8,128)S(1)}, u32[]{:S(2)}, u32[]{:S(2)}) collective-permute-start(f32[14,8,128]{2,1,0:T(8,128)S(1)} %get-tuple-element.132.own_ref), channel_id=1, source_target_pairs={{0,31},{1,2},{2,1},{3,4},{4,3},{5,6},{6,5},{7,8},{8,7},{9,10},{10,... | collective-permute-start | bytes 172040 | tf_op jit(solution)/shard_map/ppermute | solution.py:517
  32.7 8.5 %collective-permute-start.10 = (f32[14,8,128]{2,1,0:T(8,128)S(1)}, f32[14,8,128]{2,1,0:T(8,128)S(1)}, u32[]{:S(2)}, u32[]{:S(2)}) collective-permute-start(f32[14,8,128]{2,1,0:T(8,128)S(1)} %get-tuple-element.154.own_ref), channel_id=1, source_target_pairs={{0,31},{1,2},{2,1},{3,4},{4,3},{5,6},{6,5},{7,8},{8,7},{9,10},{10,... | collective-permute-start | bytes 172040 | tf_op jit(solution)/shard_map/ppermute | solution.py:517
  37.2 4.3 %collective-permute-start.8 = (f32[14,8,128]{2,1,0:T(8,128)S(1)}, f32[14,8,128]{2,1,0:T(8,128)S(1)}, u32[]{:S(2)}, u32[]{:S(2)}) collective-permute-start(f32[14,8,128]{2,1,0:T(8,128)S(1)} %get-tuple-element.146.own_ref), channel_id=1, source_target_pairs={{0,1},{1,0},{2,3},{3,2},{4,5},{5,4},{6,7},{7,6},{8,9},{9,8},{10,11... | collective-permute-start | bytes 172040 | tf_op jit(solution)/shard_map/ppermute | solution.py:518
  41.2 4.3 %collective-permute-start.11 = (f32[14,8,128]{2,1,0:T(8,128)S(1)}, f32[14,8,128]{2,1,0:T(8,128)S(1)}, u32[]{:S(2)}, u32[]{:S(2)}) collective-permute-start(f32[14,8,128]{2,1,0:T(8,128)S(1)} %get-tuple-element.156.own_ref), channel_id=1, source_target_pairs={{0,1},{1,0},{2,3},{3,2},{4,5},{5,4},{6,7},{7,6},{8,9},{9,8},{10,11... | collective-permute-start | bytes 172040 | tf_op jit(solution)/shard_map/ppermute | solution.py:518
  41.5 8.5 %collective-permute-start.9 = (f32[14,8,128]{2,1,0:T(8,128)S(1)}, f32[14,8,128]{2,1,0:T(8,128)S(1)}, u32[]{:S(2)}, u32[]{:S(2)}) collective-permute-start(f32[14,8,128]{2,1,0:T(8,128)S(1)} %get-tuple-element.153.own_ref), channel_id=1, source_target_pairs={{0,31},{1,2},{2,1},{3,4},{4,3},{5,6},{6,5},{7,8},{8,7},{9,10},{10,... | collective-permute-start | bytes 172040 | tf_op jit(solution)/shard_map/ppermute | solution.py:517
  45.5 8.5 %collective-permute-start.14 = (f32[14,8,128]{2,1,0:T(8,128)S(1)}, f32[14,8,128]{2,1,0:T(8,128)S(1)}, u32[]{:S(2)}, u32[]{:S(2)}) collective-permute-start(f32[14,8,128]{2,1,0:T(8,128)S(1)} %get-tuple-element.175.own_ref), channel_id=1, source_target_pairs={{0,31},{1,2},{2,1},{3,4},{4,3},{5,6},{6,5},{7,8},{8,7},{9,10},{10,... | collective-permute-start | bytes 172040 | tf_op jit(solution)/shard_map/ppermute | solution.py:517
  50.0 4.4 %collective-permute-start.12 = (f32[14,8,128]{2,1,0:T(8,128)S(1)}, f32[14,8,128]{2,1,0:T(8,128)S(1)}, u32[]{:S(2)}, u32[]{:S(2)}) collective-permute-start(f32[14,8,128]{2,1,0:T(8,128)S(1)} %get-tuple-element.167.own_ref), channel_id=1, source_target_pairs={{0,1},{1,0},{2,3},{3,2},{4,5},{5,4},{6,7},{7,6},{8,9},{9,8},{10,11... | collective-permute-start | bytes 172040 | tf_op jit(solution)/shard_map/ppermute | solution.py:518
  54.0 4.4 %collective-permute-start.15 = (f32[14,8,128]{2,1,0:T(8,128)S(1)}, f32[14,8,128]{2,1,0:T(8,128)S(1)}, u32[]{:S(2)}, u32[]{:S(2)}) collective-permute-start(f32[14,8,128]{2,1,0:T(8,128)S(1)} %get-tuple-element.177.own_ref), channel_id=1, source_target_pairs={{0,1},{1,0},{2,3},{3,2},{4,5},{5,4},{6,7},{7,6},{8,9},{9,8},{10,11... | collective-permute-start | bytes 172040 | tf_op jit(solution)/shard_map/ppermute | solution.py:518
  54.5 8.5 %collective-permute-start.13 = (f32[14,8,128]{2,1,0:T(8,128)S(1)}, f32[14,8,128]{2,1,0:T(8,128)S(1)}, u32[]{:S(2)}, u32[]{:S(2)}) collective-permute-start(f32[14,8,128]{2,1,0:T(8,128)S(1)} %get-tuple-element.174.own_ref), channel_id=1, source_target_pairs={{0,31},{1,2},{2,1},{3,4},{4,3},{5,6},{6,5},{7,8},{8,7},{9,10},{10,... | collective-permute-start | bytes 172040 | tf_op jit(solution)/shard_map/ppermute | solution.py:517
  58.4 8.5 %collective-permute-start.17 = (f32[14,8,128]{2,1,0:T(8,128)S(1)}, f32[14,8,128]{2,1,0:T(8,128)S(1)}, u32[]{:S(2)}, u32[]{:S(2)}) collective-permute-start(f32[14,8,128]{2,1,0:T(8,128)S(1)} %get-tuple-element.194.own_ref), channel_id=1, source_target_pairs={{0,31},{1,2},{2,1},{3,4},{4,3},{5,6},{6,5},{7,8},{8,7},{9,10},{10,... | collective-permute-start | bytes 172040 | tf_op jit(solution)/shard_map/ppermute | solution.py:517
  63.0 4.3 %collective-permute-start.16 = (f32[14,8,128]{2,1,0:T(8,128)S(1)}, f32[14,8,128]{2,1,0:T(8,128)S(1)}, u32[]{:S(2)}, u32[]{:S(2)}) collective-permute-start(f32[14,8,128]{2,1,0:T(8,128)S(1)} %get-tuple-element.188.own_ref), channel_id=1, source_target_pairs={{0,1},{1,0},{2,3},{3,2},{4,5},{5,4},{6,7},{7,6},{8,9},{9,8},{10,11... | collective-permute-start | bytes 172040 | tf_op jit(solution)/shard_map/ppermute | solution.py:518

commit v6 on v5

--- a/solution.py
+++ b/solution.py
@@ -146,17 +146,19 @@
     return [plane_sum(plane, tables, ROWS) for plane in planes + [weight]]
 
 
-def project_odd(order_ref, scal_ref, mass_ref, tr_ref, od_ref, idx_ref, slot_ref, far_ref,
+def project_odd(order_ref, scal_ref, mass_ref, tr_ref, od_ref, idx_ref, slot_ref, raw_ref,
                 order_buf, near_buf, sems):
     parity = lax.axis_index("elem") % 2
     near, far = source_plane(parity, 0), source_plane(parity, ORDER)
     copies = [pltpu.make_async_copy(order_ref, order_buf, sems.at[0])]
-    late = []
-    for side, (plane, buf, group) in enumerate(((near, near_buf, copies), (far, far_ref, late))):
-        sources = [scal_ref.at[0, plane], scal_ref.at[1, plane], mass_ref.at[plane]]
-        sources += [tr_ref.at[r, plane] for r in range(3)]
-        for r, source in enumerate(sources):
-            group.append(pltpu.make_async_copy(source, buf.at[r], sems.at[1 + 6 * side + r]))
+    for r, source in enumerate((scal_ref.at[0, near], scal_ref.at[1, near], mass_ref.at[near])):
+        copies.append(pltpu.make_async_copy(source, near_buf.at[r], sems.at[1 + r]))
+    sources = [scal_ref.at[0, far], scal_ref.at[1, far], mass_ref.at[far]]
+    sources += [tr_ref.at[r, far] for r in range(3)] + [tr_ref.at[r, near] for r in range(3)]
+    late = [
+        pltpu.make_async_copy(source, raw_ref.at[r], sems.at[4 + r])
+        for r, source in enumerate(sources)
+    ]
     for copy in copies + late:
         copy.start()
     tables = third_tables()
@@ -166,7 +168,8 @@
     slot_ref[...] = jnp.broadcast_to(order_buf[...], (SUB, LANES))
     for copy in copies[1:]:
         copy.wait()
-    send_projection(near_buf, idx, tables, signs_of(parity), od_ref)
+    planes = project(read(near_buf, 2), [read(near_buf, m) for m in range(2)], idx, tables)
+    write(od_ref, (), sum(planes, []))
     for copy in late:
         copy.wait()
 
@@ -176,16 +179,13 @@
     return first, np.float32(-time_step), np.float32(-time_step)
 
 
-def send_projection(planes_ref, idx, tables, signs, out_ref):
-    planes = project(read(planes_ref, 2), [read(planes_ref, m) for m in range(2)], idx, tables)
-    planes.extend(
-        [gather_lanes(v, idx) * signs[r] for v in read(planes_ref, 3 + r)] for r in range(3))
-    write(out_ref, (), sum(planes, []))
-
-
-def project_even(idx_ref, far_ref, ev_ref):
+def project_even(idx_ref, raw_ref, ev_ref, tf_ref):
+    idx = idx_ref[...]
     signs = signs_of(lax.axis_index("elem") % 2)
-    send_projection(far_ref, idx_ref[...], third_tables(), signs, ev_ref)
+    planes = project(read(raw_ref, 2), [read(raw_ref, m) for m in range(2)], idx, third_tables())
+    turned = [[gather_lanes(v, idx) * signs[r % 3] for v in read(raw_ref, 3 + r)] for r in range(6)]
+    write(ev_ref, (), sum(planes + turned[:3], []))
+    write(tf_ref, (), sum(turned[3:], []))
 
 
 def prepare(idx_ref, scal_ref, mass_ref, tr_ref,
@@ -360,11 +360,12 @@
         tables = third_tables()
         rot = rotations()
         if start:
-            od_ref, rod_ref, ev_ref, rev_ref, st_ref, r0_ref, ri_ref, ti_ref = refs[5:13]
+            tf_ref, rtf_ref, ev_ref, rev_ref, st_ref, r0_ref, ri_ref, ti_ref = refs[5:13]
             gn_ref, an_ref, q_ref, e7_ref, a0_ref, a7_ref, rs_ref, wp_ref = refs[13:]
             inner_open(gi_ref, ri_ref, rt_ref, ti_ref, rot, wp_ref)
-            for own, got, out in ((od_ref, rod_ref, a0_ref), (ev_ref, rev_ref, a7_ref)):
-                both_sides(transports(own, 3 * ROWS), transports(got, 3 * ROWS), tables, out)
+            both_sides(transports(tf_ref, 0), transports(rtf_ref, 0), tables, a0_ref)
+            both_sides(
+                transports(ev_ref, 3 * ROWS), transports(rev_ref, 3 * ROWS), tables, a7_ref)
             write(rs_ref, (0,), [st_ref[0, j] * r0_ref[j] for j in range(ROWS)])
             write(rs_ref, (1,), [st_ref[1, j] * r7_ref[j] for j in range(ROWS)])
         else:
@@ -528,14 +529,14 @@
 
     stay = lambda x: pltpu.with_memory_space_constraint(x, pltpu.HBM)
     bundle = (3 * ROWS + 24, SUB, LANES)
-    od, idx, slots, far = call(
-        project_odd, [bundle, (SUB, LANES), (SUB, LANES), (6,) + tile],
+    od, idx, slots, raw = call(
+        project_odd, [(3 * ROWS, SUB, LANES), (SUB, LANES), (SUB, LANES), (9,) + tile],
         (stay(element_order), stay(scal), stay(mas), stay(tr)), "project", 1, hbm=(0, 1, 2, 3),
-        scratch=[pltpu.VMEM((1, LANES), jnp.int32), pltpu.VMEM((6,) + tile, f32),
+        scratch=[pltpu.VMEM((1, LANES), jnp.int32), pltpu.VMEM((3,) + tile, f32),
                  pltpu.SemaphoreType.DMA((13,))])
     rod = swap_od(od)
-    ev = call(project_even, [bundle], (idx, far), "project", 1)
-    rev = swap_ev(ev)
+    ev, tf = call(project_even, [bundle, (24, SUB, LANES)], (idx, raw), "project", 1)
+    rev, rtf = swap_ev(ev), swap_od(tf)
     gi, q, ri, rt, ti, st = call(
         prepare, [inner, faces, (6,) + tile, (6,) + tile, (6, 2) + tile, (2,) + part],
         (idx, scal, mas, tr), "prepare", 1)
@@ -547,7 +548,7 @@
         s = 2 * n % STAGES + 1
         opening, closing, early = s == 1, s + 1 == STAGES, n == 0
         got_ev, got_od = swap_ev(cev), swap_od(cod)
-        extra = (od, rod, ev, rev, st, r0, ri, ti) if early else (acci, wp, a7)
+        extra = (tf, rtf, ev, rev, st, r0, ri, ti) if early else (acci, wp, a7)
         res = call(
             make_first_inner(1.0 / s, opening, early),
             [inner, inner, faces, face] + ([geometry, geometry, (2,) + part] if early else []),

time: 68.3 us -> 67.4 us (0.987)
  waiting for transfers between devices: 16.8 us -> 15.3 us
    ppermute x9 -> x10, waiting for transfers between devices: 14.5 us -> 12.1 us  [per_device(): swap_od = lambda x: lax.ppermute(x, 'elem', odd_pairs)]
    ppermute x9, waiting for transfers between devices: 2.29 us -> 3.28 us  [per_device(): swap_ev = lambda x: lax.ppermute(x, 'elem', even_pairs)]
    ppermute x9 -> x10, starting transfers between devices: 34.6 us -> 34.7 us  [per_device(): swap_od = lambda x: lax.ppermute(x, 'elem', odd_pairs)]
  transfers between devices with their start and end apart: 18 -> 19, of which waited for: 13 -> 15; matrix products, arithmetic and copies ran while one was open for 0% -> 0% of each run, Pallas kernels for 19% -> 20%
where the time goes in v6:
time: 67.4 us; the launch traced here: 67.3 us
  starting transfers between devices  36.3 us (54%)
  Pallas kernels  15.3 us (23%)
  waiting for transfers between devices  15.3 us (23%)
    ppermute x10, starting transfers between devices, per_device(): swap_od = lambda x: lax.ppermute(x, 'elem', odd_pairs)  34.7 us
    pallas_call x33, Pallas kernels, call(): pl.pallas_call(kernel, out_shape=shapes[0] if single else shapes, in_spec...  15.3 us
    ppermute x10, waiting for transfers between devices, per_device(): swap_od = lambda x: lax.ppermute(x, 'elem', odd_pairs)  12.1 us
    ppermute x9, waiting for transfers between devices, per_device(): swap_ev = lambda x: lax.ppermute(x, 'elem', even_pairs)  3.28 us
    ppermute x9, starting transfers between devices, per_device(): swap_ev = lambda x: lax.ppermute(x, 'elem', even_pairs)  1.6 us
  transfers between devices with their start and end apart: 19, of which 15 were waited for; matrix products, arithmetic and copies ran while one was open for 0% of the time, Pallas kernels for 20%

profile of v6, /device:TPU:0, one launch (start us, length us, event | category | flops | bytes accessed | tf_op | source)
XLA Modules:
  0.0 67.3 jit_solution(1944254685402495165)
XLA Ops:
  0.0 1.3 %project.2 = (f32[21,8,128]{2,1,0:T(8,128)S(1)}, s32[8,128]{1,0:T(8,128)S(1)}, s32[8,128]{1,0:T(8,128)S(1)}, f32[9,8,8,128]{3,2,1,0:T(8,128)S(1)}) custom-call(s32[1,128]{1,0:T(1,128)} %order_ref.1, f32[2,8,8,8,128]{4,3,2,1,0:T(8,128)} %bitcast.6, f32[8,8,8,128]{3,2,1,0:T(8,128)} %bitcast.8, f32[3,8,8,8,128]{4,3,2,1,0:T(8,128)} %bitcast.4), custom_call_target="tpu_custom_call" | custom-call | flops 1000000 | bytes 1024 | tf_op jit(solution)/shard_map/project/pallas_call | solution.py:499
  1.4 6.7 %collective-permute-start.2 = (f32[21,8,128]{2,1,0:T(8,128)S(1)}, f32[21,8,128]{2,1,0:T(8,128)S(1)}, u32[]{:S(2)}, u32[]{:S(2)}) collective-permute-start(f32[21,8,128]{2,1,0:T(8,128)S(1)} %get-tuple-element.110.own_ref), channel_id=1, source_target_pairs={{0,31},{1,2},{2,1},{3,4},{4,3},{5,6},{6,5},{7,8},{8,7},{9,10},{10,... | collective-permute-start | bytes 258056 | tf_op jit(solution)/shard_map/ppermute | solution.py:518
  8.4 1.4 %collective-permute-start.4 = (f32[24,8,128]{2,1,0:T(8,128)S(1)}, f32[24,8,128]{2,1,0:T(8,128)S(1)}, u32[]{:S(2)}, u32[]{:S(2)}) collective-permute-start(f32[24,8,128]{2,1,0:T(8,128)S(1)} %get-tuple-element.117.refs_5_), channel_id=1, source_target_pairs={{0,31},{1,2},{2,1},{3,4},{4,3},{5,6},{6,5},{7,8},{8,7},{9,10},{10,... | collective-permute-start | bytes 294920 | tf_op jit(solution)/shard_map/ppermute | solution.py:518
  9.8 2.6 %prepare.1 = (f32[2,6,8,8,128]{4,3,2,1,0:T(8,128)S(1)}, f32[2,2,7,8,128]{4,3,2,1,0:T(8,128)S(1)}, f32[6,8,8,128]{3,2,1,0:T(8,128)S(1)}, f32[6,8,8,128]{3,2,1,0:T...) custom-call(s32[8,128]{1,0:T(8,128)S(1)} %get-tuple-element.104.idx_ref, ...), custom_call_target="tpu_custom_call" | custom-call | flops 1000000 | bytes 1024 | tf_op jit(solution)/shard_map/prepare/pallas_call | solution.py:499
  12.4 0.8 %collective-permute-start.3 = (f32[14,8,128]{2,1,0:T(8,128)S(1)}, f32[14,8,128]{2,1,0:T(8,128)S(1)}, u32[]{:S(2)}, u32[]{:S(2)}) collective-permute-start(f32[14,8,128]{2,1,0:T(8,128)S(1)} %get-tuple-element.111.own_ref), channel_id=1, source_target_pairs={{0,1},{1,0},{2,3},{3,2},{4,5},{5,4},{6,7},{7,6},{8,9},{9,8},{10,11... | collective-permute-start | bytes 172040 | tf_op jit(solution)/shard_map/ppermute | solution.py:519
  13.2 1.7 %collective-permute-done.got_ref.refs_8_ = f32[45,8,128]{2,1,0:T(8,128)S(1)} collective-permute-done((f32[45,8,128]{2,1,0:T(8,128)S(1)}, f32[45,8,128]{2,1,0:T(8,128)S(1)}, u32[]{:S(2)}, u32[]{:S(2)}) %collective-permute-start) | collective-permute-done | bytes 184352 | tf_op jit(solution)/shard_map/ppermute | solution.py:519
  14.9 3.0 %collective-permute-start.1 = (f32[14,8,128]{2,1,0:T(8,128)S(1)}, f32[14,8,128]{2,1,0:T(8,128)S(1)}, u32[]{:S(2)}, u32[]{:S(2)}) collective-permute-start(f32[14,8,128]{2,1,0:T(8,128)S(1)} %get-tuple-element.109.own_ref), channel_id=1, source_target_pairs={{0,31},{1,2},{2,1},{3,4},{4,3},{5,6},{6,5},{7,8},{8,7},{9,10},{10,... | collective-permute-start | bytes 172040 | tf_op jit(solution)/shard_map/ppermute | solution.py:518
  17.9 1.0 %first.4 = (f32[2,6,8,8,128]{4,3,2,1,0:T(8,128)S(1)}, f32[2,6,8,8,128]{4,3,2,1,0:T(8,128)S(1)}, f32[2,2,7,8,128]{4,3,2,1,0:T(8,128)S(1)}, f32[2,7,8,128]{3,2,1,0...) custom-call(f32[2,7,8,128]{3,2,1,0:T(8,128)S(1)} %get-tuple-element.112.refs, ...), custom_call_target="tpu_custom_call" | custom-call | flops 1000000000 | bytes 1024 | tf_op jit(solution)/shard_map/first/pallas_call | solution.py:499
  18.9 3.4 %collective-permute-start.7 = (f32[14,8,128]{2,1,0:T(8,128)S(1)}, f32[14,8,128]{2,1,0:T(8,128)S(1)}, u32[]{:S(2)}, u32[]{:S(2)}) collective-permute-start(f32[14,8,128]{2,1,0:T(8,128)S(1)} %get-tuple-element.137.own_ref), channel_id=1, source_target_pairs={{0,31},{1,2},{2,1},{3,4},{4,3},{5,6},{6,5},{7,8},{8,7},{9,10},{10,... | collective-permute-start | bytes 172040 | tf_op jit(solution)/shard_map/ppermute | solution.py:518
  22.3 0.9 %between.4 = (f32[2,6,8,8,128]{4,3,2,1,0:T(8,128)S(1)}, f32[2,7,8,128]{3,2,1,0:T(8,128)S(1)}, f32[2,7,8,128]{3,2,1,0:T(8,128)S(1)}) custom-call(f32[2,7,8,128]{3,2,1,0:T(8,128)S(1)} %get-tuple-element.124.m7_ref, f32[2,6,8,8,128]{4,3,2,1,0:T(8,128)S(1)} %get-tuple-element.125.gi_ref, f32[3,8,8,128]{3,2,1,0:T(8,128)S(1)} %get-tuple-element.126.a7_ref.refs_7_, ...), custom_call_target="tpu_custom_call" | custom-call | flops 2000000000 | bytes 1024 | tf_op jit(solution)/shard_map/between/pallas_call | solution.py:499
  23.5 1.0 %second.3 = (f32[2,6,8,8,128]{4,3,2,1,0:T(8,128)S(1)}, f32[2,2,7,8,128]{4,3,2,1,0:T(8,128)S(1)}, f32[2,6,8,8,128]{4,3,2,1,0:T(8,128)S(1)}, f32[2,2,7,8,128]{4,3,...) custom-call(f32[2,7,8,128]{3,2,1,0:T(8,128)S(1)} %get-tuple-element.131.m0_ref, ...), custom_call_target="tpu_custom_call" | custom-call | flops 3000000000 | bytes 1024 | tf_op jit(solution)/shard_map/second/pallas_call | solution.py:499
  24.5 2.9 %collective-permute-done.7.got_ref = f32[14,8,128]{2,1,0:T(8,128)S(1)} collective-permute-done((f32[14,8,128]{2,1,0:T(8,128)S(1)}, f32[14,8,128]{2,1,0:T(8,128)S(1)}, u32[]{:S(2)}, u32[]{:S(2)}) %collective-permute-start.7) | collective-permute-done | bytes 57376 | tf_op jit(solution)/shard_map/ppermute | solution.py:518
  27.8 3.2 %collective-permute-start.6 = (f32[14,8,128]{2,1,0:T(8,128)S(1)}, f32[14,8,128]{2,1,0:T(8,128)S(1)}, u32[]{:S(2)}, u32[]{:S(2)}) collective-permute-start(f32[14,8,128]{2,1,0:T(8,128)S(1)} %get-tuple-element.136.own_ref), channel_id=1, source_target_pairs={{0,31},{1,2},{2,1},{3,4},{4,3},{5,6},{6,5},{7,8},{8,7},{9,10},{10,... | collective-permute-start | bytes 172040 | tf_op jit(solution)/shard_map/ppermute | solution.py:518
  31.0 0.4 first.5
  31.7 3.4 %collective-permute-start.11 = (f32[14,8,128]{2,1,0:T(8,128)S(1)}, f32[14,8,128]{2,1,0:T(8,128)S(1)}, u32[]{:S(2)}, u32[]{:S(2)}) collective-permute-start(f32[14,8,128]{2,1,0:T(8,128)S(1)} %get-tuple-element.158.own_ref), channel_id=1, source_target_pairs={{0,31},{1,2},{2,1},{3,4},{4,3},{5,6},{6,5},{7,8},{8,7},{9,10},{10,... | collective-permute-start | bytes 172040 | tf_op jit(solution)/shard_map/ppermute | solution.py:518
  35.1 0.9 %between.5 = (f32[2,6,8,8,128]{4,3,2,1,0:T(8,128)S(1)}, f32[2,7,8,128]{3,2,1,0:T(8,128)S(1)}, f32[2,7,8,128]{3,2,1,0:T(8,128)S(1)}) custom-call(f32[2,7,8,128]{3,2,1,0:T(8,128)S(1)} %get-tuple-element.147.m7_ref, f32[2,6,8,8,128]{4,3,2,1,0:T(8,128)S(1)} %get-tuple-element.148.gi_ref, f32[3,8,8,128]{3,2,1,0:T(8,128)S(1)} %get-tuple-element.126.a7_ref.refs_7_, ...), custom_call_target="tpu_custom_call" | custom-call | flops 2000000000 | bytes 1024 | tf_op jit(solution)/shard_map/between/pallas_call | solution.py:499
  36.4 1.0 %second.4 = (f32[2,6,8,8,128]{4,3,2,1,0:T(8,128)S(1)}, f32[2,2,7,8,128]{4,3,2,1,0:T(8,128)S(1)}, f32[2,6,8,8,128]{4,3,2,1,0:T(8,128)S(1)}, f32[2,2,7,8,128]{4,3,...) custom-call(f32[2,7,8,128]{3,2,1,0:T(8,128)S(1)} %get-tuple-element.152.m0_ref, ...), custom_call_target="tpu_custom_call" | custom-call | flops 3000000000 | bytes 1024 | tf_op jit(solution)/shard_map/second/pallas_call | solution.py:499
  37.4 2.8 %collective-permute-done.11.got_ref = f32[14,8,128]{2,1,0:T(8,128)S(1)} collective-permute-done((f32[14,8,128]{2,1,0:T(8,128)S(1)}, f32[14,8,128]{2,1,0:T(8,128)S(1)}, u32[]{:S(2)}, u32[]{:S(2)}) %collective-permute-start.11) | collective-permute-done | bytes 57376 | tf_op jit(solution)/shard_map/ppermute | solution.py:518
  40.6 3.5 %collective-permute-start.10 = (f32[14,8,128]{2,1,0:T(8,128)S(1)}, f32[14,8,128]{2,1,0:T(8,128)S(1)}, u32[]{:S(2)}, u32[]{:S(2)}) collective-permute-start(f32[14,8,128]{2,1,0:T(8,128)S(1)} %get-tuple-element.157.own_ref), channel_id=1, source_target_pairs={{0,31},{1,2},{2,1},{3,4},{4,3},{5,6},{6,5},{7,8},{8,7},{9,10},{10,... | collective-permute-start | bytes 172040 | tf_op jit(solution)/shard_map/ppermute | solution.py:518
  44.5 3.4 %collective-permute-start.15 = (f32[14,8,128]{2,1,0:T(8,128)S(1)}, f32[14,8,128]{2,1,0:T(8,128)S(1)}, u32[]{:S(2)}, u32[]{:S(2)}) collective-permute-start(f32[14,8,128]{2,1,0:T(8,128)S(1)} %get-tuple-element.179.own_ref), channel_id=1, source_target_pairs={{0,31},{1,2},{2,1},{3,4},{4,3},{5,6},{6,5},{7,8},{8,7},{9,10},{10,... | collective-permute-start | bytes 172040 | tf_op jit(solution)/shard_map/ppermute | solution.py:518
  47.9 0.9 %between.6 = (f32[2,6,8,8,128]{4,3,2,1,0:T(8,128)S(1)}, f32[2,7,8,128]{3,2,1,0:T(8,128)S(1)}, f32[2,7,8,128]{3,2,1,0:T(8,128)S(1)}) custom-call(f32[2,7,8,128]{3,2,1,0:T(8,128)S(1)} %get-tuple-element.168.m7_ref, f32[2,6,8,8,128]{4,3,2,1,0:T(8,128)S(1)} %get-tuple-element.169.gi_ref, f32[3,8,8,128]{3,2,1,0:T(8,128)S(1)} %get-tuple-element.126.a7_ref.refs_7_, ...), custom_call_target="tpu_custom_call" | custom-call | flops 2000000000 | bytes 1024 | tf_op jit(solution)/shard_map/between/pallas_call | solution.py:499
  49.4 1.0 %second.5 = (f32[2,6,8,8,128]{4,3,2,1,0:T(8,128)S(1)}, f32[2,2,7,8,128]{4,3,2,1,0:T(8,128)S(1)}, f32[2,6,8,8,128]{4,3,2,1,0:T(8,128)S(1)}, f32[2,2,7,8,128]{4,3,...) custom-call(f32[2,7,8,128]{3,2,1,0:T(8,128)S(1)} %get-tuple-element.173.m0_ref, ...), custom_call_target="tpu_custom_call" | custom-call | flops 3000000000 | bytes 1024 | tf_op jit(solution)/shard_map/second/pallas_call | solution.py:499
  50.3 2.6 %collective-permute-done.15.got_ref = f32[14,8,128]{2,1,0:T(8,128)S(1)} collective-permute-done((f32[14,8,128]{2,1,0:T(8,128)S(1)}, f32[14,8,128]{2,1,0:T(8,128)S(1)}, u32[]{:S(2)}, u32[]{:S(2)}) %collective-permute-start.15) | collective-permute-done | bytes 57376 | tf_op jit(solution)/shard_map/ppermute | solution.py:518
  53.1 0.4 collective-permute-done.13.got_ref
  53.6 3.5 %collective-permute-start.14 = (f32[14,8,128]{2,1,0:T(8,128)S(1)}, f32[14,8,128]{2,1,0:T(8,128)S(1)}, u32[]{:S(2)}, u32[]{:S(2)}) collective-permute-start(f32[14,8,128]{2,1,0:T(8,128)S(1)} %get-tuple-element.178.own_ref), channel_id=1, source_target_pairs={{0,31},{1,2},{2,1},{3,4},{4,3},{5,6},{6,5},{7,8},{8,7},{9,10},{10,... | collective-permute-start | bytes 172040 | tf_op jit(solution)/shard_map/ppermute | solution.py:518
  57.0 0.4 first.7
  57.4 3.3 %collective-permute-start.18 = (f32[14,8,128]{2,1,0:T(8,128)S(1)}, f32[14,8,128]{2,1,0:T(8,128)S(1)}, u32[]{:S(2)}, u32[]{:S(2)}) collective-permute-start(f32[14,8,128]{2,1,0:T(8,128)S(1)} %get-tuple-element.198.own_ref), channel_id=1, source_target_pairs={{0,31},{1,2},{2,1},{3,4},{4,3},{5,6},{6,5},{7,8},{8,7},{9,10},{10,... | collective-permute-start | bytes 172040 | tf_op jit(solution)/shard_map/ppermute | solution.py:518
  60.7 0.9 %between.7 = (f32[2,6,8,8,128]{4,3,2,1,0:T(8,128)S(1)}, f32[2,7,8,128]{3,2,1,0:T(8,128)S(1)}, f32[2,7,8,128]{3,2,1,0:T(8,128)S(1)}) custom-call(f32[2,7,8,128]{3,2,1,0:T(8,128)S(1)} %get-tuple-element.189.m7_ref, f32[2,6,8,8,128]{4,3,2,1,0:T(8,128)S(1)} %get-tuple-element.190.gi_ref, f32[3,8,8,128]{3,2,1,0:T(8,128)S(1)} %get-tuple-element.126.a7_ref.refs_7_, ...), custom_call_target="tpu_custom_call" | custom-call | flops 2000000000 | bytes 1024 | tf_op jit(solution)/shard_map/between/pallas_call | solution.py:499
  61.6 0.4 collective-permute-done.14.got_ref
  62.1 1.2 %last.1 = (f32[2,8,8,8,128]{4,3,2,1,0:T(8,128)}, f32[2,2,7,8,128]{4,3,2,1,0:T(8,128)S(1)}, f32[2,7,8,128]{3,2,1,0:T(8,128)S(1)}) custom-call(s32[8,128]{1,0:T(8,128)S(1)} %get-tuple-element.103.slot_ref, f32[2,7,8,128]{3,2,1,0:T(8,128)S(1)} %get-tuple-element.194.m0_ref, f32[2,7,8,128]{3,2,1,0:T(8,128)S(1)} %get-tuple-element.189.m7_ref, ...), custom_call_target="tpu_custom_call" | custom-call | flops 3000000000 | bytes 1024 | tf_op jit(solution)/shard_map/last/pallas_call | solution.py:499
  63.3 2.6 %collective-permute-done.18.got_ref = f32[14,8,128]{2,1,0:T(8,128)S(1)} collective-permute-done((f32[14,8,128]{2,1,0:T(8,128)S(1)}, f32[14,8,128]{2,1,0:T(8,128)S(1)}, u32[]{:S(2)}, u32[]{:S(2)}) %collective-permute-start.18) | collective-permute-done | bytes 57376 | tf_op jit(solution)/shard_map/ppermute | solution.py:518
  66.3 0.8 %finish.3 = f32[2,8,8,8,128]{4,3,2,1,0:T(8,128)} custom-call(s32[8,128]{1,0:T(8,128)S(1)} %get-tuple-element.103.slot_ref, f32[14,8,128]{2,1,0:T(8,128)S(1)} %get-tuple-element.192.own_ref, f32[14,8,128]{2,1,0:T(8,128)S(1)} %collective-permute-done.17.got_ref, f32[2,7,8,128]{3,2,1,0:T(8,128)S(1)} %get-tuple-element.193.e_ref, ...), custom_call_target="tpu_custom_call", output_to_operand_aliasing={{}: (6, {})} | custom-call | flops 1000000 | bytes 1024 | tf_op jit(solution)/shard_map/finish/pallas_call | solution.py:499
  (45 shorter events, 3.9 us)
Async XLA Ops:
  0.0 9.8 %copy-start = (f32[3,512,128]{2,1,0:T(8,128)S(1)}, f32[3,512,128]{2,1,0:T(8,128)}, u32[]{:S(2)}) copy-start(f32[3,512,128]{2,1,0:T(8,128)} %param.5) | copy-start | bytes 2359300
  0.0 9.8 %copy-start.1 = (f32[2,512,128]{2,1,0:T(8,128)S(1)}, f32[2,512,128]{2,1,0:T(8,128)}, u32[]{:S(2)}) copy-start(f32[2,512,128]{2,1,0:T(8,128)} %param.4) | copy-start | bytes 1572868
  1.3 8.5 %copy-start.2 = (f32[512,128]{1,0:T(8,128)S(1)}, f32[512,128]{1,0:T(8,128)}, u32[]{:S(2)}) copy-start(f32[512,128]{1,0:T(8,128)} %param.6) | copy-start | bytes 786436
  1.4 11.0 %collective-permute-start.2 = (f32[21,8,128]{2,1,0:T(8,128)S(1)}, f32[21,8,128]{2,1,0:T(8,128)S(1)}, u32[]{:S(2)}, u32[]{:S(2)}) collective-permute-start(f32[21,8,128]{2,1,0:T(8,128)S(1)} %get-tuple-element.110.own_ref), channel_id=1, source_target_pairs={{0,31},{1,2},{2,1},{3,4},{4,3},{5,6},{6,5},{7,8},{8,7},{9,10},{10,... | collective-permute-start | bytes 258056 | tf_op jit(solution)/shard_map/ppermute | solution.py:518
  8.4 6.5 %collective-permute-start = (f32[45,8,128]{2,1,0:T(8,128)S(1)}, f32[45,8,128]{2,1,0:T(8,128)S(1)}, u32[]{:S(2)}, u32[]{:S(2)}) collective-permute-start(f32[45,8,128]{2,1,0:T(8,128)S(1)} %get-tuple-element.106.own_ref.refs_7_), channel_id=1, source_target_pairs={{0,1},{1,0},{2,3},{3,2},{4,5},{5,4},{6,7},{7,6},{8,9},{9,8},{10,11... | collective-permute-start | bytes 552968 | tf_op jit(solution)/shard_map/ppermute | solution.py:519
  8.4 9.5 %collective-permute-start.4 = (f32[24,8,128]{2,1,0:T(8,128)S(1)}, f32[24,8,128]{2,1,0:T(8,128)S(1)}, u32[]{:S(2)}, u32[]{:S(2)}) collective-permute-start(f32[24,8,128]{2,1,0:T(8,128)S(1)} %get-tuple-element.117.refs_5_), channel_id=1, source_target_pairs={{0,31},{1,2},{2,1},{3,4},{4,3},{5,6},{6,5},{7,8},{8,7},{9,10},{10,... | collective-permute-start | bytes 294920 | tf_op jit(solution)/shard_map/ppermute | solution.py:518
  12.4 6.4 %collective-permute-start.3 = (f32[14,8,128]{2,1,0:T(8,128)S(1)}, f32[14,8,128]{2,1,0:T(8,128)S(1)}, u32[]{:S(2)}, u32[]{:S(2)}) collective-permute-start(f32[14,8,128]{2,1,0:T(8,128)S(1)} %get-tuple-element.111.own_ref), channel_id=1, source_target_pairs={{0,1},{1,0},{2,3},{3,2},{4,5},{5,4},{6,7},{7,6},{8,9},{9,8},{10,11... | collective-permute-start | bytes 172040 | tf_op jit(solution)/shard_map/ppermute | solution.py:519
  14.9 8.5 %collective-permute-start.1 = (f32[14,8,128]{2,1,0:T(8,128)S(1)}, f32[14,8,128]{2,1,0:T(8,128)S(1)}, u32[]{:S(2)}, u32[]{:S(2)}) collective-permute-start(f32[14,8,128]{2,1,0:T(8,128)S(1)} %get-tuple-element.109.own_ref), channel_id=1, source_target_pairs={{0,31},{1,2},{2,1},{3,4},{4,3},{5,6},{6,5},{7,8},{8,7},{9,10},{10,... | collective-permute-start | bytes 172040 | tf_op jit(solution)/shard_map/ppermute | solution.py:518
  18.9 8.5 %collective-permute-start.7 = (f32[14,8,128]{2,1,0:T(8,128)S(1)}, f32[14,8,128]{2,1,0:T(8,128)S(1)}, u32[]{:S(2)}, u32[]{:S(2)}) collective-permute-start(f32[14,8,128]{2,1,0:T(8,128)S(1)} %get-tuple-element.137.own_ref), channel_id=1, source_target_pairs={{0,31},{1,2},{2,1},{3,4},{4,3},{5,6},{6,5},{7,8},{8,7},{9,10},{10,... | collective-permute-start | bytes 172040 | tf_op jit(solution)/shard_map/ppermute | solution.py:518
  23.4 4.4 %collective-permute-start.5 = (f32[14,8,128]{2,1,0:T(8,128)S(1)}, f32[14,8,128]{2,1,0:T(8,128)S(1)}, u32[]{:S(2)}, u32[]{:S(2)}) collective-permute-start(f32[14,8,128]{2,1,0:T(8,128)S(1)} %get-tuple-element.129.own_ref), channel_id=1, source_target_pairs={{0,1},{1,0},{2,3},{3,2},{4,5},{5,4},{6,7},{7,6},{8,9},{9,8},{10,11... | collective-permute-start | bytes 172040 | tf_op jit(solution)/shard_map/ppermute | solution.py:519
  27.4 4.3 %collective-permute-start.8 = (f32[14,8,128]{2,1,0:T(8,128)S(1)}, f32[14,8,128]{2,1,0:T(8,128)S(1)}, u32[]{:S(2)}, u32[]{:S(2)}) collective-permute-start(f32[14,8,128]{2,1,0:T(8,128)S(1)} %get-tuple-element.139.own_ref), channel_id=1, source_target_pairs={{0,1},{1,0},{2,3},{3,2},{4,5},{5,4},{6,7},{7,6},{8,9},{9,8},{10,11... | collective-permute-start | bytes 172040 | tf_op jit(solution)/shard_map/ppermute | solution.py:519
  27.8 8.5 %collective-permute-start.6 = (f32[14,8,128]{2,1,0:T(8,128)S(1)}, f32[14,8,128]{2,1,0:T(8,128)S(1)}, u32[]{:S(2)}, u32[]{:S(2)}) collective-permute-start(f32[14,8,128]{2,1,0:T(8,128)S(1)} %get-tuple-element.136.own_ref), channel_id=1, source_target_pairs={{0,31},{1,2},{2,1},{3,4},{4,3},{5,6},{6,5},{7,8},{8,7},{9,10},{10,... | collective-permute-start | bytes 172040 | tf_op jit(solution)/shard_map/ppermute | solution.py:518
  31.7 8.5 %collective-permute-start.11 = (f32[14,8,128]{2,1,0:T(8,128)S(1)}, f32[14,8,128]{2,1,0:T(8,128)S(1)}, u32[]{:S(2)}, u32[]{:S(2)}) collective-permute-start(f32[14,8,128]{2,1,0:T(8,128)S(1)} %get-tuple-element.158.own_ref), channel_id=1, source_target_pairs={{0,31},{1,2},{2,1},{3,4},{4,3},{5,6},{6,5},{7,8},{8,7},{9,10},{10,... | collective-permute-start | bytes 172040 | tf_op jit(solution)/shard_map/ppermute | solution.py:518
  36.3 4.3 %collective-permute-start.9 = (f32[14,8,128]{2,1,0:T(8,128)S(1)}, f32[14,8,128]{2,1,0:T(8,128)S(1)}, u32[]{:S(2)}, u32[]{:S(2)}) collective-permute-start(f32[14,8,128]{2,1,0:T(8,128)S(1)} %get-tuple-element.150.own_ref), channel_id=1, source_target_pairs={{0,1},{1,0},{2,3},{3,2},{4,5},{5,4},{6,7},{7,6},{8,9},{9,8},{10,11... | collective-permute-start | bytes 172040 | tf_op jit(solution)/shard_map/ppermute | solution.py:519
  40.2 4.3 %collective-permute-start.12 = (f32[14,8,128]{2,1,0:T(8,128)S(1)}, f32[14,8,128]{2,1,0:T(8,128)S(1)}, u32[]{:S(2)}, u32[]{:S(2)}) collective-permute-start(f32[14,8,128]{2,1,0:T(8,128)S(1)} %get-tuple-element.160.own_ref), channel_id=1, source_target_pairs={{0,1},{1,0},{2,3},{3,2},{4,5},{5,4},{6,7},{7,6},{8,9},{9,8},{10,11... | collective-permute-start | bytes 172040 | tf_op jit(solution)/shard_map/ppermute | solution.py:519
  40.6 8.5 %collective-permute-start.10 = (f32[14,8,128]{2,1,0:T(8,128)S(1)}, f32[14,8,128]{2,1,0:T(8,128)S(1)}, u32[]{:S(2)}, u32[]{:S(2)}) collective-permute-start(f32[14,8,128]{2,1,0:T(8,128)S(1)} %get-tuple-element.157.own_ref), channel_id=1, source_target_pairs={{0,31},{1,2},{2,1},{3,4},{4,3},{5,6},{6,5},{7,8},{8,7},{9,10},{10,... | collective-permute-start | bytes 172040 | tf_op jit(solution)/shard_map/ppermute | solution.py:518
  44.5 8.5 %collective-permute-start.15 = (f32[14,8,128]{2,1,0:T(8,128)S(1)}, f32[14,8,128]{2,1,0:T(8,128)S(1)}, u32[]{:S(2)}, u32[]{:S(2)}) collective-permute-start(f32[14,8,128]{2,1,0:T(8,128)S(1)} %get-tuple-element.179.own_ref), channel_id=1, source_target_pairs={{0,31},{1,2},{2,1},{3,4},{4,3},{5,6},{6,5},{7,8},{8,7},{9,10},{10,... | collective-permute-start | bytes 172040 | tf_op jit(solution)/shard_map/ppermute | solution.py:518
  49.1 4.4 %collective-permute-start.13 = (f32[14,8,128]{2,1,0:T(8,128)S(1)}, f32[14,8,128]{2,1,0:T(8,128)S(1)}, u32[]{:S(2)}, u32[]{:S(2)}) collective-permute-start(f32[14,8,128]{2,1,0:T(8,128)S(1)} %get-tuple-element.171.own_ref), channel_id=1, source_target_pairs={{0,1},{1,0},{2,3},{3,2},{4,5},{5,4},{6,7},{7,6},{8,9},{9,8},{10,11... | collective-permute-start | bytes 172040 | tf_op jit(solution)/shard_map/ppermute | solution.py:519
  53.0 4.4 %collective-permute-start.16 = (f32[14,8,128]{2,1,0:T(8,128)S(1)}, f32[14,8,128]{2,1,0:T(8,128)S(1)}, u32[]{:S(2)}, u32[]{:S(2)}) collective-permute-start(f32[14,8,128]{2,1,0:T(8,128)S(1)} %get-tuple-element.181.own_ref), channel_id=1, source_target_pairs={{0,1},{1,0},{2,3},{3,2},{4,5},{5,4},{6,7},{7,6},{8,9},{9,8},{10,11... | collective-permute-start | bytes 172040 | tf_op jit(solution)/shard_map/ppermute | solution.py:519
  53.6 8.5 %collective-permute-start.14 = (f32[14,8,128]{2,1,0:T(8,128)S(1)}, f32[14,8,128]{2,1,0:T(8,128)S(1)}, u32[]{:S(2)}, u32[]{:S(2)}) collective-permute-start(f32[14,8,128]{2,1,0:T(8,128)S(1)} %get-tuple-element.178.own_ref), channel_id=1, source_target_pairs={{0,31},{1,2},{2,1},{3,4},{4,3},{5,6},{6,5},{7,8},{8,7},{9,10},{10,... | collective-permute-start | bytes 172040 | tf_op jit(solution)/shard_map/ppermute | solution.py:518
  57.4 8.5 %collective-permute-start.18 = (f32[14,8,128]{2,1,0:T(8,128)S(1)}, f32[14,8,128]{2,1,0:T(8,128)S(1)}, u32[]{:S(2)}, u32[]{:S(2)}) collective-permute-start(f32[14,8,128]{2,1,0:T(8,128)S(1)} %get-tuple-element.198.own_ref), channel_id=1, source_target_pairs={{0,31},{1,2},{2,1},{3,4},{4,3},{5,6},{6,5},{7,8},{8,7},{9,10},{10,... | collective-permute-start | bytes 172040 | tf_op jit(solution)/shard_map/ppermute | solution.py:518
  62.1 4.3 %collective-permute-start.17 = (f32[14,8,128]{2,1,0:T(8,128)S(1)}, f32[14,8,128]{2,1,0:T(8,128)S(1)}, u32[]{:S(2)}, u32[]{:S(2)}) collective-permute-start(f32[14,8,128]{2,1,0:T(8,128)S(1)} %get-tuple-element.192.own_ref), channel_id=1, source_target_pairs={{0,1},{1,0},{2,3},{3,2},{4,5},{5,4},{6,7},{7,6},{8,9},{9,8},{10,11... | collective-permute-start | bytes 172040 | tf_op jit(solution)/shard_map/ppermute | solution.py:519

commit v7 on v6

--- a/solution.py
+++ b/solution.py
@@ -150,14 +150,16 @@
                 order_buf, near_buf, sems):
     parity = lax.axis_index("elem") % 2
     near, far = source_plane(parity, 0), source_plane(parity, ORDER)
-    copies = [pltpu.make_async_copy(order_ref, order_buf, sems.at[0])]
-    for r, source in enumerate((scal_ref.at[0, near], scal_ref.at[1, near], mass_ref.at[near])):
-        copies.append(pltpu.make_async_copy(source, near_buf.at[r], sems.at[1 + r]))
-    sources = [scal_ref.at[0, far], scal_ref.at[1, far], mass_ref.at[far]]
-    sources += [tr_ref.at[r, far] for r in range(3)] + [tr_ref.at[r, near] for r in range(3)]
+    copies = [
+        pltpu.make_async_copy(order_ref, order_buf, sems.at[0]),
+        pltpu.make_async_copy(mass_ref.at[near], near_buf.at[2], sems.at[1]),
+        pltpu.make_async_copy(scal_ref.at[:, near], near_buf.at[pl.ds(0, 2)], sems.at[2]),
+    ]
     late = [
-        pltpu.make_async_copy(source, raw_ref.at[r], sems.at[4 + r])
-        for r, source in enumerate(sources)
+        pltpu.make_async_copy(scal_ref.at[:, far], raw_ref.at[pl.ds(0, 2)], sems.at[3]),
+        pltpu.make_async_copy(mass_ref.at[far], raw_ref.at[2], sems.at[4]),
+        pltpu.make_async_copy(tr_ref.at[:, far], raw_ref.at[pl.ds(3, 3)], sems.at[5]),
+        pltpu.make_async_copy(tr_ref.at[:, near], raw_ref.at[pl.ds(6, 3)], sems.at[6]),
     ]
     for copy in copies + late:
         copy.start()
@@ -360,9 +362,8 @@
         tables = third_tables()
         rot = rotations()
         if start:
-            tf_ref, rtf_ref, ev_ref, rev_ref, st_ref, r0_ref, ri_ref, ti_ref = refs[5:13]
-            gn_ref, an_ref, q_ref, e7_ref, a0_ref, a7_ref, rs_ref, wp_ref = refs[13:]
-            inner_open(gi_ref, ri_ref, rt_ref, ti_ref, rot, wp_ref)
+            tf_ref, rtf_ref, ev_ref, rev_ref, st_ref, r0_ref, wp_ref = refs[5:12]
+            gn_ref, an_ref, q_ref, e7_ref, a0_ref, a7_ref, rs_ref = refs[12:]
             both_sides(transports(tf_ref, 0), transports(rtf_ref, 0), tables, a0_ref)
             both_sides(
                 transports(ev_ref, 3 * ROWS), transports(rev_ref, 3 * ROWS), tables, a7_ref)
@@ -533,7 +534,7 @@
         project_odd, [(3 * ROWS, SUB, LANES), (SUB, LANES), (SUB, LANES), (9,) + tile],
         (stay(element_order), stay(scal), stay(mas), stay(tr)), "project", 1, hbm=(0, 1, 2, 3),
         scratch=[pltpu.VMEM((1, LANES), jnp.int32), pltpu.VMEM((3,) + tile, f32),
-                 pltpu.SemaphoreType.DMA((13,))])
+                 pltpu.SemaphoreType.DMA((7,))])
     rod = swap_od(od)
     ev, tf = call(project_even, [bundle, (24, SUB, LANES)], (idx, raw), "project", 1)
     rev, rtf = swap_ev(ev), swap_od(tf)
@@ -541,19 +542,23 @@
         prepare, [inner, faces, (6,) + tile, (6,) + tile, (6, 2) + tile, (2,) + part],
         (idx, scal, mas, tr), "prepare", 1)
     p0, r0, cev = call(make_field_face(0), [face, part, sent], (od, rod, q, st), "odd", 3000)
+
+    def opening_terms(gi_ref, ri_ref, rt_ref, ti_ref, after_ref, wp_ref):
+        inner_open(gi_ref, ri_ref, rt_ref, ti_ref, rotations(), wp_ref)
+
+    wp = call(opening_terms, [inner], (gi, ri, rt, ti, r0), "terms", 1)
     p7, r7, cod = call(make_field_face(1), [face, part, sent], (ev, rev, q, st), "even", 1)
-    acci, accf, wp = gi, q, gi
+    acci, accf = gi, q
     pairs = SUBSTEPS * STAGES // 2
     for n in range(pairs):
         s = 2 * n % STAGES + 1
         opening, closing, early = s == 1, s + 1 == STAGES, n == 0
         got_ev, got_od = swap_ev(cev), swap_od(cod)
-        extra = (tf, rtf, ev, rev, st, r0, ri, ti) if early else (acci, wp, a7)
+        extra = (tf, rtf, ev, rev, st, r0, wp) if early else (acci, wp, a7)
         res = call(
             make_first_inner(1.0 / s, opening, early),
             [inner, inner, faces, face] + ([geometry, geometry, (2,) + part] if early else []),
-            (p0, p7, gi, rt, r7) + extra, "first", 1000,
-            scratch=[pltpu.VMEM(inner, f32)] if early else [])
+            (p0, p7, gi, rt, r7) + extra, "first", 1000)
         gm, acci, q, e7 = res[:4]
         if early:
             a0, a7, rs = res[4:]

time: 67.4 us -> 68 us (level)
  waiting for transfers between devices: 15.3 us -> 16.3 us
    ppermute x10, waiting for transfers between devices: 12.1 us -> 14.6 us  [per_device(): swap_od = lambda x: lax.ppermute(x, 'elem', odd_pairs)]
    ppermute x9, waiting for transfers between devices: 3.28 us -> 1.67 us  [per_device(): swap_ev = lambda x: lax.ppermute(x, 'elem', even_pairs)]
    pallas_call x33 -> x34, Pallas kernels: 15.3 us -> 15.4 us  [call(): pl.pallas_call(kernel, out_shape=shapes[0] if single else shapes, in_spec...]
  transfers between devices with their start and end apart: 19 -> 19, of which waited for: 15 -> 11; matrix products, arithmetic and copies ran while one was open for 0% -> 0% of each run, Pallas kernels for 20% -> 20%
where the time goes in v7:
time: 68 us; the launch traced here: 67.8 us
  starting transfers between devices  35.8 us (53%)
  waiting for transfers between devices  16.3 us (24%)
  Pallas kernels  15.4 us (23%)
    ppermute x10, starting transfers between devices, per_device(): swap_od = lambda x: lax.ppermute(x, 'elem', odd_pairs)  34.2 us
    pallas_call x34, Pallas kernels, call(): pl.pallas_call(kernel, out_shape=shapes[0] if single else shapes, in_spec...  15.4 us
    ppermute x10, waiting for transfers between devices, per_device(): swap_od = lambda x: lax.ppermute(x, 'elem', odd_pairs)  14.6 us
    ppermute x9, waiting for transfers between devices, per_device(): swap_ev = lambda x: lax.ppermute(x, 'elem', even_pairs)  1.67 us
    ppermute x9, starting transfers between devices, per_device(): swap_ev = lambda x: lax.ppermute(x, 'elem', even_pairs)  1.6 us
  transfers between devices with their start and end apart: 19, of which 11 were waited for; matrix products, arithmetic and copies ran while one was open for 0% of the time, Pallas kernels for 20%

profile of v7, /device:TPU:0, one launch (start us, length us, event | category | flops | bytes accessed | tf_op | source)
XLA Modules:
  0.0 67.8 jit_solution(13492346720868326002)
XLA Ops:
  0.0 1.3 %project.2 = (f32[21,8,128]{2,1,0:T(8,128)S(1)}, s32[8,128]{1,0:T(8,128)S(1)}, s32[8,128]{1,0:T(8,128)S(1)}, f32[9,8,8,128]{3,2,1,0:T(8,128)S(1)}) custom-call(s32[1,128]{1,0:T(1,128)} %order_ref.1, f32[2,8,8,8,128]{4,3,2,1,0:T(8,128)} %bitcast.6, f32[8,8,8,128]{3,2,1,0:T(8,128)} %bitcast.8, f32[3,8,8,8,128]{4,3,2,1,0:T(8,128)} %bitcast.4), custom_call_target="tpu_custom_call" | custom-call | flops 1000000 | bytes 1024 | tf_op jit(solution)/shard_map/project/pallas_call | solution.py:500
  1.4 6.7 %collective-permute-start.2 = (f32[21,8,128]{2,1,0:T(8,128)S(1)}, f32[21,8,128]{2,1,0:T(8,128)S(1)}, u32[]{:S(2)}, u32[]{:S(2)}) collective-permute-start(f32[21,8,128]{2,1,0:T(8,128)S(1)} %get-tuple-element.110.own_ref), channel_id=1, source_target_pairs={{0,31},{1,2},{2,1},{3,4},{4,3},{5,6},{6,5},{7,8},{8,7},{9,10},{10,... | collective-permute-start | bytes 258056 | tf_op jit(solution)/shard_map/ppermute | solution.py:519
  8.4 1.4 %collective-permute-start.4 = (f32[24,8,128]{2,1,0:T(8,128)S(1)}, f32[24,8,128]{2,1,0:T(8,128)S(1)}, u32[]{:S(2)}, u32[]{:S(2)}) collective-permute-start(f32[24,8,128]{2,1,0:T(8,128)S(1)} %get-tuple-element.117.refs_5_), channel_id=1, source_target_pairs={{0,31},{1,2},{2,1},{3,4},{4,3},{5,6},{6,5},{7,8},{8,7},{9,10},{10,... | collective-permute-start | bytes 294920 | tf_op jit(solution)/shard_map/ppermute | solution.py:519
  9.8 2.6 %prepare.1 = (f32[2,6,8,8,128]{4,3,2,1,0:T(8,128)S(1)}, f32[2,2,7,8,128]{4,3,2,1,0:T(8,128)S(1)}, f32[6,8,8,128]{3,2,1,0:T(8,128)S(1)}, f32[6,8,8,128]{3,2,1,0:T...) custom-call(s32[8,128]{1,0:T(8,128)S(1)} %get-tuple-element.104.idx_ref, ...), custom_call_target="tpu_custom_call" | custom-call | flops 1000000 | bytes 1024 | tf_op jit(solution)/shard_map/prepare/pallas_call | solution.py:500
  12.4 0.8 %collective-permute-start.3 = (f32[14,8,128]{2,1,0:T(8,128)S(1)}, f32[14,8,128]{2,1,0:T(8,128)S(1)}, u32[]{:S(2)}, u32[]{:S(2)}) collective-permute-start(f32[14,8,128]{2,1,0:T(8,128)S(1)} %get-tuple-element.111.own_ref), channel_id=1, source_target_pairs={{0,1},{1,0},{2,3},{3,2},{4,5},{5,4},{6,7},{7,6},{8,9},{9,8},{10,11... | collective-permute-start | bytes 172040 | tf_op jit(solution)/shard_map/ppermute | solution.py:520
  13.2 0.7 %terms.1.refs_11_ = f32[2,6,8,8,128]{4,3,2,1,0:T(8,128)S(1)} custom-call(f32[2,6,8,8,128]{4,3,2,1,0:T(8,128)S(1)} %get-tuple-element.114.gi_ref.refs_2_, f32[6,8,8,128]{3,2,1,0:T(8,128)S(1)} %get-tuple-element.119.ri_ref, f32[6,8,8,128]{3,2,1,0:T(8,128)S(1)} %get-tuple-element.115.rt_ref.refs_3_, f32[6,2,8,8,128]{4,3,2,1,0:T(8,128)S(1)} %get-tuple-element.120.ti_ref, ...), custom_call_target="tpu_custom_call" | custom-call | flops 1000000 | bytes 1024 | tf_op jit(solution)/shard_map/terms/pallas_call | solution.py:500
  13.9 1.0 %collective-permute-done.got_ref.refs_8_ = f32[45,8,128]{2,1,0:T(8,128)S(1)} collective-permute-done((f32[45,8,128]{2,1,0:T(8,128)S(1)}, f32[45,8,128]{2,1,0:T(8,128)S(1)}, u32[]{:S(2)}, u32[]{:S(2)}) %collective-permute-start) | collective-permute-done | bytes 184352 | tf_op jit(solution)/shard_map/ppermute | solution.py:520
  14.9 3.7 %collective-permute-start.1 = (f32[14,8,128]{2,1,0:T(8,128)S(1)}, f32[14,8,128]{2,1,0:T(8,128)S(1)}, u32[]{:S(2)}, u32[]{:S(2)}) collective-permute-start(f32[14,8,128]{2,1,0:T(8,128)S(1)} %get-tuple-element.109.own_ref), channel_id=1, source_target_pairs={{0,31},{1,2},{2,1},{3,4},{4,3},{5,6},{6,5},{7,8},{8,7},{9,10},{10,... | collective-permute-start | bytes 172040 | tf_op jit(solution)/shard_map/ppermute | solution.py:519
  19.0 3.0 %collective-permute-start.7 = (f32[14,8,128]{2,1,0:T(8,128)S(1)}, f32[14,8,128]{2,1,0:T(8,128)S(1)}, u32[]{:S(2)}, u32[]{:S(2)}) collective-permute-start(f32[14,8,128]{2,1,0:T(8,128)S(1)} %get-tuple-element.137.own_ref), channel_id=1, source_target_pairs={{0,31},{1,2},{2,1},{3,4},{4,3},{5,6},{6,5},{7,8},{8,7},{9,10},{10,... | collective-permute-start | bytes 172040 | tf_op jit(solution)/shard_map/ppermute | solution.py:519
  22.1 0.9 %between.4 = (f32[2,6,8,8,128]{4,3,2,1,0:T(8,128)S(1)}, f32[2,7,8,128]{3,2,1,0:T(8,128)S(1)}, f32[2,7,8,128]{3,2,1,0:T(8,128)S(1)}) custom-call(f32[2,7,8,128]{3,2,1,0:T(8,128)S(1)} %get-tuple-element.124.m7_ref, f32[2,6,8,8,128]{4,3,2,1,0:T(8,128)S(1)} %get-tuple-element.125.gi_ref, f32[3,8,8,128]{3,2,1,0:T(8,128)S(1)} %get-tuple-element.126.a7_ref.refs_7_, ...), custom_call_target="tpu_custom_call" | custom-call | flops 2000000000 | bytes 1024 | tf_op jit(solution)/shard_map/between/pallas_call | solution.py:500
  23.0 0.4 collective-permute-done.1.got_ref
  23.5 1.0 %second.3 = (f32[2,6,8,8,128]{4,3,2,1,0:T(8,128)S(1)}, f32[2,2,7,8,128]{4,3,2,1,0:T(8,128)S(1)}, f32[2,6,8,8,128]{4,3,2,1,0:T(8,128)S(1)}, f32[2,2,7,8,128]{4,3,...) custom-call(f32[2,7,8,128]{3,2,1,0:T(8,128)S(1)} %get-tuple-element.131.m0_ref, ...), custom_call_target="tpu_custom_call" | custom-call | flops 3000000000 | bytes 1024 | tf_op jit(solution)/shard_map/second/pallas_call | solution.py:500
  24.5 3.0 %collective-permute-done.7.got_ref = f32[14,8,128]{2,1,0:T(8,128)S(1)} collective-permute-done((f32[14,8,128]{2,1,0:T(8,128)S(1)}, f32[14,8,128]{2,1,0:T(8,128)S(1)}, u32[]{:S(2)}, u32[]{:S(2)}) %collective-permute-start.7) | collective-permute-done | bytes 57376 | tf_op jit(solution)/shard_map/ppermute | solution.py:519
  27.7 4.0 %collective-permute-start.6 = (f32[14,8,128]{2,1,0:T(8,128)S(1)}, f32[14,8,128]{2,1,0:T(8,128)S(1)}, u32[]{:S(2)}, u32[]{:S(2)}) collective-permute-start(f32[14,8,128]{2,1,0:T(8,128)S(1)} %get-tuple-element.136.own_ref), channel_id=1, source_target_pairs={{0,31},{1,2},{2,1},{3,4},{4,3},{5,6},{6,5},{7,8},{8,7},{9,10},{10,... | collective-permute-start | bytes 172040 | tf_op jit(solution)/shard_map/ppermute | solution.py:519
  32.1 2.8 %collective-permute-start.11 = (f32[14,8,128]{2,1,0:T(8,128)S(1)}, f32[14,8,128]{2,1,0:T(8,128)S(1)}, u32[]{:S(2)}, u32[]{:S(2)}) collective-permute-start(f32[14,8,128]{2,1,0:T(8,128)S(1)} %get-tuple-element.158.own_ref), channel_id=1, source_target_pairs={{0,31},{1,2},{2,1},{3,4},{4,3},{5,6},{6,5},{7,8},{8,7},{9,10},{10,... | collective-permute-start | bytes 172040 | tf_op jit(solution)/shard_map/ppermute | solution.py:519
  34.8 0.9 %between.5 = (f32[2,6,8,8,128]{4,3,2,1,0:T(8,128)S(1)}, f32[2,7,8,128]{3,2,1,0:T(8,128)S(1)}, f32[2,7,8,128]{3,2,1,0:T(8,128)S(1)}) custom-call(f32[2,7,8,128]{3,2,1,0:T(8,128)S(1)} %get-tuple-element.147.m7_ref, f32[2,6,8,8,128]{4,3,2,1,0:T(8,128)S(1)} %get-tuple-element.148.gi_ref, f32[3,8,8,128]{3,2,1,0:T(8,128)S(1)} %get-tuple-element.126.a7_ref.refs_7_, ...), custom_call_target="tpu_custom_call" | custom-call | flops 2000000000 | bytes 1024 | tf_op jit(solution)/shard_map/between/pallas_call | solution.py:500
  35.7 0.6 collective-permute-done.6.got_ref
  36.5 1.0 %second.4 = (f32[2,6,8,8,128]{4,3,2,1,0:T(8,128)S(1)}, f32[2,2,7,8,128]{4,3,2,1,0:T(8,128)S(1)}, f32[2,6,8,8,128]{4,3,2,1,0:T(8,128)S(1)}, f32[2,2,7,8,128]{4,3,...) custom-call(f32[2,7,8,128]{3,2,1,0:T(8,128)S(1)} %get-tuple-element.152.m0_ref, ...), custom_call_target="tpu_custom_call" | custom-call | flops 3000000000 | bytes 1024 | tf_op jit(solution)/shard_map/second/pallas_call | solution.py:500
  37.4 3.1 %collective-permute-done.11.got_ref = f32[14,8,128]{2,1,0:T(8,128)S(1)} collective-permute-done((f32[14,8,128]{2,1,0:T(8,128)S(1)}, f32[14,8,128]{2,1,0:T(8,128)S(1)}, u32[]{:S(2)}, u32[]{:S(2)}) %collective-permute-start.11) | collective-permute-done | bytes 57376 | tf_op jit(solution)/shard_map/ppermute | solution.py:519
  40.7 3.8 %collective-permute-start.10 = (f32[14,8,128]{2,1,0:T(8,128)S(1)}, f32[14,8,128]{2,1,0:T(8,128)S(1)}, u32[]{:S(2)}, u32[]{:S(2)}) collective-permute-start(f32[14,8,128]{2,1,0:T(8,128)S(1)} %get-tuple-element.157.own_ref), channel_id=1, source_target_pairs={{0,31},{1,2},{2,1},{3,4},{4,3},{5,6},{6,5},{7,8},{8,7},{9,10},{10,... | collective-permute-start | bytes 172040 | tf_op jit(solution)/shard_map/ppermute | solution.py:519
  44.9 2.8 %collective-permute-start.15 = (f32[14,8,128]{2,1,0:T(8,128)S(1)}, f32[14,8,128]{2,1,0:T(8,128)S(1)}, u32[]{:S(2)}, u32[]{:S(2)}) collective-permute-start(f32[14,8,128]{2,1,0:T(8,128)S(1)} %get-tuple-element.179.own_ref), channel_id=1, source_target_pairs={{0,31},{1,2},{2,1},{3,4},{4,3},{5,6},{6,5},{7,8},{8,7},{9,10},{10,... | collective-permute-start | bytes 172040 | tf_op jit(solution)/shard_map/ppermute | solution.py:519
  47.6 0.9 %between.6 = (f32[2,6,8,8,128]{4,3,2,1,0:T(8,128)S(1)}, f32[2,7,8,128]{3,2,1,0:T(8,128)S(1)}, f32[2,7,8,128]{3,2,1,0:T(8,128)S(1)}) custom-call(f32[2,7,8,128]{3,2,1,0:T(8,128)S(1)} %get-tuple-element.168.m7_ref, f32[2,6,8,8,128]{4,3,2,1,0:T(8,128)S(1)} %get-tuple-element.169.gi_ref, f32[3,8,8,128]{3,2,1,0:T(8,128)S(1)} %get-tuple-element.126.a7_ref.refs_7_, ...), custom_call_target="tpu_custom_call" | custom-call | flops 2000000000 | bytes 1024 | tf_op jit(solution)/shard_map/between/pallas_call | solution.py:500
  48.5 0.7 collective-permute-done.10.got_ref
  49.5 1.0 %second.5 = (f32[2,6,8,8,128]{4,3,2,1,0:T(8,128)S(1)}, f32[2,2,7,8,128]{4,3,2,1,0:T(8,128)S(1)}, f32[2,6,8,8,128]{4,3,2,1,0:T(8,128)S(1)}, f32[2,2,7,8,128]{4,3,...) custom-call(f32[2,7,8,128]{3,2,1,0:T(8,128)S(1)} %get-tuple-element.173.m0_ref, ...), custom_call_target="tpu_custom_call" | custom-call | flops 3000000000 | bytes 1024 | tf_op jit(solution)/shard_map/second/pallas_call | solution.py:500
  50.5 2.9 %collective-permute-done.15.got_ref = f32[14,8,128]{2,1,0:T(8,128)S(1)} collective-permute-done((f32[14,8,128]{2,1,0:T(8,128)S(1)}, f32[14,8,128]{2,1,0:T(8,128)S(1)}, u32[]{:S(2)}, u32[]{:S(2)}) %collective-permute-start.15) | collective-permute-done | bytes 57376 | tf_op jit(solution)/shard_map/ppermute | solution.py:519
  53.7 3.8 %collective-permute-start.14 = (f32[14,8,128]{2,1,0:T(8,128)S(1)}, f32[14,8,128]{2,1,0:T(8,128)S(1)}, u32[]{:S(2)}, u32[]{:S(2)}) collective-permute-start(f32[14,8,128]{2,1,0:T(8,128)S(1)} %get-tuple-element.178.own_ref), channel_id=1, source_target_pairs={{0,31},{1,2},{2,1},{3,4},{4,3},{5,6},{6,5},{7,8},{8,7},{9,10},{10,... | collective-permute-start | bytes 172040 | tf_op jit(solution)/shard_map/ppermute | solution.py:519
  58.2 2.4 %collective-permute-start.18 = (f32[14,8,128]{2,1,0:T(8,128)S(1)}, f32[14,8,128]{2,1,0:T(8,128)S(1)}, u32[]{:S(2)}, u32[]{:S(2)}) collective-permute-start(f32[14,8,128]{2,1,0:T(8,128)S(1)} %get-tuple-element.198.own_ref), channel_id=1, source_target_pairs={{0,31},{1,2},{2,1},{3,4},{4,3},{5,6},{6,5},{7,8},{8,7},{9,10},{10,... | collective-permute-start | bytes 172040 | tf_op jit(solution)/shard_map/ppermute | solution.py:519
  60.6 0.9 %between.7 = (f32[2,6,8,8,128]{4,3,2,1,0:T(8,128)S(1)}, f32[2,7,8,128]{3,2,1,0:T(8,128)S(1)}, f32[2,7,8,128]{3,2,1,0:T(8,128)S(1)}) custom-call(f32[2,7,8,128]{3,2,1,0:T(8,128)S(1)} %get-tuple-element.189.m7_ref, f32[2,6,8,8,128]{4,3,2,1,0:T(8,128)S(1)} %get-tuple-element.190.gi_ref, f32[3,8,8,128]{3,2,1,0:T(8,128)S(1)} %get-tuple-element.126.a7_ref.refs_7_, ...), custom_call_target="tpu_custom_call" | custom-call | flops 2000000000 | bytes 1024 | tf_op jit(solution)/shard_map/between/pallas_call | solution.py:500
  61.5 0.7 collective-permute-done.14.got_ref
  62.3 1.1 %last.1 = (f32[2,8,8,8,128]{4,3,2,1,0:T(8,128)}, f32[2,2,7,8,128]{4,3,2,1,0:T(8,128)S(1)}, f32[2,7,8,128]{3,2,1,0:T(8,128)S(1)}) custom-call(s32[8,128]{1,0:T(8,128)S(1)} %get-tuple-element.103.slot_ref, f32[2,7,8,128]{3,2,1,0:T(8,128)S(1)} %get-tuple-element.194.m0_ref, f32[2,7,8,128]{3,2,1,0:T(8,128)S(1)} %get-tuple-element.189.m7_ref, ...), custom_call_target="tpu_custom_call" | custom-call | flops 3000000000 | bytes 1024 | tf_op jit(solution)/shard_map/last/pallas_call | solution.py:500
  63.5 3.3 %collective-permute-done.18.got_ref = f32[14,8,128]{2,1,0:T(8,128)S(1)} collective-permute-done((f32[14,8,128]{2,1,0:T(8,128)S(1)}, f32[14,8,128]{2,1,0:T(8,128)S(1)}, u32[]{:S(2)}, u32[]{:S(2)}) %collective-permute-start.18) | collective-permute-done | bytes 57376 | tf_op jit(solution)/shard_map/ppermute | solution.py:519
  66.9 0.8 %finish.3 = f32[2,8,8,8,128]{4,3,2,1,0:T(8,128)} custom-call(s32[8,128]{1,0:T(8,128)S(1)} %get-tuple-element.103.slot_ref, f32[14,8,128]{2,1,0:T(8,128)S(1)} %get-tuple-element.192.own_ref, f32[14,8,128]{2,1,0:T(8,128)S(1)} %collective-permute-done.17.got_ref, f32[2,7,8,128]{3,2,1,0:T(8,128)S(1)} %get-tuple-element.193.e_ref, ...), custom_call_target="tpu_custom_call", output_to_operand_aliasing={{}: (6, {})} | custom-call | flops 1000000 | bytes 1024 | tf_op jit(solution)/shard_map/finish/pallas_call | solution.py:500
  (46 shorter events, 3.8 us)
Async XLA Ops:
  0.0 9.8 %copy-start = (f32[3,512,128]{2,1,0:T(8,128)S(1)}, f32[3,512,128]{2,1,0:T(8,128)}, u32[]{:S(2)}) copy-start(f32[3,512,128]{2,1,0:T(8,128)} %param.5) | copy-start | bytes 2359300
  0.0 9.8 %copy-start.1 = (f32[2,512,128]{2,1,0:T(8,128)S(1)}, f32[2,512,128]{2,1,0:T(8,128)}, u32[]{:S(2)}) copy-start(f32[2,512,128]{2,1,0:T(8,128)} %param.4) | copy-start | bytes 1572868
  1.3 8.5 %copy-start.2 = (f32[512,128]{1,0:T(8,128)S(1)}, f32[512,128]{1,0:T(8,128)}, u32[]{:S(2)}) copy-start(f32[512,128]{1,0:T(8,128)} %param.6) | copy-start | bytes 786436
  1.4 11.0 %collective-permute-start.2 = (f32[21,8,128]{2,1,0:T(8,128)S(1)}, f32[21,8,128]{2,1,0:T(8,128)S(1)}, u32[]{:S(2)}, u32[]{:S(2)}) collective-permute-start(f32[21,8,128]{2,1,0:T(8,128)S(1)} %get-tuple-element.110.own_ref), channel_id=1, source_target_pairs={{0,31},{1,2},{2,1},{3,4},{4,3},{5,6},{6,5},{7,8},{8,7},{9,10},{10,... | collective-permute-start | bytes 258056 | tf_op jit(solution)/shard_map/ppermute | solution.py:519
  8.4 6.5 %collective-permute-start = (f32[45,8,128]{2,1,0:T(8,128)S(1)}, f32[45,8,128]{2,1,0:T(8,128)S(1)}, u32[]{:S(2)}, u32[]{:S(2)}) collective-permute-start(f32[45,8,128]{2,1,0:T(8,128)S(1)} %get-tuple-element.106.own_ref.refs_7_), channel_id=1, source_target_pairs={{0,1},{1,0},{2,3},{3,2},{4,5},{5,4},{6,7},{7,6},{8,9},{9,8},{10,11... | collective-permute-start | bytes 552968 | tf_op jit(solution)/shard_map/ppermute | solution.py:520
  8.4 10.2 %collective-permute-start.4 = (f32[24,8,128]{2,1,0:T(8,128)S(1)}, f32[24,8,128]{2,1,0:T(8,128)S(1)}, u32[]{:S(2)}, u32[]{:S(2)}) collective-permute-start(f32[24,8,128]{2,1,0:T(8,128)S(1)} %get-tuple-element.117.refs_5_), channel_id=1, source_target_pairs={{0,31},{1,2},{2,1},{3,4},{4,3},{5,6},{6,5},{7,8},{8,7},{9,10},{10,... | collective-permute-start | bytes 294920 | tf_op jit(solution)/shard_map/ppermute | solution.py:519
  12.4 6.6 %collective-permute-start.3 = (f32[14,8,128]{2,1,0:T(8,128)S(1)}, f32[14,8,128]{2,1,0:T(8,128)S(1)}, u32[]{:S(2)}, u32[]{:S(2)}) collective-permute-start(f32[14,8,128]{2,1,0:T(8,128)S(1)} %get-tuple-element.111.own_ref), channel_id=1, source_target_pairs={{0,1},{1,0},{2,3},{3,2},{4,5},{5,4},{6,7},{7,6},{8,9},{9,8},{10,11... | collective-permute-start | bytes 172040 | tf_op jit(solution)/shard_map/ppermute | solution.py:520
  14.9 8.5 %collective-permute-start.1 = (f32[14,8,128]{2,1,0:T(8,128)S(1)}, f32[14,8,128]{2,1,0:T(8,128)S(1)}, u32[]{:S(2)}, u32[]{:S(2)}) collective-permute-start(f32[14,8,128]{2,1,0:T(8,128)S(1)} %get-tuple-element.109.own_ref), channel_id=1, source_target_pairs={{0,31},{1,2},{2,1},{3,4},{4,3},{5,6},{6,5},{7,8},{8,7},{9,10},{10,... | collective-permute-start | bytes 172040 | tf_op jit(solution)/shard_map/ppermute | solution.py:519
  19.0 8.5 %collective-permute-start.7 = (f32[14,8,128]{2,1,0:T(8,128)S(1)}, f32[14,8,128]{2,1,0:T(8,128)S(1)}, u32[]{:S(2)}, u32[]{:S(2)}) collective-permute-start(f32[14,8,128]{2,1,0:T(8,128)S(1)} %get-tuple-element.137.own_ref), channel_id=1, source_target_pairs={{0,31},{1,2},{2,1},{3,4},{4,3},{5,6},{6,5},{7,8},{8,7},{9,10},{10,... | collective-permute-start | bytes 172040 | tf_op jit(solution)/shard_map/ppermute | solution.py:519
  23.4 4.3 %collective-permute-start.5 = (f32[14,8,128]{2,1,0:T(8,128)S(1)}, f32[14,8,128]{2,1,0:T(8,128)S(1)}, u32[]{:S(2)}, u32[]{:S(2)}) collective-permute-start(f32[14,8,128]{2,1,0:T(8,128)S(1)} %get-tuple-element.129.own_ref), channel_id=1, source_target_pairs={{0,1},{1,0},{2,3},{3,2},{4,5},{5,4},{6,7},{7,6},{8,9},{9,8},{10,11... | collective-permute-start | bytes 172040 | tf_op jit(solution)/shard_map/ppermute | solution.py:520
  27.5 4.5 %collective-permute-start.8 = (f32[14,8,128]{2,1,0:T(8,128)S(1)}, f32[14,8,128]{2,1,0:T(8,128)S(1)}, u32[]{:S(2)}, u32[]{:S(2)}) collective-permute-start(f32[14,8,128]{2,1,0:T(8,128)S(1)} %get-tuple-element.139.own_ref), channel_id=1, source_target_pairs={{0,1},{1,0},{2,3},{3,2},{4,5},{5,4},{6,7},{7,6},{8,9},{9,8},{10,11... | collective-permute-start | bytes 172040 | tf_op jit(solution)/shard_map/ppermute | solution.py:520
  27.7 8.6 %collective-permute-start.6 = (f32[14,8,128]{2,1,0:T(8,128)S(1)}, f32[14,8,128]{2,1,0:T(8,128)S(1)}, u32[]{:S(2)}, u32[]{:S(2)}) collective-permute-start(f32[14,8,128]{2,1,0:T(8,128)S(1)} %get-tuple-element.136.own_ref), channel_id=1, source_target_pairs={{0,31},{1,2},{2,1},{3,4},{4,3},{5,6},{6,5},{7,8},{8,7},{9,10},{10,... | collective-permute-start | bytes 172040 | tf_op jit(solution)/shard_map/ppermute | solution.py:519
  32.1 8.5 %collective-permute-start.11 = (f32[14,8,128]{2,1,0:T(8,128)S(1)}, f32[14,8,128]{2,1,0:T(8,128)S(1)}, u32[]{:S(2)}, u32[]{:S(2)}) collective-permute-start(f32[14,8,128]{2,1,0:T(8,128)S(1)} %get-tuple-element.158.own_ref), channel_id=1, source_target_pairs={{0,31},{1,2},{2,1},{3,4},{4,3},{5,6},{6,5},{7,8},{8,7},{9,10},{10,... | collective-permute-start | bytes 172040 | tf_op jit(solution)/shard_map/ppermute | solution.py:519
  36.4 4.3 %collective-permute-start.9 = (f32[14,8,128]{2,1,0:T(8,128)S(1)}, f32[14,8,128]{2,1,0:T(8,128)S(1)}, u32[]{:S(2)}, u32[]{:S(2)}) collective-permute-start(f32[14,8,128]{2,1,0:T(8,128)S(1)} %get-tuple-element.150.own_ref), channel_id=1, source_target_pairs={{0,1},{1,0},{2,3},{3,2},{4,5},{5,4},{6,7},{7,6},{8,9},{9,8},{10,11... | collective-permute-start | bytes 172040 | tf_op jit(solution)/shard_map/ppermute | solution.py:520
  40.6 4.3 %collective-permute-start.12 = (f32[14,8,128]{2,1,0:T(8,128)S(1)}, f32[14,8,128]{2,1,0:T(8,128)S(1)}, u32[]{:S(2)}, u32[]{:S(2)}) collective-permute-start(f32[14,8,128]{2,1,0:T(8,128)S(1)} %get-tuple-element.160.own_ref), channel_id=1, source_target_pairs={{0,1},{1,0},{2,3},{3,2},{4,5},{5,4},{6,7},{7,6},{8,9},{9,8},{10,11... | collective-permute-start | bytes 172040 | tf_op jit(solution)/shard_map/ppermute | solution.py:520
  40.7 8.5 %collective-permute-start.10 = (f32[14,8,128]{2,1,0:T(8,128)S(1)}, f32[14,8,128]{2,1,0:T(8,128)S(1)}, u32[]{:S(2)}, u32[]{:S(2)}) collective-permute-start(f32[14,8,128]{2,1,0:T(8,128)S(1)} %get-tuple-element.157.own_ref), channel_id=1, source_target_pairs={{0,31},{1,2},{2,1},{3,4},{4,3},{5,6},{6,5},{7,8},{8,7},{9,10},{10,... | collective-permute-start | bytes 172040 | tf_op jit(solution)/shard_map/ppermute | solution.py:519
  44.9 8.5 %collective-permute-start.15 = (f32[14,8,128]{2,1,0:T(8,128)S(1)}, f32[14,8,128]{2,1,0:T(8,128)S(1)}, u32[]{:S(2)}, u32[]{:S(2)}) collective-permute-start(f32[14,8,128]{2,1,0:T(8,128)S(1)} %get-tuple-element.179.own_ref), channel_id=1, source_target_pairs={{0,31},{1,2},{2,1},{3,4},{4,3},{5,6},{6,5},{7,8},{8,7},{9,10},{10,... | collective-permute-start | bytes 172040 | tf_op jit(solution)/shard_map/ppermute | solution.py:519
  49.2 4.4 %collective-permute-start.13 = (f32[14,8,128]{2,1,0:T(8,128)S(1)}, f32[14,8,128]{2,1,0:T(8,128)S(1)}, u32[]{:S(2)}, u32[]{:S(2)}) collective-permute-start(f32[14,8,128]{2,1,0:T(8,128)S(1)} %get-tuple-element.171.own_ref), channel_id=1, source_target_pairs={{0,1},{1,0},{2,3},{3,2},{4,5},{5,4},{6,7},{7,6},{8,9},{9,8},{10,11... | collective-permute-start | bytes 172040 | tf_op jit(solution)/shard_map/ppermute | solution.py:520
  53.4 4.8 %collective-permute-start.16 = (f32[14,8,128]{2,1,0:T(8,128)S(1)}, f32[14,8,128]{2,1,0:T(8,128)S(1)}, u32[]{:S(2)}, u32[]{:S(2)}) collective-permute-start(f32[14,8,128]{2,1,0:T(8,128)S(1)} %get-tuple-element.181.own_ref), channel_id=1, source_target_pairs={{0,1},{1,0},{2,3},{3,2},{4,5},{5,4},{6,7},{7,6},{8,9},{9,8},{10,11... | collective-permute-start | bytes 172040 | tf_op jit(solution)/shard_map/ppermute | solution.py:520
  53.7 8.5 %collective-permute-start.14 = (f32[14,8,128]{2,1,0:T(8,128)S(1)}, f32[14,8,128]{2,1,0:T(8,128)S(1)}, u32[]{:S(2)}, u32[]{:S(2)}) collective-permute-start(f32[14,8,128]{2,1,0:T(8,128)S(1)} %get-tuple-element.178.own_ref), channel_id=1, source_target_pairs={{0,31},{1,2},{2,1},{3,4},{4,3},{5,6},{6,5},{7,8},{8,7},{9,10},{10,... | collective-permute-start | bytes 172040 | tf_op jit(solution)/shard_map/ppermute | solution.py:519
  58.2 8.5 %collective-permute-start.18 = (f32[14,8,128]{2,1,0:T(8,128)S(1)}, f32[14,8,128]{2,1,0:T(8,128)S(1)}, u32[]{:S(2)}, u32[]{:S(2)}) collective-permute-start(f32[14,8,128]{2,1,0:T(8,128)S(1)} %get-tuple-element.198.own_ref), channel_id=1, source_target_pairs={{0,31},{1,2},{2,1},{3,4},{4,3},{5,6},{6,5},{7,8},{8,7},{9,10},{10,... | collective-permute-start | bytes 172040 | tf_op jit(solution)/shard_map/ppermute | solution.py:519
  62.2 4.7 %collective-permute-start.17 = (f32[14,8,128]{2,1,0:T(8,128)S(1)}, f32[14,8,128]{2,1,0:T(8,128)S(1)}, u32[]{:S(2)}, u32[]{:S(2)}) collective-permute-start(f32[14,8,128]{2,1,0:T(8,128)S(1)} %get-tuple-element.192.own_ref), channel_id=1, source_target_pairs={{0,1},{1,0},{2,3},{3,2},{4,5},{5,4},{6,7},{7,6},{8,9},{9,8},{10,11... | collective-permute-start | bytes 172040 | tf_op jit(solution)/shard_map/ppermute | solution.py:520

commit v8 on v6

--- a/solution.py
+++ b/solution.py
@@ -179,13 +179,14 @@
     return first, np.float32(-time_step), np.float32(-time_step)
 
 
-def project_even(idx_ref, raw_ref, ev_ref, tf_ref):
+def project_even(idx_ref, raw_ref, ev_ref, te_ref, to_ref):
     idx = idx_ref[...]
     signs = signs_of(lax.axis_index("elem") % 2)
     planes = project(read(raw_ref, 2), [read(raw_ref, m) for m in range(2)], idx, third_tables())
     turned = [[gather_lanes(v, idx) * signs[r % 3] for v in read(raw_ref, 3 + r)] for r in range(6)]
-    write(ev_ref, (), sum(planes + turned[:3], []))
-    write(tf_ref, (), sum(turned[3:], []))
+    write(ev_ref, (), sum(planes, []))
+    write(te_ref, (), sum(turned[:3], []))
+    write(to_ref, (), sum(turned[3:], []))
 
 
 def prepare(idx_ref, scal_ref, mass_ref, tr_ref,
@@ -297,15 +298,14 @@
         ])
 
 
-def both_sides(own, got, tables, a_ref):
-    total = [[own[r][j] + got[r][j] for j in range(8)] for r in range(3)]
+def both_sides(own_ref, got_ref, passed_ref, tables, a_ref):
+    total = [
+        [own_ref[8 * r + j] + (got_ref[8 * r + j] + passed_ref[8 * r + j]) for j in range(8)]
+        for r in range(3)
+    ]
     write(a_ref, (0,), total[1])
     write(a_ref, (1,), total[2])
     write(a_ref, (2,), plane_sum(total[0], tables, ROWS))
-
-
-def transports(ref, start):
-    return [[ref[start + 8 * r + j] for j in range(8)] for r in range(3)]
 
 
 def make_field_face(face):
@@ -360,12 +360,10 @@
         tables = third_tables()
         rot = rotations()
         if start:
-            tf_ref, rtf_ref, ev_ref, rev_ref, st_ref, r0_ref, ri_ref, ti_ref = refs[5:13]
-            gn_ref, an_ref, q_ref, e7_ref, a0_ref, a7_ref, rs_ref, wp_ref = refs[13:]
+            own_ref, got_ref, passed_ref, st_ref, r0_ref, ri_ref, ti_ref = refs[5:12]
+            gn_ref, an_ref, q_ref, e7_ref, a7_ref, rs_ref, wp_ref = refs[12:]
             inner_open(gi_ref, ri_ref, rt_ref, ti_ref, rot, wp_ref)
-            both_sides(transports(tf_ref, 0), transports(rtf_ref, 0), tables, a0_ref)
-            both_sides(
-                transports(ev_ref, 3 * ROWS), transports(rev_ref, 3 * ROWS), tables, a7_ref)
+            both_sides(own_ref, got_ref, passed_ref, tables, a7_ref)
             write(rs_ref, (0,), [st_ref[0, j] * r0_ref[j] for j in range(ROWS)])
             write(rs_ref, (1,), [st_ref[1, j] * r7_ref[j] for j in range(ROWS)])
         else:
@@ -384,13 +382,21 @@
     return first_inner
 
 
-def between(m7_ref, gi_ref, a7_ref, r7_ref, ri_ref, rt_ref, ti_ref, p0_ref, a0_ref, r0_ref,
-            wp_ref, e7_ref, e0_ref):
-    rot = rotations()
-    tables = third_tables()
-    own_terms(p0_ref, a0_ref, r0_ref, 0, rot, tables, e0_ref)
-    own_terms(m7_ref, a7_ref, r7_ref, 1, rot, tables, e7_ref)
-    inner_open(gi_ref, ri_ref, rt_ref, ti_ref, rot, wp_ref)
+def make_between(start):
+    def between(*refs):
+        m7_ref, gi_ref, a7_ref, r7_ref, ri_ref, rt_ref, ti_ref, p0_ref, r0_ref = refs[:9]
+        rot = rotations()
+        tables = third_tables()
+        if start:
+            own_ref, got_ref, passed_ref, wp_ref, e7_ref, e0_ref, a0_ref = refs[9:]
+            both_sides(own_ref, got_ref, passed_ref, tables, a0_ref)
+        else:
+            a0_ref, wp_ref, e7_ref, e0_ref = refs[9:]
+        own_terms(p0_ref, a0_ref, r0_ref, 0, rot, tables, e0_ref)
+        own_terms(m7_ref, a7_ref, r7_ref, 1, rot, tables, e7_ref)
+        inner_open(gi_ref, ri_ref, rt_ref, ti_ref, rot, wp_ref)
+
+    return between
 
 
 def face_totals(now, before, accf_ref, afn_ref, opening):
@@ -517,6 +523,11 @@
     odd_pairs = [(i, (i + 1) % count if i % 2 else (i - 1) % count) for i in range(count)]
     swap_od = lambda x: lax.ppermute(x, "elem", odd_pairs)
     swap_ev = lambda x: lax.ppermute(x, "elem", even_pairs)
+    parts = lax.axis_size("ens")
+    second_core = lambda pairs: [
+        (e * count + a, e * count + b) for e in range(1, parts, 2) for a, b in pairs
+    ]
+    hand_over = lambda x: lax.ppermute(x, "ens", [(e, e - 1) for e in range(1, parts, 2)])
     members = scalars.shape[0]
     grid = (EXT, EXT, SUB, LANES)
     scal = scalars.reshape((members,) + grid)
@@ -528,15 +539,19 @@
     f32 = jnp.float32
 
     stay = lambda x: pltpu.with_memory_space_constraint(x, pltpu.HBM)
-    bundle = (3 * ROWS + 24, SUB, LANES)
+    bundle = (24, SUB, LANES)
     od, idx, slots, raw = call(
         project_odd, [(3 * ROWS, SUB, LANES), (SUB, LANES), (SUB, LANES), (9,) + tile],
         (stay(element_order), stay(scal), stay(mas), stay(tr)), "project", 1, hbm=(0, 1, 2, 3),
         scratch=[pltpu.VMEM((1, LANES), jnp.int32), pltpu.VMEM((3,) + tile, f32),
                  pltpu.SemaphoreType.DMA((13,))])
     rod = swap_od(od)
-    ev, tf = call(project_even, [bundle, (24, SUB, LANES)], (idx, raw), "project", 1)
-    rev, rtf = swap_ev(ev), swap_od(tf)
+    ev, te, to = call(
+        project_even, [(3 * ROWS, SUB, LANES), bundle, bundle], (idx, raw), "project", 1)
+    rev = swap_ev(ev)
+    got_te = lax.ppermute(te, ("ens", "elem"), second_core(even_pairs))
+    got_to = lax.ppermute(to, ("ens", "elem"), second_core(odd_pairs))
+    passed_te, passed_to = hand_over(got_te), hand_over(got_to)
     gi, q, ri, rt, ti, st = call(
         prepare, [inner, faces, (6,) + tile, (6,) + tile, (6, 2) + tile, (2,) + part],
         (idx, scal, mas, tr), "prepare", 1)
@@ -548,21 +563,26 @@
         s = 2 * n % STAGES + 1
         opening, closing, early = s == 1, s + 1 == STAGES, n == 0
         got_ev, got_od = swap_ev(cev), swap_od(cod)
-        extra = (tf, rtf, ev, rev, st, r0, ri, ti) if early else (acci, wp, a7)
+        extra = (te, got_te, passed_te, st, r0, ri, ti) if early else (acci, wp, a7)
         res = call(
             make_first_inner(1.0 / s, opening, early),
-            [inner, inner, faces, face] + ([geometry, geometry, (2,) + part] if early else []),
+            [inner, inner, faces, face] + ([geometry, (2,) + part] if early else []),
             (p0, p7, gi, rt, r7) + extra, "first", 1000,
             scratch=[pltpu.VMEM(inner, f32)] if early else [])
         gm, acci, q, e7 = res[:4]
         if early:
-            a0, a7, rs = res[4:]
+            a7, rs = res[4:]
         m7, cod2 = call(
             make_stage_face(1, 1.0 / s, False, early), [face, sent],
             (cev, got_ev, e7, accf, q, rs, r7), "ahead", 1)
         got_od2 = swap_od(cod2)
-        wp, e7, e0 = call(
-            between, [inner, face, face], (m7, gm, a7, r7, ri, rt, ti, p0, a0, r0), "between", 2000)
+        res = call(
+            make_between(early), [inner, face, face] + ([geometry] if early else []),
+            (m7, gm, a7, r7, ri, rt, ti, p0, r0)
+            + ((to, got_to, passed_to) if early else (a0,)), "between", 2000)
+        wp, e7, e0 = res[:3]
+        if early:
+            a0 = res[3]
         m0, cev2 = call(
             make_stage_face(0, 1.0 / s, False, early), [face, sent],
             (cod, got_od, e0, accf, q, rs, r0), "behind", 1)

time: 67.4 us -> 70.7 us (1.049)
  starting transfers between devices: 36.3 us -> 42.5 us
  waiting for transfers between devices: 15.3 us -> 12.3 us
    ppermute x0 -> x4, starting transfers between devices: none -> 3.91 us  [the longest x2 2.58 us: per_device(): lax.ppermute(x, 'ens', [(e, e - 1) for e in range(1, parts, 2)])]
    ppermute x10 -> x9, waiting for transfers between devices: 12.1 us -> 8.9 us  [per_device(): swap_od = lambda x: lax.ppermute(x, 'elem', odd_pairs)]
    ppermute x9, starting transfers between devices: 1.6 us -> 3.41 us  [per_device(): swap_ev = lambda x: lax.ppermute(x, 'elem', even_pairs)]
    ppermute x10 -> x9, starting transfers between devices: 34.7 us -> 35.2 us  [per_device(): swap_od = lambda x: lax.ppermute(x, 'elem', odd_pairs)]
  transfers between devices with their start and end apart: 19 -> 22, of which waited for: 15 -> 11; matrix products, arithmetic and copies ran while one was open for 0% -> 0% of each run, Pallas kernels for 20% -> 18%
where the time goes in v8:
time: 70.7 us; the launch traced here: 70.5 us
  starting transfers between devices  42.5 us (60%)
  Pallas kernels  15.3 us (22%)
  waiting for transfers between devices  12.3 us (17%)
    ppermute x9, starting transfers between devices, per_device(): swap_od = lambda x: lax.ppermute(x, 'elem', odd_pairs)  35.2 us
    pallas_call x33, Pallas kernels, call(): pl.pallas_call(kernel, out_shape=shapes[0] if single else shapes, in_spec...  15.3 us
    ppermute x9, waiting for transfers between devices, per_device(): swap_od = lambda x: lax.ppermute(x, 'elem', odd_pairs)  8.9 us
    ppermute x9, starting transfers between devices, per_device(): swap_ev = lambda x: lax.ppermute(x, 'elem', even_pairs)  3.41 us
    ppermute x9, waiting for transfers between devices, per_device(): swap_ev = lambda x: lax.ppermute(x, 'elem', even_pairs)  3.39 us
    ppermute x2, starting transfers between devices, per_device(): lax.ppermute(x, 'ens', [(e, e - 1) for e in range(1, parts, 2)])  2.58 us
  transfers between devices with their start and end apart: 22, of which 11 were waited for; matrix products, arithmetic and copies ran while one was open for 0% of the time, Pallas kernels for 18%

profile of v8, /device:TPU:0, one launch (start us, length us, event | category | flops | bytes accessed | tf_op | source)
XLA Modules:
  0.0 70.5 jit_solution(3199820760922940613)
XLA Ops:
  0.0 1.3 %project.2 = (f32[21,8,128]{2,1,0:T(8,128)S(1)}, s32[8,128]{1,0:T(8,128)S(1)}, s32[8,128]{1,0:T(8,128)S(1)}, f32[9,8,8,128]{3,2,1,0:T(8,128)S(1)}) custom-call(s32[1,128]{1,0:T(1,128)} %order_ref.1, f32[2,8,8,8,128]{4,3,2,1,0:T(8,128)} %bitcast.6, f32[8,8,8,128]{3,2,1,0:T(8,128)} %bitcast.8, f32[3,8,8,8,128]{4,3,2,1,0:T(8,128)} %bitcast.4), custom_call_target="tpu_custom_call" | custom-call | flops 1000000 | bytes 1024 | tf_op jit(solution)/shard_map/project/pallas_call | solution.py:505
  2.3 0.7 collective-permute-start.6
  3.0 6.7 %collective-permute-start.2 = (f32[21,8,128]{2,1,0:T(8,128)S(1)}, f32[21,8,128]{2,1,0:T(8,128)S(1)}, u32[]{:S(2)}, u32[]{:S(2)}) collective-permute-start(f32[21,8,128]{2,1,0:T(8,128)S(1)} %get-tuple-element.111.own_ref), channel_id=1, source_target_pairs={{0,31},{1,2},{2,1},{3,4},{4,3},{5,6},{6,5},{7,8},{8,7},{9,10},{10,... | collective-permute-start | bytes 258056 | tf_op jit(solution)/shard_map/ppermute | solution.py:524
  9.7 2.6 %prepare.1 = (f32[2,6,8,8,128]{4,3,2,1,0:T(8,128)S(1)}, f32[2,2,7,8,128]{4,3,2,1,0:T(8,128)S(1)}, f32[6,8,8,128]{3,2,1,0:T(8,128)S(1)}, f32[6,8,8,128]{3,2,1,0:T...) custom-call(s32[8,128]{1,0:T(8,128)S(1)} %get-tuple-element.105.idx_ref, ...), custom_call_target="tpu_custom_call" | custom-call | flops 1000000 | bytes 1024 | tf_op jit(solution)/shard_map/prepare/pallas_call | solution.py:505
  12.3 1.3 %collective-permute-start.5 = (f32[24,8,128]{2,1,0:T(8,128)S(1)}, f32[24,8,128]{2,1,0:T(8,128)S(1)}, u32[]{:S(2)}, u32[]{:S(2)}) collective-permute-start(f32[24,8,128]{2,1,0:T(8,128)S(1)} %collective-permute-done.4.refs_6_), channel_id=1, source_target_pairs={{32,0},{96,64},{33,1},{97,65},{34,2},{98,66},{35,3},{99,67},{36,4}... | collective-permute-start | bytes 294920 | tf_op jit(solution)/shard_map/ppermute | solution.py:530
  13.7 1.3 %collective-permute-start.7 = (f32[24,8,128]{2,1,0:T(8,128)S(1)}, f32[24,8,128]{2,1,0:T(8,128)S(1)}, u32[]{:S(2)}, u32[]{:S(2)}) collective-permute-start(f32[24,8,128]{2,1,0:T(8,128)S(1)} %collective-permute-done.6.refs_10_), channel_id=1, source_target_pairs={{32,0},{96,64},{33,1},{97,65},{34,2},{98,66},{35,3},{99,67},{36,4}... | collective-permute-start | bytes 294920 | tf_op jit(solution)/shard_map/ppermute | solution.py:530
  15.0 2.1 %collective-permute-start.3 = (f32[14,8,128]{2,1,0:T(8,128)S(1)}, f32[14,8,128]{2,1,0:T(8,128)S(1)}, u32[]{:S(2)}, u32[]{:S(2)}) collective-permute-start(f32[14,8,128]{2,1,0:T(8,128)S(1)} %get-tuple-element.112.own_ref), channel_id=1, source_target_pairs={{0,1},{1,0},{2,3},{3,2},{4,5},{5,4},{6,7},{7,6},{8,9},{9,8},{10,11... | collective-permute-start | bytes 172040 | tf_op jit(solution)/shard_map/ppermute | solution.py:525
  17.1 1.6 %collective-permute-start.1 = (f32[14,8,128]{2,1,0:T(8,128)S(1)}, f32[14,8,128]{2,1,0:T(8,128)S(1)}, u32[]{:S(2)}, u32[]{:S(2)}) collective-permute-start(f32[14,8,128]{2,1,0:T(8,128)S(1)} %get-tuple-element.110.own_ref), channel_id=1, source_target_pairs={{0,31},{1,2},{2,1},{3,4},{4,3},{5,6},{6,5},{7,8},{8,7},{9,10},{10,... | collective-permute-start | bytes 172040 | tf_op jit(solution)/shard_map/ppermute | solution.py:524
  18.7 1.0 %first.4 = (f32[2,6,8,8,128]{4,3,2,1,0:T(8,128)S(1)}, f32[2,6,8,8,128]{4,3,2,1,0:T(8,128)S(1)}, f32[2,2,7,8,128]{4,3,2,1,0:T(8,128)S(1)}, f32[2,7,8,128]{3,2,1,0...) custom-call(f32[2,7,8,128]{3,2,1,0:T(8,128)S(1)} %get-tuple-element.113.refs_0_.refs_7_.p0_ref, ...), custom_call_target="tpu_custom_call" | custom-call | flops 1000000000 | bytes 1024 | tf_op jit(solution)/shard_map/first/pallas_call | solution.py:505
  19.7 4.9 %collective-permute-start.10 = (f32[14,8,128]{2,1,0:T(8,128)S(1)}, f32[14,8,128]{2,1,0:T(8,128)S(1)}, u32[]{:S(2)}, u32[]{:S(2)}) collective-permute-start(f32[14,8,128]{2,1,0:T(8,128)S(1)} %get-tuple-element.139.own_ref), channel_id=1, source_target_pairs={{0,31},{1,2},{2,1},{3,4},{4,3},{5,6},{6,5},{7,8},{8,7},{9,10},{10,... | collective-permute-start | bytes 172040 | tf_op jit(solution)/shard_map/ppermute | solution.py:524
  24.5 0.9 %between.4 = (f32[2,6,8,8,128]{4,3,2,1,0:T(8,128)S(1)}, f32[2,7,8,128]{3,2,1,0:T(8,128)S(1)}, f32[2,7,8,128]{3,2,1,0:T(8,128)S(1)}, f32[3,8,8,128]{3,2,1,0:T(8,128)S(1)}) custom-call(f32[2,7,8,128]{3,2,1,0:T(8,128)S(1)} %get-tuple-element.125.refs_0_.m7_ref, f32[2,6,8,8,128]{4,3,2,1,0:T(8,128)S(1)} %get-tuple-element.126.refs_1_, ...), custom_call_target="tpu_custom_call" | custom-call | flops 2000000000 | bytes 1024 | tf_op jit(solution)/shard_map/between/pallas_call | solution.py:505
  25.7 1.0 %second.3 = (f32[2,6,8,8,128]{4,3,2,1,0:T(8,128)S(1)}, f32[2,2,7,8,128]{4,3,2,1,0:T(8,128)S(1)}, f32[2,6,8,8,128]{4,3,2,1,0:T(8,128)S(1)}, f32[2,2,7,8,128]{4,3,...) custom-call(f32[2,7,8,128]{3,2,1,0:T(8,128)S(1)} %get-tuple-element.132.m0_ref, ...), custom_call_target="tpu_custom_call" | custom-call | flops 3000000000 | bytes 1024 | tf_op jit(solution)/shard_map/second/pallas_call | solution.py:505
  26.7 1.5 %collective-permute-done.10.got_ref = f32[14,8,128]{2,1,0:T(8,128)S(1)} collective-permute-done((f32[14,8,128]{2,1,0:T(8,128)S(1)}, f32[14,8,128]{2,1,0:T(8,128)S(1)}, u32[]{:S(2)}, u32[]{:S(2)}) %collective-permute-start.10) | collective-permute-done | bytes 57376 | tf_op jit(solution)/shard_map/ppermute | solution.py:524
  28.8 1.1 %collective-permute-done.8.got_ref = f32[14,8,128]{2,1,0:T(8,128)S(1)} collective-permute-done((f32[14,8,128]{2,1,0:T(8,128)S(1)}, f32[14,8,128]{2,1,0:T(8,128)S(1)}, u32[]{:S(2)}, u32[]{:S(2)}) %collective-permute-start.8) | collective-permute-done | bytes 57376 | tf_op jit(solution)/shard_map/ppermute | solution.py:525
  29.9 3.6 %collective-permute-start.9 = (f32[14,8,128]{2,1,0:T(8,128)S(1)}, f32[14,8,128]{2,1,0:T(8,128)S(1)}, u32[]{:S(2)}, u32[]{:S(2)}) collective-permute-start(f32[14,8,128]{2,1,0:T(8,128)S(1)} %get-tuple-element.138.own_ref), channel_id=1, source_target_pairs={{0,31},{1,2},{2,1},{3,4},{4,3},{5,6},{6,5},{7,8},{8,7},{9,10},{10,... | collective-permute-start | bytes 172040 | tf_op jit(solution)/shard_map/ppermute | solution.py:524
  33.9 4.2 %collective-permute-start.14 = (f32[14,8,128]{2,1,0:T(8,128)S(1)}, f32[14,8,128]{2,1,0:T(8,128)S(1)}, u32[]{:S(2)}, u32[]{:S(2)}) collective-permute-start(f32[14,8,128]{2,1,0:T(8,128)S(1)} %get-tuple-element.160.own_ref), channel_id=1, source_target_pairs={{0,31},{1,2},{2,1},{3,4},{4,3},{5,6},{6,5},{7,8},{8,7},{9,10},{10,... | collective-permute-start | bytes 172040 | tf_op jit(solution)/shard_map/ppermute | solution.py:524
  38.0 0.9 %between.5 = (f32[2,6,8,8,128]{4,3,2,1,0:T(8,128)S(1)}, f32[2,7,8,128]{3,2,1,0:T(8,128)S(1)}, f32[2,7,8,128]{3,2,1,0:T(8,128)S(1)}) custom-call(f32[2,7,8,128]{3,2,1,0:T(8,128)S(1)} %get-tuple-element.149.refs_0_.m7_ref, f32[2,6,8,8,128]{4,3,2,1,0:T(8,128)S(1)} %get-tuple-element.150.refs_1_, f32[3,8,8,128]{3,2,1,0:T(8,128)S(1)} %get-tuple-element.127.refs_2_.refs_7_, ...), custom_call_target="tpu_custom_call" | custom-call | flops 2000000000 | bytes 1024 | tf_op jit(solution)/shard_map/between/pallas_call | solution.py:505
  39.1 1.0 %second.4 = (f32[2,6,8,8,128]{4,3,2,1,0:T(8,128)S(1)}, f32[2,2,7,8,128]{4,3,2,1,0:T(8,128)S(1)}, f32[2,6,8,8,128]{4,3,2,1,0:T(8,128)S(1)}, f32[2,2,7,8,128]{4,3,...) custom-call(f32[2,7,8,128]{3,2,1,0:T(8,128)S(1)} %get-tuple-element.154.m0_ref, ...), custom_call_target="tpu_custom_call" | custom-call | flops 3000000000 | bytes 1024 | tf_op jit(solution)/shard_map/second/pallas_call | solution.py:505
  40.1 2.3 %collective-permute-done.14.got_ref = f32[14,8,128]{2,1,0:T(8,128)S(1)} collective-permute-done((f32[14,8,128]{2,1,0:T(8,128)S(1)}, f32[14,8,128]{2,1,0:T(8,128)S(1)}, u32[]{:S(2)}, u32[]{:S(2)}) %collective-permute-start.14) | collective-permute-done | bytes 57376 | tf_op jit(solution)/shard_map/ppermute | solution.py:524
  42.5 0.8 %collective-permute-done.12.got_ref = f32[14,8,128]{2,1,0:T(8,128)S(1)} collective-permute-done((f32[14,8,128]{2,1,0:T(8,128)S(1)}, f32[14,8,128]{2,1,0:T(8,128)S(1)}, u32[]{:S(2)}, u32[]{:S(2)}) %collective-permute-start.12) | collective-permute-done | bytes 57376 | tf_op jit(solution)/shard_map/ppermute | solution.py:525
  43.3 3.4 %collective-permute-start.13 = (f32[14,8,128]{2,1,0:T(8,128)S(1)}, f32[14,8,128]{2,1,0:T(8,128)S(1)}, u32[]{:S(2)}, u32[]{:S(2)}) collective-permute-start(f32[14,8,128]{2,1,0:T(8,128)S(1)} %get-tuple-element.159.own_ref), channel_id=1, source_target_pairs={{0,31},{1,2},{2,1},{3,4},{4,3},{5,6},{6,5},{7,8},{8,7},{9,10},{10,... | collective-permute-start | bytes 172040 | tf_op jit(solution)/shard_map/ppermute | solution.py:524
  47.1 4.1 %collective-permute-start.18 = (f32[14,8,128]{2,1,0:T(8,128)S(1)}, f32[14,8,128]{2,1,0:T(8,128)S(1)}, u32[]{:S(2)}, u32[]{:S(2)}) collective-permute-start(f32[14,8,128]{2,1,0:T(8,128)S(1)} %get-tuple-element.181.own_ref), channel_id=1, source_target_pairs={{0,31},{1,2},{2,1},{3,4},{4,3},{5,6},{6,5},{7,8},{8,7},{9,10},{10,... | collective-permute-start | bytes 172040 | tf_op jit(solution)/shard_map/ppermute | solution.py:524
  51.2 0.9 %between.6 = (f32[2,6,8,8,128]{4,3,2,1,0:T(8,128)S(1)}, f32[2,7,8,128]{3,2,1,0:T(8,128)S(1)}, f32[2,7,8,128]{3,2,1,0:T(8,128)S(1)}) custom-call(f32[2,7,8,128]{3,2,1,0:T(8,128)S(1)} %get-tuple-element.170.refs_0_.m7_ref, f32[2,6,8,8,128]{4,3,2,1,0:T(8,128)S(1)} %get-tuple-element.171.refs_1_, f32[3,8,8,128]{3,2,1,0:T(8,128)S(1)} %get-tuple-element.127.refs_2_.refs_7_, ...), custom_call_target="tpu_custom_call" | custom-call | flops 2000000000 | bytes 1024 | tf_op jit(solution)/shard_map/between/pallas_call | solution.py:505
  52.6 1.0 %second.5 = (f32[2,6,8,8,128]{4,3,2,1,0:T(8,128)S(1)}, f32[2,2,7,8,128]{4,3,2,1,0:T(8,128)S(1)}, f32[2,6,8,8,128]{4,3,2,1,0:T(8,128)S(1)}, f32[2,2,7,8,128]{4,3,...) custom-call(f32[2,7,8,128]{3,2,1,0:T(8,128)S(1)} %get-tuple-element.175.m0_ref, ...), custom_call_target="tpu_custom_call" | custom-call | flops 3000000000 | bytes 1024 | tf_op jit(solution)/shard_map/second/pallas_call | solution.py:505
  53.6 2.1 %collective-permute-done.18.got_ref = f32[14,8,128]{2,1,0:T(8,128)S(1)} collective-permute-done((f32[14,8,128]{2,1,0:T(8,128)S(1)}, f32[14,8,128]{2,1,0:T(8,128)S(1)}, u32[]{:S(2)}, u32[]{:S(2)}) %collective-permute-start.18) | collective-permute-done | bytes 57376 | tf_op jit(solution)/shard_map/ppermute | solution.py:524
  55.8 1.0 %collective-permute-done.16.got_ref = f32[14,8,128]{2,1,0:T(8,128)S(1)} collective-permute-done((f32[14,8,128]{2,1,0:T(8,128)S(1)}, f32[14,8,128]{2,1,0:T(8,128)S(1)}, u32[]{:S(2)}, u32[]{:S(2)}) %collective-permute-start.16) | collective-permute-done | bytes 57376 | tf_op jit(solution)/shard_map/ppermute | solution.py:525
  56.8 3.2 %collective-permute-start.17 = (f32[14,8,128]{2,1,0:T(8,128)S(1)}, f32[14,8,128]{2,1,0:T(8,128)S(1)}, u32[]{:S(2)}, u32[]{:S(2)}) collective-permute-start(f32[14,8,128]{2,1,0:T(8,128)S(1)} %get-tuple-element.180.own_ref), channel_id=1, source_target_pairs={{0,31},{1,2},{2,1},{3,4},{4,3},{5,6},{6,5},{7,8},{8,7},{9,10},{10,... | collective-permute-start | bytes 172040 | tf_op jit(solution)/shard_map/ppermute | solution.py:524
  60.4 3.6 %collective-permute-start.21 = (f32[14,8,128]{2,1,0:T(8,128)S(1)}, f32[14,8,128]{2,1,0:T(8,128)S(1)}, u32[]{:S(2)}, u32[]{:S(2)}) collective-permute-start(f32[14,8,128]{2,1,0:T(8,128)S(1)} %get-tuple-element.200.own_ref), channel_id=1, source_target_pairs={{0,31},{1,2},{2,1},{3,4},{4,3},{5,6},{6,5},{7,8},{8,7},{9,10},{10,... | collective-permute-start | bytes 172040 | tf_op jit(solution)/shard_map/ppermute | solution.py:524
  64.0 0.9 %between.7 = (f32[2,6,8,8,128]{4,3,2,1,0:T(8,128)S(1)}, f32[2,7,8,128]{3,2,1,0:T(8,128)S(1)}, f32[2,7,8,128]{3,2,1,0:T(8,128)S(1)}) custom-call(f32[2,7,8,128]{3,2,1,0:T(8,128)S(1)} %get-tuple-element.191.refs_0_.m7_ref, f32[2,6,8,8,128]{4,3,2,1,0:T(8,128)S(1)} %get-tuple-element.192.refs_1_, f32[3,8,8,128]{3,2,1,0:T(8,128)S(1)} %get-tuple-element.127.refs_2_.refs_7_, ...), custom_call_target="tpu_custom_call" | custom-call | flops 2000000000 | bytes 1024 | tf_op jit(solution)/shard_map/between/pallas_call | solution.py:505
  65.4 1.1 %last.1 = (f32[2,8,8,8,128]{4,3,2,1,0:T(8,128)}, f32[2,2,7,8,128]{4,3,2,1,0:T(8,128)S(1)}, f32[2,7,8,128]{3,2,1,0:T(8,128)S(1)}) custom-call(s32[8,128]{1,0:T(8,128)S(1)} %get-tuple-element.104.slot_ref, f32[2,7,8,128]{3,2,1,0:T(8,128)S(1)} %get-tuple-element.196.m0_ref, f32[2,7,8,128]{3,2,1,0:T(8,128)S(1)} %get-tuple-element.191.refs_0_.m7_ref, ...), custom_call_target="tpu_custom_call" | custom-call | flops 3000000000 | bytes 1024 | tf_op jit(solution)/shard_map/last/pallas_call | solution.py:505
  66.5 2.3 %collective-permute-done.21.got_ref = f32[14,8,128]{2,1,0:T(8,128)S(1)} collective-permute-done((f32[14,8,128]{2,1,0:T(8,128)S(1)}, f32[14,8,128]{2,1,0:T(8,128)S(1)}, u32[]{:S(2)}, u32[]{:S(2)}) %collective-permute-start.21) | collective-permute-done | bytes 57376 | tf_op jit(solution)/shard_map/ppermute | solution.py:524
  69.6 0.8 %finish.3 = f32[2,8,8,8,128]{4,3,2,1,0:T(8,128)} custom-call(s32[8,128]{1,0:T(8,128)S(1)} %get-tuple-element.104.slot_ref, f32[14,8,128]{2,1,0:T(8,128)S(1)} %get-tuple-element.194.own_ref, f32[14,8,128]{2,1,0:T(8,128)S(1)} %collective-permute-done.20.got_ref, f32[2,7,8,128]{3,2,1,0:T(8,128)S(1)} %get-tuple-element.195.e_ref, ...), custom_call_target="tpu_custom_call", output_to_operand_aliasing={{}: (6, {})} | custom-call | flops 1000000 | bytes 1024 | tf_op jit(solution)/shard_map/finish/pallas_call | solution.py:505
  (51 shorter events, 5.2 us)
Async XLA Ops:
  0.0 9.7 %copy-start = (f32[3,512,128]{2,1,0:T(8,128)S(1)}, f32[3,512,128]{2,1,0:T(8,128)}, u32[]{:S(2)}) copy-start(f32[3,512,128]{2,1,0:T(8,128)} %param.5) | copy-start | bytes 2359300
  0.0 9.7 %copy-start.1 = (f32[2,512,128]{2,1,0:T(8,128)S(1)}, f32[2,512,128]{2,1,0:T(8,128)}, u32[]{:S(2)}) copy-start(f32[2,512,128]{2,1,0:T(8,128)} %param.4) | copy-start | bytes 1572868
  1.3 8.4 %copy-start.2 = (f32[512,128]{1,0:T(8,128)S(1)}, f32[512,128]{1,0:T(8,128)}, u32[]{:S(2)}) copy-start(f32[512,128]{1,0:T(8,128)} %param.6) | copy-start | bytes 786436
  1.7 10.7 %collective-permute-start.4 = (f32[24,8,128]{2,1,0:T(8,128)S(1)}, f32[24,8,128]{2,1,0:T(8,128)S(1)}, u32[]{:S(2)}, u32[]{:S(2)}) collective-permute-start(f32[24,8,128]{2,1,0:T(8,128)S(1)} %get-tuple-element.118.refs_5_), channel_id=1, source_target_pairs={{32,33},{33,32},{34,35},{35,34},{36,37},{37,36},{38,39},{39,38},{4... | collective-permute-start | bytes 294920 | tf_op jit(solution)/shard_map/ppermute | solution.py:552
  2.3 11.3 %collective-permute-start.6 = (f32[24,8,128]{2,1,0:T(8,128)S(1)}, f32[24,8,128]{2,1,0:T(8,128)S(1)}, u32[]{:S(2)}, u32[]{:S(2)}) collective-permute-start(f32[24,8,128]{2,1,0:T(8,128)S(1)} %get-tuple-element.128.refs_9_), channel_id=1, source_target_pairs={{32,63},{33,34},{34,33},{35,36},{36,35},{37,38},{38,37},{39,40},{4... | collective-permute-start | bytes 294920 | tf_op jit(solution)/shard_map/ppermute | solution.py:553
  3.0 12.0 %collective-permute-start.2 = (f32[21,8,128]{2,1,0:T(8,128)S(1)}, f32[21,8,128]{2,1,0:T(8,128)S(1)}, u32[]{:S(2)}, u32[]{:S(2)}) collective-permute-start(f32[21,8,128]{2,1,0:T(8,128)S(1)} %get-tuple-element.111.own_ref), channel_id=1, source_target_pairs={{0,31},{1,2},{2,1},{3,4},{4,3},{5,6},{6,5},{7,8},{8,7},{9,10},{10,... | collective-permute-start | bytes 258056 | tf_op jit(solution)/shard_map/ppermute | solution.py:524
  9.7 7.4 %collective-permute-start = (f32[21,8,128]{2,1,0:T(8,128)S(1)}, f32[21,8,128]{2,1,0:T(8,128)S(1)}, u32[]{:S(2)}, u32[]{:S(2)}) collective-permute-start(f32[21,8,128]{2,1,0:T(8,128)S(1)} %get-tuple-element.107.own_ref), channel_id=1, source_target_pairs={{0,1},{1,0},{2,3},{3,2},{4,5},{5,4},{6,7},{7,6},{8,9},{9,8},{10,11... | collective-permute-start | bytes 258056 | tf_op jit(solution)/shard_map/ppermute | solution.py:525
  12.3 6.3 %collective-permute-start.5 = (f32[24,8,128]{2,1,0:T(8,128)S(1)}, f32[24,8,128]{2,1,0:T(8,128)S(1)}, u32[]{:S(2)}, u32[]{:S(2)}) collective-permute-start(f32[24,8,128]{2,1,0:T(8,128)S(1)} %collective-permute-done.4.refs_6_), channel_id=1, source_target_pairs={{32,0},{96,64},{33,1},{97,65},{34,2},{98,66},{35,3},{99,67},{36,4}... | collective-permute-start | bytes 294920 | tf_op jit(solution)/shard_map/ppermute | solution.py:530
  13.7 10.9 %collective-permute-start.7 = (f32[24,8,128]{2,1,0:T(8,128)S(1)}, f32[24,8,128]{2,1,0:T(8,128)S(1)}, u32[]{:S(2)}, u32[]{:S(2)}) collective-permute-start(f32[24,8,128]{2,1,0:T(8,128)S(1)} %collective-permute-done.6.refs_10_), channel_id=1, source_target_pairs={{32,0},{96,64},{33,1},{97,65},{34,2},{98,66},{35,3},{99,67},{36,4}... | collective-permute-start | bytes 294920 | tf_op jit(solution)/shard_map/ppermute | solution.py:530
  15.0 4.6 %collective-permute-start.3 = (f32[14,8,128]{2,1,0:T(8,128)S(1)}, f32[14,8,128]{2,1,0:T(8,128)S(1)}, u32[]{:S(2)}, u32[]{:S(2)}) collective-permute-start(f32[14,8,128]{2,1,0:T(8,128)S(1)} %get-tuple-element.112.own_ref), channel_id=1, source_target_pairs={{0,1},{1,0},{2,3},{3,2},{4,5},{5,4},{6,7},{7,6},{8,9},{9,8},{10,11... | collective-permute-start | bytes 172040 | tf_op jit(solution)/shard_map/ppermute | solution.py:525
  17.1 8.5 %collective-permute-start.1 = (f32[14,8,128]{2,1,0:T(8,128)S(1)}, f32[14,8,128]{2,1,0:T(8,128)S(1)}, u32[]{:S(2)}, u32[]{:S(2)}) collective-permute-start(f32[14,8,128]{2,1,0:T(8,128)S(1)} %get-tuple-element.110.own_ref), channel_id=1, source_target_pairs={{0,31},{1,2},{2,1},{3,4},{4,3},{5,6},{6,5},{7,8},{8,7},{9,10},{10,... | collective-permute-start | bytes 172040 | tf_op jit(solution)/shard_map/ppermute | solution.py:524
  19.7 8.5 %collective-permute-start.10 = (f32[14,8,128]{2,1,0:T(8,128)S(1)}, f32[14,8,128]{2,1,0:T(8,128)S(1)}, u32[]{:S(2)}, u32[]{:S(2)}) collective-permute-start(f32[14,8,128]{2,1,0:T(8,128)S(1)} %get-tuple-element.139.own_ref), channel_id=1, source_target_pairs={{0,31},{1,2},{2,1},{3,4},{4,3},{5,6},{6,5},{7,8},{8,7},{9,10},{10,... | collective-permute-start | bytes 172040 | tf_op jit(solution)/shard_map/ppermute | solution.py:524
  25.6 4.3 %collective-permute-start.8 = (f32[14,8,128]{2,1,0:T(8,128)S(1)}, f32[14,8,128]{2,1,0:T(8,128)S(1)}, u32[]{:S(2)}, u32[]{:S(2)}) collective-permute-start(f32[14,8,128]{2,1,0:T(8,128)S(1)} %get-tuple-element.130.own_ref), channel_id=1, source_target_pairs={{0,1},{1,0},{2,3},{3,2},{4,5},{5,4},{6,7},{7,6},{8,9},{9,8},{10,11... | collective-permute-start | bytes 172040 | tf_op jit(solution)/shard_map/ppermute | solution.py:525
  28.2 5.7 %collective-permute-start.11 = (f32[14,8,128]{2,1,0:T(8,128)S(1)}, f32[14,8,128]{2,1,0:T(8,128)S(1)}, u32[]{:S(2)}, u32[]{:S(2)}) collective-permute-start(f32[14,8,128]{2,1,0:T(8,128)S(1)} %get-tuple-element.141.own_ref), channel_id=1, source_target_pairs={{0,1},{1,0},{2,3},{3,2},{4,5},{5,4},{6,7},{7,6},{8,9},{9,8},{10,11... | collective-permute-start | bytes 172040 | tf_op jit(solution)/shard_map/ppermute | solution.py:525
  29.9 9.0 %collective-permute-start.9 = (f32[14,8,128]{2,1,0:T(8,128)S(1)}, f32[14,8,128]{2,1,0:T(8,128)S(1)}, u32[]{:S(2)}, u32[]{:S(2)}) collective-permute-start(f32[14,8,128]{2,1,0:T(8,128)S(1)} %get-tuple-element.138.own_ref), channel_id=1, source_target_pairs={{0,31},{1,2},{2,1},{3,4},{4,3},{5,6},{6,5},{7,8},{8,7},{9,10},{10,... | collective-permute-start | bytes 172040 | tf_op jit(solution)/shard_map/ppermute | solution.py:524
  33.9 8.5 %collective-permute-start.14 = (f32[14,8,128]{2,1,0:T(8,128)S(1)}, f32[14,8,128]{2,1,0:T(8,128)S(1)}, u32[]{:S(2)}, u32[]{:S(2)}) collective-permute-start(f32[14,8,128]{2,1,0:T(8,128)S(1)} %get-tuple-element.160.own_ref), channel_id=1, source_target_pairs={{0,31},{1,2},{2,1},{3,4},{4,3},{5,6},{6,5},{7,8},{8,7},{9,10},{10,... | collective-permute-start | bytes 172040 | tf_op jit(solution)/shard_map/ppermute | solution.py:524
  39.0 4.3 %collective-permute-start.12 = (f32[14,8,128]{2,1,0:T(8,128)S(1)}, f32[14,8,128]{2,1,0:T(8,128)S(1)}, u32[]{:S(2)}, u32[]{:S(2)}) collective-permute-start(f32[14,8,128]{2,1,0:T(8,128)S(1)} %get-tuple-element.152.own_ref), channel_id=1, source_target_pairs={{0,1},{1,0},{2,3},{3,2},{4,5},{5,4},{6,7},{7,6},{8,9},{9,8},{10,11... | collective-permute-start | bytes 172040 | tf_op jit(solution)/shard_map/ppermute | solution.py:525
  42.4 4.7 %collective-permute-start.15 = (f32[14,8,128]{2,1,0:T(8,128)S(1)}, f32[14,8,128]{2,1,0:T(8,128)S(1)}, u32[]{:S(2)}, u32[]{:S(2)}) collective-permute-start(f32[14,8,128]{2,1,0:T(8,128)S(1)} %get-tuple-element.162.own_ref), channel_id=1, source_target_pairs={{0,1},{1,0},{2,3},{3,2},{4,5},{5,4},{6,7},{7,6},{8,9},{9,8},{10,11... | collective-permute-start | bytes 172040 | tf_op jit(solution)/shard_map/ppermute | solution.py:525
  43.3 9.0 %collective-permute-start.13 = (f32[14,8,128]{2,1,0:T(8,128)S(1)}, f32[14,8,128]{2,1,0:T(8,128)S(1)}, u32[]{:S(2)}, u32[]{:S(2)}) collective-permute-start(f32[14,8,128]{2,1,0:T(8,128)S(1)} %get-tuple-element.159.own_ref), channel_id=1, source_target_pairs={{0,31},{1,2},{2,1},{3,4},{4,3},{5,6},{6,5},{7,8},{8,7},{9,10},{10,... | collective-permute-start | bytes 172040 | tf_op jit(solution)/shard_map/ppermute | solution.py:524
  47.1 8.6 %collective-permute-start.18 = (f32[14,8,128]{2,1,0:T(8,128)S(1)}, f32[14,8,128]{2,1,0:T(8,128)S(1)}, u32[]{:S(2)}, u32[]{:S(2)}) collective-permute-start(f32[14,8,128]{2,1,0:T(8,128)S(1)} %get-tuple-element.181.own_ref), channel_id=1, source_target_pairs={{0,31},{1,2},{2,1},{3,4},{4,3},{5,6},{6,5},{7,8},{8,7},{9,10},{10,... | collective-permute-start | bytes 172040 | tf_op jit(solution)/shard_map/ppermute | solution.py:524
  52.3 4.4 %collective-permute-start.16 = (f32[14,8,128]{2,1,0:T(8,128)S(1)}, f32[14,8,128]{2,1,0:T(8,128)S(1)}, u32[]{:S(2)}, u32[]{:S(2)}) collective-permute-start(f32[14,8,128]{2,1,0:T(8,128)S(1)} %get-tuple-element.173.own_ref), channel_id=1, source_target_pairs={{0,1},{1,0},{2,3},{3,2},{4,5},{5,4},{6,7},{7,6},{8,9},{9,8},{10,11... | collective-permute-start | bytes 172040 | tf_op jit(solution)/shard_map/ppermute | solution.py:525
  55.7 4.7 %collective-permute-start.19 = (f32[14,8,128]{2,1,0:T(8,128)S(1)}, f32[14,8,128]{2,1,0:T(8,128)S(1)}, u32[]{:S(2)}, u32[]{:S(2)}) collective-permute-start(f32[14,8,128]{2,1,0:T(8,128)S(1)} %get-tuple-element.183.own_ref), channel_id=1, source_target_pairs={{0,1},{1,0},{2,3},{3,2},{4,5},{5,4},{6,7},{7,6},{8,9},{9,8},{10,11... | collective-permute-start | bytes 172040 | tf_op jit(solution)/shard_map/ppermute | solution.py:525
  56.8 8.5 %collective-permute-start.17 = (f32[14,8,128]{2,1,0:T(8,128)S(1)}, f32[14,8,128]{2,1,0:T(8,128)S(1)}, u32[]{:S(2)}, u32[]{:S(2)}) collective-permute-start(f32[14,8,128]{2,1,0:T(8,128)S(1)} %get-tuple-element.180.own_ref), channel_id=1, source_target_pairs={{0,31},{1,2},{2,1},{3,4},{4,3},{5,6},{6,5},{7,8},{8,7},{9,10},{10,... | collective-permute-start | bytes 172040 | tf_op jit(solution)/shard_map/ppermute | solution.py:524
  60.4 8.5 %collective-permute-start.21 = (f32[14,8,128]{2,1,0:T(8,128)S(1)}, f32[14,8,128]{2,1,0:T(8,128)S(1)}, u32[]{:S(2)}, u32[]{:S(2)}) collective-permute-start(f32[14,8,128]{2,1,0:T(8,128)S(1)} %get-tuple-element.200.own_ref), channel_id=1, source_target_pairs={{0,31},{1,2},{2,1},{3,4},{4,3},{5,6},{6,5},{7,8},{8,7},{9,10},{10,... | collective-permute-start | bytes 172040 | tf_op jit(solution)/shard_map/ppermute | solution.py:524
  65.3 4.3 %collective-permute-start.20 = (f32[14,8,128]{2,1,0:T(8,128)S(1)}, f32[14,8,128]{2,1,0:T(8,128)S(1)}, u32[]{:S(2)}, u32[]{:S(2)}) collective-permute-start(f32[14,8,128]{2,1,0:T(8,128)S(1)} %get-tuple-element.194.own_ref), channel_id=1, source_target_pairs={{0,1},{1,0},{2,3},{3,2},{4,5},{5,4},{6,7},{7,6},{8,9},{9,8},{10,11... | collective-permute-start | bytes 172040 | tf_op jit(solution)/shard_map/ppermute | solution.py:525

commit v9 on v6

--- a/solution.py
+++ b/solution.py
@@ -360,10 +360,9 @@
         tables = third_tables()
         rot = rotations()
         if start:
-            tf_ref, rtf_ref, ev_ref, rev_ref, st_ref, r0_ref, ri_ref, ti_ref = refs[5:13]
-            gn_ref, an_ref, q_ref, e7_ref, a0_ref, a7_ref, rs_ref, wp_ref = refs[13:]
+            ev_ref, rev_ref, st_ref, r0_ref, ri_ref, ti_ref = refs[5:11]
+            gn_ref, an_ref, q_ref, e7_ref, a7_ref, rs_ref, wp_ref = refs[11:]
             inner_open(gi_ref, ri_ref, rt_ref, ti_ref, rot, wp_ref)
-            both_sides(transports(tf_ref, 0), transports(rtf_ref, 0), tables, a0_ref)
             both_sides(
                 transports(ev_ref, 3 * ROWS), transports(rev_ref, 3 * ROWS), tables, a7_ref)
             write(rs_ref, (0,), [st_ref[0, j] * r0_ref[j] for j in range(ROWS)])
@@ -384,13 +383,21 @@
     return first_inner
 
 
-def between(m7_ref, gi_ref, a7_ref, r7_ref, ri_ref, rt_ref, ti_ref, p0_ref, a0_ref, r0_ref,
-            wp_ref, e7_ref, e0_ref):
-    rot = rotations()
-    tables = third_tables()
-    own_terms(p0_ref, a0_ref, r0_ref, 0, rot, tables, e0_ref)
-    own_terms(m7_ref, a7_ref, r7_ref, 1, rot, tables, e7_ref)
-    inner_open(gi_ref, ri_ref, rt_ref, ti_ref, rot, wp_ref)
+def make_between(start):
+    def between(*refs):
+        m7_ref, gi_ref, a7_ref, r7_ref, ri_ref, rt_ref, ti_ref, p0_ref, r0_ref = refs[:9]
+        rot = rotations()
+        tables = third_tables()
+        if start:
+            tf_ref, rtf_ref, wp_ref, e7_ref, e0_ref, a0_ref = refs[9:]
+            both_sides(transports(tf_ref, 0), transports(rtf_ref, 0), tables, a0_ref)
+        else:
+            a0_ref, wp_ref, e7_ref, e0_ref = refs[9:]
+        own_terms(p0_ref, a0_ref, r0_ref, 0, rot, tables, e0_ref)
+        own_terms(m7_ref, a7_ref, r7_ref, 1, rot, tables, e7_ref)
+        inner_open(gi_ref, ri_ref, rt_ref, ti_ref, rot, wp_ref)
+
+    return between
 
 
 def face_totals(now, before, accf_ref, afn_ref, opening):
@@ -473,13 +480,12 @@
         dst = source_plane(lax.axis_index("elem") % 2, face * ORDER)
         copies = []
         for m in range(2):
+            write(buf, (m,), final_face(face, scale, slot_ref, own_ref, got_ref, e_ref, accf_ref, m))
+            copies.append(pltpu.make_async_copy(buf.at[m], out_ref.at[m, dst], sems.at[0, m]))
             copies.append(
                 pltpu.make_async_copy(near_ref.at[m], out_ref.at[m, ORDER - dst], sems.at[1, m])
             )
-            copies[-1].start()
-        for m in range(2):
-            write(buf, (m,), final_face(face, scale, slot_ref, own_ref, got_ref, e_ref, accf_ref, m))
-            copies.append(pltpu.make_async_copy(buf.at[m], out_ref.at[m, dst], sems.at[0, m]))
+            copies[-2].start()
             copies[-1].start()
         for copy in copies:
             copy.wait()
@@ -548,21 +554,25 @@
         s = 2 * n % STAGES + 1
         opening, closing, early = s == 1, s + 1 == STAGES, n == 0
         got_ev, got_od = swap_ev(cev), swap_od(cod)
-        extra = (tf, rtf, ev, rev, st, r0, ri, ti) if early else (acci, wp, a7)
+        extra = (ev, rev, st, r0, ri, ti) if early else (acci, wp, a7)
         res = call(
             make_first_inner(1.0 / s, opening, early),
-            [inner, inner, faces, face] + ([geometry, geometry, (2,) + part] if early else []),
+            [inner, inner, faces, face] + ([geometry, (2,) + part] if early else []),
             (p0, p7, gi, rt, r7) + extra, "first", 1000,
             scratch=[pltpu.VMEM(inner, f32)] if early else [])
         gm, acci, q, e7 = res[:4]
         if early:
-            a0, a7, rs = res[4:]
+            a7, rs = res[4:]
         m7, cod2 = call(
             make_stage_face(1, 1.0 / s, False, early), [face, sent],
             (cev, got_ev, e7, accf, q, rs, r7), "ahead", 1)
         got_od2 = swap_od(cod2)
-        wp, e7, e0 = call(
-            between, [inner, face, face], (m7, gm, a7, r7, ri, rt, ti, p0, a0, r0), "between", 2000)
+        res = call(
+            make_between(early), [inner, face, face] + ([geometry] if early else []),
+            (m7, gm, a7, r7, ri, rt, ti, p0, r0) + ((tf, rtf) if early else (a0,)), "between", 2000)
+        wp, e7, e0 = res[:3]
+        if early:
+            a0 = res[3]
         m0, cev2 = call(
             make_stage_face(0, 1.0 / s, False, early), [face, sent],
             (cod, got_od, e0, accf, q, rs, r0), "behind", 1)

time: 67.4 us -> 67.4 us (level)
  transfers between devices with their start and end apart: 19 -> 19, of which waited for: 15 -> 14; matrix products, arithmetic and copies ran while one was open for 0% -> 0% of each run, Pallas kernels for 20% -> 20%
where the time goes in v9:
time: 67.4 us; the launch traced here: 67.3 us
  starting transfers between devices  36.3 us (54%)
  waiting for transfers between devices  15.4 us (23%)
  Pallas kernels  15.3 us (23%)
    ppermute x10, starting transfers between devices, per_device(): swap_od = lambda x: lax.ppermute(x, 'elem', odd_pairs)  34.7 us
    pallas_call x33, Pallas kernels, call(): pl.pallas_call(kernel, out_shape=shapes[0] if single else shapes, in_spec...  15.3 us
    ppermute x10, waiting for transfers between devices, per_device(): swap_od = lambda x: lax.ppermute(x, 'elem', odd_pairs)  12.1 us
    ppermute x9, waiting for transfers between devices, per_device(): swap_ev = lambda x: lax.ppermute(x, 'elem', even_pairs)  3.32 us
    ppermute x9, starting transfers between devices, per_device(): swap_ev = lambda x: lax.ppermute(x, 'elem', even_pairs)  1.6 us
  transfers between devices with their start and end apart: 19, of which 14 were waited for; matrix products, arithmetic and copies ran while one was open for 0% of the time, Pallas kernels for 20%

profile of v9, /device:TPU:0, one launch (start us, length us, event | category | flops | bytes accessed | tf_op | source)
XLA Modules:
  0.0 67.3 jit_solution(1103113167874060135)
XLA Ops:
  0.0 1.3 %project.2 = (f32[21,8,128]{2,1,0:T(8,128)S(1)}, s32[8,128]{1,0:T(8,128)S(1)}, s32[8,128]{1,0:T(8,128)S(1)}, f32[9,8,8,128]{3,2,1,0:T(8,128)S(1)}) custom-call(s32[1,128]{1,0:T(1,128)} %order_ref.1, f32[2,8,8,8,128]{4,3,2,1,0:T(8,128)} %bitcast.6, f32[8,8,8,128]{3,2,1,0:T(8,128)} %bitcast.8, f32[3,8,8,8,128]{4,3,2,1,0:T(8,128)} %bitcast.4), custom_call_target="tpu_custom_call" | custom-call | flops 1000000 | bytes 1024 | tf_op jit(solution)/shard_map/project/pallas_call | solution.py:505
  1.4 6.7 %collective-permute-start.2 = (f32[21,8,128]{2,1,0:T(8,128)S(1)}, f32[21,8,128]{2,1,0:T(8,128)S(1)}, u32[]{:S(2)}, u32[]{:S(2)}) collective-permute-start(f32[21,8,128]{2,1,0:T(8,128)S(1)} %get-tuple-element.110.own_ref), channel_id=1, source_target_pairs={{0,31},{1,2},{2,1},{3,4},{4,3},{5,6},{6,5},{7,8},{8,7},{9,10},{10,... | collective-permute-start | bytes 258056 | tf_op jit(solution)/shard_map/ppermute | solution.py:524
  8.4 1.4 %collective-permute-start.4 = (f32[24,8,128]{2,1,0:T(8,128)S(1)}, f32[24,8,128]{2,1,0:T(8,128)S(1)}, u32[]{:S(2)}, u32[]{:S(2)}) collective-permute-start(f32[24,8,128]{2,1,0:T(8,128)S(1)} %get-tuple-element.126.refs_9_), channel_id=1, source_target_pairs={{0,31},{1,2},{2,1},{3,4},{4,3},{5,6},{6,5},{7,8},{8,7},{9,10},{10,... | collective-permute-start | bytes 294920 | tf_op jit(solution)/shard_map/ppermute | solution.py:524
  9.8 2.6 %prepare.1 = (f32[2,6,8,8,128]{4,3,2,1,0:T(8,128)S(1)}, f32[2,2,7,8,128]{4,3,2,1,0:T(8,128)S(1)}, f32[6,8,8,128]{3,2,1,0:T(8,128)S(1)}, f32[6,8,8,128]{3,2,1,0:T...) custom-call(s32[8,128]{1,0:T(8,128)S(1)} %get-tuple-element.104.idx_ref, ...), custom_call_target="tpu_custom_call" | custom-call | flops 1000000 | bytes 1024 | tf_op jit(solution)/shard_map/prepare/pallas_call | solution.py:505
  12.4 0.8 %collective-permute-start.3 = (f32[14,8,128]{2,1,0:T(8,128)S(1)}, f32[14,8,128]{2,1,0:T(8,128)S(1)}, u32[]{:S(2)}, u32[]{:S(2)}) collective-permute-start(f32[14,8,128]{2,1,0:T(8,128)S(1)} %get-tuple-element.111.own_ref), channel_id=1, source_target_pairs={{0,1},{1,0},{2,3},{3,2},{4,5},{5,4},{6,7},{7,6},{8,9},{9,8},{10,11... | collective-permute-start | bytes 172040 | tf_op jit(solution)/shard_map/ppermute | solution.py:525
  13.2 1.7 %collective-permute-done.got_ref.refs_6_ = f32[45,8,128]{2,1,0:T(8,128)S(1)} collective-permute-done((f32[45,8,128]{2,1,0:T(8,128)S(1)}, f32[45,8,128]{2,1,0:T(8,128)S(1)}, u32[]{:S(2)}, u32[]{:S(2)}) %collective-permute-start) | collective-permute-done | bytes 184352 | tf_op jit(solution)/shard_map/ppermute | solution.py:525
  14.9 3.0 %collective-permute-start.1 = (f32[14,8,128]{2,1,0:T(8,128)S(1)}, f32[14,8,128]{2,1,0:T(8,128)S(1)}, u32[]{:S(2)}, u32[]{:S(2)}) collective-permute-start(f32[14,8,128]{2,1,0:T(8,128)S(1)} %get-tuple-element.109.own_ref), channel_id=1, source_target_pairs={{0,31},{1,2},{2,1},{3,4},{4,3},{5,6},{6,5},{7,8},{8,7},{9,10},{10,... | collective-permute-start | bytes 172040 | tf_op jit(solution)/shard_map/ppermute | solution.py:524
  17.9 1.0 %first.4 = (f32[2,6,8,8,128]{4,3,2,1,0:T(8,128)S(1)}, f32[2,6,8,8,128]{4,3,2,1,0:T(8,128)S(1)}, f32[2,2,7,8,128]{4,3,2,1,0:T(8,128)S(1)}, f32[2,7,8,128]{3,2,1,0...) custom-call(f32[2,7,8,128]{3,2,1,0:T(8,128)S(1)} %get-tuple-element.112.refs_0_.refs_7_.p0_ref, ...), custom_call_target="tpu_custom_call" | custom-call | flops 1000000000 | bytes 1024 | tf_op jit(solution)/shard_map/first/pallas_call | solution.py:505
  18.9 3.4 %collective-permute-start.7 = (f32[14,8,128]{2,1,0:T(8,128)S(1)}, f32[14,8,128]{2,1,0:T(8,128)S(1)}, u32[]{:S(2)}, u32[]{:S(2)}) collective-permute-start(f32[14,8,128]{2,1,0:T(8,128)S(1)} %get-tuple-element.137.own_ref), channel_id=1, source_target_pairs={{0,31},{1,2},{2,1},{3,4},{4,3},{5,6},{6,5},{7,8},{8,7},{9,10},{10,... | collective-permute-start | bytes 172040 | tf_op jit(solution)/shard_map/ppermute | solution.py:524
  22.3 0.9 %between.4 = (f32[2,6,8,8,128]{4,3,2,1,0:T(8,128)S(1)}, f32[2,7,8,128]{3,2,1,0:T(8,128)S(1)}, f32[2,7,8,128]{3,2,1,0:T(8,128)S(1)}, f32[3,8,8,128]{3,2,1,0:T(8,128)S(1)}) custom-call(f32[2,7,8,128]{3,2,1,0:T(8,128)S(1)} %get-tuple-element.123.refs_0_.m7_ref, f32[2,6,8,8,128]{4,3,2,1,0:T(8,128)S(1)} %get-tuple-element.124.refs_1_, ...), custom_call_target="tpu_custom_call" | custom-call | flops 2000000000 | bytes 1024 | tf_op jit(solution)/shard_map/between/pallas_call | solution.py:505
  23.5 1.0 %second.3 = (f32[2,6,8,8,128]{4,3,2,1,0:T(8,128)S(1)}, f32[2,2,7,8,128]{4,3,2,1,0:T(8,128)S(1)}, f32[2,6,8,8,128]{4,3,2,1,0:T(8,128)S(1)}, f32[2,2,7,8,128]{4,3,...) custom-call(f32[2,7,8,128]{3,2,1,0:T(8,128)S(1)} %get-tuple-element.130.m0_ref, ...), custom_call_target="tpu_custom_call" | custom-call | flops 3000000000 | bytes 1024 | tf_op jit(solution)/shard_map/second/pallas_call | solution.py:505
  24.5 2.9 %collective-permute-done.7.got_ref = f32[14,8,128]{2,1,0:T(8,128)S(1)} collective-permute-done((f32[14,8,128]{2,1,0:T(8,128)S(1)}, f32[14,8,128]{2,1,0:T(8,128)S(1)}, u32[]{:S(2)}, u32[]{:S(2)}) %collective-permute-start.7) | collective-permute-done | bytes 57376 | tf_op jit(solution)/shard_map/ppermute | solution.py:524
  27.8 3.2 %collective-permute-start.6 = (f32[14,8,128]{2,1,0:T(8,128)S(1)}, f32[14,8,128]{2,1,0:T(8,128)S(1)}, u32[]{:S(2)}, u32[]{:S(2)}) collective-permute-start(f32[14,8,128]{2,1,0:T(8,128)S(1)} %get-tuple-element.136.own_ref), channel_id=1, source_target_pairs={{0,31},{1,2},{2,1},{3,4},{4,3},{5,6},{6,5},{7,8},{8,7},{9,10},{10,... | collective-permute-start | bytes 172040 | tf_op jit(solution)/shard_map/ppermute | solution.py:524
  31.0 0.4 first.5
  31.7 3.4 %collective-permute-start.11 = (f32[14,8,128]{2,1,0:T(8,128)S(1)}, f32[14,8,128]{2,1,0:T(8,128)S(1)}, u32[]{:S(2)}, u32[]{:S(2)}) collective-permute-start(f32[14,8,128]{2,1,0:T(8,128)S(1)} %get-tuple-element.158.own_ref), channel_id=1, source_target_pairs={{0,31},{1,2},{2,1},{3,4},{4,3},{5,6},{6,5},{7,8},{8,7},{9,10},{10,... | collective-permute-start | bytes 172040 | tf_op jit(solution)/shard_map/ppermute | solution.py:524
  35.1 0.9 %between.5 = (f32[2,6,8,8,128]{4,3,2,1,0:T(8,128)S(1)}, f32[2,7,8,128]{3,2,1,0:T(8,128)S(1)}, f32[2,7,8,128]{3,2,1,0:T(8,128)S(1)}) custom-call(f32[2,7,8,128]{3,2,1,0:T(8,128)S(1)} %get-tuple-element.147.refs_0_.m7_ref, f32[2,6,8,8,128]{4,3,2,1,0:T(8,128)S(1)} %get-tuple-element.148.refs_1_, f32[3,8,8,128]{3,2,1,0:T(8,128)S(1)} %get-tuple-element.125.refs_2_.refs_7_, ...), custom_call_target="tpu_custom_call" | custom-call | flops 2000000000 | bytes 1024 | tf_op jit(solution)/shard_map/between/pallas_call | solution.py:505
  36.4 1.0 %second.4 = (f32[2,6,8,8,128]{4,3,2,1,0:T(8,128)S(1)}, f32[2,2,7,8,128]{4,3,2,1,0:T(8,128)S(1)}, f32[2,6,8,8,128]{4,3,2,1,0:T(8,128)S(1)}, f32[2,2,7,8,128]{4,3,...) custom-call(f32[2,7,8,128]{3,2,1,0:T(8,128)S(1)} %get-tuple-element.152.m0_ref, ...), custom_call_target="tpu_custom_call" | custom-call | flops 3000000000 | bytes 1024 | tf_op jit(solution)/shard_map/second/pallas_call | solution.py:505
  37.4 2.8 %collective-permute-done.11.got_ref = f32[14,8,128]{2,1,0:T(8,128)S(1)} collective-permute-done((f32[14,8,128]{2,1,0:T(8,128)S(1)}, f32[14,8,128]{2,1,0:T(8,128)S(1)}, u32[]{:S(2)}, u32[]{:S(2)}) %collective-permute-start.11) | collective-permute-done | bytes 57376 | tf_op jit(solution)/shard_map/ppermute | solution.py:524
  40.6 3.5 %collective-permute-start.10 = (f32[14,8,128]{2,1,0:T(8,128)S(1)}, f32[14,8,128]{2,1,0:T(8,128)S(1)}, u32[]{:S(2)}, u32[]{:S(2)}) collective-permute-start(f32[14,8,128]{2,1,0:T(8,128)S(1)} %get-tuple-element.157.own_ref), channel_id=1, source_target_pairs={{0,31},{1,2},{2,1},{3,4},{4,3},{5,6},{6,5},{7,8},{8,7},{9,10},{10,... | collective-permute-start | bytes 172040 | tf_op jit(solution)/shard_map/ppermute | solution.py:524
  44.5 3.4 %collective-permute-start.15 = (f32[14,8,128]{2,1,0:T(8,128)S(1)}, f32[14,8,128]{2,1,0:T(8,128)S(1)}, u32[]{:S(2)}, u32[]{:S(2)}) collective-permute-start(f32[14,8,128]{2,1,0:T(8,128)S(1)} %get-tuple-element.179.own_ref), channel_id=1, source_target_pairs={{0,31},{1,2},{2,1},{3,4},{4,3},{5,6},{6,5},{7,8},{8,7},{9,10},{10,... | collective-permute-start | bytes 172040 | tf_op jit(solution)/shard_map/ppermute | solution.py:524
  47.9 0.9 %between.6 = (f32[2,6,8,8,128]{4,3,2,1,0:T(8,128)S(1)}, f32[2,7,8,128]{3,2,1,0:T(8,128)S(1)}, f32[2,7,8,128]{3,2,1,0:T(8,128)S(1)}) custom-call(f32[2,7,8,128]{3,2,1,0:T(8,128)S(1)} %get-tuple-element.168.refs_0_.m7_ref, f32[2,6,8,8,128]{4,3,2,1,0:T(8,128)S(1)} %get-tuple-element.169.refs_1_, f32[3,8,8,128]{3,2,1,0:T(8,128)S(1)} %get-tuple-element.125.refs_2_.refs_7_, ...), custom_call_target="tpu_custom_call" | custom-call | flops 2000000000 | bytes 1024 | tf_op jit(solution)/shard_map/between/pallas_call | solution.py:505
  49.4 1.0 %second.5 = (f32[2,6,8,8,128]{4,3,2,1,0:T(8,128)S(1)}, f32[2,2,7,8,128]{4,3,2,1,0:T(8,128)S(1)}, f32[2,6,8,8,128]{4,3,2,1,0:T(8,128)S(1)}, f32[2,2,7,8,128]{4,3,...) custom-call(f32[2,7,8,128]{3,2,1,0:T(8,128)S(1)} %get-tuple-element.173.m0_ref, ...), custom_call_target="tpu_custom_call" | custom-call | flops 3000000000 | bytes 1024 | tf_op jit(solution)/shard_map/second/pallas_call | solution.py:505
  50.3 2.6 %collective-permute-done.15.got_ref = f32[14,8,128]{2,1,0:T(8,128)S(1)} collective-permute-done((f32[14,8,128]{2,1,0:T(8,128)S(1)}, f32[14,8,128]{2,1,0:T(8,128)S(1)}, u32[]{:S(2)}, u32[]{:S(2)}) %collective-permute-start.15) | collective-permute-done | bytes 57376 | tf_op jit(solution)/shard_map/ppermute | solution.py:524
  53.1 0.5 collective-permute-done.13.got_ref
  53.6 3.5 %collective-permute-start.14 = (f32[14,8,128]{2,1,0:T(8,128)S(1)}, f32[14,8,128]{2,1,0:T(8,128)S(1)}, u32[]{:S(2)}, u32[]{:S(2)}) collective-permute-start(f32[14,8,128]{2,1,0:T(8,128)S(1)} %get-tuple-element.178.own_ref), channel_id=1, source_target_pairs={{0,31},{1,2},{2,1},{3,4},{4,3},{5,6},{6,5},{7,8},{8,7},{9,10},{10,... | collective-permute-start | bytes 172040 | tf_op jit(solution)/shard_map/ppermute | solution.py:524
  57.0 0.4 first.7
  57.4 3.3 %collective-permute-start.18 = (f32[14,8,128]{2,1,0:T(8,128)S(1)}, f32[14,8,128]{2,1,0:T(8,128)S(1)}, u32[]{:S(2)}, u32[]{:S(2)}) collective-permute-start(f32[14,8,128]{2,1,0:T(8,128)S(1)} %get-tuple-element.198.own_ref), channel_id=1, source_target_pairs={{0,31},{1,2},{2,1},{3,4},{4,3},{5,6},{6,5},{7,8},{8,7},{9,10},{10,... | collective-permute-start | bytes 172040 | tf_op jit(solution)/shard_map/ppermute | solution.py:524
  60.7 0.9 %between.7 = (f32[2,6,8,8,128]{4,3,2,1,0:T(8,128)S(1)}, f32[2,7,8,128]{3,2,1,0:T(8,128)S(1)}, f32[2,7,8,128]{3,2,1,0:T(8,128)S(1)}) custom-call(f32[2,7,8,128]{3,2,1,0:T(8,128)S(1)} %get-tuple-element.189.refs_0_.m7_ref, f32[2,6,8,8,128]{4,3,2,1,0:T(8,128)S(1)} %get-tuple-element.190.refs_1_, f32[3,8,8,128]{3,2,1,0:T(8,128)S(1)} %get-tuple-element.125.refs_2_.refs_7_, ...), custom_call_target="tpu_custom_call" | custom-call | flops 2000000000 | bytes 1024 | tf_op jit(solution)/shard_map/between/pallas_call | solution.py:505
  61.6 0.5 collective-permute-done.14.got_ref
  62.2 1.1 %last.1 = (f32[2,8,8,8,128]{4,3,2,1,0:T(8,128)}, f32[2,2,7,8,128]{4,3,2,1,0:T(8,128)S(1)}, f32[2,7,8,128]{3,2,1,0:T(8,128)S(1)}) custom-call(s32[8,128]{1,0:T(8,128)S(1)} %get-tuple-element.103.slot_ref, f32[2,7,8,128]{3,2,1,0:T(8,128)S(1)} %get-tuple-element.194.m0_ref, f32[2,7,8,128]{3,2,1,0:T(8,128)S(1)} %get-tuple-element.189.refs_0_.m7_ref, ...), custom_call_target="tpu_custom_call" | custom-call | flops 3000000000 | bytes 1024 | tf_op jit(solution)/shard_map/last/pallas_call | solution.py:505
  63.3 2.6 %collective-permute-done.18.got_ref = f32[14,8,128]{2,1,0:T(8,128)S(1)} collective-permute-done((f32[14,8,128]{2,1,0:T(8,128)S(1)}, f32[14,8,128]{2,1,0:T(8,128)S(1)}, u32[]{:S(2)}, u32[]{:S(2)}) %collective-permute-start.18) | collective-permute-done | bytes 57376 | tf_op jit(solution)/shard_map/ppermute | solution.py:524
  66.3 0.8 %finish.3 = f32[2,8,8,8,128]{4,3,2,1,0:T(8,128)} custom-call(s32[8,128]{1,0:T(8,128)S(1)} %get-tuple-element.103.slot_ref, f32[14,8,128]{2,1,0:T(8,128)S(1)} %get-tuple-element.192.own_ref, f32[14,8,128]{2,1,0:T(8,128)S(1)} %collective-permute-done.17.got_ref, f32[2,7,8,128]{3,2,1,0:T(8,128)S(1)} %get-tuple-element.193.e_ref, ...), custom_call_target="tpu_custom_call", output_to_operand_aliasing={{}: (6, {})} | custom-call | flops 1000000 | bytes 1024 | tf_op jit(solution)/shard_map/finish/pallas_call | solution.py:505
  (45 shorter events, 3.9 us)
Async XLA Ops:
  0.0 9.8 %copy-start = (f32[3,512,128]{2,1,0:T(8,128)S(1)}, f32[3,512,128]{2,1,0:T(8,128)}, u32[]{:S(2)}) copy-start(f32[3,512,128]{2,1,0:T(8,128)} %param.5) | copy-start | bytes 2359300
  0.0 9.8 %copy-start.1 = (f32[2,512,128]{2,1,0:T(8,128)S(1)}, f32[2,512,128]{2,1,0:T(8,128)}, u32[]{:S(2)}) copy-start(f32[2,512,128]{2,1,0:T(8,128)} %param.4) | copy-start | bytes 1572868
  1.3 8.5 %copy-start.2 = (f32[512,128]{1,0:T(8,128)S(1)}, f32[512,128]{1,0:T(8,128)}, u32[]{:S(2)}) copy-start(f32[512,128]{1,0:T(8,128)} %param.6) | copy-start | bytes 786436
  1.4 11.0 %collective-permute-start.2 = (f32[21,8,128]{2,1,0:T(8,128)S(1)}, f32[21,8,128]{2,1,0:T(8,128)S(1)}, u32[]{:S(2)}, u32[]{:S(2)}) collective-permute-start(f32[21,8,128]{2,1,0:T(8,128)S(1)} %get-tuple-element.110.own_ref), channel_id=1, source_target_pairs={{0,31},{1,2},{2,1},{3,4},{4,3},{5,6},{6,5},{7,8},{8,7},{9,10},{10,... | collective-permute-start | bytes 258056 | tf_op jit(solution)/shard_map/ppermute | solution.py:524
  8.4 6.5 %collective-permute-start = (f32[45,8,128]{2,1,0:T(8,128)S(1)}, f32[45,8,128]{2,1,0:T(8,128)S(1)}, u32[]{:S(2)}, u32[]{:S(2)}) collective-permute-start(f32[45,8,128]{2,1,0:T(8,128)S(1)} %get-tuple-element.106.own_ref.refs_5_), channel_id=1, source_target_pairs={{0,1},{1,0},{2,3},{3,2},{4,5},{5,4},{6,7},{7,6},{8,9},{9,8},{10,11... | collective-permute-start | bytes 552968 | tf_op jit(solution)/shard_map/ppermute | solution.py:525
  8.4 13.9 %collective-permute-start.4 = (f32[24,8,128]{2,1,0:T(8,128)S(1)}, f32[24,8,128]{2,1,0:T(8,128)S(1)}, u32[]{:S(2)}, u32[]{:S(2)}) collective-permute-start(f32[24,8,128]{2,1,0:T(8,128)S(1)} %get-tuple-element.126.refs_9_), channel_id=1, source_target_pairs={{0,31},{1,2},{2,1},{3,4},{4,3},{5,6},{6,5},{7,8},{8,7},{9,10},{10,... | collective-permute-start | bytes 294920 | tf_op jit(solution)/shard_map/ppermute | solution.py:524
  12.4 6.4 %collective-permute-start.3 = (f32[14,8,128]{2,1,0:T(8,128)S(1)}, f32[14,8,128]{2,1,0:T(8,128)S(1)}, u32[]{:S(2)}, u32[]{:S(2)}) collective-permute-start(f32[14,8,128]{2,1,0:T(8,128)S(1)} %get-tuple-element.111.own_ref), channel_id=1, source_target_pairs={{0,1},{1,0},{2,3},{3,2},{4,5},{5,4},{6,7},{7,6},{8,9},{9,8},{10,11... | collective-permute-start | bytes 172040 | tf_op jit(solution)/shard_map/ppermute | solution.py:525
  14.9 8.5 %collective-permute-start.1 = (f32[14,8,128]{2,1,0:T(8,128)S(1)}, f32[14,8,128]{2,1,0:T(8,128)S(1)}, u32[]{:S(2)}, u32[]{:S(2)}) collective-permute-start(f32[14,8,128]{2,1,0:T(8,128)S(1)} %get-tuple-element.109.own_ref), channel_id=1, source_target_pairs={{0,31},{1,2},{2,1},{3,4},{4,3},{5,6},{6,5},{7,8},{8,7},{9,10},{10,... | collective-permute-start | bytes 172040 | tf_op jit(solution)/shard_map/ppermute | solution.py:524
  18.9 8.5 %collective-permute-start.7 = (f32[14,8,128]{2,1,0:T(8,128)S(1)}, f32[14,8,128]{2,1,0:T(8,128)S(1)}, u32[]{:S(2)}, u32[]{:S(2)}) collective-permute-start(f32[14,8,128]{2,1,0:T(8,128)S(1)} %get-tuple-element.137.own_ref), channel_id=1, source_target_pairs={{0,31},{1,2},{2,1},{3,4},{4,3},{5,6},{6,5},{7,8},{8,7},{9,10},{10,... | collective-permute-start | bytes 172040 | tf_op jit(solution)/shard_map/ppermute | solution.py:524
  23.4 4.4 %collective-permute-start.5 = (f32[14,8,128]{2,1,0:T(8,128)S(1)}, f32[14,8,128]{2,1,0:T(8,128)S(1)}, u32[]{:S(2)}, u32[]{:S(2)}) collective-permute-start(f32[14,8,128]{2,1,0:T(8,128)S(1)} %get-tuple-element.128.own_ref), channel_id=1, source_target_pairs={{0,1},{1,0},{2,3},{3,2},{4,5},{5,4},{6,7},{7,6},{8,9},{9,8},{10,11... | collective-permute-start | bytes 172040 | tf_op jit(solution)/shard_map/ppermute | solution.py:525
  27.4 4.3 %collective-permute-start.8 = (f32[14,8,128]{2,1,0:T(8,128)S(1)}, f32[14,8,128]{2,1,0:T(8,128)S(1)}, u32[]{:S(2)}, u32[]{:S(2)}) collective-permute-start(f32[14,8,128]{2,1,0:T(8,128)S(1)} %get-tuple-element.139.own_ref), channel_id=1, source_target_pairs={{0,1},{1,0},{2,3},{3,2},{4,5},{5,4},{6,7},{7,6},{8,9},{9,8},{10,11... | collective-permute-start | bytes 172040 | tf_op jit(solution)/shard_map/ppermute | solution.py:525
  27.8 8.5 %collective-permute-start.6 = (f32[14,8,128]{2,1,0:T(8,128)S(1)}, f32[14,8,128]{2,1,0:T(8,128)S(1)}, u32[]{:S(2)}, u32[]{:S(2)}) collective-permute-start(f32[14,8,128]{2,1,0:T(8,128)S(1)} %get-tuple-element.136.own_ref), channel_id=1, source_target_pairs={{0,31},{1,2},{2,1},{3,4},{4,3},{5,6},{6,5},{7,8},{8,7},{9,10},{10,... | collective-permute-start | bytes 172040 | tf_op jit(solution)/shard_map/ppermute | solution.py:524
  31.7 8.5 %collective-permute-start.11 = (f32[14,8,128]{2,1,0:T(8,128)S(1)}, f32[14,8,128]{2,1,0:T(8,128)S(1)}, u32[]{:S(2)}, u32[]{:S(2)}) collective-permute-start(f32[14,8,128]{2,1,0:T(8,128)S(1)} %get-tuple-element.158.own_ref), channel_id=1, source_target_pairs={{0,31},{1,2},{2,1},{3,4},{4,3},{5,6},{6,5},{7,8},{8,7},{9,10},{10,... | collective-permute-start | bytes 172040 | tf_op jit(solution)/shard_map/ppermute | solution.py:524
  36.3 4.3 %collective-permute-start.9 = (f32[14,8,128]{2,1,0:T(8,128)S(1)}, f32[14,8,128]{2,1,0:T(8,128)S(1)}, u32[]{:S(2)}, u32[]{:S(2)}) collective-permute-start(f32[14,8,128]{2,1,0:T(8,128)S(1)} %get-tuple-element.150.own_ref), channel_id=1, source_target_pairs={{0,1},{1,0},{2,3},{3,2},{4,5},{5,4},{6,7},{7,6},{8,9},{9,8},{10,11... | collective-permute-start | bytes 172040 | tf_op jit(solution)/shard_map/ppermute | solution.py:525
  40.2 4.3 %collective-permute-start.12 = (f32[14,8,128]{2,1,0:T(8,128)S(1)}, f32[14,8,128]{2,1,0:T(8,128)S(1)}, u32[]{:S(2)}, u32[]{:S(2)}) collective-permute-start(f32[14,8,128]{2,1,0:T(8,128)S(1)} %get-tuple-element.160.own_ref), channel_id=1, source_target_pairs={{0,1},{1,0},{2,3},{3,2},{4,5},{5,4},{6,7},{7,6},{8,9},{9,8},{10,11... | collective-permute-start | bytes 172040 | tf_op jit(solution)/shard_map/ppermute | solution.py:525
  40.6 8.5 %collective-permute-start.10 = (f32[14,8,128]{2,1,0:T(8,128)S(1)}, f32[14,8,128]{2,1,0:T(8,128)S(1)}, u32[]{:S(2)}, u32[]{:S(2)}) collective-permute-start(f32[14,8,128]{2,1,0:T(8,128)S(1)} %get-tuple-element.157.own_ref), channel_id=1, source_target_pairs={{0,31},{1,2},{2,1},{3,4},{4,3},{5,6},{6,5},{7,8},{8,7},{9,10},{10,... | collective-permute-start | bytes 172040 | tf_op jit(solution)/shard_map/ppermute | solution.py:524
  44.5 8.5 %collective-permute-start.15 = (f32[14,8,128]{2,1,0:T(8,128)S(1)}, f32[14,8,128]{2,1,0:T(8,128)S(1)}, u32[]{:S(2)}, u32[]{:S(2)}) collective-permute-start(f32[14,8,128]{2,1,0:T(8,128)S(1)} %get-tuple-element.179.own_ref), channel_id=1, source_target_pairs={{0,31},{1,2},{2,1},{3,4},{4,3},{5,6},{6,5},{7,8},{8,7},{9,10},{10,... | collective-permute-start | bytes 172040 | tf_op jit(solution)/shard_map/ppermute | solution.py:524
  49.1 4.4 %collective-permute-start.13 = (f32[14,8,128]{2,1,0:T(8,128)S(1)}, f32[14,8,128]{2,1,0:T(8,128)S(1)}, u32[]{:S(2)}, u32[]{:S(2)}) collective-permute-start(f32[14,8,128]{2,1,0:T(8,128)S(1)} %get-tuple-element.171.own_ref), channel_id=1, source_target_pairs={{0,1},{1,0},{2,3},{3,2},{4,5},{5,4},{6,7},{7,6},{8,9},{9,8},{10,11... | collective-permute-start | bytes 172040 | tf_op jit(solution)/shard_map/ppermute | solution.py:525
  53.0 4.4 %collective-permute-start.16 = (f32[14,8,128]{2,1,0:T(8,128)S(1)}, f32[14,8,128]{2,1,0:T(8,128)S(1)}, u32[]{:S(2)}, u32[]{:S(2)}) collective-permute-start(f32[14,8,128]{2,1,0:T(8,128)S(1)} %get-tuple-element.181.own_ref), channel_id=1, source_target_pairs={{0,1},{1,0},{2,3},{3,2},{4,5},{5,4},{6,7},{7,6},{8,9},{9,8},{10,11... | collective-permute-start | bytes 172040 | tf_op jit(solution)/shard_map/ppermute | solution.py:525
  53.6 8.5 %collective-permute-start.14 = (f32[14,8,128]{2,1,0:T(8,128)S(1)}, f32[14,8,128]{2,1,0:T(8,128)S(1)}, u32[]{:S(2)}, u32[]{:S(2)}) collective-permute-start(f32[14,8,128]{2,1,0:T(8,128)S(1)} %get-tuple-element.178.own_ref), channel_id=1, source_target_pairs={{0,31},{1,2},{2,1},{3,4},{4,3},{5,6},{6,5},{7,8},{8,7},{9,10},{10,... | collective-permute-start | bytes 172040 | tf_op jit(solution)/shard_map/ppermute | solution.py:524
  57.4 8.5 %collective-permute-start.18 = (f32[14,8,128]{2,1,0:T(8,128)S(1)}, f32[14,8,128]{2,1,0:T(8,128)S(1)}, u32[]{:S(2)}, u32[]{:S(2)}) collective-permute-start(f32[14,8,128]{2,1,0:T(8,128)S(1)} %get-tuple-element.198.own_ref), channel_id=1, source_target_pairs={{0,31},{1,2},{2,1},{3,4},{4,3},{5,6},{6,5},{7,8},{8,7},{9,10},{10,... | collective-permute-start | bytes 172040 | tf_op jit(solution)/shard_map/ppermute | solution.py:524
  62.1 4.3 %collective-permute-start.17 = (f32[14,8,128]{2,1,0:T(8,128)S(1)}, f32[14,8,128]{2,1,0:T(8,128)S(1)}, u32[]{:S(2)}, u32[]{:S(2)}) collective-permute-start(f32[14,8,128]{2,1,0:T(8,128)S(1)} %get-tuple-element.192.own_ref), channel_id=1, source_target_pairs={{0,1},{1,0},{2,3},{3,2},{4,5},{5,4},{6,7},{7,6},{8,9},{9,8},{10,11... | collective-permute-start | bytes 172040 | tf_op jit(solution)/shard_map/ppermute | solution.py:525

commit v10 on v9

--- a/solution.py
+++ b/solution.py
@@ -179,17 +179,16 @@
     return first, np.float32(-time_step), np.float32(-time_step)
 
 
-def project_even(idx_ref, raw_ref, ev_ref, tf_ref):
+def project_even(idx_ref, raw_ref, ev_ref):
     idx = idx_ref[...]
     signs = signs_of(lax.axis_index("elem") % 2)
     planes = project(read(raw_ref, 2), [read(raw_ref, m) for m in range(2)], idx, third_tables())
-    turned = [[gather_lanes(v, idx) * signs[r % 3] for v in read(raw_ref, 3 + r)] for r in range(6)]
-    write(ev_ref, (), sum(planes + turned[:3], []))
-    write(tf_ref, (), sum(turned[3:], []))
-
-
-def prepare(idx_ref, scal_ref, mass_ref, tr_ref,
-            gi_ref, q_ref, ri_ref, rt_ref, ti_ref, st_ref):
+    turned = [[gather_lanes(v, idx) * signs[r % 3] for v in read(raw_ref, 3 + r)] for r in range(3)]
+    write(ev_ref, (), sum(planes + turned, []))
+
+
+def prepare(idx_ref, scal_ref, mass_ref, tr_ref, raw_ref,
+            gi_ref, q_ref, ri_ref, rt_ref, ti_ref, st_ref, tf_ref):
     parity = lax.axis_index("elem") % 2
     idx = idx_ref[...]
     tables = third_tables()
@@ -200,6 +199,10 @@
         planes = [read(scal_ref, m, src) for m in range(2)] + [read(mass_ref, src)]
         return planes + [read(tr_ref, r, src) for r in range(3)]
 
+    for r in range(3):
+        turned = [gather_lanes(v, idx) * signs[r] for v in read(raw_ref, 6 + r)]
+        for j in range(8):
+            tf_ref[8 * r + j] = turned[j]
     faces = [read(tr_ref, 0, source_plane(parity, face * ORDER)) for face in range(2)]
     ahead = load(1)
     for face in range(2):
@@ -541,11 +544,13 @@
         scratch=[pltpu.VMEM((1, LANES), jnp.int32), pltpu.VMEM((3,) + tile, f32),
                  pltpu.SemaphoreType.DMA((13,))])
     rod = swap_od(od)
-    ev, tf = call(project_even, [bundle, (24, SUB, LANES)], (idx, raw), "project", 1)
-    rev, rtf = swap_ev(ev), swap_od(tf)
-    gi, q, ri, rt, ti, st = call(
-        prepare, [inner, faces, (6,) + tile, (6,) + tile, (6, 2) + tile, (2,) + part],
-        (idx, scal, mas, tr), "prepare", 1)
+    ev = call(project_even, [bundle], (idx, raw), "project", 1)
+    rev = swap_ev(ev)
+    gi, q, ri, rt, ti, st, tf = call(
+        prepare,
+        [inner, faces, (6,) + tile, (6,) + tile, (6, 2) + tile, (2,) + part, (24, SUB, LANES)],
+        (idx, scal, mas, tr, raw), "prepare", 1)
+    rtf = swap_od(tf)
     p0, r0, cev = call(make_field_face(0), [face, part, sent], (od, rod, q, st), "odd", 3000)
     p7, r7, cod = call(make_field_face(1), [face, part, sent], (ev, rev, q, st), "even", 1)
     acci, accf, wp = gi, q, gi

time: 67.4 us -> 67.8 us (level)
    ppermute x10, waiting for transfers between devices: 12.1 us -> 13.4 us  [per_device(): swap_od = lambda x: lax.ppermute(x, 'elem', odd_pairs)]
    ppermute x9, waiting for transfers between devices: 3.32 us -> 2.41 us  [per_device(): swap_ev = lambda x: lax.ppermute(x, 'elem', even_pairs)]
  transfers between devices with their start and end apart: 19 -> 19, of which waited for: 14 -> 12; matrix products, arithmetic and copies ran while one was open for 0% -> 0% of each run, Pallas kernels for 20% -> 20%
where the time goes in v10:
time: 67.8 us; the launch traced here: 67.6 us
  starting transfers between devices  35.7 us (53%)
  waiting for transfers between devices  15.9 us (23%)
  Pallas kernels  15.7 us (23%)
    ppermute x10, starting transfers between devices, per_device(): swap_od = lambda x: lax.ppermute(x, 'elem', odd_pairs)  34.1 us
    pallas_call x33, Pallas kernels, call(): pl.pallas_call(kernel, out_shape=shapes[0] if single else shapes, in_spec...  15.7 us
    ppermute x10, waiting for transfers between devices, per_device(): swap_od = lambda x: lax.ppermute(x, 'elem', odd_pairs)  13.4 us
    ppermute x9, waiting for transfers between devices, per_device(): swap_ev = lambda x: lax.ppermute(x, 'elem', even_pairs)  2.41 us
    ppermute x9, starting transfers between devices, per_device(): swap_ev = lambda x: lax.ppermute(x, 'elem', even_pairs)  1.61 us
  transfers between devices with their start and end apart: 19, of which 12 were waited for; matrix products, arithmetic and copies ran while one was open for 0% of the time, Pallas kernels for 20%

profile of v10, /device:TPU:0, one launch (start us, length us, event | category | flops | bytes accessed | tf_op | source)
XLA Modules:
  0.0 67.6 jit_solution(7742551700761859064)
XLA Ops:
  0.0 1.3 %project.2 = (f32[21,8,128]{2,1,0:T(8,128)S(1)}, s32[8,128]{1,0:T(8,128)S(1)}, s32[8,128]{1,0:T(8,128)S(1)}, f32[9,8,8,128]{3,2,1,0:T(8,128)S(1)}) custom-call(s32[1,128]{1,0:T(1,128)} %order_ref.1, f32[2,8,8,8,128]{4,3,2,1,0:T(8,128)} %bitcast.6, f32[8,8,8,128]{3,2,1,0:T(8,128)} %bitcast.8, f32[3,8,8,8,128]{4,3,2,1,0:T(8,128)} %bitcast.4), custom_call_target="tpu_custom_call" | custom-call | flops 1000000 | bytes 1024 | tf_op jit(solution)/shard_map/project/pallas_call | solution.py:508
  1.4 6.7 %collective-permute-start.2 = (f32[21,8,128]{2,1,0:T(8,128)S(1)}, f32[21,8,128]{2,1,0:T(8,128)S(1)}, u32[]{:S(2)}, u32[]{:S(2)}) collective-permute-start(f32[21,8,128]{2,1,0:T(8,128)S(1)} %get-tuple-element.108.own_ref), channel_id=1, source_target_pairs={{0,31},{1,2},{2,1},{3,4},{4,3},{5,6},{6,5},{7,8},{8,7},{9,10},{10,... | collective-permute-start | bytes 258056 | tf_op jit(solution)/shard_map/ppermute | solution.py:527
  8.5 3.0 %prepare.1 = (f32[2,6,8,8,128]{4,3,2,1,0:T(8,128)S(1)}, f32[2,2,7,8,128]{4,3,2,1,0:T(8,128)S(1)}, f32[6,8,8,128]{3,2,1,0:T(8,128)S(1)}, f32[6,8,8,128]{3,2,1,0:T...) custom-call(s32[8,128]{1,0:T(8,128)S(1)} %get-tuple-element.103.idx_ref, ...), custom_call_target="tpu_custom_call" | custom-call | flops 1000000 | bytes 1024 | tf_op jit(solution)/shard_map/prepare/pallas_call | solution.py:508
  11.5 1.4 %collective-permute-start.4 = (f32[24,8,128]{2,1,0:T(8,128)S(1)}, f32[24,8,128]{2,1,0:T(8,128)S(1)}, u32[]{:S(2)}, u32[]{:S(2)}) collective-permute-start(f32[24,8,128]{2,1,0:T(8,128)S(1)} %get-tuple-element.124.refs_9_), channel_id=1, source_target_pairs={{0,31},{1,2},{2,1},{3,4},{4,3},{5,6},{6,5},{7,8},{8,7},{9,10},{10,... | collective-permute-start | bytes 294920 | tf_op jit(solution)/shard_map/ppermute | solution.py:527
  12.9 0.8 %collective-permute-start.3 = (f32[14,8,128]{2,1,0:T(8,128)S(1)}, f32[14,8,128]{2,1,0:T(8,128)S(1)}, u32[]{:S(2)}, u32[]{:S(2)}) collective-permute-start(f32[14,8,128]{2,1,0:T(8,128)S(1)} %get-tuple-element.109.own_ref), channel_id=1, source_target_pairs={{0,1},{1,0},{2,3},{3,2},{4,5},{5,4},{6,7},{7,6},{8,9},{9,8},{10,11... | collective-permute-start | bytes 172040 | tf_op jit(solution)/shard_map/ppermute | solution.py:528
  13.7 0.9 %collective-permute-done.got_ref.refs_6_ = f32[45,8,128]{2,1,0:T(8,128)S(1)} collective-permute-done((f32[45,8,128]{2,1,0:T(8,128)S(1)}, f32[45,8,128]{2,1,0:T(8,128)S(1)}, u32[]{:S(2)}, u32[]{:S(2)}) %collective-permute-start) | collective-permute-done | bytes 184352 | tf_op jit(solution)/shard_map/ppermute | solution.py:528
  14.6 3.5 %collective-permute-start.1 = (f32[14,8,128]{2,1,0:T(8,128)S(1)}, f32[14,8,128]{2,1,0:T(8,128)S(1)}, u32[]{:S(2)}, u32[]{:S(2)}) collective-permute-start(f32[14,8,128]{2,1,0:T(8,128)S(1)} %get-tuple-element.107.own_ref), channel_id=1, source_target_pairs={{0,31},{1,2},{2,1},{3,4},{4,3},{5,6},{6,5},{7,8},{8,7},{9,10},{10,... | collective-permute-start | bytes 172040 | tf_op jit(solution)/shard_map/ppermute | solution.py:527
  18.0 1.0 %first.4 = (f32[2,6,8,8,128]{4,3,2,1,0:T(8,128)S(1)}, f32[2,6,8,8,128]{4,3,2,1,0:T(8,128)S(1)}, f32[2,2,7,8,128]{4,3,2,1,0:T(8,128)S(1)}, f32[2,7,8,128]{3,2,1,0...) custom-call(f32[2,7,8,128]{3,2,1,0:T(8,128)S(1)} %get-tuple-element.110.refs_0_.refs_7_.p0_ref, ...), custom_call_target="tpu_custom_call" | custom-call | flops 1000000000 | bytes 1024 | tf_op jit(solution)/shard_map/first/pallas_call | solution.py:508
  19.0 3.2 %collective-permute-start.7 = (f32[14,8,128]{2,1,0:T(8,128)S(1)}, f32[14,8,128]{2,1,0:T(8,128)S(1)}, u32[]{:S(2)}, u32[]{:S(2)}) collective-permute-start(f32[14,8,128]{2,1,0:T(8,128)S(1)} %get-tuple-element.135.own_ref), channel_id=1, source_target_pairs={{0,31},{1,2},{2,1},{3,4},{4,3},{5,6},{6,5},{7,8},{8,7},{9,10},{10,... | collective-permute-start | bytes 172040 | tf_op jit(solution)/shard_map/ppermute | solution.py:527
  22.2 0.9 %between.4 = (f32[2,6,8,8,128]{4,3,2,1,0:T(8,128)S(1)}, f32[2,7,8,128]{3,2,1,0:T(8,128)S(1)}, f32[2,7,8,128]{3,2,1,0:T(8,128)S(1)}, f32[3,8,8,128]{3,2,1,0:T(8,128)S(1)}) custom-call(f32[2,7,8,128]{3,2,1,0:T(8,128)S(1)} %get-tuple-element.121.refs_0_.m7_ref, f32[2,6,8,8,128]{4,3,2,1,0:T(8,128)S(1)} %get-tuple-element.122.refs_1_, ...), custom_call_target="tpu_custom_call" | custom-call | flops 2000000000 | bytes 1024 | tf_op jit(solution)/shard_map/between/pallas_call | solution.py:508
  23.2 1.0 %second.3 = (f32[2,6,8,8,128]{4,3,2,1,0:T(8,128)S(1)}, f32[2,2,7,8,128]{4,3,2,1,0:T(8,128)S(1)}, f32[2,6,8,8,128]{4,3,2,1,0:T(8,128)S(1)}, f32[2,2,7,8,128]{4,3,...) custom-call(f32[2,7,8,128]{3,2,1,0:T(8,128)S(1)} %get-tuple-element.128.m0_ref, ...), custom_call_target="tpu_custom_call" | custom-call | flops 3000000000 | bytes 1024 | tf_op jit(solution)/shard_map/second/pallas_call | solution.py:508
  24.2 3.3 %collective-permute-done.7.got_ref = f32[14,8,128]{2,1,0:T(8,128)S(1)} collective-permute-done((f32[14,8,128]{2,1,0:T(8,128)S(1)}, f32[14,8,128]{2,1,0:T(8,128)S(1)}, u32[]{:S(2)}, u32[]{:S(2)}) %collective-permute-start.7) | collective-permute-done | bytes 57376 | tf_op jit(solution)/shard_map/ppermute | solution.py:527
  27.7 3.4 %collective-permute-start.6 = (f32[14,8,128]{2,1,0:T(8,128)S(1)}, f32[14,8,128]{2,1,0:T(8,128)S(1)}, u32[]{:S(2)}, u32[]{:S(2)}) collective-permute-start(f32[14,8,128]{2,1,0:T(8,128)S(1)} %get-tuple-element.134.own_ref), channel_id=1, source_target_pairs={{0,31},{1,2},{2,1},{3,4},{4,3},{5,6},{6,5},{7,8},{8,7},{9,10},{10,... | collective-permute-start | bytes 172040 | tf_op jit(solution)/shard_map/ppermute | solution.py:527
  31.8 3.1 %collective-permute-start.11 = (f32[14,8,128]{2,1,0:T(8,128)S(1)}, f32[14,8,128]{2,1,0:T(8,128)S(1)}, u32[]{:S(2)}, u32[]{:S(2)}) collective-permute-start(f32[14,8,128]{2,1,0:T(8,128)S(1)} %get-tuple-element.156.own_ref), channel_id=1, source_target_pairs={{0,31},{1,2},{2,1},{3,4},{4,3},{5,6},{6,5},{7,8},{8,7},{9,10},{10,... | collective-permute-start | bytes 172040 | tf_op jit(solution)/shard_map/ppermute | solution.py:527
  35.0 0.9 %between.5 = (f32[2,6,8,8,128]{4,3,2,1,0:T(8,128)S(1)}, f32[2,7,8,128]{3,2,1,0:T(8,128)S(1)}, f32[2,7,8,128]{3,2,1,0:T(8,128)S(1)}) custom-call(f32[2,7,8,128]{3,2,1,0:T(8,128)S(1)} %get-tuple-element.145.refs_0_.m7_ref, f32[2,6,8,8,128]{4,3,2,1,0:T(8,128)S(1)} %get-tuple-element.146.refs_1_, f32[3,8,8,128]{3,2,1,0:T(8,128)S(1)} %get-tuple-element.123.refs_2_.refs_7_, ...), custom_call_target="tpu_custom_call" | custom-call | flops 2000000000 | bytes 1024 | tf_op jit(solution)/shard_map/between/pallas_call | solution.py:508
  35.9 0.8 %collective-permute-done.6.got_ref = f32[14,8,128]{2,1,0:T(8,128)S(1)} collective-permute-done((f32[14,8,128]{2,1,0:T(8,128)S(1)}, f32[14,8,128]{2,1,0:T(8,128)S(1)}, u32[]{:S(2)}, u32[]{:S(2)}) %collective-permute-start.6) | collective-permute-done | bytes 57376 | tf_op jit(solution)/shard_map/ppermute | solution.py:527
  36.7 1.0 %second.4 = (f32[2,6,8,8,128]{4,3,2,1,0:T(8,128)S(1)}, f32[2,2,7,8,128]{4,3,2,1,0:T(8,128)S(1)}, f32[2,6,8,8,128]{4,3,2,1,0:T(8,128)S(1)}, f32[2,2,7,8,128]{4,3,...) custom-call(f32[2,7,8,128]{3,2,1,0:T(8,128)S(1)} %get-tuple-element.150.m0_ref, ...), custom_call_target="tpu_custom_call" | custom-call | flops 3000000000 | bytes 1024 | tf_op jit(solution)/shard_map/second/pallas_call | solution.py:508
  37.7 2.6 %collective-permute-done.11.got_ref = f32[14,8,128]{2,1,0:T(8,128)S(1)} collective-permute-done((f32[14,8,128]{2,1,0:T(8,128)S(1)}, f32[14,8,128]{2,1,0:T(8,128)S(1)}, u32[]{:S(2)}, u32[]{:S(2)}) %collective-permute-start.11) | collective-permute-done | bytes 57376 | tf_op jit(solution)/shard_map/ppermute | solution.py:527
  40.4 0.5 collective-permute-done.9.got_ref
  40.9 3.5 %collective-permute-start.10 = (f32[14,8,128]{2,1,0:T(8,128)S(1)}, f32[14,8,128]{2,1,0:T(8,128)S(1)}, u32[]{:S(2)}, u32[]{:S(2)}) collective-permute-start(f32[14,8,128]{2,1,0:T(8,128)S(1)} %get-tuple-element.155.own_ref), channel_id=1, source_target_pairs={{0,31},{1,2},{2,1},{3,4},{4,3},{5,6},{6,5},{7,8},{8,7},{9,10},{10,... | collective-permute-start | bytes 172040 | tf_op jit(solution)/shard_map/ppermute | solution.py:527
  44.8 2.9 %collective-permute-start.15 = (f32[14,8,128]{2,1,0:T(8,128)S(1)}, f32[14,8,128]{2,1,0:T(8,128)S(1)}, u32[]{:S(2)}, u32[]{:S(2)}) collective-permute-start(f32[14,8,128]{2,1,0:T(8,128)S(1)} %get-tuple-element.177.own_ref), channel_id=1, source_target_pairs={{0,31},{1,2},{2,1},{3,4},{4,3},{5,6},{6,5},{7,8},{8,7},{9,10},{10,... | collective-permute-start | bytes 172040 | tf_op jit(solution)/shard_map/ppermute | solution.py:527
  47.7 0.9 %between.6 = (f32[2,6,8,8,128]{4,3,2,1,0:T(8,128)S(1)}, f32[2,7,8,128]{3,2,1,0:T(8,128)S(1)}, f32[2,7,8,128]{3,2,1,0:T(8,128)S(1)}) custom-call(f32[2,7,8,128]{3,2,1,0:T(8,128)S(1)} %get-tuple-element.166.refs_0_.m7_ref, f32[2,6,8,8,128]{4,3,2,1,0:T(8,128)S(1)} %get-tuple-element.167.refs_1_, f32[3,8,8,128]{3,2,1,0:T(8,128)S(1)} %get-tuple-element.123.refs_2_.refs_7_, ...), custom_call_target="tpu_custom_call" | custom-call | flops 2000000000 | bytes 1024 | tf_op jit(solution)/shard_map/between/pallas_call | solution.py:508
  48.6 0.8 %collective-permute-done.10.got_ref = f32[14,8,128]{2,1,0:T(8,128)S(1)} collective-permute-done((f32[14,8,128]{2,1,0:T(8,128)S(1)}, f32[14,8,128]{2,1,0:T(8,128)S(1)}, u32[]{:S(2)}, u32[]{:S(2)}) %collective-permute-start.10) | collective-permute-done | bytes 57376 | tf_op jit(solution)/shard_map/ppermute | solution.py:527
  49.7 1.0 %second.5 = (f32[2,6,8,8,128]{4,3,2,1,0:T(8,128)S(1)}, f32[2,2,7,8,128]{4,3,2,1,0:T(8,128)S(1)}, f32[2,6,8,8,128]{4,3,2,1,0:T(8,128)S(1)}, f32[2,2,7,8,128]{4,3,...) custom-call(f32[2,7,8,128]{3,2,1,0:T(8,128)S(1)} %get-tuple-element.171.m0_ref, ...), custom_call_target="tpu_custom_call" | custom-call | flops 3000000000 | bytes 1024 | tf_op jit(solution)/shard_map/second/pallas_call | solution.py:508
  50.7 2.6 %collective-permute-done.15.got_ref = f32[14,8,128]{2,1,0:T(8,128)S(1)} collective-permute-done((f32[14,8,128]{2,1,0:T(8,128)S(1)}, f32[14,8,128]{2,1,0:T(8,128)S(1)}, u32[]{:S(2)}, u32[]{:S(2)}) %collective-permute-start.15) | collective-permute-done | bytes 57376 | tf_op jit(solution)/shard_map/ppermute | solution.py:527
  53.9 3.5 %collective-permute-start.14 = (f32[14,8,128]{2,1,0:T(8,128)S(1)}, f32[14,8,128]{2,1,0:T(8,128)S(1)}, u32[]{:S(2)}, u32[]{:S(2)}) collective-permute-start(f32[14,8,128]{2,1,0:T(8,128)S(1)} %get-tuple-element.176.own_ref), channel_id=1, source_target_pairs={{0,31},{1,2},{2,1},{3,4},{4,3},{5,6},{6,5},{7,8},{8,7},{9,10},{10,... | collective-permute-start | bytes 172040 | tf_op jit(solution)/shard_map/ppermute | solution.py:527
  57.8 2.9 %collective-permute-start.18 = (f32[14,8,128]{2,1,0:T(8,128)S(1)}, f32[14,8,128]{2,1,0:T(8,128)S(1)}, u32[]{:S(2)}, u32[]{:S(2)}) collective-permute-start(f32[14,8,128]{2,1,0:T(8,128)S(1)} %get-tuple-element.196.own_ref), channel_id=1, source_target_pairs={{0,31},{1,2},{2,1},{3,4},{4,3},{5,6},{6,5},{7,8},{8,7},{9,10},{10,... | collective-permute-start | bytes 172040 | tf_op jit(solution)/shard_map/ppermute | solution.py:527
  60.7 0.9 %between.7 = (f32[2,6,8,8,128]{4,3,2,1,0:T(8,128)S(1)}, f32[2,7,8,128]{3,2,1,0:T(8,128)S(1)}, f32[2,7,8,128]{3,2,1,0:T(8,128)S(1)}) custom-call(f32[2,7,8,128]{3,2,1,0:T(8,128)S(1)} %get-tuple-element.187.refs_0_.m7_ref, f32[2,6,8,8,128]{4,3,2,1,0:T(8,128)S(1)} %get-tuple-element.188.refs_1_, f32[3,8,8,128]{3,2,1,0:T(8,128)S(1)} %get-tuple-element.123.refs_2_.refs_7_, ...), custom_call_target="tpu_custom_call" | custom-call | flops 2000000000 | bytes 1024 | tf_op jit(solution)/shard_map/between/pallas_call | solution.py:508
  61.6 0.8 %collective-permute-done.14.got_ref = f32[14,8,128]{2,1,0:T(8,128)S(1)} collective-permute-done((f32[14,8,128]{2,1,0:T(8,128)S(1)}, f32[14,8,128]{2,1,0:T(8,128)S(1)}, u32[]{:S(2)}, u32[]{:S(2)}) %collective-permute-start.14) | collective-permute-done | bytes 57376 | tf_op jit(solution)/shard_map/ppermute | solution.py:527
  62.5 1.1 %last.1 = (f32[2,8,8,8,128]{4,3,2,1,0:T(8,128)}, f32[2,2,7,8,128]{4,3,2,1,0:T(8,128)S(1)}, f32[2,7,8,128]{3,2,1,0:T(8,128)S(1)}) custom-call(s32[8,128]{1,0:T(8,128)S(1)} %get-tuple-element.102.slot_ref, f32[2,7,8,128]{3,2,1,0:T(8,128)S(1)} %get-tuple-element.192.m0_ref, f32[2,7,8,128]{3,2,1,0:T(8,128)S(1)} %get-tuple-element.187.refs_0_.m7_ref, ...), custom_call_target="tpu_custom_call" | custom-call | flops 3000000000 | bytes 1024 | tf_op jit(solution)/shard_map/last/pallas_call | solution.py:508
  63.6 2.6 %collective-permute-done.18.got_ref = f32[14,8,128]{2,1,0:T(8,128)S(1)} collective-permute-done((f32[14,8,128]{2,1,0:T(8,128)S(1)}, f32[14,8,128]{2,1,0:T(8,128)S(1)}, u32[]{:S(2)}, u32[]{:S(2)}) %collective-permute-start.18) | collective-permute-done | bytes 57376 | tf_op jit(solution)/shard_map/ppermute | solution.py:527
  66.7 0.8 %finish.3 = f32[2,8,8,8,128]{4,3,2,1,0:T(8,128)} custom-call(s32[8,128]{1,0:T(8,128)S(1)} %get-tuple-element.102.slot_ref, f32[14,8,128]{2,1,0:T(8,128)S(1)} %get-tuple-element.190.own_ref, f32[14,8,128]{2,1,0:T(8,128)S(1)} %collective-permute-done.17.got_ref, f32[2,7,8,128]{3,2,1,0:T(8,128)S(1)} %get-tuple-element.191.e_ref, ...), custom_call_target="tpu_custom_call", output_to_operand_aliasing={{}: (6, {})} | custom-call | flops 1000000 | bytes 1024 | tf_op jit(solution)/shard_map/finish/pallas_call | solution.py:508
  (45 shorter events, 3.8 us)
Async XLA Ops:
  0.0 8.4 %copy-start = (f32[3,512,128]{2,1,0:T(8,128)S(1)}, f32[3,512,128]{2,1,0:T(8,128)}, u32[]{:S(2)}) copy-start(f32[3,512,128]{2,1,0:T(8,128)} %param.5) | copy-start | bytes 2359300
  0.0 8.5 %copy-start.1 = (f32[2,512,128]{2,1,0:T(8,128)S(1)}, f32[2,512,128]{2,1,0:T(8,128)}, u32[]{:S(2)}) copy-start(f32[2,512,128]{2,1,0:T(8,128)} %param.4) | copy-start | bytes 1572868
  1.3 7.1 %copy-start.2 = (f32[512,128]{1,0:T(8,128)S(1)}, f32[512,128]{1,0:T(8,128)}, u32[]{:S(2)}) copy-start(f32[512,128]{1,0:T(8,128)} %param.6) | copy-start | bytes 786436
  1.4 11.5 %collective-permute-start.2 = (f32[21,8,128]{2,1,0:T(8,128)S(1)}, f32[21,8,128]{2,1,0:T(8,128)S(1)}, u32[]{:S(2)}, u32[]{:S(2)}) collective-permute-start(f32[21,8,128]{2,1,0:T(8,128)S(1)} %get-tuple-element.108.own_ref), channel_id=1, source_target_pairs={{0,31},{1,2},{2,1},{3,4},{4,3},{5,6},{6,5},{7,8},{8,7},{9,10},{10,... | collective-permute-start | bytes 258056 | tf_op jit(solution)/shard_map/ppermute | solution.py:527
  8.4 6.2 %collective-permute-start = (f32[45,8,128]{2,1,0:T(8,128)S(1)}, f32[45,8,128]{2,1,0:T(8,128)S(1)}, u32[]{:S(2)}, u32[]{:S(2)}) collective-permute-start(f32[45,8,128]{2,1,0:T(8,128)S(1)} %project.3.own_ref.refs_5_), channel_id=1, source_target_pairs={{0,1},{1,0},{2,3},{3,2},{4,5},{5,4},{6,7},{7,6},{8,9},{9,8},{10,11... | collective-permute-start | bytes 552968 | tf_op jit(solution)/shard_map/ppermute | solution.py:528
  11.5 10.7 %collective-permute-start.4 = (f32[24,8,128]{2,1,0:T(8,128)S(1)}, f32[24,8,128]{2,1,0:T(8,128)S(1)}, u32[]{:S(2)}, u32[]{:S(2)}) collective-permute-start(f32[24,8,128]{2,1,0:T(8,128)S(1)} %get-tuple-element.124.refs_9_), channel_id=1, source_target_pairs={{0,31},{1,2},{2,1},{3,4},{4,3},{5,6},{6,5},{7,8},{8,7},{9,10},{10,... | collective-permute-start | bytes 294920 | tf_op jit(solution)/shard_map/ppermute | solution.py:527
  12.9 6.1 %collective-permute-start.3 = (f32[14,8,128]{2,1,0:T(8,128)S(1)}, f32[14,8,128]{2,1,0:T(8,128)S(1)}, u32[]{:S(2)}, u32[]{:S(2)}) collective-permute-start(f32[14,8,128]{2,1,0:T(8,128)S(1)} %get-tuple-element.109.own_ref), channel_id=1, source_target_pairs={{0,1},{1,0},{2,3},{3,2},{4,5},{5,4},{6,7},{7,6},{8,9},{9,8},{10,11... | collective-permute-start | bytes 172040 | tf_op jit(solution)/shard_map/ppermute | solution.py:528
  14.6 8.5 %collective-permute-start.1 = (f32[14,8,128]{2,1,0:T(8,128)S(1)}, f32[14,8,128]{2,1,0:T(8,128)S(1)}, u32[]{:S(2)}, u32[]{:S(2)}) collective-permute-start(f32[14,8,128]{2,1,0:T(8,128)S(1)} %get-tuple-element.107.own_ref), channel_id=1, source_target_pairs={{0,31},{1,2},{2,1},{3,4},{4,3},{5,6},{6,5},{7,8},{8,7},{9,10},{10,... | collective-permute-start | bytes 172040 | tf_op jit(solution)/shard_map/ppermute | solution.py:527
  19.0 8.5 %collective-permute-start.7 = (f32[14,8,128]{2,1,0:T(8,128)S(1)}, f32[14,8,128]{2,1,0:T(8,128)S(1)}, u32[]{:S(2)}, u32[]{:S(2)}) collective-permute-start(f32[14,8,128]{2,1,0:T(8,128)S(1)} %get-tuple-element.135.own_ref), channel_id=1, source_target_pairs={{0,31},{1,2},{2,1},{3,4},{4,3},{5,6},{6,5},{7,8},{8,7},{9,10},{10,... | collective-permute-start | bytes 172040 | tf_op jit(solution)/shard_map/ppermute | solution.py:527
  23.1 4.5 %collective-permute-start.5 = (f32[14,8,128]{2,1,0:T(8,128)S(1)}, f32[14,8,128]{2,1,0:T(8,128)S(1)}, u32[]{:S(2)}, u32[]{:S(2)}) collective-permute-start(f32[14,8,128]{2,1,0:T(8,128)S(1)} %get-tuple-element.126.own_ref), channel_id=1, source_target_pairs={{0,1},{1,0},{2,3},{3,2},{4,5},{5,4},{6,7},{7,6},{8,9},{9,8},{10,11... | collective-permute-start | bytes 172040 | tf_op jit(solution)/shard_map/ppermute | solution.py:528
  27.5 4.3 %collective-permute-start.8 = (f32[14,8,128]{2,1,0:T(8,128)S(1)}, f32[14,8,128]{2,1,0:T(8,128)S(1)}, u32[]{:S(2)}, u32[]{:S(2)}) collective-permute-start(f32[14,8,128]{2,1,0:T(8,128)S(1)} %get-tuple-element.137.own_ref), channel_id=1, source_target_pairs={{0,1},{1,0},{2,3},{3,2},{4,5},{5,4},{6,7},{7,6},{8,9},{9,8},{10,11... | collective-permute-start | bytes 172040 | tf_op jit(solution)/shard_map/ppermute | solution.py:528
  27.7 9.0 %collective-permute-start.6 = (f32[14,8,128]{2,1,0:T(8,128)S(1)}, f32[14,8,128]{2,1,0:T(8,128)S(1)}, u32[]{:S(2)}, u32[]{:S(2)}) collective-permute-start(f32[14,8,128]{2,1,0:T(8,128)S(1)} %get-tuple-element.134.own_ref), channel_id=1, source_target_pairs={{0,31},{1,2},{2,1},{3,4},{4,3},{5,6},{6,5},{7,8},{8,7},{9,10},{10,... | collective-permute-start | bytes 172040 | tf_op jit(solution)/shard_map/ppermute | solution.py:527
  31.8 8.5 %collective-permute-start.11 = (f32[14,8,128]{2,1,0:T(8,128)S(1)}, f32[14,8,128]{2,1,0:T(8,128)S(1)}, u32[]{:S(2)}, u32[]{:S(2)}) collective-permute-start(f32[14,8,128]{2,1,0:T(8,128)S(1)} %get-tuple-element.156.own_ref), channel_id=1, source_target_pairs={{0,31},{1,2},{2,1},{3,4},{4,3},{5,6},{6,5},{7,8},{8,7},{9,10},{10,... | collective-permute-start | bytes 172040 | tf_op jit(solution)/shard_map/ppermute | solution.py:527
  36.6 4.3 %collective-permute-start.9 = (f32[14,8,128]{2,1,0:T(8,128)S(1)}, f32[14,8,128]{2,1,0:T(8,128)S(1)}, u32[]{:S(2)}, u32[]{:S(2)}) collective-permute-start(f32[14,8,128]{2,1,0:T(8,128)S(1)} %get-tuple-element.148.own_ref), channel_id=1, source_target_pairs={{0,1},{1,0},{2,3},{3,2},{4,5},{5,4},{6,7},{7,6},{8,9},{9,8},{10,11... | collective-permute-start | bytes 172040 | tf_op jit(solution)/shard_map/ppermute | solution.py:528
  40.3 4.5 %collective-permute-start.12 = (f32[14,8,128]{2,1,0:T(8,128)S(1)}, f32[14,8,128]{2,1,0:T(8,128)S(1)}, u32[]{:S(2)}, u32[]{:S(2)}) collective-permute-start(f32[14,8,128]{2,1,0:T(8,128)S(1)} %get-tuple-element.158.own_ref), channel_id=1, source_target_pairs={{0,1},{1,0},{2,3},{3,2},{4,5},{5,4},{6,7},{7,6},{8,9},{9,8},{10,11... | collective-permute-start | bytes 172040 | tf_op jit(solution)/shard_map/ppermute | solution.py:528
  40.9 8.5 %collective-permute-start.10 = (f32[14,8,128]{2,1,0:T(8,128)S(1)}, f32[14,8,128]{2,1,0:T(8,128)S(1)}, u32[]{:S(2)}, u32[]{:S(2)}) collective-permute-start(f32[14,8,128]{2,1,0:T(8,128)S(1)} %get-tuple-element.155.own_ref), channel_id=1, source_target_pairs={{0,31},{1,2},{2,1},{3,4},{4,3},{5,6},{6,5},{7,8},{8,7},{9,10},{10,... | collective-permute-start | bytes 172040 | tf_op jit(solution)/shard_map/ppermute | solution.py:527
  44.8 8.5 %collective-permute-start.15 = (f32[14,8,128]{2,1,0:T(8,128)S(1)}, f32[14,8,128]{2,1,0:T(8,128)S(1)}, u32[]{:S(2)}, u32[]{:S(2)}) collective-permute-start(f32[14,8,128]{2,1,0:T(8,128)S(1)} %get-tuple-element.177.own_ref), channel_id=1, source_target_pairs={{0,31},{1,2},{2,1},{3,4},{4,3},{5,6},{6,5},{7,8},{8,7},{9,10},{10,... | collective-permute-start | bytes 172040 | tf_op jit(solution)/shard_map/ppermute | solution.py:527
  49.4 4.4 %collective-permute-start.13 = (f32[14,8,128]{2,1,0:T(8,128)S(1)}, f32[14,8,128]{2,1,0:T(8,128)S(1)}, u32[]{:S(2)}, u32[]{:S(2)}) collective-permute-start(f32[14,8,128]{2,1,0:T(8,128)S(1)} %get-tuple-element.169.own_ref), channel_id=1, source_target_pairs={{0,1},{1,0},{2,3},{3,2},{4,5},{5,4},{6,7},{7,6},{8,9},{9,8},{10,11... | collective-permute-start | bytes 172040 | tf_op jit(solution)/shard_map/ppermute | solution.py:528
  53.3 4.4 %collective-permute-start.16 = (f32[14,8,128]{2,1,0:T(8,128)S(1)}, f32[14,8,128]{2,1,0:T(8,128)S(1)}, u32[]{:S(2)}, u32[]{:S(2)}) collective-permute-start(f32[14,8,128]{2,1,0:T(8,128)S(1)} %get-tuple-element.179.own_ref), channel_id=1, source_target_pairs={{0,1},{1,0},{2,3},{3,2},{4,5},{5,4},{6,7},{7,6},{8,9},{9,8},{10,11... | collective-permute-start | bytes 172040 | tf_op jit(solution)/shard_map/ppermute | solution.py:528
  53.9 8.5 %collective-permute-start.14 = (f32[14,8,128]{2,1,0:T(8,128)S(1)}, f32[14,8,128]{2,1,0:T(8,128)S(1)}, u32[]{:S(2)}, u32[]{:S(2)}) collective-permute-start(f32[14,8,128]{2,1,0:T(8,128)S(1)} %get-tuple-element.176.own_ref), channel_id=1, source_target_pairs={{0,31},{1,2},{2,1},{3,4},{4,3},{5,6},{6,5},{7,8},{8,7},{9,10},{10,... | collective-permute-start | bytes 172040 | tf_op jit(solution)/shard_map/ppermute | solution.py:527
  57.8 8.5 %collective-permute-start.18 = (f32[14,8,128]{2,1,0:T(8,128)S(1)}, f32[14,8,128]{2,1,0:T(8,128)S(1)}, u32[]{:S(2)}, u32[]{:S(2)}) collective-permute-start(f32[14,8,128]{2,1,0:T(8,128)S(1)} %get-tuple-element.196.own_ref), channel_id=1, source_target_pairs={{0,31},{1,2},{2,1},{3,4},{4,3},{5,6},{6,5},{7,8},{8,7},{9,10},{10,... | collective-permute-start | bytes 172040 | tf_op jit(solution)/shard_map/ppermute | solution.py:527
  62.4 4.3 %collective-permute-start.17 = (f32[14,8,128]{2,1,0:T(8,128)S(1)}, f32[14,8,128]{2,1,0:T(8,128)S(1)}, u32[]{:S(2)}, u32[]{:S(2)}) collective-permute-start(f32[14,8,128]{2,1,0:T(8,128)S(1)} %get-tuple-element.190.own_ref), channel_id=1, source_target_pairs={{0,1},{1,0},{2,3},{3,2},{4,5},{5,4},{6,7},{7,6},{8,9},{9,8},{10,11... | collective-permute-start | bytes 172040 | tf_op jit(solution)/shard_map/ppermute | solution.py:528

commit v11 on v10

--- a/solution.py
+++ b/solution.py
@@ -154,7 +154,7 @@
     for r, source in enumerate((scal_ref.at[0, near], scal_ref.at[1, near], mass_ref.at[near])):
         copies.append(pltpu.make_async_copy(source, near_buf.at[r], sems.at[1 + r]))
     sources = [scal_ref.at[0, far], scal_ref.at[1, far], mass_ref.at[far]]
-    sources += [tr_ref.at[r, far] for r in range(3)] + [tr_ref.at[r, near] for r in range(3)]
+    sources += [tr_ref.at[r, far] for r in range(3)]
     late = [
         pltpu.make_async_copy(source, raw_ref.at[r], sems.at[4 + r])
         for r, source in enumerate(sources)
@@ -187,7 +187,7 @@
     write(ev_ref, (), sum(planes + turned, []))
 
 
-def prepare(idx_ref, scal_ref, mass_ref, tr_ref, raw_ref,
+def prepare(idx_ref, scal_ref, mass_ref, tr_ref,
             gi_ref, q_ref, ri_ref, rt_ref, ti_ref, st_ref, tf_ref):
     parity = lax.axis_index("elem") % 2
     idx = idx_ref[...]
@@ -200,7 +200,7 @@
         return planes + [read(tr_ref, r, src) for r in range(3)]
 
     for r in range(3):
-        turned = [gather_lanes(v, idx) * signs[r] for v in read(raw_ref, 6 + r)]
+        turned = [gather_lanes(v, idx) * signs[r] for v in read(tr_ref, r, source_plane(parity, 0))]
         for j in range(8):
             tf_ref[8 * r + j] = turned[j]
     faces = [read(tr_ref, 0, source_plane(parity, face * ORDER)) for face in range(2)]
@@ -539,17 +539,17 @@
     stay = lambda x: pltpu.with_memory_space_constraint(x, pltpu.HBM)
     bundle = (3 * ROWS + 24, SUB, LANES)
     od, idx, slots, raw = call(
-        project_odd, [(3 * ROWS, SUB, LANES), (SUB, LANES), (SUB, LANES), (9,) + tile],
+        project_odd, [(3 * ROWS, SUB, LANES), (SUB, LANES), (SUB, LANES), (6,) + tile],
         (stay(element_order), stay(scal), stay(mas), stay(tr)), "project", 1, hbm=(0, 1, 2, 3),
         scratch=[pltpu.VMEM((1, LANES), jnp.int32), pltpu.VMEM((3,) + tile, f32),
-                 pltpu.SemaphoreType.DMA((13,))])
+                 pltpu.SemaphoreType.DMA((10,))])
     rod = swap_od(od)
     ev = call(project_even, [bundle], (idx, raw), "project", 1)
     rev = swap_ev(ev)
     gi, q, ri, rt, ti, st, tf = call(
         prepare,
         [inner, faces, (6,) + tile, (6,) + tile, (6, 2) + tile, (2,) + part, (24, SUB, LANES)],
-        (idx, scal, mas, tr, raw), "prepare", 1)
+        (idx, scal, mas, tr), "prepare", 1)
     rtf = swap_od(tf)
     p0, r0, cev = call(make_field_face(0), [face, part, sent], (od, rod, q, st), "odd", 3000)
     p7, r7, cod = call(make_field_face(1), [face, part, sent], (ev, rev, q, st), "even", 1)

time: 67.8 us -> 67.7 us (level)
  no operation moved by 1% of the time
where the time goes in v11:
time: 67.7 us; the launch traced here: 67.6 us
  starting transfers between devices  35.8 us (53%)
  waiting for transfers between devices  15.9 us (23%)
  Pallas kernels  15.5 us (23%)
    ppermute x10, starting transfers between devices, per_device(): swap_od = lambda x: lax.ppermute(x, 'elem', odd_pairs)  34.2 us
    pallas_call x33, Pallas kernels, call(): pl.pallas_call(kernel, out_shape=shapes[0] if single else shapes, in_spec...  15.5 us
    ppermute x10, waiting for transfers between devices, per_device(): swap_od = lambda x: lax.ppermute(x, 'elem', odd_pairs)  13.5 us
    ppermute x9, waiting for transfers between devices, per_device(): swap_ev = lambda x: lax.ppermute(x, 'elem', even_pairs)  2.39 us
    ppermute x9, starting transfers between devices, per_device(): swap_ev = lambda x: lax.ppermute(x, 'elem', even_pairs)  1.61 us
  transfers between devices with their start and end apart: 19, of which 12 were waited for; matrix products, arithmetic and copies ran while one was open for 0% of the time, Pallas kernels for 20%

profile of v11, /device:TPU:0, one launch (start us, length us, event | category | flops | bytes accessed | tf_op | source)
XLA Modules:
  0.0 67.6 jit_solution(7944837477557284246)
XLA Ops:
  0.0 1.3 %project.2 = (f32[21,8,128]{2,1,0:T(8,128)S(1)}, s32[8,128]{1,0:T(8,128)S(1)}, s32[8,128]{1,0:T(8,128)S(1)}, f32[6,8,8,128]{3,2,1,0:T(8,128)S(1)}) custom-call(s32[1,128]{1,0:T(1,128)} %order_ref.1, f32[2,8,8,8,128]{4,3,2,1,0:T(8,128)} %bitcast.6, f32[8,8,8,128]{3,2,1,0:T(8,128)} %bitcast.8, f32[3,8,8,8,128]{4,3,2,1,0:T(8,128)} %bitcast.4), custom_call_target="tpu_custom_call" | custom-call | flops 1000000 | bytes 1024 | tf_op jit(solution)/shard_map/project/pallas_call | solution.py:508
  1.3 6.7 %collective-permute-start.2 = (f32[21,8,128]{2,1,0:T(8,128)S(1)}, f32[21,8,128]{2,1,0:T(8,128)S(1)}, u32[]{:S(2)}, u32[]{:S(2)}) collective-permute-start(f32[21,8,128]{2,1,0:T(8,128)S(1)} %get-tuple-element.108.own_ref), channel_id=1, source_target_pairs={{0,31},{1,2},{2,1},{3,4},{4,3},{5,6},{6,5},{7,8},{8,7},{9,10},{10,... | collective-permute-start | bytes 258056 | tf_op jit(solution)/shard_map/ppermute | solution.py:527
  8.4 3.0 %prepare.1 = (f32[2,6,8,8,128]{4,3,2,1,0:T(8,128)S(1)}, f32[2,2,7,8,128]{4,3,2,1,0:T(8,128)S(1)}, f32[6,8,8,128]{3,2,1,0:T(8,128)S(1)}, f32[6,8,8,128]{3,2,1,0:T...) custom-call(s32[8,128]{1,0:T(8,128)S(1)} %get-tuple-element.103.idx_ref, ...), custom_call_target="tpu_custom_call" | custom-call | flops 1000000 | bytes 1024 | tf_op jit(solution)/shard_map/prepare/pallas_call | solution.py:508
  11.4 1.4 %collective-permute-start.4 = (f32[24,8,128]{2,1,0:T(8,128)S(1)}, f32[24,8,128]{2,1,0:T(8,128)S(1)}, u32[]{:S(2)}, u32[]{:S(2)}) collective-permute-start(f32[24,8,128]{2,1,0:T(8,128)S(1)} %get-tuple-element.124.refs_9_), channel_id=1, source_target_pairs={{0,31},{1,2},{2,1},{3,4},{4,3},{5,6},{6,5},{7,8},{8,7},{9,10},{10,... | collective-permute-start | bytes 294920 | tf_op jit(solution)/shard_map/ppermute | solution.py:527
  12.9 0.8 %collective-permute-start.3 = (f32[14,8,128]{2,1,0:T(8,128)S(1)}, f32[14,8,128]{2,1,0:T(8,128)S(1)}, u32[]{:S(2)}, u32[]{:S(2)}) collective-permute-start(f32[14,8,128]{2,1,0:T(8,128)S(1)} %get-tuple-element.109.own_ref), channel_id=1, source_target_pairs={{0,1},{1,0},{2,3},{3,2},{4,5},{5,4},{6,7},{7,6},{8,9},{9,8},{10,11... | collective-permute-start | bytes 172040 | tf_op jit(solution)/shard_map/ppermute | solution.py:528
  13.6 0.9 %collective-permute-done.got_ref.refs_6_ = f32[45,8,128]{2,1,0:T(8,128)S(1)} collective-permute-done((f32[45,8,128]{2,1,0:T(8,128)S(1)}, f32[45,8,128]{2,1,0:T(8,128)S(1)}, u32[]{:S(2)}, u32[]{:S(2)}) %collective-permute-start) | collective-permute-done | bytes 184352 | tf_op jit(solution)/shard_map/ppermute | solution.py:528
  14.5 3.5 %collective-permute-start.1 = (f32[14,8,128]{2,1,0:T(8,128)S(1)}, f32[14,8,128]{2,1,0:T(8,128)S(1)}, u32[]{:S(2)}, u32[]{:S(2)}) collective-permute-start(f32[14,8,128]{2,1,0:T(8,128)S(1)} %get-tuple-element.107.own_ref), channel_id=1, source_target_pairs={{0,31},{1,2},{2,1},{3,4},{4,3},{5,6},{6,5},{7,8},{8,7},{9,10},{10,... | collective-permute-start | bytes 172040 | tf_op jit(solution)/shard_map/ppermute | solution.py:527
  18.0 0.9 %first.4 = (f32[2,6,8,8,128]{4,3,2,1,0:T(8,128)S(1)}, f32[2,6,8,8,128]{4,3,2,1,0:T(8,128)S(1)}, f32[2,2,7,8,128]{4,3,2,1,0:T(8,128)S(1)}, f32[2,7,8,128]{3,2,1,0...) custom-call(f32[2,7,8,128]{3,2,1,0:T(8,128)S(1)} %get-tuple-element.110.refs_0_.refs_7_.p0_ref, ...), custom_call_target="tpu_custom_call" | custom-call | flops 1000000000 | bytes 1024 | tf_op jit(solution)/shard_map/first/pallas_call | solution.py:508
  19.0 3.2 %collective-permute-start.7 = (f32[14,8,128]{2,1,0:T(8,128)S(1)}, f32[14,8,128]{2,1,0:T(8,128)S(1)}, u32[]{:S(2)}, u32[]{:S(2)}) collective-permute-start(f32[14,8,128]{2,1,0:T(8,128)S(1)} %get-tuple-element.135.own_ref), channel_id=1, source_target_pairs={{0,31},{1,2},{2,1},{3,4},{4,3},{5,6},{6,5},{7,8},{8,7},{9,10},{10,... | collective-permute-start | bytes 172040 | tf_op jit(solution)/shard_map/ppermute | solution.py:527
  22.2 0.9 %between.4 = (f32[2,6,8,8,128]{4,3,2,1,0:T(8,128)S(1)}, f32[2,7,8,128]{3,2,1,0:T(8,128)S(1)}, f32[2,7,8,128]{3,2,1,0:T(8,128)S(1)}, f32[3,8,8,128]{3,2,1,0:T(8,128)S(1)}) custom-call(f32[2,7,8,128]{3,2,1,0:T(8,128)S(1)} %get-tuple-element.121.refs_0_.m7_ref, f32[2,6,8,8,128]{4,3,2,1,0:T(8,128)S(1)} %get-tuple-element.122.refs_1_, ...), custom_call_target="tpu_custom_call" | custom-call | flops 2000000000 | bytes 1024 | tf_op jit(solution)/shard_map/between/pallas_call | solution.py:508
  23.2 1.0 %second.3 = (f32[2,6,8,8,128]{4,3,2,1,0:T(8,128)S(1)}, f32[2,2,7,8,128]{4,3,2,1,0:T(8,128)S(1)}, f32[2,6,8,8,128]{4,3,2,1,0:T(8,128)S(1)}, f32[2,2,7,8,128]{4,3,...) custom-call(f32[2,7,8,128]{3,2,1,0:T(8,128)S(1)} %get-tuple-element.128.m0_ref, ...), custom_call_target="tpu_custom_call" | custom-call | flops 3000000000 | bytes 1024 | tf_op jit(solution)/shard_map/second/pallas_call | solution.py:508
  24.1 3.3 %collective-permute-done.7.got_ref = f32[14,8,128]{2,1,0:T(8,128)S(1)} collective-permute-done((f32[14,8,128]{2,1,0:T(8,128)S(1)}, f32[14,8,128]{2,1,0:T(8,128)S(1)}, u32[]{:S(2)}, u32[]{:S(2)}) %collective-permute-start.7) | collective-permute-done | bytes 57376 | tf_op jit(solution)/shard_map/ppermute | solution.py:527
  27.6 3.4 %collective-permute-start.6 = (f32[14,8,128]{2,1,0:T(8,128)S(1)}, f32[14,8,128]{2,1,0:T(8,128)S(1)}, u32[]{:S(2)}, u32[]{:S(2)}) collective-permute-start(f32[14,8,128]{2,1,0:T(8,128)S(1)} %get-tuple-element.134.own_ref), channel_id=1, source_target_pairs={{0,31},{1,2},{2,1},{3,4},{4,3},{5,6},{6,5},{7,8},{8,7},{9,10},{10,... | collective-permute-start | bytes 172040 | tf_op jit(solution)/shard_map/ppermute | solution.py:527
  31.8 3.2 %collective-permute-start.11 = (f32[14,8,128]{2,1,0:T(8,128)S(1)}, f32[14,8,128]{2,1,0:T(8,128)S(1)}, u32[]{:S(2)}, u32[]{:S(2)}) collective-permute-start(f32[14,8,128]{2,1,0:T(8,128)S(1)} %get-tuple-element.156.own_ref), channel_id=1, source_target_pairs={{0,31},{1,2},{2,1},{3,4},{4,3},{5,6},{6,5},{7,8},{8,7},{9,10},{10,... | collective-permute-start | bytes 172040 | tf_op jit(solution)/shard_map/ppermute | solution.py:527
  34.9 0.9 %between.5 = (f32[2,6,8,8,128]{4,3,2,1,0:T(8,128)S(1)}, f32[2,7,8,128]{3,2,1,0:T(8,128)S(1)}, f32[2,7,8,128]{3,2,1,0:T(8,128)S(1)}) custom-call(f32[2,7,8,128]{3,2,1,0:T(8,128)S(1)} %get-tuple-element.145.refs_0_.m7_ref, f32[2,6,8,8,128]{4,3,2,1,0:T(8,128)S(1)} %get-tuple-element.146.refs_1_, f32[3,8,8,128]{3,2,1,0:T(8,128)S(1)} %get-tuple-element.123.refs_2_.refs_7_, ...), custom_call_target="tpu_custom_call" | custom-call | flops 2000000000 | bytes 1024 | tf_op jit(solution)/shard_map/between/pallas_call | solution.py:508
  35.8 0.8 %collective-permute-done.6.got_ref = f32[14,8,128]{2,1,0:T(8,128)S(1)} collective-permute-done((f32[14,8,128]{2,1,0:T(8,128)S(1)}, f32[14,8,128]{2,1,0:T(8,128)S(1)}, u32[]{:S(2)}, u32[]{:S(2)}) %collective-permute-start.6) | collective-permute-done | bytes 57376 | tf_op jit(solution)/shard_map/ppermute | solution.py:527
  36.7 1.0 %second.4 = (f32[2,6,8,8,128]{4,3,2,1,0:T(8,128)S(1)}, f32[2,2,7,8,128]{4,3,2,1,0:T(8,128)S(1)}, f32[2,6,8,8,128]{4,3,2,1,0:T(8,128)S(1)}, f32[2,2,7,8,128]{4,3,...) custom-call(f32[2,7,8,128]{3,2,1,0:T(8,128)S(1)} %get-tuple-element.150.m0_ref, ...), custom_call_target="tpu_custom_call" | custom-call | flops 3000000000 | bytes 1024 | tf_op jit(solution)/shard_map/second/pallas_call | solution.py:508
  37.7 2.6 %collective-permute-done.11.got_ref = f32[14,8,128]{2,1,0:T(8,128)S(1)} collective-permute-done((f32[14,8,128]{2,1,0:T(8,128)S(1)}, f32[14,8,128]{2,1,0:T(8,128)S(1)}, u32[]{:S(2)}, u32[]{:S(2)}) %collective-permute-start.11) | collective-permute-done | bytes 57376 | tf_op jit(solution)/shard_map/ppermute | solution.py:527
  40.4 0.5 collective-permute-done.9.got_ref
  40.9 3.5 %collective-permute-start.10 = (f32[14,8,128]{2,1,0:T(8,128)S(1)}, f32[14,8,128]{2,1,0:T(8,128)S(1)}, u32[]{:S(2)}, u32[]{:S(2)}) collective-permute-start(f32[14,8,128]{2,1,0:T(8,128)S(1)} %get-tuple-element.155.own_ref), channel_id=1, source_target_pairs={{0,31},{1,2},{2,1},{3,4},{4,3},{5,6},{6,5},{7,8},{8,7},{9,10},{10,... | collective-permute-start | bytes 172040 | tf_op jit(solution)/shard_map/ppermute | solution.py:527
  44.8 2.9 %collective-permute-start.15 = (f32[14,8,128]{2,1,0:T(8,128)S(1)}, f32[14,8,128]{2,1,0:T(8,128)S(1)}, u32[]{:S(2)}, u32[]{:S(2)}) collective-permute-start(f32[14,8,128]{2,1,0:T(8,128)S(1)} %get-tuple-element.177.own_ref), channel_id=1, source_target_pairs={{0,31},{1,2},{2,1},{3,4},{4,3},{5,6},{6,5},{7,8},{8,7},{9,10},{10,... | collective-permute-start | bytes 172040 | tf_op jit(solution)/shard_map/ppermute | solution.py:527
  47.7 0.9 %between.6 = (f32[2,6,8,8,128]{4,3,2,1,0:T(8,128)S(1)}, f32[2,7,8,128]{3,2,1,0:T(8,128)S(1)}, f32[2,7,8,128]{3,2,1,0:T(8,128)S(1)}) custom-call(f32[2,7,8,128]{3,2,1,0:T(8,128)S(1)} %get-tuple-element.166.refs_0_.m7_ref, f32[2,6,8,8,128]{4,3,2,1,0:T(8,128)S(1)} %get-tuple-element.167.refs_1_, f32[3,8,8,128]{3,2,1,0:T(8,128)S(1)} %get-tuple-element.123.refs_2_.refs_7_, ...), custom_call_target="tpu_custom_call" | custom-call | flops 2000000000 | bytes 1024 | tf_op jit(solution)/shard_map/between/pallas_call | solution.py:508
  48.6 0.8 %collective-permute-done.10.got_ref = f32[14,8,128]{2,1,0:T(8,128)S(1)} collective-permute-done((f32[14,8,128]{2,1,0:T(8,128)S(1)}, f32[14,8,128]{2,1,0:T(8,128)S(1)}, u32[]{:S(2)}, u32[]{:S(2)}) %collective-permute-start.10) | collective-permute-done | bytes 57376 | tf_op jit(solution)/shard_map/ppermute | solution.py:527
  49.7 0.9 %second.5 = (f32[2,6,8,8,128]{4,3,2,1,0:T(8,128)S(1)}, f32[2,2,7,8,128]{4,3,2,1,0:T(8,128)S(1)}, f32[2,6,8,8,128]{4,3,2,1,0:T(8,128)S(1)}, f32[2,2,7,8,128]{4,3,...) custom-call(f32[2,7,8,128]{3,2,1,0:T(8,128)S(1)} %get-tuple-element.171.m0_ref, ...), custom_call_target="tpu_custom_call" | custom-call | flops 3000000000 | bytes 1024 | tf_op jit(solution)/shard_map/second/pallas_call | solution.py:508
  50.6 2.7 %collective-permute-done.15.got_ref = f32[14,8,128]{2,1,0:T(8,128)S(1)} collective-permute-done((f32[14,8,128]{2,1,0:T(8,128)S(1)}, f32[14,8,128]{2,1,0:T(8,128)S(1)}, u32[]{:S(2)}, u32[]{:S(2)}) %collective-permute-start.15) | collective-permute-done | bytes 57376 | tf_op jit(solution)/shard_map/ppermute | solution.py:527
  53.9 3.5 %collective-permute-start.14 = (f32[14,8,128]{2,1,0:T(8,128)S(1)}, f32[14,8,128]{2,1,0:T(8,128)S(1)}, u32[]{:S(2)}, u32[]{:S(2)}) collective-permute-start(f32[14,8,128]{2,1,0:T(8,128)S(1)} %get-tuple-element.176.own_ref), channel_id=1, source_target_pairs={{0,31},{1,2},{2,1},{3,4},{4,3},{5,6},{6,5},{7,8},{8,7},{9,10},{10,... | collective-permute-start | bytes 172040 | tf_op jit(solution)/shard_map/ppermute | solution.py:527
  57.8 2.9 %collective-permute-start.18 = (f32[14,8,128]{2,1,0:T(8,128)S(1)}, f32[14,8,128]{2,1,0:T(8,128)S(1)}, u32[]{:S(2)}, u32[]{:S(2)}) collective-permute-start(f32[14,8,128]{2,1,0:T(8,128)S(1)} %get-tuple-element.196.own_ref), channel_id=1, source_target_pairs={{0,31},{1,2},{2,1},{3,4},{4,3},{5,6},{6,5},{7,8},{8,7},{9,10},{10,... | collective-permute-start | bytes 172040 | tf_op jit(solution)/shard_map/ppermute | solution.py:527
  60.7 0.9 %between.7 = (f32[2,6,8,8,128]{4,3,2,1,0:T(8,128)S(1)}, f32[2,7,8,128]{3,2,1,0:T(8,128)S(1)}, f32[2,7,8,128]{3,2,1,0:T(8,128)S(1)}) custom-call(f32[2,7,8,128]{3,2,1,0:T(8,128)S(1)} %get-tuple-element.187.refs_0_.m7_ref, f32[2,6,8,8,128]{4,3,2,1,0:T(8,128)S(1)} %get-tuple-element.188.refs_1_, f32[3,8,8,128]{3,2,1,0:T(8,128)S(1)} %get-tuple-element.123.refs_2_.refs_7_, ...), custom_call_target="tpu_custom_call" | custom-call | flops 2000000000 | bytes 1024 | tf_op jit(solution)/shard_map/between/pallas_call | solution.py:508
  61.6 0.8 %collective-permute-done.14.got_ref = f32[14,8,128]{2,1,0:T(8,128)S(1)} collective-permute-done((f32[14,8,128]{2,1,0:T(8,128)S(1)}, f32[14,8,128]{2,1,0:T(8,128)S(1)}, u32[]{:S(2)}, u32[]{:S(2)}) %collective-permute-start.14) | collective-permute-done | bytes 57376 | tf_op jit(solution)/shard_map/ppermute | solution.py:527
  62.5 1.1 %last.1 = (f32[2,8,8,8,128]{4,3,2,1,0:T(8,128)}, f32[2,2,7,8,128]{4,3,2,1,0:T(8,128)S(1)}, f32[2,7,8,128]{3,2,1,0:T(8,128)S(1)}) custom-call(s32[8,128]{1,0:T(8,128)S(1)} %get-tuple-element.102.slot_ref, f32[2,7,8,128]{3,2,1,0:T(8,128)S(1)} %get-tuple-element.192.m0_ref, f32[2,7,8,128]{3,2,1,0:T(8,128)S(1)} %get-tuple-element.187.refs_0_.m7_ref, ...), custom_call_target="tpu_custom_call" | custom-call | flops 3000000000 | bytes 1024 | tf_op jit(solution)/shard_map/last/pallas_call | solution.py:508
  63.6 2.6 %collective-permute-done.18.got_ref = f32[14,8,128]{2,1,0:T(8,128)S(1)} collective-permute-done((f32[14,8,128]{2,1,0:T(8,128)S(1)}, f32[14,8,128]{2,1,0:T(8,128)S(1)}, u32[]{:S(2)}, u32[]{:S(2)}) %collective-permute-start.18) | collective-permute-done | bytes 57376 | tf_op jit(solution)/shard_map/ppermute | solution.py:527
  66.6 0.8 %finish.3 = f32[2,8,8,8,128]{4,3,2,1,0:T(8,128)} custom-call(s32[8,128]{1,0:T(8,128)S(1)} %get-tuple-element.102.slot_ref, f32[14,8,128]{2,1,0:T(8,128)S(1)} %get-tuple-element.190.own_ref, f32[14,8,128]{2,1,0:T(8,128)S(1)} %collective-permute-done.17.got_ref, f32[2,7,8,128]{3,2,1,0:T(8,128)S(1)} %get-tuple-element.191.e_ref, ...), custom_call_target="tpu_custom_call", output_to_operand_aliasing={{}: (6, {})} | custom-call | flops 1000000 | bytes 1024 | tf_op jit(solution)/shard_map/finish/pallas_call | solution.py:508
  (45 shorter events, 3.8 us)
Async XLA Ops:
  0.0 8.4 %copy-start = (f32[3,512,128]{2,1,0:T(8,128)S(1)}, f32[3,512,128]{2,1,0:T(8,128)}, u32[]{:S(2)}) copy-start(f32[3,512,128]{2,1,0:T(8,128)} %param.5) | copy-start | bytes 2359300
  0.0 8.4 %copy-start.1 = (f32[2,512,128]{2,1,0:T(8,128)S(1)}, f32[2,512,128]{2,1,0:T(8,128)}, u32[]{:S(2)}) copy-start(f32[2,512,128]{2,1,0:T(8,128)} %param.4) | copy-start | bytes 1572868
  1.3 7.1 %copy-start.2 = (f32[512,128]{1,0:T(8,128)S(1)}, f32[512,128]{1,0:T(8,128)}, u32[]{:S(2)}) copy-start(f32[512,128]{1,0:T(8,128)} %param.6) | copy-start | bytes 786436
  1.3 11.5 %collective-permute-start.2 = (f32[21,8,128]{2,1,0:T(8,128)S(1)}, f32[21,8,128]{2,1,0:T(8,128)S(1)}, u32[]{:S(2)}, u32[]{:S(2)}) collective-permute-start(f32[21,8,128]{2,1,0:T(8,128)S(1)} %get-tuple-element.108.own_ref), channel_id=1, source_target_pairs={{0,31},{1,2},{2,1},{3,4},{4,3},{5,6},{6,5},{7,8},{8,7},{9,10},{10,... | collective-permute-start | bytes 258056 | tf_op jit(solution)/shard_map/ppermute | solution.py:527
  8.3 6.2 %collective-permute-start = (f32[45,8,128]{2,1,0:T(8,128)S(1)}, f32[45,8,128]{2,1,0:T(8,128)S(1)}, u32[]{:S(2)}, u32[]{:S(2)}) collective-permute-start(f32[45,8,128]{2,1,0:T(8,128)S(1)} %project.3.own_ref.refs_5_), channel_id=1, source_target_pairs={{0,1},{1,0},{2,3},{3,2},{4,5},{5,4},{6,7},{7,6},{8,9},{9,8},{10,11... | collective-permute-start | bytes 552968 | tf_op jit(solution)/shard_map/ppermute | solution.py:528
  11.4 10.7 %collective-permute-start.4 = (f32[24,8,128]{2,1,0:T(8,128)S(1)}, f32[24,8,128]{2,1,0:T(8,128)S(1)}, u32[]{:S(2)}, u32[]{:S(2)}) collective-permute-start(f32[24,8,128]{2,1,0:T(8,128)S(1)} %get-tuple-element.124.refs_9_), channel_id=1, source_target_pairs={{0,31},{1,2},{2,1},{3,4},{4,3},{5,6},{6,5},{7,8},{8,7},{9,10},{10,... | collective-permute-start | bytes 294920 | tf_op jit(solution)/shard_map/ppermute | solution.py:527
  12.9 6.1 %collective-permute-start.3 = (f32[14,8,128]{2,1,0:T(8,128)S(1)}, f32[14,8,128]{2,1,0:T(8,128)S(1)}, u32[]{:S(2)}, u32[]{:S(2)}) collective-permute-start(f32[14,8,128]{2,1,0:T(8,128)S(1)} %get-tuple-element.109.own_ref), channel_id=1, source_target_pairs={{0,1},{1,0},{2,3},{3,2},{4,5},{5,4},{6,7},{7,6},{8,9},{9,8},{10,11... | collective-permute-start | bytes 172040 | tf_op jit(solution)/shard_map/ppermute | solution.py:528
  14.5 8.5 %collective-permute-start.1 = (f32[14,8,128]{2,1,0:T(8,128)S(1)}, f32[14,8,128]{2,1,0:T(8,128)S(1)}, u32[]{:S(2)}, u32[]{:S(2)}) collective-permute-start(f32[14,8,128]{2,1,0:T(8,128)S(1)} %get-tuple-element.107.own_ref), channel_id=1, source_target_pairs={{0,31},{1,2},{2,1},{3,4},{4,3},{5,6},{6,5},{7,8},{8,7},{9,10},{10,... | collective-permute-start | bytes 172040 | tf_op jit(solution)/shard_map/ppermute | solution.py:527
  19.0 8.5 %collective-permute-start.7 = (f32[14,8,128]{2,1,0:T(8,128)S(1)}, f32[14,8,128]{2,1,0:T(8,128)S(1)}, u32[]{:S(2)}, u32[]{:S(2)}) collective-permute-start(f32[14,8,128]{2,1,0:T(8,128)S(1)} %get-tuple-element.135.own_ref), channel_id=1, source_target_pairs={{0,31},{1,2},{2,1},{3,4},{4,3},{5,6},{6,5},{7,8},{8,7},{9,10},{10,... | collective-permute-start | bytes 172040 | tf_op jit(solution)/shard_map/ppermute | solution.py:527
  23.1 4.5 %collective-permute-start.5 = (f32[14,8,128]{2,1,0:T(8,128)S(1)}, f32[14,8,128]{2,1,0:T(8,128)S(1)}, u32[]{:S(2)}, u32[]{:S(2)}) collective-permute-start(f32[14,8,128]{2,1,0:T(8,128)S(1)} %get-tuple-element.126.own_ref), channel_id=1, source_target_pairs={{0,1},{1,0},{2,3},{3,2},{4,5},{5,4},{6,7},{7,6},{8,9},{9,8},{10,11... | collective-permute-start | bytes 172040 | tf_op jit(solution)/shard_map/ppermute | solution.py:528
  27.5 4.3 %collective-permute-start.8 = (f32[14,8,128]{2,1,0:T(8,128)S(1)}, f32[14,8,128]{2,1,0:T(8,128)S(1)}, u32[]{:S(2)}, u32[]{:S(2)}) collective-permute-start(f32[14,8,128]{2,1,0:T(8,128)S(1)} %get-tuple-element.137.own_ref), channel_id=1, source_target_pairs={{0,1},{1,0},{2,3},{3,2},{4,5},{5,4},{6,7},{7,6},{8,9},{9,8},{10,11... | collective-permute-start | bytes 172040 | tf_op jit(solution)/shard_map/ppermute | solution.py:528
  27.6 9.0 %collective-permute-start.6 = (f32[14,8,128]{2,1,0:T(8,128)S(1)}, f32[14,8,128]{2,1,0:T(8,128)S(1)}, u32[]{:S(2)}, u32[]{:S(2)}) collective-permute-start(f32[14,8,128]{2,1,0:T(8,128)S(1)} %get-tuple-element.134.own_ref), channel_id=1, source_target_pairs={{0,31},{1,2},{2,1},{3,4},{4,3},{5,6},{6,5},{7,8},{8,7},{9,10},{10,... | collective-permute-start | bytes 172040 | tf_op jit(solution)/shard_map/ppermute | solution.py:527
  31.8 8.5 %collective-permute-start.11 = (f32[14,8,128]{2,1,0:T(8,128)S(1)}, f32[14,8,128]{2,1,0:T(8,128)S(1)}, u32[]{:S(2)}, u32[]{:S(2)}) collective-permute-start(f32[14,8,128]{2,1,0:T(8,128)S(1)} %get-tuple-element.156.own_ref), channel_id=1, source_target_pairs={{0,31},{1,2},{2,1},{3,4},{4,3},{5,6},{6,5},{7,8},{8,7},{9,10},{10,... | collective-permute-start | bytes 172040 | tf_op jit(solution)/shard_map/ppermute | solution.py:527
  36.6 4.3 %collective-permute-start.9 = (f32[14,8,128]{2,1,0:T(8,128)S(1)}, f32[14,8,128]{2,1,0:T(8,128)S(1)}, u32[]{:S(2)}, u32[]{:S(2)}) collective-permute-start(f32[14,8,128]{2,1,0:T(8,128)S(1)} %get-tuple-element.148.own_ref), channel_id=1, source_target_pairs={{0,1},{1,0},{2,3},{3,2},{4,5},{5,4},{6,7},{7,6},{8,9},{9,8},{10,11... | collective-permute-start | bytes 172040 | tf_op jit(solution)/shard_map/ppermute | solution.py:528
  40.3 4.5 %collective-permute-start.12 = (f32[14,8,128]{2,1,0:T(8,128)S(1)}, f32[14,8,128]{2,1,0:T(8,128)S(1)}, u32[]{:S(2)}, u32[]{:S(2)}) collective-permute-start(f32[14,8,128]{2,1,0:T(8,128)S(1)} %get-tuple-element.158.own_ref), channel_id=1, source_target_pairs={{0,1},{1,0},{2,3},{3,2},{4,5},{5,4},{6,7},{7,6},{8,9},{9,8},{10,11... | collective-permute-start | bytes 172040 | tf_op jit(solution)/shard_map/ppermute | solution.py:528
  40.9 8.5 %collective-permute-start.10 = (f32[14,8,128]{2,1,0:T(8,128)S(1)}, f32[14,8,128]{2,1,0:T(8,128)S(1)}, u32[]{:S(2)}, u32[]{:S(2)}) collective-permute-start(f32[14,8,128]{2,1,0:T(8,128)S(1)} %get-tuple-element.155.own_ref), channel_id=1, source_target_pairs={{0,31},{1,2},{2,1},{3,4},{4,3},{5,6},{6,5},{7,8},{8,7},{9,10},{10,... | collective-permute-start | bytes 172040 | tf_op jit(solution)/shard_map/ppermute | solution.py:527
  44.8 8.5 %collective-permute-start.15 = (f32[14,8,128]{2,1,0:T(8,128)S(1)}, f32[14,8,128]{2,1,0:T(8,128)S(1)}, u32[]{:S(2)}, u32[]{:S(2)}) collective-permute-start(f32[14,8,128]{2,1,0:T(8,128)S(1)} %get-tuple-element.177.own_ref), channel_id=1, source_target_pairs={{0,31},{1,2},{2,1},{3,4},{4,3},{5,6},{6,5},{7,8},{8,7},{9,10},{10,... | collective-permute-start | bytes 172040 | tf_op jit(solution)/shard_map/ppermute | solution.py:527
  49.4 4.4 %collective-permute-start.13 = (f32[14,8,128]{2,1,0:T(8,128)S(1)}, f32[14,8,128]{2,1,0:T(8,128)S(1)}, u32[]{:S(2)}, u32[]{:S(2)}) collective-permute-start(f32[14,8,128]{2,1,0:T(8,128)S(1)} %get-tuple-element.169.own_ref), channel_id=1, source_target_pairs={{0,1},{1,0},{2,3},{3,2},{4,5},{5,4},{6,7},{7,6},{8,9},{9,8},{10,11... | collective-permute-start | bytes 172040 | tf_op jit(solution)/shard_map/ppermute | solution.py:528
  53.3 4.4 %collective-permute-start.16 = (f32[14,8,128]{2,1,0:T(8,128)S(1)}, f32[14,8,128]{2,1,0:T(8,128)S(1)}, u32[]{:S(2)}, u32[]{:S(2)}) collective-permute-start(f32[14,8,128]{2,1,0:T(8,128)S(1)} %get-tuple-element.179.own_ref), channel_id=1, source_target_pairs={{0,1},{1,0},{2,3},{3,2},{4,5},{5,4},{6,7},{7,6},{8,9},{9,8},{10,11... | collective-permute-start | bytes 172040 | tf_op jit(solution)/shard_map/ppermute | solution.py:528
  53.9 8.5 %collective-permute-start.14 = (f32[14,8,128]{2,1,0:T(8,128)S(1)}, f32[14,8,128]{2,1,0:T(8,128)S(1)}, u32[]{:S(2)}, u32[]{:S(2)}) collective-permute-start(f32[14,8,128]{2,1,0:T(8,128)S(1)} %get-tuple-element.176.own_ref), channel_id=1, source_target_pairs={{0,31},{1,2},{2,1},{3,4},{4,3},{5,6},{6,5},{7,8},{8,7},{9,10},{10,... | collective-permute-start | bytes 172040 | tf_op jit(solution)/shard_map/ppermute | solution.py:527
  57.8 8.5 %collective-permute-start.18 = (f32[14,8,128]{2,1,0:T(8,128)S(1)}, f32[14,8,128]{2,1,0:T(8,128)S(1)}, u32[]{:S(2)}, u32[]{:S(2)}) collective-permute-start(f32[14,8,128]{2,1,0:T(8,128)S(1)} %get-tuple-element.196.own_ref), channel_id=1, source_target_pairs={{0,31},{1,2},{2,1},{3,4},{4,3},{5,6},{6,5},{7,8},{8,7},{9,10},{10,... | collective-permute-start | bytes 172040 | tf_op jit(solution)/shard_map/ppermute | solution.py:527
  62.4 4.3 %collective-permute-start.17 = (f32[14,8,128]{2,1,0:T(8,128)S(1)}, f32[14,8,128]{2,1,0:T(8,128)S(1)}, u32[]{:S(2)}, u32[]{:S(2)}) collective-permute-start(f32[14,8,128]{2,1,0:T(8,128)S(1)} %get-tuple-element.190.own_ref), channel_id=1, source_target_pairs={{0,1},{1,0},{2,3},{3,2},{4,5},{5,4},{6,7},{7,6},{8,9},{9,8},{10,11... | collective-permute-start | bytes 172040 | tf_op jit(solution)/shard_map/ppermute | solution.py:528
